TPU v7x, 256 devices: a whole 4x4x8 slice. The times are simulated.
256 devices in a mesh: row: 32 (over x_lo, z, core), blk: 8 (over y, x_hi).
Axes of the slice: x: 4 (x_hi: 2, x_lo: 2; x = x_hi * 2 + x_lo), y: 4, z: 8, core: 2. Of those that a mesh axis runs over, the one named last changes fastest.
Arguments:
- embeddings: bfloat16 [65536, 192], P(('row', 'blk')), may hold values from -30 to 30
- vectors: float32 [65536, 16], P(('row', 'blk')), may hold values from -6 to 6
Outputs:
- basis: float32 [65536, 16], P(('row', 'blk'))
- triangle: float32 [16, 16], replicated
All inputs are finite; a program needn't handle non-finite values.
Results may differ from a plain program's by a relative error of at most 0.0088.
Values may be sent and summed in bfloat16 or wider, within the bound.
No kernel may reach another device: no remote copies, remote signals or barrier semaphores. Data moves between devices by JAX's collectives and lax.ppermute only.
A program may use at most 64 MiB of HBM per device.

v0:
```python
import functools
import math

import jax
import jax.numpy as jnp
from jax import lax
from jax.sharding import Mesh
from jax.sharding import PartitionSpec as P

ROW_BLK = ("row_0", "row_1", "row_2", "blk_0", "blk_1")
ROW = ("row_0", "row_1", "row_2")
BLK = ("blk_0", "blk_1")


sharpness = 10.0
epsilon = 1e-06


def one_axis_at_a_time(shard, axes):
    return functools.reduce(lax.psum, axes, shard)


def joined_along(tiles, dim):
    tiles = jnp.moveaxis(tiles, 0, dim)
    lengths = tiles.shape
    return tiles.reshape(*lengths[:dim], lengths[dim] * lengths[dim + 1], *lengths[dim + 2 :])


def gather_in_order(shard, axes, turns):
    tiles = shard
    for k in turns:
        tiles = lax.all_gather(tiles, axes[k])
    done = turns[::-1]
    back = [done.index(k) for k in range(len(axes))]
    tiles = tiles.transpose(*back, *range(len(axes), tiles.ndim))
    return tiles.reshape(-1, *shard.shape)


def gather_axes(shard, axes, turns, dim):
    return joined_along(gather_in_order(shard, axes, turns), dim)


def sent_to_all(shard, axis):
    copies = jnp.broadcast_to(shard, (lax.axis_size(axis), *shard.shape))
    return lax.all_to_all(copies, axis, split_axis=0, concat_axis=0, tiled=True)


def collect(shard, axis, dim):
    return joined_along(sent_to_all(shard, axis), dim)


def in_blocks(shard, dim, count):
    before, after = (shard.shape[:dim], shard.shape[dim + 1 :])
    return jnp.moveaxis(shard.reshape(*before, count, -1, *after), dim, 0)


def sent_and_summed(shard, axis, dim):
    count = lax.axis_size(axis)
    tiles = lax.all_to_all(in_blocks(shard, dim, count), axis, 0, 0, tiled=True)
    return jnp.sum(tiles, axis=0)


def sent_together(arrays, axis, dim, along):
    widths = [a.shape[along] for a in arrays]
    both = jnp.concatenate(arrays, axis=along)
    filled = lax.all_gather(both, axis, axis=dim, tiled=True)
    return tuple(jnp.split(filled, [sum(widths[:k]) for k in range(1, len(widths))], axis=along))


def normalize(embeddings):
    values = embeddings.astype(jnp.float32)
    return (values * lax.rsqrt(jnp.sum(values * values, axis=1, keepdims=True) + epsilon)).astype(
        jnp.bfloat16
    )


def affinity(block_rows, columns):
    scores = lax.dot_general(
        block_rows, columns, (((1,), (1,)), ((), ())), preferred_element_type=jnp.float32
    )
    return jnp.exp(sharpness * (scores - 1.0))


def row_blocks(panel):
    return panel.reshape(-1, math.gcd(panel.shape[0], 512), panel.shape[1])


def panel_degree(blocks, columns):

    def one_block(block_rows):
        return jnp.sum(affinity(block_rows, columns), axis=1)

    return lax.map(one_block, blocks).reshape(-1)


def panel_apply(blocks, columns, weights):

    def one_block(block_rows):
        tile = affinity(block_rows, columns).astype(jnp.bfloat16)
        return jnp.dot(tile, weights, preferred_element_type=jnp.float32)

    return lax.map(one_block, blocks).reshape(-1, weights.shape[1])


def gram_total(projected):
    local_gram = jnp.dot(projected.T, projected, precision=lax.Precision.HIGHEST)
    return one_axis_at_a_time(local_gram, ROW_BLK)


def finish(projected, gram_matrix):
    factor = jnp.linalg.cholesky(gram_matrix)
    basis = jax.scipy.linalg.solve_triangular(factor, projected.T, lower=True).T
    return (basis, factor.T)


def per_device(embeddings, vectors):
    unit_rows = normalize(embeddings)
    panel = gather_axes(unit_rows, ROW, (0, 1, 2), 0)
    blocks = row_blocks(panel)
    partial_degree = panel_degree(blocks, collect(unit_rows, BLK, 0))
    degree = sent_and_summed(partial_degree, ROW, 0)
    inverse_root = lax.rsqrt(degree)
    weighted = (vectors * inverse_root[:, None]).astype(jnp.bfloat16)
    column_pieces = sent_together((unit_rows, weighted), BLK, 0, 1)
    panel_sum = panel_apply(blocks, column_pieces[0], column_pieces[1])
    projected = sent_and_summed(panel_sum, ROW, 0) * inverse_root[:, None]
    gram_matrix = gram_total(projected)
    return finish(projected, gram_matrix)


def solution(mesh):
    torus = Mesh(mesh.devices.reshape(2, 8, 2, 4, 2), ("row_0", "row_1", "row_2", "blk_0", "blk_1"))
    placed = (P(ROW_BLK, None), P(ROW_BLK, None))
    return jax.shard_map(
        per_device, mesh=torus, in_specs=placed, out_specs=(P(ROW_BLK, None), P()), check_vma=False
    )
```

profile of v0, /device:TPU:1, one launch (start us, length us, event | category | flops | bytes accessed | tf_op | source)
XLA Modules:
  0.0 282.2 jit_solution(10037022250447392165)
XLA Ops:
  7.2 0.9 fusion.13
  8.2 0.9 fusion.14
  9.1 4.7 %all-gather = bf16[512,192]{0,1:T(8,128)(2,1)S(1)} all-gather(bf16[256,192]{0,1:T(8,128)(2,1)S(1)} %fusion.14), channel_id=2, replica_groups=mesh['row_0'=2,'row_1'=8,'row_2'=2,'blk_0'=4,'blk_1'=2] {'row_0'}, dimensions={0}, use_global_device_ids=true | all-gather | bytes 294912 | tf_op jit(solution)/shard_map/all_gather | solution.py:32
  13.8 0.7 copy.60
  14.5 40.6 %all-gather.6.cloned.1.call-done = bf16[16,256,192]{1,2,0:T(8,128)(2,1)} async-done(((bf16[2,256,192]{1,2,0:T(8,128)(2,1)}), bf16[16,256,192]{1,2,0:T(8,128)(2,1)}) %all-gather.6.cloned.1.call-update) | async-done | bytes 1572880 | tf_op jit(solution)/shard_map/all_gather | solution.py:32
  55.2 0.9 broadcast_in_dim.30
  56.1 6.4 %all-to-all-start = ((bf16[8,256,192]{1,2,0:T(8,128)(2,1)}), bf16[8,256,192]{1,2,0:T(8,128)(2,1)S(1)}, u32[]{:S(2)}, u32[]{:S(2)}) async-start(bf16[8,256,192]{1,2,0:T(8,128)(2,1)} %broadcast_in_dim.30), calls=%async_computation | async-start | bytes 1572864 | tf_op jit(solution)/shard_map/all_to_all | solution.py:45
  62.6 10.6 %all-to-all-done = bf16[8,256,192]{1,2,0:T(8,128)(2,1)S(1)} async-done(((bf16[8,256,192]{1,2,0:T(8,128)(2,1)}), bf16[8,256,192]{1,2,0:T(8,128)(2,1)S(1)}, u32[]{:S(2)}, u32[]{:S(2)}) %all-to-all-start) | async-done | bytes 786464 | tf_op jit(solution)/shard_map/all_to_all | solution.py:45
  73.1 0.5 copy.48
  73.6 4.0 %all-gather.8.cloned.1.call-done = bf16[16,2,256,192]{2,3,1,0:T(8,128)(2,1)} async-done(((bf16[8,2,256,192]{2,3,1,0:T(8,128)(2,1)}), bf16[16,2,256,192]{2,3,1,0:T(8,128)(2,1)}) %all-gather.8.cloned.1.call-update) | async-done | bytes 3145744 | tf_op jit(solution)/shard_map/all_gather | solution.py:32
  77.6 6.0 %copy.49 = bf16[2,8,2,256,192]{4,3,2,1,0:T(8,128)(2,1)} copy(bf16[2,8,2,256,192]{3,4,0,1,2:T(8,128)(2,1)} %bitcast.51) | data formatting | bytes 6291456 | tf_op jit(solution)/shard_map/while | solution.py:102
  83.6 32.5 %while.24 = (s32[]{:T(128)}, f32[16,512]{1,0:T(8,128)S(1)}, bf16[16,512,192]{2,1,0:T(8,128)(2,1)}, bf16[2048,192]{1,0:T(8,128)(2,1)S(1)}, s32[]{:T(128)}, /*index=5*/s32[]{:T(128)}) while((s32[]{:T(128)}, f32[16,512]{1,0:T(8,128)S(1)}, bf16[16,512,192]{2,1,0:T(8,128)(2,1)}, bf16[2048,192]{1,0:T(8,128)(2,1)S(1)}, s32[]{:T(128)}, ...), condition=%wide.region_3.4_spmd, body=%wide.region_1.3_spmd.sunk | while | flops 405798400 | bytes 1055305 | solution.py:93
  83.6 2.0 exponential_reduce_fusion.2
  85.7 1.9 exponential_reduce_fusion.2
  87.7 1.9 exponential_reduce_fusion.2
  89.7 1.9 exponential_reduce_fusion.2
  91.8 1.9 exponential_reduce_fusion.2
  93.8 1.9 exponential_reduce_fusion.2
  95.8 1.9 exponential_reduce_fusion.2
  97.9 1.9 exponential_reduce_fusion.2
  99.9 2.0 exponential_reduce_fusion.2
  101.9 2.0 exponential_reduce_fusion.2
  104.0 1.9 exponential_reduce_fusion.2
  106.0 2.0 exponential_reduce_fusion.2
  108.0 2.0 exponential_reduce_fusion.2
  110.1 1.9 exponential_reduce_fusion.2
  112.1 2.0 exponential_reduce_fusion.2
  114.1 2.0 exponential_reduce_fusion.2
  116.1 0.6 all_to_all.13
  116.8 8.0 %all-to-all-start.1 = ((f32[32,1,256]{2,1,0:T(1,128)}), f32[32,1,256]{2,1,0:T(1,128)S(1)}, u32[]{:S(2)}, u32[]{:S(2)}) async-start(f32[32,1,256]{2,1,0:T(1,128)} %all_to_all.13), calls=%async_computation.1 | async-start | bytes 65536 | tf_op jit(solution)/shard_map/all_to_all | solution.py:59
  124.8 7.9 %all-to-all-done.1 = f32[32,1,256]{2,1,0:T(1,128)S(1)} async-done(((f32[32,1,256]{2,1,0:T(1,128)}), f32[32,1,256]{2,1,0:T(1,128)S(1)}, u32[]{:S(2)}, u32[]{:S(2)}) %all-to-all-start.1) | async-done | bytes 32800 | tf_op jit(solution)/shard_map/all_to_all | solution.py:59
  132.8 33.3 %all_gather.27 = bf16[2048,208]{0,1:T(8,128)(2,1)S(1)} all-gather(bf16[256,208]{0,1:T(8,128)(2,1)S(1)} %pad_maximum_fusion), channel_id=1, replica_groups=mesh['row_0'=2,'row_1'=8,'row_2'=2,'blk_0'=4,'blk_1'=2] {'blk_0','blk_1'}, dimensions={0}, use_global_device_ids=true | all-gather | bytes 958464 | tf_op jit(solution)/shard_map/all_gather | solution.py:66
  166.3 0.5 copy.41
  166.8 40.0 %while.25 = (s32[]{:T(128)}, f32[16,512,16]{1,0,2:T(8,128)S(1)}, bf16[16,512,192]{2,1,0:T(8,128)(2,1)}, bf16[2048,192]{1,0:T(8,128)(2,1)S(1)}, bf16[2048,16]{0,1:T(8,128)(2,1)S(1)}, /*index=5*/s32[]{:T(128)}, s32[]{:T(128)}) while((s32[]{:T(128)}, f32[16,512,16]{1,0,2:T(8,128)S(1)}, bf16[16,512,192]{2,1,0:T(8,128)(2,1)}, ...), condition=%wide.region_6.7_spmd, body=%wide.region_5.6_spmd.sunk | while | flops 439353344 | bytes 1278545 | solution.py:102
  166.8 2.3 fusion.38
  169.1 0.1 dynamic_update_slice.17
  169.3 2.3 fusion.38
  171.8 2.3 fusion.38
  174.3 2.3 fusion.38
  176.8 2.3 fusion.38
  179.3 2.3 fusion.38
  181.8 2.3 fusion.38
  184.3 2.3 fusion.38
  186.8 2.3 fusion.38
  189.3 2.3 fusion.38
  191.8 2.3 fusion.38
  194.3 2.3 fusion.38
  196.8 2.3 fusion.38
  199.3 2.3 fusion.38
  201.8 2.3 fusion.38
  204.3 2.3 fusion.38
  206.9 0.3 copy.43
  207.2 24.1 %all_to_all.19 = f32[32,256,16]{1,2,0:T(8,128)S(1)} all-to-all(f32[32,256,16]{1,2,0:T(8,128)S(1)} %copy.43), channel_id=1, replica_groups=mesh['row_0'=2,'row_1'=8,'row_2'=2,'blk_0'=4,'blk_1'=2] {'row_0','row_1'..., dimensions={0} | all-to-all | bytes 1048576 | tf_op jit(solution)/shard_map/all_to_all | solution.py:59
  231.4 3.8 %psum.35 = f32[16,16]{0,1:T(8,128)S(1)} all-reduce(f32[16,16]{0,1:T(8,128)S(1)} %fusion.17), channel_id=1, replica_groups=mesh['row_0'=2,'row_1'=8,'row_2'=2,'blk_0'=4,'blk_1'=2] {'row_0'}, use_global_device_ids=true, to_apply=%region_8.9 | all-reduce | flops 256 | bytes 2048 | tf_op jit(solution)/shard_map/psum | solution.py:20
  235.3 12.5 %psum.36 = f32[16,16]{0,1:T(8,128)S(1)} all-reduce(f32[16,16]{0,1:T(8,128)S(1)} %psum.35), channel_id=1, replica_groups=mesh['row_0'=2,'row_1'=8,'row_2'=2,'blk_0'=4,'blk_1'=2] {'row_1'}, use_global_device_ids=true, to_apply=%region_9.10 | all-reduce | flops 256 | bytes 2048 | tf_op jit(solution)/shard_map/psum | solution.py:20
  247.8 8.4 %psum.37 = f32[16,16]{0,1:T(8,128)S(1)} all-reduce(f32[16,16]{0,1:T(8,128)S(1)} %psum.36), channel_id=1, replica_groups=mesh['row_0'=2,'row_1'=8,'row_2'=2,'blk_0'=4,'blk_1'=2] {'row_2'}, use_global_device_ids=true, to_apply=%region_10.11 | all-reduce | flops 256 | bytes 2048 | tf_op jit(solution)/shard_map/psum | solution.py:20
  256.2 6.5 %psum.38 = f32[16,16]{0,1:T(8,128)S(1)} all-reduce(f32[16,16]{0,1:T(8,128)S(1)} %psum.37), channel_id=1, replica_groups=mesh['row_0'=2,'row_1'=8,'row_2'=2,'blk_0'=4,'blk_1'=2] {'blk_0'}, use_global_device_ids=true, to_apply=%region_11.12 | all-reduce | flops 256 | bytes 2048 | tf_op jit(solution)/shard_map/psum | solution.py:20
  262.7 7.1 %psum.39 = f32[16,16]{0,1:T(8,128)S(1)} all-reduce(f32[16,16]{0,1:T(8,128)S(1)} %psum.38), channel_id=1, replica_groups=mesh['row_0'=2,'row_1'=8,'row_2'=2,'blk_0'=4,'blk_1'=2] {'blk_1'}, use_global_device_ids=true, to_apply=%region_12.13 | all-reduce | flops 256 | bytes 2048 | tf_op jit(solution)/shard_map/psum | solution.py:20
  269.8 1.5 cholesky.16
  271.3 0.6 compare_reduce_fusion
  272.0 0.6 fusion.23
  272.6 1.2 custom-call.7
  273.8 0.8 fusion.15
  274.7 0.7 copy.46
  (68 shorter events, 4.5 us)
Async XLA Ops:
  7.2 48.0 %all-gather.6.cloned.1.call-start = ((), (), s32[]{:S(2)}) async-start(), calls=%async_computation.3 | async-start | bytes 1769472 | tf_op jit(solution)/shard_map/all_gather | solution.py:32
  14.5 63.2 %all-gather.8.cloned.1.call-start = ((), (), s32[]{:S(2)}) async-start(), calls=%async_computation.4 | async-start | bytes 4718592 | tf_op jit(solution)/shard_map/all_gather | solution.py:32
  56.1 17.0 %all-to-all-start = ((bf16[8,256,192]{1,2,0:T(8,128)(2,1)}), bf16[8,256,192]{1,2,0:T(8,128)(2,1)S(1)}, u32[]{:S(2)}, u32[]{:S(2)}) async-start(bf16[8,256,192]{1,2,0:T(8,128)(2,1)} %broadcast_in_dim.30), calls=%async_computation | async-start | bytes 1572864 | tf_op jit(solution)/shard_map/all_to_all | solution.py:45
  83.6 49.2 %copy-start = (f32[256,16]{0,1:T(8,128)S(1)}, f32[256,16]{0,1:T(8,128)}, u32[]{:S(2)}) copy-start(f32[256,16]{0,1:T(8,128)} %param.7) | copy-start | bytes 49156
  116.8 16.0 %all-to-all-start.1 = ((f32[32,1,256]{2,1,0:T(1,128)}), f32[32,1,256]{2,1,0:T(1,128)S(1)}, u32[]{:S(2)}, u32[]{:S(2)}) async-start(f32[32,1,256]{2,1,0:T(1,128)} %all_to_all.13), calls=%async_computation.1 | async-start | bytes 65536 | tf_op jit(solution)/shard_map/all_to_all | solution.py:59
Sparse Core Ops, SparseCore 0:
  14.6 40.5 all-gather.5
  57.0 20.6 all-gather.7
where the time goes:
time: 286 us; the launch traced here: 282 us
  blocking collectives  100 us (35%)
  matrix products  68.6 us (24%)
  waiting for transfers between devices  63.2 us (22%)
  starting transfers between devices  14.5 us (5%)
  local copies, waits for them, and re-layouts  14.5 us (5%)
  between operations  14.2 us (5%)
  other arithmetic  5.99 us (2%)
    all_gather x2, waiting for transfers between devices, gather_in_order(): tiles = lax.all_gather(tiles, axes[k])  44.7 us
    psum x5, blocking collectives, one_axis_at_a_time(): return functools.reduce(lax.psum, axes, shard)  38.3 us
    dot_general x16, matrix products, one_block(): return jnp.dot(tile, weights, preferred_element_type=jnp.float32)  36.4 us
    all_gather x1, blocking collectives, sent_together(): filled = lax.all_gather(both, axis, axis=dim, tiled=True)  33.3 us
    dot_general x16, matrix products, affinity(): lax.dot_general(block_rows, columns, (((1,), (1,)), ((), ())), preferred_...  31.2 us
    all_to_all x1, blocking collectives, sent_and_summed(): tiles = lax.all_to_all(in_blocks(shard, dim, count), axis, 0, 0, tiled=True)  24.1 us
    all_to_all x1, waiting for transfers between devices, sent_to_all(): return lax.all_to_all(copies, axis, split_axis=0, concat_axis=0, tiled=True)  10.6 us
    all_to_all x1, starting transfers between devices, sent_and_summed(): tiles = lax.all_to_all(in_blocks(shard, dim, count), axis, 0, 0, tiled=True)  8.02 us
  transfers between devices with their start and end apart: 4, of which 4 were waited for; matrix products, arithmetic and copies ran while one was open for 1% of the time, Pallas kernels for 0%

commit v1 on v0

v1 whole, which is shorter than its diff:
```python
import functools

import jax
import jax.numpy as jnp
from jax import lax
from jax.experimental import pallas as pl
from jax.experimental.pallas import tpu as pltpu
from jax.sharding import Mesh
from jax.sharding import PartitionSpec as P

AXES = ("xl", "z", "core", "y", "xh")
SIZES = (2, 8, 2, 4, 2)
ROWS = ("z", "core")
COLS = ("xl", "y", "xh")
NR = 16
NC = 16
SEG = 256
DIM = 192
VEC = 16
WIDE = DIM + 2 * VEC
SCALE = 14.426950408889634
EPS = 1e-6
MIB = 1 << 20
F32 = jnp.float32
BF16 = jnp.bfloat16
HI = lax.Precision.HIGHEST


def params(mib):
    return pltpu.CompilerParams(vmem_limit_bytes=mib * MIB)


def vmem():
    return pl.BlockSpec(memory_space=pltpu.VMEM)


def smem():
    return pl.BlockSpec(memory_space=pltpu.SMEM)


def nt(a, b, **kw):
    return lax.dot_general(a, b, (((1,), (1,)), ((), ())), preferred_element_type=F32, **kw)


def unit_kernel(e_ref, v_ref, o_ref, many_ref):
    e = e_ref[...].astype(F32)
    u = e * lax.rsqrt(jnp.sum(e * e, axis=1, keepdims=True) + EPS)
    o_ref[0:DIM, :] = u.T.astype(BF16)
    v = v_ref[...].T
    hi = v.astype(BF16)
    o_ref[DIM : DIM + VEC, :] = hi
    o_ref[DIM + VEC : WIDE, :] = (v - hi.astype(F32)).astype(BF16)
    for k in range(NC):
        many_ref[k] = o_ref[...]


def affinity_kernel(pos_ref, t_ref, *refs):
    near, far = refs[0:8], refs[8:16]
    b_ref, deg_ref, s_ref = refs[16:19]
    z, core = pos_ref[0], pos_ref[1]
    for k in range(8):
        zz = lax.rem(z + 8 - k, 8)
        s_ref[zz * 2 + core] = near[k][0:DIM, :]
        s_ref[zz * 2 + 1 - core] = far[k][0:DIM, :]

    def column_piece(t, carry):
        lhs = t_ref[t, 0:DIM, :].T
        total = jnp.zeros((SEG, 128), F32)
        for s in range(NR):
            score = jnp.dot(lhs, s_ref[s], preferred_element_type=F32)
            tile = jnp.exp2(score * SCALE - SCALE)
            total = total + tile[:, 0:128] + tile[:, 128:256]
            b_ref[s, pl.ds(t * SEG, SEG), :] = tile.astype(BF16)
        sums = nt(jnp.ones((8, 128), F32), total, precision=HI)
        deg_ref[0, pl.ds(t, 1), :] = sums[0:1, :]
        return carry

    lax.fori_loop(0, NC, column_piece, 0)
    for k in range(1, NC):
        deg_ref[k] = deg_ref[0]


def apply_kernel(pos_ref, deg_ref, t_ref, b_ref, p_ref, own_ref, root_ref, w_ref):
    root_ref[...] = lax.rsqrt(jnp.sum(deg_ref[...], axis=0))
    own_ref[...] = root_ref[pl.ds(pos_ref[0], 1), :]
    for t in range(NC):
        v = t_ref[t, DIM : DIM + VEC, :].astype(F32) + t_ref[t, DIM + VEC : WIDE, :].astype(F32)
        w_ref[:, t * SEG : (t + 1) * SEG] = (v * root_ref[t : t + 1, :]).astype(BF16)

    def row_piece(s, carry):
        p_ref[s] = jnp.dot(w_ref[...], b_ref[s], preferred_element_type=F32)
        return carry

    lax.fori_loop(0, NR, row_piece, 0)


def project_kernel(p_ref, own_ref, q_ref, gram_ref):
    q = jnp.sum(p_ref[...], axis=0) * own_ref[...]
    q_ref[...] = q
    gram = nt(q, q, precision=HI)
    for k in range(NR):
        gram_ref[k] = gram


def finish(q, gram):
    factor = jnp.linalg.cholesky(gram)
    basis = jax.scipy.linalg.solve_triangular(factor, q, lower=True).T
    return (basis, factor.T)


def to_all(copies, axes):
    return lax.all_to_all(copies, axes, split_axis=0, concat_axis=0, tiled=True)


def shape(*dims, dtype=F32):
    return jax.ShapeDtypeStruct(dims, dtype)


def per_device(embeddings, vectors):
    z, core = lax.axis_index("z"), lax.axis_index("core")
    column = lax.axis_index(COLS)
    unit, unit_copies = pl.pallas_call(
        unit_kernel,
        out_shape=(shape(WIDE, SEG, dtype=BF16), shape(NC, WIDE, SEG, dtype=BF16)),
        name="unit",
    )(embeddings, vectors)
    near = [unit]
    for k in range(1, 8):
        near.append(lax.ppermute(unit, "z", [(i, (i + k) % 8) for i in range(8)]))
    far = [lax.ppermute(a, "core", [(0, 1), (1, 0)]) for a in near]
    columns = to_all(unit_copies, COLS)
    block, degree = pl.pallas_call(
        affinity_kernel,
        out_shape=(shape(NR, NC * SEG, SEG, dtype=BF16), shape(NC, NC, SEG)),
        in_specs=[smem()] + [vmem()] * 17,
        out_specs=(vmem(), vmem()),
        scratch_shapes=[pltpu.VMEM((NR, DIM, SEG), BF16)],
        compiler_params=params(56),
        name="affinity",
    )(jnp.stack([z, core]), columns, *near, *far)
    degree = to_all(degree, COLS)
    product, own = pl.pallas_call(
        apply_kernel,
        out_shape=(shape(NR, VEC, SEG), shape(1, SEG)),
        in_specs=[smem(), vmem(), vmem(), vmem()],
        out_specs=(vmem(), vmem()),
        scratch_shapes=[pltpu.VMEM((NC, SEG), F32), pltpu.VMEM((VEC, NC * SEG), BF16)],
        compiler_params=params(56),
        name="apply",
    )(jnp.stack([column]), degree, columns, block)
    product = to_all(product, ROWS)
    projected, gram = pl.pallas_call(
        project_kernel,
        out_shape=(shape(VEC, SEG), shape(NR, VEC, VEC)),
        name="project",
    )(product, own)
    gram = jnp.sum(to_all(gram, ROWS), axis=0)
    gram = jnp.sum(to_all(jnp.broadcast_to(gram, (NC, VEC, VEC)), COLS), axis=0)
    return finish(projected, gram)


def solution(mesh):
    torus = Mesh(mesh.devices.reshape(SIZES), AXES)
    placed = (P(AXES, None), P(AXES, None))
    return jax.shard_map(
        per_device, mesh=torus, in_specs=placed, out_specs=(P(AXES, None), P()), check_vma=False
    )
```

time: 286 us -> 165 us (0.58); the launches traced: 282 us -> 164 us
  matrix products: 68.6 us -> 1.52 us
  blocking collectives: 100 us -> 39.4 us
  Pallas kernels: 0 us -> 55.2 us
  waiting for transfers between devices: 63.2 us -> 14.6 us
  starting transfers between devices: 14.5 us -> 38.3 us
  between operations: 14.2 us -> 0.88 us
  local copies, waits for them, and re-layouts: 14.5 us -> 8.27 us
    dot_general x33 -> x0, matrix products: 67.8 us -> none  [the longest x16 36.4 us: one_block(): return jnp.dot(tile, weights, preferred_element_type=jnp.float32)]
    pallas_call x0 -> x4, Pallas kernels: none -> 55.2 us  [the longest x1 32.6 us: per_device(): pl.pallas_call(affinity_kernel, out_shape=(shape(NR, NC * SEG, SEG, dtype...]
    all_gather x2 -> x0, waiting for transfers between devices: 44.7 us -> none  [gather_in_order(): tiles = lax.all_gather(tiles, axes[k])]
    psum x5 -> x0, blocking collectives: 38.3 us -> none  [one_axis_at_a_time(): return functools.reduce(lax.psum, axes, shard)]
    all_gather x2 -> x0, blocking collectives: 38.1 us -> none  [the longest x1 33.3 us: sent_together(): filled = lax.all_gather(both, axis, axis=dim, tiled=True)]
    ppermute x0 -> x15, starting transfers between devices: none -> 23.9 us  [the longest x7 19.6 us: per_device(): near.append(lax.ppermute(unit, 'z', [(i, (i + k) % 8) for i in range(8)]))]
    all_to_all x1 -> x3, blocking collectives: 24.1 us -> 39.4 us  [to_all(): return lax.all_to_all(copies, axes, split_axis=0, concat_axis=0, tiled=True)]
    all_to_all x2, waiting for transfers between devices: 18.5 us -> 7.76 us  [to_all(): return lax.all_to_all(copies, axes, split_axis=0, concat_axis=0, tiled=True)]
  transfers between devices with their start and end apart: 4 -> 17, of which waited for: 4 -> 4; matrix products, arithmetic and copies ran while one was open for 1% -> 0% of each run, Pallas kernels for 0% -> 0%
where the time goes in v1:
time: 165 us; the launch traced here: 164 us
  Pallas kernels  55.2 us (33%)
  blocking collectives  39.4 us (24%)
  starting transfers between devices  38.3 us (23%)
  waiting for transfers between devices  14.6 us (9%)
  local copies, waits for them, and re-layouts  8.27 us (5%)
  other arithmetic  6.08 us (4%)
    all_to_all x3, blocking collectives, to_all(): return lax.all_to_all(copies, axes, split_axis=0, concat_axis=0, tiled=True)  39.4 us
    pallas_call x1, Pallas kernels, per_device(): pl.pallas_call(affinity_kernel, out_shape=(shape(NR, NC * SEG, SEG, dtype...  32.6 us
    ppermute x7, starting transfers between devices, per_device(): near.append(lax.ppermute(unit, 'z', [(i, (i + k) % 8) for i in range(8)]))  19.6 us
    pallas_call x1, Pallas kernels, per_device(): pl.pallas_call(apply_kernel, out_shape=(shape(NR, VEC, SEG), shape(1, SEG...  18.2 us
    all_to_all x2, starting transfers between devices, to_all(): return lax.all_to_all(copies, axes, split_axis=0, concat_axis=0, tiled=True)  14.4 us
    all_to_all x2, waiting for transfers between devices, to_all(): return lax.all_to_all(copies, axes, split_axis=0, concat_axis=0, tiled=True)  7.76 us
    unnamed x43, local copies, waits for them, and re-layouts  7.67 us
    ppermute x7, waiting for transfers between devices, per_device(): near.append(lax.ppermute(unit, 'z', [(i, (i + k) % 8) for i in range(8)]))  6.49 us
  transfers between devices with their start and end apart: 17, of which 4 were waited for; matrix products, arithmetic and copies ran while one was open for 0% of the time, Pallas kernels for 0%

profile of v1, /device:TPU:1, one launch (start us, length us, event | category | flops | bytes accessed | tf_op | source)
XLA Modules:
  0.0 164.2 jit_solution(9676759030151794375)
XLA Ops:
  0.6 1.6 %copy.8.e_ref = bf16[256,192]{1,0:T(8,128)(2,1)} copy(bf16[256,192]{0,1:T(8,128)(2,1)} %param.2) | data formatting | bytes 196608 | tf_op args[0]
  2.3 1.5 copy.9.v_ref
  3.7 2.6 %unit.1 = (bf16[224,256]{1,0:T(8,128)(2,1)}, bf16[16,224,256]{2,1,0:T(8,128)(2,1)}) custom-call(bf16[256,192]{1,0:T(8,128)(2,1)} %copy.8.e_ref, f32[256,16]{1,0:T(8,128)} %copy.9.v_ref), custom_call_target="tpu_custom_call" | custom-call | tf_op jit(solution)/shard_map/unit/pallas_call | solution.py:122
  6.4 7.7 %all-to-all-start = ((bf16[16,224,256]{2,1,0:T(8,128)(2,1)}), bf16[16,224,256]{2,1,0:T(8,128)(2,1)S(1)}, u32[]{:S(2)}, u32[]{:S(2)}) async-start(bf16[16,224,256]{2,1,0:T(8,128)(2,1)} %get-tuple-element.10), calls=%async_computation | async-start | bytes 3670016 | tf_op jit(solution)/shard_map/all_to_all | solution.py:112
  14.1 4.4 %collective-permute-start.2 = (bf16[224,256]{1,0:T(8,128)(2,1)S(1)}, bf16[224,256]{1,0:T(8,128)(2,1)S(1)}, u32[]{:S(2)}, u32[]{:S(2)}) collective-permute-start(bf16[224,256]{1,0:T(8,128)(2,1)S(1)} %copy-done.2), channel_id=1, source_target_pairs={{0,48},{16,64},{32,80},{48,96},{64,112},{80,0},{96,16},{112,32},{1... | collective-permute-start | bytes 344072 | tf_op jit(solution)/shard_map/ppermute | solution.py:129
  18.5 4.2 %collective-permute-start.3 = (bf16[224,256]{1,0:T(8,128)(2,1)S(1)}, bf16[224,256]{1,0:T(8,128)(2,1)S(1)}, u32[]{:S(2)}, u32[]{:S(2)}) collective-permute-start(bf16[224,256]{1,0:T(8,128)(2,1)S(1)} %copy-done.2), channel_id=1, source_target_pairs={{0,64},{16,80},{32,96},{48,112},{64,0},{80,16},{96,32},{112,48},{1... | collective-permute-start | bytes 344072 | tf_op jit(solution)/shard_map/ppermute | solution.py:129
  22.8 2.8 %collective-permute-start.4 = (bf16[224,256]{1,0:T(8,128)(2,1)S(1)}, bf16[224,256]{1,0:T(8,128)(2,1)S(1)}, u32[]{:S(2)}, u32[]{:S(2)}) collective-permute-start(bf16[224,256]{1,0:T(8,128)(2,1)S(1)} %copy-done.2), channel_id=1, source_target_pairs={{0,80},{16,96},{32,112},{48,0},{64,16},{80,32},{96,48},{112,64},{1... | collective-permute-start | bytes 344072 | tf_op jit(solution)/shard_map/ppermute | solution.py:129
  25.6 0.0 collective-permute-start.5
  25.6 0.4 collective-permute-start.6
  26.0 0.0 collective-permute-done.2.refs_3_
  26.0 3.4 %collective-permute-start = (bf16[224,256]{1,0:T(8,128)(2,1)S(1)}, bf16[224,256]{1,0:T(8,128)(2,1)S(1)}, u32[]{:S(2)}, u32[]{:S(2)}) collective-permute-start(bf16[224,256]{1,0:T(8,128)(2,1)S(1)} %copy-done.2), channel_id=1, source_target_pairs={{0,16},{16,32},{32,48},{48,64},{64,80},{80,96},{96,112},{112,0},{1... | collective-permute-start | bytes 344072 | tf_op jit(solution)/shard_map/ppermute | solution.py:129
  29.4 1.6 %collective-permute-done.3.refs_4_ = bf16[224,256]{1,0:T(8,128)(2,1)S(1)} collective-permute-done((bf16[224,256]{1,0:T(8,128)(2,1)S(1)}, bf16[224,256]{1,0:T(8,128)(2,1)S(1)}, u32[]{:S(2)}, u32[]{:S(2)}) %collective-permute-start.3) | collective-permute-done | bytes 114720 | tf_op jit(solution)/shard_map/ppermute | solution.py:129
  31.0 4.3 %collective-permute-start.1 = (bf16[224,256]{1,0:T(8,128)(2,1)S(1)}, bf16[224,256]{1,0:T(8,128)(2,1)S(1)}, u32[]{:S(2)}, u32[]{:S(2)}) collective-permute-start(bf16[224,256]{1,0:T(8,128)(2,1)S(1)} %copy-done.2), channel_id=1, source_target_pairs={{0,32},{16,48},{32,64},{48,80},{64,96},{80,112},{96,0},{112,16},{1... | collective-permute-start | bytes 344072 | tf_op jit(solution)/shard_map/ppermute | solution.py:129
  35.3 0.0 collective-permute-done.4.refs_5_
  35.3 1.8 %collective-permute-start.7 = (bf16[224,256]{1,0:T(8,128)(2,1)S(1)}, bf16[224,256]{1,0:T(8,128)(2,1)S(1)}, u32[]{:S(2)}, u32[]{:S(2)}) collective-permute-start(bf16[224,256]{1,0:T(8,128)(2,1)S(1)} %copy-done.2), channel_id=1, source_target_pairs={{0,8},{8,0},{1,9},{9,1},{2,10},{10,2},{3,11},{11,3},{4,12},{12,4},... | collective-permute-start | bytes 344072 | tf_op jit(solution)/shard_map/ppermute | solution.py:130
  37.1 4.8 %collective-permute-done.5.refs_6_ = bf16[224,256]{1,0:T(8,128)(2,1)S(1)} collective-permute-done((bf16[224,256]{1,0:T(8,128)(2,1)S(1)}, bf16[224,256]{1,0:T(8,128)(2,1)S(1)}, u32[]{:S(2)}, u32[]{:S(2)}) %collective-permute-start.5) | collective-permute-done | bytes 114720 | tf_op jit(solution)/shard_map/ppermute | solution.py:129
  42.0 0.6 collective-permute-start.10
  42.5 0.0 collective-permute-done.6.refs_7_
  42.6 0.7 collective-permute-start.11
  43.3 0.0 collective-permute-done.refs_1_
  43.3 0.1 collective-permute-start.12
  43.4 0.0 collective-permute-done.1.refs_2_
  43.4 0.4 collective-permute-start.13
  43.8 0.0 collective-permute-done.7.refs_8_
  43.8 0.1 collective-permute-start.14
  43.9 0.0 collective-permute-done.10.refs_11_
  43.9 0.4 collective-permute-start.8
  44.3 0.0 collective-permute-done.11.refs_12_
  44.3 0.3 collective-permute-start.9
  44.6 0.7 pad_add_fusion.pos_ref
  45.2 0.0 collective-permute-done.12.refs_13_
  45.2 0.0 collective-permute-done.13.refs_14_
  45.3 0.0 collective-permute-done.8.refs_9_
  45.3 0.3 collective-permute-done.9.refs_10_
  45.6 0.0 all-to-all-done.t_ref
  45.7 0.1 copy-done.13
  45.9 0.0 copy-done.14
  45.9 0.1 copy-done.15
  46.0 0.0 copy-done.16
  46.0 0.2 copy-done.17
  46.3 1.3 copy-done
  47.5 32.6 %affinity.1 = (bf16[16,4096,256]{2,1,0:T(8,128)(2,1)}, f32[16,16,256]{2,1,0:T(8,128)}) custom-call(s32[2]{0:T(128)} %pad_add_fusion.pos_ref, bf16[16,224,256]{2,1,0:T(8,128)(2,1)} %copy-done, bf16[224,256]{1,0:T(8,128)(2,1)} %get-tuple-element.11.refs_0_, bf16[224,256]{1,0:T(8,128)(2,1)} %copy-done.8, bf16[224,256]{1,0:T(8,128)(2,1)} %copy-done.9, ...), custom_call_target="tpu_custom_call" | custom-call | tf_op jit(solution)/shard_map/affinity/pallas_call | solution.py:132
  80.1 6.7 %all-to-all-start.1 = ((f32[16,16,256]{2,1,0:T(8,128)}), f32[16,16,256]{2,1,0:T(8,128)S(1)}, u32[]{:S(2)}, u32[]{:S(2)}) async-start(f32[16,16,256]{2,1,0:T(8,128)} %get-tuple-element.12), calls=%async_computation.1 | async-start | bytes 524288 | tf_op jit(solution)/shard_map/all_to_all | solution.py:112
  86.8 7.8 %all-to-all-done.1.deg_ref = f32[16,16,256]{2,1,0:T(8,128)S(1)} async-done(((f32[16,16,256]{2,1,0:T(8,128)}), f32[16,16,256]{2,1,0:T(8,128)S(1)}, u32[]{:S(2)}, u32[]{:S(2)}) %all-to-all-start.1) | async-done | bytes 262176 | tf_op jit(solution)/shard_map/all_to_all | solution.py:112
  94.6 0.7 copy-done.1
  95.3 18.2 %apply.1 = (f32[16,16,256]{2,1,0:T(8,128)}, f32[1,256]{1,0:T(1,128)}) custom-call(s32[1]{0:T(128)} %bitcast.pos_ref, f32[16,16,256]{2,1,0:T(8,128)} %copy-done.1, bf16[16,224,256]{2,1,0:T(8,128)(2,1)} %copy-done, bf16[16,4096,256]{2,1,0:T(8,128)(2,1)} %get-tuple-element.13.b_ref), custom_call_target="tpu_custom_call" | custom-call | tf_op jit(solution)/shard_map/apply/pallas_call | solution.py:142
  113.5 20.0 %all_to_all.25.p_ref = f32[16,16,256]{2,1,0:T(8,128)} all-to-all(f32[16,16,256]{2,1,0:T(8,128)} %get-tuple-element.14), channel_id=1, replica_groups=mesh['xl'=2,'z'=8,'core'=2,'y'=4,'xh'=2] {'z','core'}, dimensions={0} | all-to-all | bytes 524288 | tf_op jit(solution)/shard_map/all_to_all | solution.py:112
  133.5 1.8 %project.1 = (f32[16,256]{1,0:T(8,128)}, f32[16,16,16]{2,1,0:T(8,128)}) custom-call(f32[16,16,256]{2,1,0:T(8,128)} %all_to_all.25.p_ref, f32[1,256]{1,0:T(1,128)} %get-tuple-element.15.own_ref), custom_call_target="tpu_custom_call" | custom-call | tf_op jit(solution)/shard_map/project/pallas_call | solution.py:152
  135.2 1.0 reshape.14
  136.2 10.0 %all_to_all.26 = f32[16,1,256]{2,1,0:T(1,128)S(1)} all-to-all(f32[16,1,256]{2,1,0:T(1,128)S(1)} %reshape.14), channel_id=1, replica_groups=mesh['xl'=2,'z'=8,'core'=2,'y'=4,'xh'=2] {'z','core'}, dimensions={0} | all-to-all | bytes 32768 | tf_op jit(solution)/shard_map/all_to_all | solution.py:112
  146.3 0.5 broadcast.53
  146.8 0.7 reduce.6
  147.5 0.1 reshape.15
  147.6 0.1 reshape.16
  147.7 9.3 %all_to_all.27 = f32[16,1,256]{2,1,0:T(1,128)S(1)} all-to-all(f32[16,1,256]{2,1,0:T(1,128)S(1)} %reshape.16), channel_id=1, replica_groups=mesh['xl'=2,'z'=8,'core'=2,'y'=4,'xh'=2] {'xl','y','xh'}, dimensions={0} | all-to-all | bytes 32768 | tf_op jit(solution)/shard_map/all_to_all | solution.py:112
  157.1 0.7 reduce.7
  157.8 0.1 reshape.17
  157.9 0.1 copy.10
  158.0 1.5 cholesky.16
  159.5 0.6 compare_reduce_fusion
  160.1 0.6 fusion.3
  160.8 1.2 custom-call.7
  162.0 0.7 copy.11
  162.7 1.5 fusion
  (35 shorter events, 0.2 us)
Async XLA Ops:
  6.4 7.7 %copy-start.2 = (bf16[224,256]{1,0:T(8,128)(2,1)S(1)}, bf16[224,256]{1,0:T(8,128)(2,1)}, u32[]{:S(2)}) copy-start(bf16[224,256]{1,0:T(8,128)(2,1)} %get-tuple-element.11.refs_0_) | copy-start | bytes 344068
  6.4 39.2 %all-to-all-start = ((bf16[16,224,256]{2,1,0:T(8,128)(2,1)}), bf16[16,224,256]{2,1,0:T(8,128)(2,1)S(1)}, u32[]{:S(2)}, u32[]{:S(2)}) async-start(bf16[16,224,256]{2,1,0:T(8,128)(2,1)} %get-tuple-element.10), calls=%async_computation | async-start | bytes 3670016 | tf_op jit(solution)/shard_map/all_to_all | solution.py:112
  14.1 11.9 %collective-permute-start.2 = (bf16[224,256]{1,0:T(8,128)(2,1)S(1)}, bf16[224,256]{1,0:T(8,128)(2,1)S(1)}, u32[]{:S(2)}, u32[]{:S(2)}) collective-permute-start(bf16[224,256]{1,0:T(8,128)(2,1)S(1)} %copy-done.2), channel_id=1, source_target_pairs={{0,48},{16,64},{32,80},{48,96},{64,112},{80,0},{96,16},{112,32},{1... | collective-permute-start | bytes 344072 | tf_op jit(solution)/shard_map/ppermute | solution.py:129
  18.5 12.5 %collective-permute-start.3 = (bf16[224,256]{1,0:T(8,128)(2,1)S(1)}, bf16[224,256]{1,0:T(8,128)(2,1)S(1)}, u32[]{:S(2)}, u32[]{:S(2)}) collective-permute-start(bf16[224,256]{1,0:T(8,128)(2,1)S(1)} %copy-done.2), channel_id=1, source_target_pairs={{0,64},{16,80},{32,96},{48,112},{64,0},{80,16},{96,32},{112,48},{1... | collective-permute-start | bytes 344072 | tf_op jit(solution)/shard_map/ppermute | solution.py:129
  22.8 12.6 %collective-permute-start.4 = (bf16[224,256]{1,0:T(8,128)(2,1)S(1)}, bf16[224,256]{1,0:T(8,128)(2,1)S(1)}, u32[]{:S(2)}, u32[]{:S(2)}) collective-permute-start(bf16[224,256]{1,0:T(8,128)(2,1)S(1)} %copy-done.2), channel_id=1, source_target_pairs={{0,80},{16,96},{32,112},{48,0},{64,16},{80,32},{96,48},{112,64},{1... | collective-permute-start | bytes 344072 | tf_op jit(solution)/shard_map/ppermute | solution.py:129
  25.6 16.4 %collective-permute-start.5 = (bf16[224,256]{1,0:T(8,128)(2,1)S(1)}, bf16[224,256]{1,0:T(8,128)(2,1)S(1)}, u32[]{:S(2)}, u32[]{:S(2)}) collective-permute-start(bf16[224,256]{1,0:T(8,128)(2,1)S(1)} %copy-done.2), channel_id=1, source_target_pairs={{0,96},{16,112},{32,0},{48,16},{64,32},{80,48},{96,64},{112,80},{1... | collective-permute-start | bytes 344072 | tf_op jit(solution)/shard_map/ppermute | solution.py:129
  25.6 17.0 %collective-permute-start.6 = (bf16[224,256]{1,0:T(8,128)(2,1)S(1)}, bf16[224,256]{1,0:T(8,128)(2,1)S(1)}, u32[]{:S(2)}, u32[]{:S(2)}) collective-permute-start(bf16[224,256]{1,0:T(8,128)(2,1)S(1)} %copy-done.2), channel_id=1, source_target_pairs={{0,112},{16,0},{32,16},{48,32},{64,48},{80,64},{96,80},{112,96},{1... | collective-permute-start | bytes 344072 | tf_op jit(solution)/shard_map/ppermute | solution.py:129
  26.0 19.7 %copy-start.3 = (bf16[224,256]{1,0:T(8,128)(2,1)}, bf16[224,256]{1,0:T(8,128)(2,1)S(1)}, u32[]{:S(2)}) copy-start(bf16[224,256]{1,0:T(8,128)(2,1)S(1)} %collective-permute-done.2.refs_3_) | copy-start | bytes 344068
  26.0 17.3 %collective-permute-start = (bf16[224,256]{1,0:T(8,128)(2,1)S(1)}, bf16[224,256]{1,0:T(8,128)(2,1)S(1)}, u32[]{:S(2)}, u32[]{:S(2)}) collective-permute-start(bf16[224,256]{1,0:T(8,128)(2,1)S(1)} %copy-done.2), channel_id=1, source_target_pairs={{0,16},{16,32},{32,48},{48,64},{64,80},{80,96},{96,112},{112,0},{1... | collective-permute-start | bytes 344072 | tf_op jit(solution)/shard_map/ppermute | solution.py:129
  31.0 14.6 %copy-start.4 = (bf16[224,256]{1,0:T(8,128)(2,1)}, bf16[224,256]{1,0:T(8,128)(2,1)S(1)}, u32[]{:S(2)}) copy-start(bf16[224,256]{1,0:T(8,128)(2,1)S(1)} %collective-permute-done.3.refs_4_) | copy-start | bytes 344068
  31.0 12.4 %collective-permute-start.1 = (bf16[224,256]{1,0:T(8,128)(2,1)S(1)}, bf16[224,256]{1,0:T(8,128)(2,1)S(1)}, u32[]{:S(2)}, u32[]{:S(2)}) collective-permute-start(bf16[224,256]{1,0:T(8,128)(2,1)S(1)} %copy-done.2), channel_id=1, source_target_pairs={{0,32},{16,48},{32,64},{48,80},{64,96},{80,112},{96,0},{112,16},{1... | collective-permute-start | bytes 344072 | tf_op jit(solution)/shard_map/ppermute | solution.py:129
  35.3 10.3 %copy-start.5 = (bf16[224,256]{1,0:T(8,128)(2,1)}, bf16[224,256]{1,0:T(8,128)(2,1)S(1)}, u32[]{:S(2)}) copy-start(bf16[224,256]{1,0:T(8,128)(2,1)S(1)} %collective-permute-done.4.refs_5_) | copy-start | bytes 344068
  35.3 8.4 %collective-permute-start.7 = (bf16[224,256]{1,0:T(8,128)(2,1)S(1)}, bf16[224,256]{1,0:T(8,128)(2,1)S(1)}, u32[]{:S(2)}, u32[]{:S(2)}) collective-permute-start(bf16[224,256]{1,0:T(8,128)(2,1)S(1)} %copy-done.2), channel_id=1, source_target_pairs={{0,8},{8,0},{1,9},{9,1},{2,10},{10,2},{3,11},{11,3},{4,12},{12,4},... | collective-permute-start | bytes 344072 | tf_op jit(solution)/shard_map/ppermute | solution.py:130
  42.0 3.7 %copy-start.6 = (bf16[224,256]{1,0:T(8,128)(2,1)}, bf16[224,256]{1,0:T(8,128)(2,1)S(1)}, u32[]{:S(2)}) copy-start(bf16[224,256]{1,0:T(8,128)(2,1)S(1)} %collective-permute-done.5.refs_6_) | copy-start | bytes 344068
  42.0 1.9 %collective-permute-start.10 = (bf16[224,256]{1,0:T(8,128)(2,1)S(1)}, bf16[224,256]{1,0:T(8,128)(2,1)S(1)}, u32[]{:S(2)}, u32[]{:S(2)}) collective-permute-start(bf16[224,256]{1,0:T(8,128)(2,1)S(1)} %collective-permute-done.2.refs_3_), channel_id=1, source_target_pairs={{0,8},{8,0},{1,9},{9,1},{2,10},{10,2},{3,11},{11,3},{4,12},{12,4},... | collective-permute-start | bytes 344072 | tf_op jit(solution)/shard_map/ppermute | solution.py:130
  42.6 3.1 %copy-start.7 = (bf16[224,256]{1,0:T(8,128)(2,1)}, bf16[224,256]{1,0:T(8,128)(2,1)S(1)}, u32[]{:S(2)}) copy-start(bf16[224,256]{1,0:T(8,128)(2,1)S(1)} %collective-permute-done.6.refs_7_) | copy-start | bytes 344068
  42.6 1.7 %collective-permute-start.11 = (bf16[224,256]{1,0:T(8,128)(2,1)S(1)}, bf16[224,256]{1,0:T(8,128)(2,1)S(1)}, u32[]{:S(2)}, u32[]{:S(2)}) collective-permute-start(bf16[224,256]{1,0:T(8,128)(2,1)S(1)} %collective-permute-done.3.refs_4_), channel_id=1, source_target_pairs={{0,8},{8,0},{1,9},{9,1},{2,10},{10,2},{3,11},{11,3},{4,12},{12,4},... | collective-permute-start | bytes 344072 | tf_op jit(solution)/shard_map/ppermute | solution.py:130
  43.3 2.4 %copy-start.8 = (bf16[224,256]{1,0:T(8,128)(2,1)}, bf16[224,256]{1,0:T(8,128)(2,1)S(1)}, u32[]{:S(2)}) copy-start(bf16[224,256]{1,0:T(8,128)(2,1)S(1)} %collective-permute-done.refs_1_) | copy-start | bytes 344068
  43.3 2.0 %collective-permute-start.12 = (bf16[224,256]{1,0:T(8,128)(2,1)S(1)}, bf16[224,256]{1,0:T(8,128)(2,1)S(1)}, u32[]{:S(2)}, u32[]{:S(2)}) collective-permute-start(bf16[224,256]{1,0:T(8,128)(2,1)S(1)} %collective-permute-done.4.refs_5_), channel_id=1, source_target_pairs={{0,8},{8,0},{1,9},{9,1},{2,10},{10,2},{3,11},{11,3},{4,12},{12,4},... | collective-permute-start | bytes 344072 | tf_op jit(solution)/shard_map/ppermute | solution.py:130
  43.4 2.3 %copy-start.9 = (bf16[224,256]{1,0:T(8,128)(2,1)}, bf16[224,256]{1,0:T(8,128)(2,1)S(1)}, u32[]{:S(2)}) copy-start(bf16[224,256]{1,0:T(8,128)(2,1)S(1)} %collective-permute-done.1.refs_2_) | copy-start | bytes 344068
  43.4 1.9 %collective-permute-start.13 = (bf16[224,256]{1,0:T(8,128)(2,1)S(1)}, bf16[224,256]{1,0:T(8,128)(2,1)S(1)}, u32[]{:S(2)}, u32[]{:S(2)}) collective-permute-start(bf16[224,256]{1,0:T(8,128)(2,1)S(1)} %collective-permute-done.5.refs_6_), channel_id=1, source_target_pairs={{0,8},{8,0},{1,9},{9,1},{2,10},{10,2},{3,11},{11,3},{4,12},{12,4},... | collective-permute-start | bytes 344072 | tf_op jit(solution)/shard_map/ppermute | solution.py:130
  43.8 1.9 %copy-start.10 = (bf16[224,256]{1,0:T(8,128)(2,1)}, bf16[224,256]{1,0:T(8,128)(2,1)S(1)}, u32[]{:S(2)}) copy-start(bf16[224,256]{1,0:T(8,128)(2,1)S(1)} %collective-permute-done.7.refs_8_) | copy-start | bytes 344068
  43.8 1.5 collective-permute-start.14
  43.9 1.8 %copy-start.11 = (bf16[224,256]{1,0:T(8,128)(2,1)}, bf16[224,256]{1,0:T(8,128)(2,1)S(1)}, u32[]{:S(2)}) copy-start(bf16[224,256]{1,0:T(8,128)(2,1)S(1)} %collective-permute-done.10.refs_11_) | copy-start | bytes 344068
  43.9 1.4 collective-permute-start.8
  44.3 1.4 copy-start.12
  44.3 1.3 collective-permute-start.9
  45.2 0.6 copy-start.13
  45.2 0.7 copy-start.14
  45.3 0.7 copy-start.15
  45.3 0.7 copy-start.16
  45.6 0.6 copy-start.17
  46.3 1.3 copy-start
  80.1 14.4 %all-to-all-start.1 = ((f32[16,16,256]{2,1,0:T(8,128)}), f32[16,16,256]{2,1,0:T(8,128)S(1)}, u32[]{:S(2)}, u32[]{:S(2)}) async-start(f32[16,16,256]{2,1,0:T(8,128)} %get-tuple-element.12), calls=%async_computation.1 | async-start | bytes 524288 | tf_op jit(solution)/shard_map/all_to_all | solution.py:112
  94.6 0.7 copy-start.1

commit v2 on v1

v2 whole, which is shorter than its diff:
```python
import jax
import jax.numpy as jnp
from jax import lax
from jax.experimental import pallas as pl
from jax.experimental.pallas import tpu as pltpu
from jax.sharding import Mesh
from jax.sharding import PartitionSpec as P

AXES = ("xl", "z", "core", "y", "xh")
SIZES = (2, 8, 2, 4, 2)
ROWS = ("z", "core")
COLS = ("xl", "y", "xh")
ALL = 256
NR = 16
NC = 16
SEG = 256
DIM = 192
VEC = 16
SCALE = 14.426950408889634
EPS = 1e-6
MIB = 1 << 20
F32 = jnp.float32
BF16 = jnp.bfloat16
HI = lax.Precision.HIGHEST


def params(mib):
    return pltpu.CompilerParams(vmem_limit_bytes=mib * MIB)


def vmem():
    return pl.BlockSpec(memory_space=pltpu.VMEM)


def smem():
    return pl.BlockSpec(memory_space=pltpu.SMEM)


def nt(a, b, **kw):
    return lax.dot_general(a, b, (((1,), (1,)), ((), ())), preferred_element_type=F32, **kw)


def unit_kernel(e_ref, u_ref, many_ref):
    e = e_ref[...].astype(F32)
    u_ref[...] = (e * lax.rsqrt(jnp.sum(e * e, axis=0, keepdims=True) + EPS)).astype(BF16)
    for k in range(NC):
        many_ref[k] = u_ref[...]


def affinity_kernel(pos_ref, t_ref, *refs):
    near, far = refs[0:8], refs[8:16]
    b_ref, deg_ref, s_ref, c_ref, acc_ref = refs[16:21]
    z, core = pos_ref[0], pos_ref[1]
    step = pl.program_id(0)

    @pl.when(step == 0)
    def _():
        for k in range(8):
            zz = lax.rem(z + 8 - k, 8)
            s_ref[zz * 2 + core] = near[k][...]
            s_ref[zz * 2 + 1 - core] = far[k][...]
        for t in range(NC):
            c_ref[t] = t_ref[t].T
        acc_ref[...] = jnp.zeros_like(acc_ref)

    for t in range(NC):
        total = acc_ref[t]
        for j in range(2):
            score = jnp.dot(c_ref[t], s_ref[step * 2 + j], preferred_element_type=F32)
            tile = jnp.exp2(score * SCALE)
            total = total + (tile[:, 0:128] + tile[:, 128:256])
            b_ref[j, t * SEG : (t + 1) * SEG, :] = tile.astype(BF16)
        acc_ref[t] = total

    @pl.when(step == NR // 2 - 1)
    def _():
        for t in range(NC):
            sums = nt(jnp.ones((8, 128), F32), acc_ref[t], precision=HI)
            deg_ref[0, t : t + 1, :] = sums[0:1, :]
        for k in range(1, NC):
            deg_ref[k] = deg_ref[0]


def apply_kernel(pos_ref, deg_ref, v_ref, b_ref, p_ref, own_ref, root_ref, w_ref):
    @pl.when(pl.program_id(0) == 0)
    def _():
        root_ref[...] = lax.rsqrt(jnp.sum(deg_ref[...], axis=0))
        own_ref[...] = root_ref[pl.ds(pos_ref[0], 1), :]
        for t in range(NC):
            w_ref[:, t * SEG : (t + 1) * SEG] = (v_ref[t] * root_ref[t : t + 1, :]).astype(BF16)

    p_ref[0] = jnp.dot(w_ref[...], b_ref[0], preferred_element_type=F32)


def project_kernel(p_ref, own_ref, q_ref, gram_ref):
    q = jnp.sum(p_ref[...], axis=0) * own_ref[...]
    q_ref[...] = q
    down = jnp.concatenate([jnp.broadcast_to(q[a : a + 1], (VEC, SEG)) for a in range(VEC)], axis=0)
    pairs = down * jnp.concatenate([q] * VEC, axis=0)
    gram = nt(jnp.ones((8, SEG), F32), pairs, precision=HI)[0:1]
    flat = jnp.concatenate([gram[:, 0:128], gram[:, 128:256]], axis=0)
    gram_ref[...] = jnp.broadcast_to(flat[None], (ALL, 2, 128))


def finish_kernel(gram_ref, q_ref, basis_ref, triangle_ref):
    flat = jnp.sum(gram_ref[...], axis=0)
    row = lax.broadcasted_iota(jnp.int32, (VEC, 128), 0)
    lane = lax.broadcasted_iota(jnp.int32, (VEC, 128), 1)
    low = jnp.where(lane // VEC == row, flat[0:1], 0.0)
    high = jnp.where(lane // VEC == row - 8, flat[1:2], 0.0)
    pick = jnp.where(
        lax.broadcasted_iota(jnp.int32, (128, 128), 0) % VEC
        == lax.broadcasted_iota(jnp.int32, (128, 128), 1),
        1.0,
        0.0,
    )
    g = jnp.dot(low + high, pick, preferred_element_type=F32, precision=HI)
    q = q_ref[...]
    wide = lax.broadcasted_iota(jnp.int32, (VEC, SEG), 0)
    for k in range(VEC):
        column = jnp.sum(jnp.where(lane == k, g, 0.0), axis=1, keepdims=True)
        inverse = lax.rsqrt(column[k : k + 1, :])
        factor = column * inverse
        top_g = g[k : k + 1, :] * inverse
        top_q = q[k : k + 1, :] * inverse
        g = jnp.where(row == k, top_g, jnp.where(row > k, g - factor * top_g, g))
        q = jnp.where(wide == k, top_q, jnp.where(wide > k, q - factor * top_q, q))
    basis_ref[...] = q
    triangle_ref[...] = jnp.where(lane >= row, g, 0.0)[:, 0:VEC]


def to_all(copies, axes):
    return lax.all_to_all(copies, axes, split_axis=0, concat_axis=0, tiled=True)


def shape(*dims, dtype=F32):
    return jax.ShapeDtypeStruct(dims, dtype)


def per_device(embeddings, vectors):
    z, core = lax.axis_index("z"), lax.axis_index("core")
    column = lax.axis_index(COLS)
    unit, unit_copies = pl.pallas_call(
        unit_kernel,
        out_shape=(shape(DIM, SEG, dtype=BF16), shape(NC, DIM, SEG, dtype=BF16)),
        name="unit",
    )(embeddings.T)
    near = [unit]
    for k in range(1, 8):
        near.append(lax.ppermute(unit, "z", [(i, (i + k) % 8) for i in range(8)]))
    far = [lax.ppermute(a, "core", [(0, 1), (1, 0)]) for a in near]
    columns = to_all(unit_copies, COLS)
    vector_columns = to_all(jnp.broadcast_to(vectors.T, (NC, VEC, SEG)), COLS)
    block, degree = pl.pallas_call(
        affinity_kernel,
        grid=(NR // 2,),
        out_shape=(shape(NR, NC * SEG, SEG, dtype=BF16), shape(NC, NC, SEG)),
        in_specs=[smem()] + [vmem()] * 17,
        out_specs=(pl.BlockSpec((2, NC * SEG, SEG), lambda i: (i, 0, 0)), vmem()),
        scratch_shapes=[
            pltpu.VMEM((NR, DIM, SEG), BF16),
            pltpu.VMEM((NC, SEG, DIM), BF16),
            pltpu.VMEM((NC, SEG, 128), F32),
        ],
        compiler_params=params(32),
        cost_estimate=pl.CostEstimate(
            flops=2 * 256 * 4096 * 4096, transcendentals=4096 * 4096, bytes_accessed=1 << 23
        ),
        name="affinity",
    )(jnp.stack([z, core]), columns, *near, *far)
    degree = to_all(degree, COLS)
    product, own = pl.pallas_call(
        apply_kernel,
        out_shape=(shape(NR, VEC, SEG), shape(1, SEG)),
        grid=(NR,),
        in_specs=[smem(), vmem(), vmem(), pl.BlockSpec((1, NC * SEG, SEG), lambda i: (i, 0, 0))],
        out_specs=(pl.BlockSpec((1, VEC, SEG), lambda i: (i, 0, 0)), vmem()),
        scratch_shapes=[pltpu.VMEM((NC, SEG), F32), pltpu.VMEM((VEC, NC * SEG), BF16)],
        compiler_params=params(44),
        name="apply",
    )(jnp.stack([column]), degree, vector_columns, block)
    product = to_all(product, ROWS)
    projected, gram = pl.pallas_call(
        project_kernel,
        out_shape=(shape(VEC, SEG), shape(ALL, 2, 128)),
        name="project",
    )(product, own)
    gram = to_all(gram, AXES)
    basis, triangle = pl.pallas_call(
        finish_kernel,
        out_shape=(shape(VEC, SEG), shape(VEC, VEC)),
        name="finish",
    )(gram, projected)
    return basis.T, triangle


def solution(mesh):
    torus = Mesh(mesh.devices.reshape(SIZES), AXES)
    placed = (P(AXES, None), P(AXES, None))
    return jax.shard_map(
        per_device, mesh=torus, in_specs=placed, out_specs=(P(AXES, None), P()), check_vma=False
    )
```

time: 165 us -> 143 us (0.87)
  Pallas kernels: 55.2 us -> 42.9 us
  local copies, waits for them, and re-layouts: 8.27 us -> 0.76 us
  other arithmetic: 6.08 us -> 0.07 us
  starting transfers between devices: 38.3 us -> 43.6 us
    pallas_call x3 -> x4, Pallas kernels: 37 us -> 25.3 us  [the longest x1 17.6 us: per_device(): pl.pallas_call(affinity_kernel, grid=(NR // 2,), out_shape=(shape(NR, NC...]
    unnamed x43 -> x6, local copies, waits for them, and re-layouts: 7.67 us -> 0.01 us
    all_to_all x2 -> x3, starting transfers between devices: 14.4 us -> 21 us  [to_all(): return lax.all_to_all(copies, axes, split_axis=0, concat_axis=0, tiled=True)]
    another operation x4 -> x0, other arithmetic: 3.36 us -> none  [the longest x3 2.13 us: finish(): factor = jnp.linalg.cholesky(gram)]
    ppermute x7, starting transfers between devices: 19.6 us -> 17.7 us  [per_device(): near.append(lax.ppermute(unit, 'z', [(i, (i + k) % 8) for i in range(8)]))]
    all_to_all x3 -> x2, blocking collectives: 39.4 us -> 40.8 us  [to_all(): return lax.all_to_all(copies, axes, split_axis=0, concat_axis=0, tiled=True)]
    all_to_all x2 -> x3, waiting for transfers between devices: 7.76 us -> 7.72 us  [to_all(): return lax.all_to_all(copies, axes, split_axis=0, concat_axis=0, tiled=True)]
  transfers between devices with their start and end apart: 17 -> 18, of which waited for: 4 -> 4; matrix products, arithmetic and copies ran while one was open for 0% -> 1% of each run, Pallas kernels for 0% -> 12%
where the time goes in v2:
time: 143 us; the launch traced here: 142 us
  starting transfers between devices  43.6 us (30%)
  Pallas kernels  42.9 us (30%)
  blocking collectives  40.8 us (29%)
  waiting for transfers between devices  13.1 us (9%)
    all_to_all x2, blocking collectives, to_all(): return lax.all_to_all(copies, axes, split_axis=0, concat_axis=0, tiled=True)  40.8 us
    all_to_all x3, starting transfers between devices, to_all(): return lax.all_to_all(copies, axes, split_axis=0, concat_axis=0, tiled=True)  21 us
    ppermute x7, starting transfers between devices, per_device(): near.append(lax.ppermute(unit, 'z', [(i, (i + k) % 8) for i in range(8)]))  17.7 us
    pallas_call x1, Pallas kernels, per_device(): pl.pallas_call(affinity_kernel, grid=(NR // 2,), out_shape=(shape(NR, NC...  17.6 us
    pallas_call x1, Pallas kernels, per_device(): pl.pallas_call(apply_kernel, out_shape=(shape(NR, VEC, SEG), shape(1, SEG...  17.6 us
    all_to_all x3, waiting for transfers between devices, to_all(): return lax.all_to_all(copies, axes, split_axis=0, concat_axis=0, tiled=True)  7.72 us
    ppermute x7, waiting for transfers between devices, per_device(): near.append(lax.ppermute(unit, 'z', [(i, (i + k) % 8) for i in range(8)]))  5.35 us
    ppermute x8, starting transfers between devices, per_device(): far = [lax.ppermute(a, 'core', [(0, 1), (1, 0)]) for a in near]  4.96 us
  transfers between devices with their start and end apart: 18, of which 4 were waited for; matrix products, arithmetic and copies ran while one was open for 1% of the time, Pallas kernels for 12%

profile of v2, /device:TPU:1, one launch (start us, length us, event | category | flops | bytes accessed | tf_op | source)
XLA Modules:
  0.0 141.9 jit_solution(3214144690292382281)
XLA Ops:
  0.6 2.2 %unit.1 = (bf16[192,256]{1,0:T(8,128)(2,1)}, bf16[16,192,256]{2,1,0:T(8,128)(2,1)}) custom-call(bf16[192,256]{1,0:T(8,128)(2,1)} %bitcast.6), custom_call_target="tpu_custom_call" | custom-call | tf_op jit(solution)/shard_map/unit/pallas_call | solution.py:143
  2.9 0.0 copy-start.1
  2.9 0.0 copy-start.2
  2.9 7.7 %all-to-all-start = ((bf16[16,192,256]{2,1,0:T(8,128)(2,1)}), bf16[16,192,256]{2,1,0:T(8,128)(2,1)S(1)}, u32[]{:S(2)}, u32[]{:S(2)}) async-start(bf16[16,192,256]{2,1,0:T(8,128)(2,1)} %get-tuple-element.12), calls=%async_computation | async-start | bytes 3145728 | tf_op jit(solution)/shard_map/all_to_all | solution.py:133
  10.6 0.0 copy-done.1
  10.6 4.4 %collective-permute-start.2 = (bf16[192,256]{1,0:T(8,128)(2,1)S(1)}, bf16[192,256]{1,0:T(8,128)(2,1)S(1)}, u32[]{:S(2)}, u32[]{:S(2)}) collective-permute-start(bf16[192,256]{1,0:T(8,128)(2,1)S(1)} %copy-done.1), channel_id=1, source_target_pairs={{0,48},{16,64},{32,80},{48,96},{64,112},{80,0},{96,16},{112,32},{1... | collective-permute-start | bytes 294920 | tf_op jit(solution)/shard_map/ppermute | solution.py:150
  15.0 4.2 %collective-permute-start.3 = (bf16[192,256]{1,0:T(8,128)(2,1)S(1)}, bf16[192,256]{1,0:T(8,128)(2,1)S(1)}, u32[]{:S(2)}, u32[]{:S(2)}) collective-permute-start(bf16[192,256]{1,0:T(8,128)(2,1)S(1)} %copy-done.1), channel_id=1, source_target_pairs={{0,64},{16,80},{32,96},{48,112},{64,0},{80,16},{96,32},{112,48},{1... | collective-permute-start | bytes 294920 | tf_op jit(solution)/shard_map/ppermute | solution.py:150
  19.2 2.8 %collective-permute-start.4 = (bf16[192,256]{1,0:T(8,128)(2,1)S(1)}, bf16[192,256]{1,0:T(8,128)(2,1)S(1)}, u32[]{:S(2)}, u32[]{:S(2)}) collective-permute-start(bf16[192,256]{1,0:T(8,128)(2,1)S(1)} %copy-done.1), channel_id=1, source_target_pairs={{0,80},{16,96},{32,112},{48,0},{64,16},{80,32},{96,48},{112,64},{1... | collective-permute-start | bytes 294920 | tf_op jit(solution)/shard_map/ppermute | solution.py:150
  22.1 0.0 collective-permute-start.5
  22.1 0.4 collective-permute-start.6
  22.4 0.0 collective-permute-done.2.refs_3_
  22.4 2.0 %collective-permute-start = (bf16[192,256]{1,0:T(8,128)(2,1)S(1)}, bf16[192,256]{1,0:T(8,128)(2,1)S(1)}, u32[]{:S(2)}, u32[]{:S(2)}) collective-permute-start(bf16[192,256]{1,0:T(8,128)(2,1)S(1)} %copy-done.1), channel_id=1, source_target_pairs={{0,16},{16,32},{32,48},{48,64},{64,80},{80,96},{96,112},{112,0},{1... | collective-permute-start | bytes 294920 | tf_op jit(solution)/shard_map/ppermute | solution.py:150
  24.5 0.9 collective-permute-done.3.refs_4_
  25.4 3.8 %collective-permute-start.1 = (bf16[192,256]{1,0:T(8,128)(2,1)S(1)}, bf16[192,256]{1,0:T(8,128)(2,1)S(1)}, u32[]{:S(2)}, u32[]{:S(2)}) collective-permute-start(bf16[192,256]{1,0:T(8,128)(2,1)S(1)} %copy-done.1), channel_id=1, source_target_pairs={{0,32},{16,48},{32,64},{48,80},{64,96},{80,112},{96,0},{112,16},{1... | collective-permute-start | bytes 294920 | tf_op jit(solution)/shard_map/ppermute | solution.py:150
  29.2 0.1 collective-permute-done.4.refs_5_
  29.2 2.6 %collective-permute-start.7 = (bf16[192,256]{1,0:T(8,128)(2,1)S(1)}, bf16[192,256]{1,0:T(8,128)(2,1)S(1)}, u32[]{:S(2)}, u32[]{:S(2)}) collective-permute-start(bf16[192,256]{1,0:T(8,128)(2,1)S(1)} %copy-done.1), channel_id=1, source_target_pairs={{0,8},{8,0},{1,9},{9,1},{2,10},{10,2},{3,11},{11,3},{4,12},{12,4},... | collective-permute-start | bytes 294920 | tf_op jit(solution)/shard_map/ppermute | solution.py:151
  31.8 4.4 %collective-permute-done.5.refs_6_ = bf16[192,256]{1,0:T(8,128)(2,1)S(1)} collective-permute-done((bf16[192,256]{1,0:T(8,128)(2,1)S(1)}, bf16[192,256]{1,0:T(8,128)(2,1)S(1)}, u32[]{:S(2)}, u32[]{:S(2)}) %collective-permute-start.5) | collective-permute-done | bytes 98336 | tf_op jit(solution)/shard_map/ppermute | solution.py:150
  36.2 0.8 collective-permute-start.10
  37.0 0.0 collective-permute-done.6.refs_7_
  37.0 0.0 collective-permute-start.11
  37.0 0.0 collective-permute-done.refs_1_
  37.0 0.5 collective-permute-start.12
  37.5 0.0 collective-permute-done.1.refs_2_
  37.6 0.2 collective-permute-start.13
  37.8 0.0 collective-permute-done.7.refs_8_
  37.8 0.3 collective-permute-start.14
  38.1 0.0 collective-permute-done.10.refs_11_
  38.1 0.3 collective-permute-start.8
  38.3 0.0 collective-permute-done.11.refs_12_
  38.3 0.2 collective-permute-start.9
  38.6 0.1 pad_add_fusion.pos_ref
  38.7 0.0 all-to-all-done.t_ref
  38.7 0.0 copy-done.2
  38.7 0.7 broadcast_in_dim.3
  39.4 6.7 %all-to-all-start.2 = ((f32[16,16,256]{2,1,0:T(8,128)}), f32[16,16,256]{2,1,0:T(8,128)S(1)}, u32[]{:S(2)}, u32[]{:S(2)}) async-start(f32[16,16,256]{2,1,0:T(8,128)} %broadcast_in_dim.3), calls=%async_computation.2 | async-start | bytes 524288 | tf_op jit(solution)/shard_map/all_to_all | solution.py:133
  46.1 0.0 collective-permute-done.12.refs_13_
  46.1 0.0 collective-permute-done.13.refs_14_
  46.1 0.0 collective-permute-done.14.refs_15_
  46.1 0.0 collective-permute-done.8.refs_9_
  46.1 0.0 collective-permute-done.9.refs_10_
  46.1 17.6 %affinity.1 = (bf16[16,4096,256]{2,1,0:T(8,128)(2,1)}, f32[16,16,256]{2,1,0:T(8,128)}) custom-call(s32[2]{0:T(128)S(1)} %pad_add_fusion.pos_ref, bf16[16,192,256]{2,1,0:T(8,128)(2,1)S(1)} %all-to-all-done.t_ref, bf16[192,256]{1,0:T(8,128)(2,1)S(1)} %copy-done.1, bf16[192,256]{1,0:T(8,128)(2,1)S(1)} %collective-permute-done.refs_1_, ...), custom_call_target="tpu_custom_call" | custom-call | flops 8589934592 | bytes 8388608 | tf_op jit(solution)/shard_map/affinity/pallas_call | solution.py:154
  63.8 0.0 all-to-all-done.2.v_ref
  63.8 6.6 %all-to-all-start.1 = ((f32[16,16,256]{2,1,0:T(8,128)}), f32[16,16,256]{2,1,0:T(8,128)S(1)}, u32[]{:S(2)}, u32[]{:S(2)}) async-start(f32[16,16,256]{2,1,0:T(8,128)} %get-tuple-element.14), calls=%async_computation.1 | async-start | bytes 524288 | tf_op jit(solution)/shard_map/all_to_all | solution.py:133
  70.4 7.7 %all-to-all-done.1.deg_ref = f32[16,16,256]{2,1,0:T(8,128)S(1)} async-done(((f32[16,16,256]{2,1,0:T(8,128)}), f32[16,16,256]{2,1,0:T(8,128)S(1)}, u32[]{:S(2)}, u32[]{:S(2)}) %all-to-all-start.1) | async-done | bytes 262176 | tf_op jit(solution)/shard_map/all_to_all | solution.py:133
  78.2 17.6 %apply.1 = (f32[16,16,256]{2,1,0:T(8,128)S(1)}, f32[1,256]{1,0:T(1,128)S(1)}) custom-call(s32[1]{0:T(128)} %bitcast.pos_ref, f32[16,16,256]{2,1,0:T(8,128)S(1)} %all-to-all-done.1.deg_ref, f32[16,16,256]{2,1,0:T(8,128)S(1)} %all-to-all-done.2.v_ref, bf16[16,4096,256]{2,1,0:T(8,128)(2,1)} %get-tuple-element.15.b_ref), custom_call_target="tpu_custom_call" | custom-call | tf_op jit(solution)/shard_map/apply/pallas_call | solution.py:172
  95.7 0.0 copy-start
  95.7 19.6 %all_to_all.25.p_ref = f32[16,16,256]{2,1,0:T(8,128)} all-to-all(f32[16,16,256]{2,1,0:T(8,128)S(1)} %get-tuple-element.16), channel_id=1, replica_groups=mesh['xl'=2,'z'=8,'core'=2,'y'=4,'xh'=2] {'z','core'}, dimensions={0} | all-to-all | bytes 524288 | tf_op jit(solution)/shard_map/all_to_all | solution.py:133
  115.3 0.0 copy-done
  115.3 2.1 %project.1 = (f32[16,256]{1,0:T(8,128)}, f32[256,2,128]{2,1,0:T(2,128)}) custom-call(f32[16,16,256]{2,1,0:T(8,128)} %all_to_all.25.p_ref, f32[1,256]{1,0:T(1,128)} %copy-done), custom_call_target="tpu_custom_call" | custom-call | tf_op jit(solution)/shard_map/project/pallas_call | solution.py:183
  117.4 21.2 %all_to_all.26.gram_ref = f32[256,2,128]{2,1,0:T(2,128)} all-to-all(f32[256,2,128]{2,1,0:T(2,128)} %get-tuple-element.18), channel_id=1, replica_groups=mesh['xl'=2,'z'=8,'core'=2,'y'=4,'xh'=2] {'xl','z','core','y','xh'}, dimensions={0} | all-to-all | bytes 524288 | tf_op jit(solution)/shard_map/all_to_all | solution.py:133
  138.6 3.4 %finish.1 = (f32[16,256]{1,0:T(8,128)}, f32[16,16]{1,0:T(8,128)}) custom-call(f32[256,2,128]{2,1,0:T(2,128)} %all_to_all.26.gram_ref, f32[16,256]{1,0:T(8,128)} %get-tuple-element.19.q_ref), custom_call_target="tpu_custom_call" | custom-call | tf_op jit(solution)/shard_map/finish/pallas_call | solution.py:189
Async XLA Ops:
  2.9 7.7 %copy-start.1 = (bf16[192,256]{1,0:T(8,128)(2,1)S(1)}, bf16[192,256]{1,0:T(8,128)(2,1)}, u32[]{:S(2)}) copy-start(bf16[192,256]{1,0:T(8,128)(2,1)} %get-tuple-element.13.refs_0_) | copy-start | bytes 294916
  2.9 35.8 %copy-start.2 = (f32[256,16]{0,1:T(8,128)S(1)}, f32[256,16]{0,1:T(8,128)}, u32[]{:S(2)}) copy-start(f32[256,16]{0,1:T(8,128)} %param.3) | copy-start | bytes 49156
  2.9 35.8 %all-to-all-start = ((bf16[16,192,256]{2,1,0:T(8,128)(2,1)}), bf16[16,192,256]{2,1,0:T(8,128)(2,1)S(1)}, u32[]{:S(2)}, u32[]{:S(2)}) async-start(bf16[16,192,256]{2,1,0:T(8,128)(2,1)} %get-tuple-element.12), calls=%async_computation | async-start | bytes 3145728 | tf_op jit(solution)/shard_map/all_to_all | solution.py:133
  10.6 11.9 %collective-permute-start.2 = (bf16[192,256]{1,0:T(8,128)(2,1)S(1)}, bf16[192,256]{1,0:T(8,128)(2,1)S(1)}, u32[]{:S(2)}, u32[]{:S(2)}) collective-permute-start(bf16[192,256]{1,0:T(8,128)(2,1)S(1)} %copy-done.1), channel_id=1, source_target_pairs={{0,48},{16,64},{32,80},{48,96},{64,112},{80,0},{96,16},{112,32},{1... | collective-permute-start | bytes 294920 | tf_op jit(solution)/shard_map/ppermute | solution.py:150
  15.0 10.4 %collective-permute-start.3 = (bf16[192,256]{1,0:T(8,128)(2,1)S(1)}, bf16[192,256]{1,0:T(8,128)(2,1)S(1)}, u32[]{:S(2)}, u32[]{:S(2)}) collective-permute-start(bf16[192,256]{1,0:T(8,128)(2,1)S(1)} %copy-done.1), channel_id=1, source_target_pairs={{0,64},{16,80},{32,96},{48,112},{64,0},{80,16},{96,32},{112,48},{1... | collective-permute-start | bytes 294920 | tf_op jit(solution)/shard_map/ppermute | solution.py:150
  19.2 10.0 %collective-permute-start.4 = (bf16[192,256]{1,0:T(8,128)(2,1)S(1)}, bf16[192,256]{1,0:T(8,128)(2,1)S(1)}, u32[]{:S(2)}, u32[]{:S(2)}) collective-permute-start(bf16[192,256]{1,0:T(8,128)(2,1)S(1)} %copy-done.1), channel_id=1, source_target_pairs={{0,80},{16,96},{32,112},{48,0},{64,16},{80,32},{96,48},{112,64},{1... | collective-permute-start | bytes 294920 | tf_op jit(solution)/shard_map/ppermute | solution.py:150
  22.1 14.1 %collective-permute-start.5 = (bf16[192,256]{1,0:T(8,128)(2,1)S(1)}, bf16[192,256]{1,0:T(8,128)(2,1)S(1)}, u32[]{:S(2)}, u32[]{:S(2)}) collective-permute-start(bf16[192,256]{1,0:T(8,128)(2,1)S(1)} %copy-done.1), channel_id=1, source_target_pairs={{0,96},{16,112},{32,0},{48,16},{64,32},{80,48},{96,64},{112,80},{1... | collective-permute-start | bytes 294920 | tf_op jit(solution)/shard_map/ppermute | solution.py:150
  22.1 15.0 %collective-permute-start.6 = (bf16[192,256]{1,0:T(8,128)(2,1)S(1)}, bf16[192,256]{1,0:T(8,128)(2,1)S(1)}, u32[]{:S(2)}, u32[]{:S(2)}) collective-permute-start(bf16[192,256]{1,0:T(8,128)(2,1)S(1)} %copy-done.1), channel_id=1, source_target_pairs={{0,112},{16,0},{32,16},{48,32},{64,48},{80,64},{96,80},{112,96},{1... | collective-permute-start | bytes 294920 | tf_op jit(solution)/shard_map/ppermute | solution.py:150
  22.4 14.6 %collective-permute-start = (bf16[192,256]{1,0:T(8,128)(2,1)S(1)}, bf16[192,256]{1,0:T(8,128)(2,1)S(1)}, u32[]{:S(2)}, u32[]{:S(2)}) collective-permute-start(bf16[192,256]{1,0:T(8,128)(2,1)S(1)} %copy-done.1), channel_id=1, source_target_pairs={{0,16},{16,32},{32,48},{48,64},{64,80},{80,96},{96,112},{112,0},{1... | collective-permute-start | bytes 294920 | tf_op jit(solution)/shard_map/ppermute | solution.py:150
  25.4 12.2 %collective-permute-start.1 = (bf16[192,256]{1,0:T(8,128)(2,1)S(1)}, bf16[192,256]{1,0:T(8,128)(2,1)S(1)}, u32[]{:S(2)}, u32[]{:S(2)}) collective-permute-start(bf16[192,256]{1,0:T(8,128)(2,1)S(1)} %copy-done.1), channel_id=1, source_target_pairs={{0,32},{16,48},{32,64},{48,80},{64,96},{80,112},{96,0},{112,16},{1... | collective-permute-start | bytes 294920 | tf_op jit(solution)/shard_map/ppermute | solution.py:150
  29.2 8.5 %collective-permute-start.7 = (bf16[192,256]{1,0:T(8,128)(2,1)S(1)}, bf16[192,256]{1,0:T(8,128)(2,1)S(1)}, u32[]{:S(2)}, u32[]{:S(2)}) collective-permute-start(bf16[192,256]{1,0:T(8,128)(2,1)S(1)} %copy-done.1), channel_id=1, source_target_pairs={{0,8},{8,0},{1,9},{9,1},{2,10},{10,2},{3,11},{11,3},{4,12},{12,4},... | collective-permute-start | bytes 294920 | tf_op jit(solution)/shard_map/ppermute | solution.py:151
  36.2 1.9 %collective-permute-start.10 = (bf16[192,256]{1,0:T(8,128)(2,1)S(1)}, bf16[192,256]{1,0:T(8,128)(2,1)S(1)}, u32[]{:S(2)}, u32[]{:S(2)}) collective-permute-start(bf16[192,256]{1,0:T(8,128)(2,1)S(1)} %collective-permute-done.2.refs_3_), channel_id=1, source_target_pairs={{0,8},{8,0},{1,9},{9,1},{2,10},{10,2},{3,11},{11,3},{4,12},{12,4},... | collective-permute-start | bytes 294920 | tf_op jit(solution)/shard_map/ppermute | solution.py:151
  37.0 1.3 collective-permute-start.11
  37.0 9.0 %collective-permute-start.12 = (bf16[192,256]{1,0:T(8,128)(2,1)S(1)}, bf16[192,256]{1,0:T(8,128)(2,1)S(1)}, u32[]{:S(2)}, u32[]{:S(2)}) collective-permute-start(bf16[192,256]{1,0:T(8,128)(2,1)S(1)} %collective-permute-done.4.refs_5_), channel_id=1, source_target_pairs={{0,8},{8,0},{1,9},{9,1},{2,10},{10,2},{3,11},{11,3},{4,12},{12,4},... | collective-permute-start | bytes 294920 | tf_op jit(solution)/shard_map/ppermute | solution.py:151
  37.6 8.5 %collective-permute-start.13 = (bf16[192,256]{1,0:T(8,128)(2,1)S(1)}, bf16[192,256]{1,0:T(8,128)(2,1)S(1)}, u32[]{:S(2)}, u32[]{:S(2)}) collective-permute-start(bf16[192,256]{1,0:T(8,128)(2,1)S(1)} %collective-permute-done.5.refs_6_), channel_id=1, source_target_pairs={{0,8},{8,0},{1,9},{9,1},{2,10},{10,2},{3,11},{11,3},{4,12},{12,4},... | collective-permute-start | bytes 294920 | tf_op jit(solution)/shard_map/ppermute | solution.py:151
  37.8 8.3 %collective-permute-start.14 = (bf16[192,256]{1,0:T(8,128)(2,1)S(1)}, bf16[192,256]{1,0:T(8,128)(2,1)S(1)}, u32[]{:S(2)}, u32[]{:S(2)}) collective-permute-start(bf16[192,256]{1,0:T(8,128)(2,1)S(1)} %collective-permute-done.6.refs_7_), channel_id=1, source_target_pairs={{0,8},{8,0},{1,9},{9,1},{2,10},{10,2},{3,11},{11,3},{4,12},{12,4},... | collective-permute-start | bytes 294920 | tf_op jit(solution)/shard_map/ppermute | solution.py:151
  38.1 8.0 %collective-permute-start.8 = (bf16[192,256]{1,0:T(8,128)(2,1)S(1)}, bf16[192,256]{1,0:T(8,128)(2,1)S(1)}, u32[]{:S(2)}, u32[]{:S(2)}) collective-permute-start(bf16[192,256]{1,0:T(8,128)(2,1)S(1)} %collective-permute-done.refs_1_), channel_id=1, source_target_pairs={{0,8},{8,0},{1,9},{9,1},{2,10},{10,2},{3,11},{11,3},{4,12},{12,4},... | collective-permute-start | bytes 294920 | tf_op jit(solution)/shard_map/ppermute | solution.py:151
  38.3 7.8 %collective-permute-start.9 = (bf16[192,256]{1,0:T(8,128)(2,1)S(1)}, bf16[192,256]{1,0:T(8,128)(2,1)S(1)}, u32[]{:S(2)}, u32[]{:S(2)}) collective-permute-start(bf16[192,256]{1,0:T(8,128)(2,1)S(1)} %collective-permute-done.1.refs_2_), channel_id=1, source_target_pairs={{0,8},{8,0},{1,9},{9,1},{2,10},{10,2},{3,11},{11,3},{4,12},{12,4},... | collective-permute-start | bytes 294920 | tf_op jit(solution)/shard_map/ppermute | solution.py:151
  39.4 24.4 %all-to-all-start.2 = ((f32[16,16,256]{2,1,0:T(8,128)}), f32[16,16,256]{2,1,0:T(8,128)S(1)}, u32[]{:S(2)}, u32[]{:S(2)}) async-start(f32[16,16,256]{2,1,0:T(8,128)} %broadcast_in_dim.3), calls=%async_computation.2 | async-start | bytes 524288 | tf_op jit(solution)/shard_map/all_to_all | solution.py:133
  63.8 14.4 %all-to-all-start.1 = ((f32[16,16,256]{2,1,0:T(8,128)}), f32[16,16,256]{2,1,0:T(8,128)S(1)}, u32[]{:S(2)}, u32[]{:S(2)}) async-start(f32[16,16,256]{2,1,0:T(8,128)} %get-tuple-element.14), calls=%async_computation.1 | async-start | bytes 524288 | tf_op jit(solution)/shard_map/all_to_all | solution.py:133
  95.7 19.6 %copy-start = (f32[1,256]{1,0:T(1,128)}, f32[1,256]{1,0:T(1,128)S(1)}, u32[]{:S(2)}) copy-start(f32[1,256]{1,0:T(1,128)S(1)} %get-tuple-element.17.own_ref) | copy-start | bytes 3076

commit v3 on v2

v3 whole, which is shorter than its diff:
```python
import jax
import jax.numpy as jnp
from jax import lax
from jax.experimental import pallas as pl
from jax.experimental.pallas import tpu as pltpu
from jax.sharding import Mesh
from jax.sharding import PartitionSpec as P

AXES = ("xl", "z", "core", "y", "xh")
SIZES = (2, 8, 2, 4, 2)
ROWS = ("z", "core")
COLS = ("xl", "y", "xh")
CHIPS = 128
NR = 16
NC = 16
SEG = 256
DIM = 192
VEC = 16
WIDE = DIM + 2 * VEC
DEPTH = 6
SCALE = 14.426950408889634
UNSCALE = 4.5399929762484854e-05
EPS = 1e-6
MIB = 1 << 20
F32 = jnp.float32
BF16 = jnp.bfloat16
HI = lax.Precision.HIGHEST


def params(mib):
    return pltpu.CompilerParams(vmem_limit_bytes=mib * MIB)


def vmem():
    return pl.BlockSpec(memory_space=pltpu.VMEM)


def smem():
    return pl.BlockSpec(memory_space=pltpu.SMEM)


def nt(a, b, **kw):
    return lax.dot_general(a, b, (((1,), (1,)), ((), ())), preferred_element_type=F32, **kw)


def unit_kernel(e_ref, v_ref, u_ref, many_ref):
    e = e_ref[...].astype(F32)
    u = (e * lax.rsqrt(jnp.sum(e * e, axis=0, keepdims=True) + EPS)).astype(BF16)
    u_ref[...] = u
    v = v_ref[...]
    high = v.astype(BF16)
    low = (v - high.astype(F32)).astype(BF16)
    for k in range(NC):
        many_ref[k, 0:DIM, :] = u
        many_ref[k, DIM : DIM + VEC, :] = high
        many_ref[k, DIM + VEC : WIDE, :] = low


def affinity_kernel(pos_ref, t_ref, *refs):
    pairs, lone = refs[0:7], refs[7:9]
    b_ref, deg_ref, s_ref = refs[9:12]
    z, core = pos_ref[0], pos_ref[1]
    step = pl.program_id(0)

    def place(chip, side, rows):
        s_ref[lax.rem(chip + 16, 8) * 2 + side] = rows.T

    @pl.when(step == 0)
    def _():
        sign = 1 - 2 * core
        place(z, core, pairs[0][0])
        place(z, 1 - core, pairs[0][1])
        for k in range(1, 4):
            place(z - k * sign, core, pairs[2 * k - 1][0])
            place(z - k * sign, 1 - core, pairs[2 * k - 1][1])
            place(z + k * sign, 1 - core, pairs[2 * k][0])
            place(z + k * sign, core, pairs[2 * k][1])
        place(z + 4, core, lone[0][...])
        place(z + 4, 1 - core, lone[1][...])

    for j in range(2):
        piece = t_ref[step * 2 + j, 0:DIM, :]
        total = jnp.zeros((8, SEG), F32)
        for r in range(NR):
            score = jnp.dot(s_ref[r], piece, preferred_element_type=F32)
            tile = jnp.exp2(score * SCALE)
            total = total + jnp.sum(tile.reshape(SEG // 8, 8, SEG), axis=0)
            b_ref[j, r * SEG : (r + 1) * SEG, :] = tile.astype(BF16)
        sums = jnp.sum(total, axis=0, keepdims=True) * UNSCALE
        for k in range(NC):
            deg_ref[k, pl.ds(step * 2 + j, 1), :] = sums


def apply_kernel(pos_ref, deg_ref, t_ref, b_ref, p_ref, own_ref, root_ref, held_ref, sem_ref):
    def fetch(t):
        slot = t % DEPTH
        return pltpu.make_async_copy(b_ref.at[t], held_ref.at[slot], sem_ref.at[slot])

    for t in range(DEPTH):
        fetch(t).start()
    root_ref[...] = lax.rsqrt(jnp.sum(deg_ref[...], axis=0))
    own_ref[...] = root_ref[pl.ds(pos_ref[0], 1), :] * UNSCALE
    for t in range(NC):
        v = t_ref[t, DIM : DIM + VEC, :].astype(F32) + t_ref[t, DIM + VEC : WIDE, :].astype(F32)
        w = (v * root_ref[t : t + 1, :]).astype(BF16)
        fetch(t).wait()
        for r in range(NR):
            part = nt(w, held_ref[t % DEPTH, r * SEG : (r + 1) * SEG, :])
            p_ref[r] = part if t == 0 else p_ref[r] + part
        if t + DEPTH < NC:
            fetch(t + DEPTH).start()


def project_kernel(p_ref, own_ref, q_ref, gram_ref):
    q = jnp.sum(p_ref[...], axis=0) * own_ref[...]
    q_ref[...] = q
    down = jnp.concatenate([jnp.broadcast_to(q[a : a + 1], (VEC, SEG)) for a in range(VEC)], axis=0)
    pairs = down * jnp.concatenate([q] * VEC, axis=0)
    gram = nt(jnp.ones((8, SEG), F32), pairs, precision=HI)[0:1]
    flat = jnp.concatenate([gram[:, 0:128], gram[:, 128:256]], axis=0)
    gram_ref[...] = flat


def finish_kernel(gram_ref, q_ref, basis_ref, triangle_ref):
    flat = jnp.sum(gram_ref[...], axis=0)
    row = lax.broadcasted_iota(jnp.int32, (VEC, 128), 0)
    lane = lax.broadcasted_iota(jnp.int32, (VEC, 128), 1)
    low = jnp.where(lane // VEC == row, flat[0:1], 0.0)
    high = jnp.where(lane // VEC == row - 8, flat[1:2], 0.0)
    pick = jnp.where(
        lax.broadcasted_iota(jnp.int32, (128, 128), 0) % VEC
        == lax.broadcasted_iota(jnp.int32, (128, 128), 1),
        1.0,
        0.0,
    )
    g = jnp.dot(low + high, pick, preferred_element_type=F32, precision=HI)
    q = q_ref[...]
    wide = lax.broadcasted_iota(jnp.int32, (VEC, SEG), 0)
    for k in range(VEC):
        column = jnp.sum(jnp.where(lane == k, g, 0.0), axis=1, keepdims=True)
        inverse = lax.rsqrt(column[k : k + 1, :])
        factor = column * inverse
        top_g = g[k : k + 1, :] * inverse
        top_q = q[k : k + 1, :] * inverse
        g = jnp.where(row == k, top_g, jnp.where(row > k, g - factor * top_g, g))
        q = jnp.where(wide == k, top_q, jnp.where(wide > k, q - factor * top_q, q))
    basis_ref[...] = q
    triangle_ref[...] = jnp.where(lane >= row, g, 0.0)[:, 0:VEC]


def to_all(copies, axes):
    return lax.all_to_all(copies, axes, split_axis=0, concat_axis=0, tiled=True)


def shape(*dims, dtype=F32):
    return jax.ShapeDtypeStruct(dims, dtype)


def across(a):
    return lax.ppermute(a, "core", [(0, 1), (1, 0)])


def along(a, hops):
    turns = []
    for z in range(8):
        turns += [(z * 2, (z + hops) % 8 * 2), (z * 2 + 1, (z - hops) % 8 * 2 + 1)]
    return lax.ppermute(a, ROWS, turns)


def per_device(embeddings, vectors):
    z, core = lax.axis_index("z"), lax.axis_index("core")
    column = lax.axis_index(COLS)
    unit, unit_copies = pl.pallas_call(
        unit_kernel,
        out_shape=(shape(DIM, SEG, dtype=BF16), shape(NC, WIDE, SEG, dtype=BF16)),
        name="unit",
    )(embeddings.T, vectors.T)
    columns = to_all(unit_copies, COLS)
    pair = jnp.stack([unit, across(unit)])
    one, two = along(pair, 1), along(pair, 2)
    three, four = along(two, 1), along(two[0], 2)
    pairs = (pair, one, across(one), two, across(two), three, across(three))
    block, degree = pl.pallas_call(
        affinity_kernel,
        grid=(NC // 2,),
        out_shape=(shape(NC, NR * SEG, SEG, dtype=BF16), shape(NC, NC, SEG)),
        in_specs=[smem()] + [vmem()] * 10,
        out_specs=(pl.BlockSpec((2, NR * SEG, SEG), lambda i: (i, 0, 0)), vmem()),
        scratch_shapes=[pltpu.VMEM((NR, SEG, DIM), BF16)],
        compiler_params=params(32),
        cost_estimate=pl.CostEstimate(
            flops=2 * 256 * 4096 * 4096, transcendentals=4096 * 4096, bytes_accessed=1 << 25
        ),
        name="affinity",
    )(jnp.stack([z, core]), columns, *pairs, four, across(four))
    degree = to_all(degree, COLS)
    product, own = pl.pallas_call(
        apply_kernel,
        out_shape=(shape(NR, VEC, SEG), shape(1, SEG)),
        in_specs=[smem(), vmem(), vmem(), pl.BlockSpec(memory_space=pl.ANY)],
        out_specs=(vmem(), vmem()),
        scratch_shapes=[
            pltpu.VMEM((NC, SEG), F32),
            pltpu.VMEM((DEPTH, NR * SEG, SEG), BF16),
            pltpu.SemaphoreType.DMA((DEPTH,)),
        ],
        compiler_params=params(44),
        name="apply",
    )(jnp.stack([column]), degree, columns, block)
    product = to_all(product, ROWS)
    projected, gram = pl.pallas_call(
        project_kernel,
        out_shape=(shape(VEC, SEG), shape(2, 128)),
        name="project",
    )(product, own)
    gram = jnp.broadcast_to(gram + across(gram), (CHIPS, 2, 128))
    gram = to_all(gram, ("xl", "z", "y", "xh"))
    basis, triangle = pl.pallas_call(
        finish_kernel,
        out_shape=(shape(VEC, SEG), shape(VEC, VEC)),
        name="finish",
    )(gram, projected)
    return basis.T, triangle


def solution(mesh):
    torus = Mesh(mesh.devices.reshape(SIZES), AXES)
    placed = (P(AXES, None), P(AXES, None))
    return jax.shard_map(
        per_device, mesh=torus, in_specs=placed, out_specs=(P(AXES, None), P()), check_vma=False
    )
```

time: 143 us -> 124 us (0.87)
  starting transfers between devices: 43.6 us -> 29.9 us
  Pallas kernels: 42.9 us -> 34.4 us
  waiting for transfers between devices: 13.1 us -> 18.1 us
    all_to_all x3 -> x2, starting transfers between devices: 21 us -> 12.1 us  [to_all(): return lax.all_to_all(copies, axes, split_axis=0, concat_axis=0, tiled=True)]
    pallas_call x1, Pallas kernels: 17.6 us -> 11.6 us  [per_device(): pl.pallas_call(apply_kernel, out_shape=(shape(NR, VEC, SEG), shape(1, SEG...]
    ppermute x15 -> x10, starting transfers between devices: 22.6 us -> 17.8 us  [the longest x4 11 us: along(): return lax.ppermute(a, ROWS, turns)]
    all_to_all x3 -> x2, waiting for transfers between devices: 7.72 us -> 10.3 us  [to_all(): return lax.all_to_all(copies, axes, split_axis=0, concat_axis=0, tiled=True)]
    ppermute x15 -> x10, waiting for transfers between devices: 5.37 us -> 7.82 us  [the longest x4 4.65 us: along(): return lax.ppermute(a, ROWS, turns)]
    pallas_call x2, Pallas kernels: 19.7 us -> 17.3 us  [the longest x1 15.4 us: per_device(): pl.pallas_call(affinity_kernel, grid=(NC // 2,), out_shape=(shape(NC, NR...]
  transfers between devices with their start and end apart: 18 -> 12, of which waited for: 4 -> 8; matrix products, arithmetic and copies ran while one was open for 1% -> 0% of each run, Pallas kernels for 12% -> 0%
where the time goes in v3:
time: 124 us; the launch traced here: 123 us
  blocking collectives  39.5 us (32%)
  Pallas kernels  34.4 us (28%)
  starting transfers between devices  29.9 us (24%)
  waiting for transfers between devices  18.1 us (15%)
    all_to_all x2, blocking collectives, to_all(): return lax.all_to_all(copies, axes, split_axis=0, concat_axis=0, tiled=True)  39.5 us
    pallas_call x1, Pallas kernels, per_device(): pl.pallas_call(affinity_kernel, grid=(NC // 2,), out_shape=(shape(NC, NR...  15.4 us
    all_to_all x2, starting transfers between devices, to_all(): return lax.all_to_all(copies, axes, split_axis=0, concat_axis=0, tiled=True)  12.1 us
    pallas_call x1, Pallas kernels, per_device(): pl.pallas_call(apply_kernel, out_shape=(shape(NR, VEC, SEG), shape(1, SEG...  11.6 us
    ppermute x4, starting transfers between devices, along(): return lax.ppermute(a, ROWS, turns)  11 us
    all_to_all x2, waiting for transfers between devices, to_all(): return lax.all_to_all(copies, axes, split_axis=0, concat_axis=0, tiled=True)  10.3 us
    ppermute x6, starting transfers between devices, across(): return lax.ppermute(a, 'core', [(0, 1), (1, 0)])  6.82 us
    ppermute x4, waiting for transfers between devices, along(): return lax.ppermute(a, ROWS, turns)  4.65 us
  transfers between devices with their start and end apart: 12, of which 8 were waited for; matrix products, arithmetic and copies ran while one was open for 0% of the time, Pallas kernels for 0%

profile of v3, /device:TPU:1, one launch (start us, length us, event | category | flops | bytes accessed | tf_op | source)
XLA Modules:
  0.0 123.4 jit_solution(3295502423772025164)
XLA Ops:
  0.6 2.3 %unit.1 = (bf16[192,256]{1,0:T(8,128)(2,1)}, bf16[16,224,256]{2,1,0:T(8,128)(2,1)}) custom-call(bf16[192,256]{1,0:T(8,128)(2,1)} %bitcast.10, f32[16,256]{1,0:T(8,128)} %bitcast.13), custom_call_target="tpu_custom_call" | custom-call | tf_op jit(solution)/shard_map/unit/pallas_call | solution.py:173
  2.9 0.0 copy-start.1
  2.9 7.7 %all-to-all-start = ((bf16[16,224,256]{2,1,0:T(8,128)(2,1)}), bf16[16,224,256]{2,1,0:T(8,128)(2,1)S(1)}, u32[]{:S(2)}, u32[]{:S(2)}) async-start(bf16[16,224,256]{2,1,0:T(8,128)(2,1)} %get-tuple-element.12), calls=%async_computation | async-start | bytes 3670016 | tf_op jit(solution)/shard_map/all_to_all | solution.py:152
  10.7 0.0 copy-done.1
  10.7 1.0 collective-permute-start
  11.7 0.9 collective-permute-done
  12.7 6.1 %collective-permute-start.3 = (bf16[2,192,256]{2,1,0:T(8,128)(2,1)S(1)}, bf16[2,192,256]{2,1,0:T(8,128)(2,1)S(1)}, u32[]{:S(2)}, u32[]{:S(2)}) collective-permute-start(bf16[2,192,256]{2,1,0:T(8,128)(2,1)S(1)} %pad_maximum_fusion.refs_0_), channel_id=1, source_target_pairs={{0,32},{8,104},{16,48},{24,120},{32,64},{40,8},{48,80},{56,24},{64... | collective-permute-start | bytes 589832 | tf_op jit(solution)/shard_map/ppermute | solution.py:167
  18.8 0.7 collective-permute-start.1
  19.5 4.0 %collective-permute-done.3.refs_3_ = bf16[2,192,256]{2,1,0:T(8,128)(2,1)S(1)} collective-permute-done((bf16[2,192,256]{2,1,0:T(8,128)(2,1)S(1)}, bf16[2,192,256]{2,1,0:T(8,128)(2,1)S(1)}, u32[]{:S(2)}, u32[]{:S(2)}) %collective-permute-start.3) | collective-permute-done | bytes 196640 | tf_op jit(solution)/shard_map/ppermute | solution.py:167
  23.5 2.3 %collective-permute-start.5 = (bf16[2,192,256]{2,1,0:T(8,128)(2,1)S(1)}, bf16[2,192,256]{2,1,0:T(8,128)(2,1)S(1)}, u32[]{:S(2)}, u32[]{:S(2)}) collective-permute-start(bf16[2,192,256]{2,1,0:T(8,128)(2,1)S(1)} %collective-permute-done.3.refs_3_), channel_id=1, source_target_pairs={{0,16},{8,120},{16,32},{24,8},{32,48},{40,24},{48,64},{56,40},{64,... | collective-permute-start | bytes 589832 | tf_op jit(solution)/shard_map/ppermute | solution.py:167
  25.8 1.9 %collective-permute-start.7 = (bf16[192,256]{1,0:T(8,128)(2,1)S(1)}, bf16[192,256]{1,0:T(8,128)(2,1)S(1)}, u32[]{:S(2)}, u32[]{:S(2)}) collective-permute-start(bf16[192,256]{1,0:T(8,128)(2,1)S(1)} %slice_bitcast_fusion), channel_id=1, source_target_pairs={{0,32},{8,104},{16,48},{24,120},{32,64},{40,8},{48,80},{56,24},{64... | collective-permute-start | bytes 294920 | tf_op jit(solution)/shard_map/ppermute | solution.py:167
  27.7 0.0 collective-permute-start.4
  27.7 0.0 collective-permute-done.1.refs_1_
  27.7 0.5 collective-permute-start.2
  28.2 0.1 collective-permute-done.5.refs_5_
  28.4 2.7 %collective-permute-start.6 = (bf16[2,192,256]{2,1,0:T(8,128)(2,1)S(1)}, bf16[2,192,256]{2,1,0:T(8,128)(2,1)S(1)}, u32[]{:S(2)}, u32[]{:S(2)}) collective-permute-start(bf16[2,192,256]{2,1,0:T(8,128)(2,1)S(1)} %collective-permute-done.5.refs_5_), channel_id=1, source_target_pairs={{0,8},{8,0},{1,9},{9,1},{2,10},{10,2},{3,11},{11,3},{4,12},{12,4},... | collective-permute-start | bytes 589832 | tf_op jit(solution)/shard_map/ppermute | solution.py:160
  31.0 0.5 collective-permute-done.7.refs_7_
  31.6 2.6 %collective-permute-start.8 = (bf16[192,256]{1,0:T(8,128)(2,1)S(1)}, bf16[192,256]{1,0:T(8,128)(2,1)S(1)}, u32[]{:S(2)}, u32[]{:S(2)}) collective-permute-start(bf16[192,256]{1,0:T(8,128)(2,1)S(1)} %collective-permute-done.7.refs_7_), channel_id=1, source_target_pairs={{0,8},{8,0},{1,9},{9,1},{2,10},{10,2},{3,11},{11,3},{4,12},{12,4},... | collective-permute-start | bytes 294920 | tf_op jit(solution)/shard_map/ppermute | solution.py:160
  34.2 0.1 pad_add_fusion.pos_ref
  34.2 0.9 collective-permute-done.8.refs_8_
  35.1 0.0 collective-permute-done.4.refs_4_
  35.1 0.0 collective-permute-done.2.refs_2_
  35.1 0.0 collective-permute-done.6.refs_6_
  35.1 2.6 %all-to-all-done.t_ref = bf16[16,224,256]{2,1,0:T(8,128)(2,1)S(1)} async-done(((bf16[16,224,256]{2,1,0:T(8,128)(2,1)}), bf16[16,224,256]{2,1,0:T(8,128)(2,1)S(1)}, u32[]{:S(2)}, u32[]{:S(2)}) %all-to-all-start) | async-done | bytes 1835040 | tf_op jit(solution)/shard_map/all_to_all | solution.py:152
  37.8 15.4 %affinity.1 = (bf16[16,4096,256]{2,1,0:T(8,128)(2,1)}, f32[16,16,256]{2,1,0:T(8,128)}) custom-call(s32[2]{0:T(128)S(1)} %pad_add_fusion.pos_ref, bf16[16,224,256]{2,1,0:T(8,128)(2,1)S(1)} %all-to-all-done.t_ref, bf16[2,192,256]{2,1,0:T(8,128)(2,1)S(1)} %pad_maximum_fusion.refs_0_, bf16[2,192,256]{2,1,0:T(8,128)(2,1)S(1)} %collective-permute-done.1.refs_1_, ...), custom_call_target="tpu_custom_call" | custom-call | flops 8589934592 | bytes 33554432 | tf_op jit(solution)/shard_map/affinity/pallas_call | solution.py:183
  53.2 4.4 %all-to-all-start.1 = ((f32[16,16,256]{2,1,0:T(8,128)}), f32[16,16,256]{2,1,0:T(8,128)S(1)}, u32[]{:S(2)}, u32[]{:S(2)}) async-start(f32[16,16,256]{2,1,0:T(8,128)} %get-tuple-element.14), calls=%async_computation.1 | async-start | bytes 524288 | tf_op jit(solution)/shard_map/all_to_all | solution.py:152
  57.6 7.7 %all-to-all-done.1.deg_ref = f32[16,16,256]{2,1,0:T(8,128)S(1)} async-done(((f32[16,16,256]{2,1,0:T(8,128)}), f32[16,16,256]{2,1,0:T(8,128)S(1)}, u32[]{:S(2)}, u32[]{:S(2)}) %all-to-all-start.1) | async-done | bytes 262176 | tf_op jit(solution)/shard_map/all_to_all | solution.py:152
  65.3 11.6 %apply.1 = (f32[16,16,256]{2,1,0:T(8,128)S(1)}, f32[1,256]{1,0:T(1,128)S(1)}) custom-call(s32[1]{0:T(128)} %bitcast.pos_ref, f32[16,16,256]{2,1,0:T(8,128)S(1)} %all-to-all-done.1.deg_ref, bf16[16,224,256]{2,1,0:T(8,128)(2,1)S(1)} %all-to-all-done.t_ref, bf16[16,4096,256]{2,1,0:T(8,128)(2,1)} %get-tuple-element.15.b_ref), custom_call_target="tpu_custom_call" | custom-call | tf_op jit(solution)/shard_map/apply/pallas_call | solution.py:197
  76.8 0.0 copy-start
  76.8 22.1 %all_to_all.20.p_ref = f32[16,16,256]{2,1,0:T(8,128)} all-to-all(f32[16,16,256]{2,1,0:T(8,128)S(1)} %get-tuple-element.16), channel_id=1, replica_groups=mesh['xl'=2,'z'=8,'core'=2,'y'=4,'xh'=2] {'z','core'}, dimensions={0} | all-to-all | bytes 524288 | tf_op jit(solution)/shard_map/all_to_all | solution.py:152
  98.9 0.0 copy-done
  98.9 1.9 %project.1 = (f32[16,256]{1,0:T(8,128)}, f32[2,128]{1,0:T(2,128)}) custom-call(f32[16,16,256]{2,1,0:T(8,128)} %all_to_all.20.p_ref, f32[1,256]{1,0:T(1,128)} %copy-done), custom_call_target="tpu_custom_call" | custom-call | tf_op jit(solution)/shard_map/project/pallas_call | solution.py:211
  100.8 0.0 collective-permute-start.9
  100.8 1.3 %collective-permute-done.9 = f32[2,128]{1,0:T(2,128)S(1)} collective-permute-done((f32[2,128]{1,0:T(2,128)}, f32[2,128]{1,0:T(2,128)S(1)}, u32[]{:S(2)}, u32[]{:S(2)}) %collective-permute-start.9) | collective-permute-done | bytes 1056 | tf_op jit(solution)/shard_map/ppermute | solution.py:160
  102.1 0.7 add.11
  102.8 17.4 %all_to_all.21.gram_ref = f32[128,2,128]{2,1,0:T(2,128)} all-to-all(f32[128,2,128]{2,1,0:T(2,128)S(1)} %broadcast_in_dim.3), channel_id=1, replica_groups=mesh['xl'=2,'z'=8,'core'=2,'y'=4,'xh'=2] {'xl','z','y','xh'}, dimensions={0} | all-to-all | bytes 262144 | tf_op jit(solution)/shard_map/all_to_all | solution.py:152
  120.3 3.2 %finish.1 = (f32[16,256]{1,0:T(8,128)}, f32[16,16]{1,0:T(8,128)}) custom-call(f32[128,2,128]{2,1,0:T(2,128)} %all_to_all.21.gram_ref, f32[16,256]{1,0:T(8,128)} %get-tuple-element.19.q_ref), custom_call_target="tpu_custom_call" | custom-call | tf_op jit(solution)/shard_map/finish/pallas_call | solution.py:218
  (3 shorter events, 0.1 us)
Async XLA Ops:
  2.9 7.7 %copy-start.1 = (bf16[192,256]{1,0:T(8,128)(2,1)S(1)}, bf16[192,256]{1,0:T(8,128)(2,1)}, u32[]{:S(2)}) copy-start(bf16[192,256]{1,0:T(8,128)(2,1)} %get-tuple-element.13) | copy-start | bytes 294916
  2.9 34.8 %all-to-all-start = ((bf16[16,224,256]{2,1,0:T(8,128)(2,1)}), bf16[16,224,256]{2,1,0:T(8,128)(2,1)S(1)}, u32[]{:S(2)}, u32[]{:S(2)}) async-start(bf16[16,224,256]{2,1,0:T(8,128)(2,1)} %get-tuple-element.12), calls=%async_computation | async-start | bytes 3670016 | tf_op jit(solution)/shard_map/all_to_all | solution.py:152
  10.7 2.0 %collective-permute-start = (bf16[192,256]{1,0:T(8,128)(2,1)S(1)}, bf16[192,256]{1,0:T(8,128)(2,1)S(1)}, u32[]{:S(2)}, u32[]{:S(2)}) collective-permute-start(bf16[192,256]{1,0:T(8,128)(2,1)S(1)} %copy-done.1), channel_id=1, source_target_pairs={{0,8},{8,0},{1,9},{9,1},{2,10},{10,2},{3,11},{11,3},{4,12},{12,4},... | collective-permute-start | bytes 294920 | tf_op jit(solution)/shard_map/ppermute | solution.py:160
  12.7 10.8 %collective-permute-start.3 = (bf16[2,192,256]{2,1,0:T(8,128)(2,1)S(1)}, bf16[2,192,256]{2,1,0:T(8,128)(2,1)S(1)}, u32[]{:S(2)}, u32[]{:S(2)}) collective-permute-start(bf16[2,192,256]{2,1,0:T(8,128)(2,1)S(1)} %pad_maximum_fusion.refs_0_), channel_id=1, source_target_pairs={{0,32},{8,104},{16,48},{24,120},{32,64},{40,8},{48,80},{56,24},{64... | collective-permute-start | bytes 589832 | tf_op jit(solution)/shard_map/ppermute | solution.py:167
  18.8 8.9 %collective-permute-start.1 = (bf16[2,192,256]{2,1,0:T(8,128)(2,1)S(1)}, bf16[2,192,256]{2,1,0:T(8,128)(2,1)S(1)}, u32[]{:S(2)}, u32[]{:S(2)}) collective-permute-start(bf16[2,192,256]{2,1,0:T(8,128)(2,1)S(1)} %pad_maximum_fusion.refs_0_), channel_id=1, source_target_pairs={{0,16},{8,120},{16,32},{24,8},{32,48},{40,24},{48,64},{56,40},{64,... | collective-permute-start | bytes 589832 | tf_op jit(solution)/shard_map/ppermute | solution.py:167
  23.5 4.9 %collective-permute-start.5 = (bf16[2,192,256]{2,1,0:T(8,128)(2,1)S(1)}, bf16[2,192,256]{2,1,0:T(8,128)(2,1)S(1)}, u32[]{:S(2)}, u32[]{:S(2)}) collective-permute-start(bf16[2,192,256]{2,1,0:T(8,128)(2,1)S(1)} %collective-permute-done.3.refs_3_), channel_id=1, source_target_pairs={{0,16},{8,120},{16,32},{24,8},{32,48},{40,24},{48,64},{56,40},{64,... | collective-permute-start | bytes 589832 | tf_op jit(solution)/shard_map/ppermute | solution.py:167
  25.8 5.8 %collective-permute-start.7 = (bf16[192,256]{1,0:T(8,128)(2,1)S(1)}, bf16[192,256]{1,0:T(8,128)(2,1)S(1)}, u32[]{:S(2)}, u32[]{:S(2)}) collective-permute-start(bf16[192,256]{1,0:T(8,128)(2,1)S(1)} %slice_bitcast_fusion), channel_id=1, source_target_pairs={{0,32},{8,104},{16,48},{24,120},{32,64},{40,8},{48,80},{56,24},{64... | collective-permute-start | bytes 294920 | tf_op jit(solution)/shard_map/ppermute | solution.py:167
  27.7 7.4 %collective-permute-start.4 = (bf16[2,192,256]{2,1,0:T(8,128)(2,1)S(1)}, bf16[2,192,256]{2,1,0:T(8,128)(2,1)S(1)}, u32[]{:S(2)}, u32[]{:S(2)}) collective-permute-start(bf16[2,192,256]{2,1,0:T(8,128)(2,1)S(1)} %collective-permute-done.3.refs_3_), channel_id=1, source_target_pairs={{0,8},{8,0},{1,9},{9,1},{2,10},{10,2},{3,11},{11,3},{4,12},{12,4},... | collective-permute-start | bytes 589832 | tf_op jit(solution)/shard_map/ppermute | solution.py:160
  27.7 7.4 %collective-permute-start.2 = (bf16[2,192,256]{2,1,0:T(8,128)(2,1)S(1)}, bf16[2,192,256]{2,1,0:T(8,128)(2,1)S(1)}, u32[]{:S(2)}, u32[]{:S(2)}) collective-permute-start(bf16[2,192,256]{2,1,0:T(8,128)(2,1)S(1)} %collective-permute-done.1.refs_1_), channel_id=1, source_target_pairs={{0,8},{8,0},{1,9},{9,1},{2,10},{10,2},{3,11},{11,3},{4,12},{12,4},... | collective-permute-start | bytes 589832 | tf_op jit(solution)/shard_map/ppermute | solution.py:160
  28.4 6.7 %collective-permute-start.6 = (bf16[2,192,256]{2,1,0:T(8,128)(2,1)S(1)}, bf16[2,192,256]{2,1,0:T(8,128)(2,1)S(1)}, u32[]{:S(2)}, u32[]{:S(2)}) collective-permute-start(bf16[2,192,256]{2,1,0:T(8,128)(2,1)S(1)} %collective-permute-done.5.refs_5_), channel_id=1, source_target_pairs={{0,8},{8,0},{1,9},{9,1},{2,10},{10,2},{3,11},{11,3},{4,12},{12,4},... | collective-permute-start | bytes 589832 | tf_op jit(solution)/shard_map/ppermute | solution.py:160
  31.6 3.5 %collective-permute-start.8 = (bf16[192,256]{1,0:T(8,128)(2,1)S(1)}, bf16[192,256]{1,0:T(8,128)(2,1)S(1)}, u32[]{:S(2)}, u32[]{:S(2)}) collective-permute-start(bf16[192,256]{1,0:T(8,128)(2,1)S(1)} %collective-permute-done.7.refs_7_), channel_id=1, source_target_pairs={{0,8},{8,0},{1,9},{9,1},{2,10},{10,2},{3,11},{11,3},{4,12},{12,4},... | collective-permute-start | bytes 294920 | tf_op jit(solution)/shard_map/ppermute | solution.py:160
  53.2 12.0 %all-to-all-start.1 = ((f32[16,16,256]{2,1,0:T(8,128)}), f32[16,16,256]{2,1,0:T(8,128)S(1)}, u32[]{:S(2)}, u32[]{:S(2)}) async-start(f32[16,16,256]{2,1,0:T(8,128)} %get-tuple-element.14), calls=%async_computation.1 | async-start | bytes 524288 | tf_op jit(solution)/shard_map/all_to_all | solution.py:152
  76.8 22.1 %copy-start = (f32[1,256]{1,0:T(1,128)}, f32[1,256]{1,0:T(1,128)S(1)}, u32[]{:S(2)}) copy-start(f32[1,256]{1,0:T(1,128)S(1)} %get-tuple-element.17.own_ref) | copy-start | bytes 3076
  100.8 1.4 %collective-permute-start.9 = (f32[2,128]{1,0:T(2,128)}, f32[2,128]{1,0:T(2,128)S(1)}, u32[]{:S(2)}, u32[]{:S(2)}) collective-permute-start(f32[2,128]{1,0:T(2,128)} %get-tuple-element.18), channel_id=1, source_target_pairs={{0,8},{8,0},{1,9},{9,1},{2,10},{10,2},{3,11},{11,3},{4,12},{12,4},... | collective-permute-start | bytes 3080 | tf_op jit(solution)/shard_map/ppermute | solution.py:160

commit v4 on v3

--- a/solution.py
+++ b/solution.py
@@ -11,6 +11,7 @@
 ROWS = ("z", "core")
 COLS = ("xl", "y", "xh")
 CHIPS = 128
+HALF = 8
 NR = 16
 NC = 16
 SEG = 256
@@ -43,20 +44,34 @@
     return lax.dot_general(a, b, (((1,), (1,)), ((), ())), preferred_element_type=F32, **kw)
 
 
-def unit_kernel(e_ref, v_ref, u_ref, many_ref):
+def unit_kernel(e_ref, v_ref, u_ref, own_ref, many_ref):
     e = e_ref[...].astype(F32)
     u = (e * lax.rsqrt(jnp.sum(e * e, axis=0, keepdims=True) + EPS)).astype(BF16)
     u_ref[...] = u
     v = v_ref[...]
     high = v.astype(BF16)
     low = (v - high.astype(F32)).astype(BF16)
-    for k in range(NC):
-        many_ref[k, 0:DIM, :] = u
-        many_ref[k, DIM : DIM + VEC, :] = high
-        many_ref[k, DIM + VEC : WIDE, :] = low
-
-
-def affinity_kernel(pos_ref, t_ref, *refs):
+    own_ref[0:DIM, :] = u
+    own_ref[DIM : DIM + VEC, :] = high
+    own_ref[DIM + VEC : WIDE, :] = low
+    for k in range(HALF):
+        many_ref[k] = own_ref[...]
+
+
+def score_pieces(step, t_ref, s_ref, b_ref, keep):
+    for j in range(2):
+        t = step * 2 + j
+        piece = t_ref[t, 0:DIM, :]
+        total = jnp.zeros((8, SEG), F32)
+        for r in range(NR):
+            score = jnp.dot(s_ref[r], piece, preferred_element_type=F32)
+            tile = jnp.exp2(score * SCALE)
+            total = total + jnp.sum(tile.reshape(SEG // 8, 8, SEG), axis=0)
+            b_ref[j, r * SEG : (r + 1) * SEG, :] = tile.astype(BF16)
+        keep(t, jnp.sum(total, axis=0, keepdims=True) * UNSCALE)
+
+
+def first_kernel(pos_ref, t_ref, *refs):
     pairs, lone = refs[0:7], refs[7:9]
     b_ref, deg_ref, s_ref = refs[9:12]
     z, core = pos_ref[0], pos_ref[1]
@@ -78,35 +93,56 @@
         place(z + 4, core, lone[0][...])
         place(z + 4, 1 - core, lone[1][...])
 
-    for j in range(2):
-        piece = t_ref[step * 2 + j, 0:DIM, :]
-        total = jnp.zeros((8, SEG), F32)
-        for r in range(NR):
-            score = jnp.dot(s_ref[r], piece, preferred_element_type=F32)
-            tile = jnp.exp2(score * SCALE)
-            total = total + jnp.sum(tile.reshape(SEG // 8, 8, SEG), axis=0)
-            b_ref[j, r * SEG : (r + 1) * SEG, :] = tile.astype(BF16)
-        sums = jnp.sum(total, axis=0, keepdims=True) * UNSCALE
+    def keep(t, sums):
+        deg_ref[pl.ds(t, 1), :] = sums
+
+    score_pieces(step, t_ref, s_ref, b_ref, keep)
+
+
+def second_kernel(pos_ref, t_ref, s_ref, first_ref, b_ref, deg_ref):
+    xh = pos_ref[2]
+    step = pl.program_id(0)
+
+    @pl.when(step == 0)
+    def _():
+        for t in range(HALF):
+            for k in range(NC):
+                deg_ref[k, pl.ds(t * 2 + xh, 1), :] = first_ref[t : t + 1, :]
+
+    def keep(t, sums):
         for k in range(NC):
-            deg_ref[k, pl.ds(step * 2 + j, 1), :] = sums
-
-
-def apply_kernel(pos_ref, deg_ref, t_ref, b_ref, p_ref, own_ref, root_ref, held_ref, sem_ref):
+            deg_ref[k, pl.ds(t * 2 + 1 - xh, 1), :] = sums
+
+    score_pieces(step, t_ref, s_ref, b_ref, keep)
+
+
+def apply_kernel(pos_ref, deg_ref, *refs):
+    columns, blocks = refs[0:2], refs[2:4]
+    mine_ref, other_ref, own_ref, root_ref, held_ref, sem_ref = refs[4:10]
+    core, xh = pos_ref[1], pos_ref[2]
+
     def fetch(t):
         slot = t % DEPTH
-        return pltpu.make_async_copy(b_ref.at[t], held_ref.at[slot], sem_ref.at[slot])
+        return pltpu.make_async_copy(
+            blocks[t // HALF].at[t % HALF], held_ref.at[slot], sem_ref.at[slot]
+        )
 
     for t in range(DEPTH):
         fetch(t).start()
     root_ref[...] = lax.rsqrt(jnp.sum(deg_ref[...], axis=0))
-    own_ref[...] = root_ref[pl.ds(pos_ref[0], 1), :] * UNSCALE
+    own_ref[...] = root_ref[pl.ds(pos_ref[3], 1), :] * UNSCALE
     for t in range(NC):
-        v = t_ref[t, DIM : DIM + VEC, :].astype(F32) + t_ref[t, DIM + VEC : WIDE, :].astype(F32)
-        w = (v * root_ref[t : t + 1, :]).astype(BF16)
+        c = t % HALF
+        t_ref = columns[t // HALF]
+        root = root_ref[pl.ds(c * 2 + (xh if t < HALF else 1 - xh), 1), :]
+        v = t_ref[c, DIM : DIM + VEC, :].astype(F32) + t_ref[c, DIM + VEC : WIDE, :].astype(F32)
+        w = (v * root).astype(BF16)
         fetch(t).wait()
-        for r in range(NR):
-            part = nt(w, held_ref[t % DEPTH, r * SEG : (r + 1) * SEG, :])
-            p_ref[r] = part if t == 0 else p_ref[r] + part
+        for r in range(NR // 2):
+            for side, p_ref in ((core, mine_ref), (1 - core, other_ref)):
+                rows = pl.ds(pl.multiple_of((r * 2 + side) * SEG, SEG), SEG)
+                part = nt(w, held_ref[t % DEPTH, rows, :])
+                p_ref[r] = part if t == 0 else p_ref[r] + part
         if t + DEPTH < NC:
             fetch(t + DEPTH).start()
 
@@ -168,37 +204,55 @@
 
 
 def per_device(embeddings, vectors):
-    z, core = lax.axis_index("z"), lax.axis_index("core")
-    column = lax.axis_index(COLS)
-    unit, unit_copies = pl.pallas_call(
+    z, core, xh = lax.axis_index("z"), lax.axis_index("core"), lax.axis_index("xh")
+    position = jnp.stack([z, core, xh, lax.axis_index(COLS)])
+    unit, own_column, copies = pl.pallas_call(
         unit_kernel,
-        out_shape=(shape(DIM, SEG, dtype=BF16), shape(NC, WIDE, SEG, dtype=BF16)),
+        out_shape=(
+            shape(DIM, SEG, dtype=BF16),
+            shape(WIDE, SEG, dtype=BF16),
+            shape(HALF, WIDE, SEG, dtype=BF16),
+        ),
         name="unit",
     )(embeddings.T, vectors.T)
-    columns = to_all(unit_copies, COLS)
+    first_columns = to_all(copies, ("xl", "y"))
+    partner = lax.ppermute(own_column, "xh", [(0, 1), (1, 0)])
+    second_columns = to_all(jnp.broadcast_to(partner, (HALF, WIDE, SEG)), ("xl", "y"))
     pair = jnp.stack([unit, across(unit)])
     one, two = along(pair, 1), along(pair, 2)
     three, four = along(two, 1), along(two[0], 2)
     pairs = (pair, one, across(one), two, across(two), three, across(three))
-    block, degree = pl.pallas_call(
-        affinity_kernel,
-        grid=(NC // 2,),
-        out_shape=(shape(NC, NR * SEG, SEG, dtype=BF16), shape(NC, NC, SEG)),
+    cost = pl.CostEstimate(
+        flops=256 * 4096 * 4096, transcendentals=2048 * 4096, bytes_accessed=1 << 24
+    )
+    half = pltpu.HBM((HALF, NR * SEG, SEG), BF16)
+    half_spec = pl.BlockSpec((2, NR * SEG, SEG), lambda i: (i, 0, 0))
+    first_block, first_degree, rows = pl.pallas_call(
+        first_kernel,
+        grid=(HALF // 2,),
+        out_shape=(half, shape(HALF, SEG), shape(NR, SEG, DIM, dtype=BF16)),
         in_specs=[smem()] + [vmem()] * 10,
-        out_specs=(pl.BlockSpec((2, NR * SEG, SEG), lambda i: (i, 0, 0)), vmem()),
-        scratch_shapes=[pltpu.VMEM((NR, SEG, DIM), BF16)],
+        out_specs=(half_spec, vmem(), vmem()),
         compiler_params=params(32),
-        cost_estimate=pl.CostEstimate(
-            flops=2 * 256 * 4096 * 4096, transcendentals=4096 * 4096, bytes_accessed=1 << 25
-        ),
-        name="affinity",
-    )(jnp.stack([z, core]), columns, *pairs, four, across(four))
+        cost_estimate=cost,
+        name="first_affinity",
+    )(position, first_columns, *pairs, four, across(four))
+    second_block, degree = pl.pallas_call(
+        second_kernel,
+        grid=(HALF // 2,),
+        out_shape=(half, shape(NC, NC, SEG)),
+        in_specs=[smem()] + [vmem()] * 3,
+        out_specs=(half_spec, vmem()),
+        compiler_params=params(32),
+        cost_estimate=cost,
+        name="second_affinity",
+    )(position, second_columns, rows, first_degree)
     degree = to_all(degree, COLS)
-    product, own = pl.pallas_call(
+    mine, other, own = pl.pallas_call(
         apply_kernel,
-        out_shape=(shape(NR, VEC, SEG), shape(1, SEG)),
-        in_specs=[smem(), vmem(), vmem(), pl.BlockSpec(memory_space=pl.ANY)],
-        out_specs=(vmem(), vmem()),
+        out_shape=(shape(HALF, VEC, SEG), shape(HALF, VEC, SEG), shape(1, SEG)),
+        in_specs=[smem()] + [vmem()] * 3 + [pl.BlockSpec(memory_space=pl.ANY)] * 2,
+        out_specs=(vmem(), vmem(), vmem()),
         scratch_shapes=[
             pltpu.VMEM((NC, SEG), F32),
             pltpu.VMEM((DEPTH, NR * SEG, SEG), BF16),
@@ -206,8 +260,8 @@
         ],
         compiler_params=params(44),
         name="apply",
-    )(jnp.stack([column]), degree, columns, block)
-    product = to_all(product, ROWS)
+    )(position, degree, first_columns, second_columns, first_block, second_block)
+    product = to_all(mine + across(other), "z")
     projected, gram = pl.pallas_call(
         project_kernel,
         out_shape=(shape(VEC, SEG), shape(2, 128)),

time: 124 us -> 131 us (1.056)
  waiting for transfers between devices: 18.1 us -> 7.61 us
  blocking collectives: 39.5 us -> 45.5 us
  starting transfers between devices: 29.9 us -> 34.9 us
  local copies, waits for them, and re-layouts: 0.06 us -> 3.97 us
  Pallas kernels: 34.4 us -> 36.4 us
    all_to_all x2, waiting for transfers between devices: 10.3 us -> 0.01 us  [to_all(): return lax.all_to_all(copies, axes, split_axis=0, concat_axis=0, tiled=True)]
    all_to_all x2 -> x3, blocking collectives: 39.5 us -> 45.5 us  [to_all(): return lax.all_to_all(copies, axes, split_axis=0, concat_axis=0, tiled=True)]
    unnamed x4 -> x6, local copies, waits for them, and re-layouts: 0.01 us -> 2.93 us
    ppermute x0 -> x1, starting transfers between devices: none -> 2.45 us  [per_device(): partner = lax.ppermute(own_column, 'xh', [(0, 1), (1, 0)])]
    pallas_call x2 -> x3, Pallas kernels: 27 us -> 29.4 us  [the longest x1 12.1 us: per_device(): pl.pallas_call(apply_kernel, out_shape=(shape(HALF, VEC, SEG), shape(HALF...]
    ppermute x4, starting transfers between devices: 11 us -> 12.9 us  [along(): return lax.ppermute(a, ROWS, turns)]
    ppermute x6 -> x7, starting transfers between devices: 6.82 us -> 8.39 us  [across(): return lax.ppermute(a, 'core', [(0, 1), (1, 0)])]
    ppermute x6 -> x7, waiting for transfers between devices: 3.17 us -> 4.05 us  [across(): return lax.ppermute(a, 'core', [(0, 1), (1, 0)])]
  transfers between devices with their start and end apart: 12 -> 14, of which waited for: 8 -> 6; matrix products, arithmetic and copies ran while one was open for 0% -> 2% of each run, Pallas kernels for 0% -> 7%
where the time goes in v4:
time: 131 us
  blocking collectives  45.5 us (35%)
  Pallas kernels  36.4 us (28%)
  starting transfers between devices  34.9 us (27%)
  waiting for transfers between devices  7.61 us (6%)
  local copies, waits for them, and re-layouts  3.97 us (3%)
  other arithmetic  1.69 us (1%)
    all_to_all x3, blocking collectives, to_all(): return lax.all_to_all(copies, axes, split_axis=0, concat_axis=0, tiled=True)  45.5 us
    ppermute x4, starting transfers between devices, along(): return lax.ppermute(a, ROWS, turns)  12.9 us
    pallas_call x1, Pallas kernels, per_device(): pl.pallas_call(apply_kernel, out_shape=(shape(HALF, VEC, SEG), shape(HALF...  12.1 us
    all_to_all x2, starting transfers between devices, to_all(): return lax.all_to_all(copies, axes, split_axis=0, concat_axis=0, tiled=True)  11.1 us
    pallas_call x1, Pallas kernels, per_device(): pl.pallas_call(first_kernel, grid=(HALF // 2,), out_shape=(half, shape(HA...  8.94 us
    ppermute x7, starting transfers between devices, across(): return lax.ppermute(a, 'core', [(0, 1), (1, 0)])  8.39 us
    pallas_call x1, Pallas kernels, per_device(): pl.pallas_call(second_kernel, grid=(HALF // 2,), out_shape=(half, shape(N...  8.33 us
    ppermute x7, waiting for transfers between devices, across(): return lax.ppermute(a, 'core', [(0, 1), (1, 0)])  4.05 us
  transfers between devices with their start and end apart: 14, of which 6 were waited for; matrix products, arithmetic and copies ran while one was open for 2% of the time, Pallas kernels for 7%

profile of v4, /device:TPU:1, one launch (start us, length us, event | category | flops | bytes accessed | tf_op | source)
XLA Modules:
  0.0 130.7 jit_solution(16129675006143861126)
XLA Ops:
  0.6 2.0 %unit.1 = (bf16[192,256]{1,0:T(8,128)(2,1)}, bf16[224,256]{1,0:T(8,128)(2,1)}, bf16[8,224,256]{2,1,0:T(8,128)(2,1)}) custom-call(bf16[192,256]{1,0:T(8,128)(2,1)} %bitcast.11, f32[16,256]{1,0:T(8,128)} %bitcast.14), custom_call_target="tpu_custom_call" | custom-call | tf_op jit(solution)/shard_map/unit/pallas_call | solution.py:209
  2.7 5.9 %all-to-all-start.1 = ((bf16[8,224,256]{2,1,0:T(8,128)(2,1)}), bf16[8,224,256]{2,1,0:T(8,128)(2,1)S(1)}, u32[]{:S(2)}, u32[]{:S(2)}) async-start(bf16[8,224,256]{2,1,0:T(8,128)(2,1)} %get-tuple-element.18), calls=%async_computation.1 | async-start | bytes 1835008 | tf_op jit(solution)/shard_map/all_to_all | solution.py:188
  8.6 1.0 collective-permute-start.1
  9.6 1.2 collective-permute-done.1
  10.7 0.9 pad_maximum_fusion.refs_0_
  11.7 6.1 %collective-permute-start.4 = (bf16[2,192,256]{2,1,0:T(8,128)(2,1)S(1)}, bf16[2,192,256]{2,1,0:T(8,128)(2,1)S(1)}, u32[]{:S(2)}, u32[]{:S(2)}) collective-permute-start(bf16[2,192,256]{2,1,0:T(8,128)(2,1)S(1)} %pad_maximum_fusion.refs_0_), channel_id=1, source_target_pairs={{0,32},{8,104},{16,48},{24,120},{32,64},{40,8},{48,80},{56,24},{64... | collective-permute-start | bytes 589832 | tf_op jit(solution)/shard_map/ppermute | solution.py:203
  17.7 2.5 %collective-permute-start = (bf16[224,256]{1,0:T(8,128)(2,1)}, bf16[224,256]{1,0:T(8,128)(2,1)S(1)}, u32[]{:S(2)}, u32[]{:S(2)}) collective-permute-start(bf16[224,256]{1,0:T(8,128)(2,1)} %get-tuple-element.17), channel_id=1, source_target_pairs={{0,1},{1,0},{2,3},{3,2},{4,5},{5,4},{6,7},{7,6},{8,9},{9,8},{10,11... | collective-permute-start | bytes 344072 | tf_op jit(solution)/shard_map/ppermute | solution.py:219
  20.2 0.7 collective-permute-start.2
  20.9 1.5 %collective-permute-done.4.refs_3_ = bf16[2,192,256]{2,1,0:T(8,128)(2,1)S(1)} collective-permute-done((bf16[2,192,256]{2,1,0:T(8,128)(2,1)S(1)}, bf16[2,192,256]{2,1,0:T(8,128)(2,1)S(1)}, u32[]{:S(2)}, u32[]{:S(2)}) %collective-permute-start.4) | collective-permute-done | bytes 196640 | tf_op jit(solution)/shard_map/ppermute | solution.py:203
  22.4 2.3 %collective-permute-start.6 = (bf16[2,192,256]{2,1,0:T(8,128)(2,1)S(1)}, bf16[2,192,256]{2,1,0:T(8,128)(2,1)S(1)}, u32[]{:S(2)}, u32[]{:S(2)}) collective-permute-start(bf16[2,192,256]{2,1,0:T(8,128)(2,1)S(1)} %collective-permute-done.4.refs_3_), channel_id=1, source_target_pairs={{0,16},{8,120},{16,32},{24,8},{32,48},{40,24},{48,64},{56,40},{64,... | collective-permute-start | bytes 589832 | tf_op jit(solution)/shard_map/ppermute | solution.py:203
  24.7 0.0 collective-permute-done
  24.7 0.0 all-to-all-done.1.t_ref.refs_0_
  24.7 1.0 broadcast_in_dim.6
  25.7 5.2 %all-to-all-start = ((bf16[8,224,256]{2,1,0:T(8,128)(2,1)}), bf16[8,224,256]{2,1,0:T(8,128)(2,1)S(1)}, u32[]{:S(2)}, u32[]{:S(2)}) async-start(bf16[8,224,256]{2,1,0:T(8,128)(2,1)} %broadcast_in_dim.6), calls=%async_computation | async-start | bytes 1835008 | tf_op jit(solution)/shard_map/all_to_all | solution.py:188
  30.9 3.9 %collective-permute-start.8 = (bf16[192,256]{1,0:T(8,128)(2,1)S(1)}, bf16[192,256]{1,0:T(8,128)(2,1)S(1)}, u32[]{:S(2)}, u32[]{:S(2)}) collective-permute-start(bf16[192,256]{1,0:T(8,128)(2,1)S(1)} %slice_bitcast_fusion), channel_id=1, source_target_pairs={{0,32},{8,104},{16,48},{24,120},{32,64},{40,8},{48,80},{56,24},{64... | collective-permute-start | bytes 294920 | tf_op jit(solution)/shard_map/ppermute | solution.py:203
  34.8 0.0 collective-permute-start.5
  34.8 0.0 collective-permute-done.2.refs_1_
  34.8 0.5 collective-permute-start.3
  35.3 0.0 collective-permute-done.6.refs_5_
  35.3 0.1 collective-permute-start.7
  35.4 2.0 %collective-permute-done.8.refs_7_ = bf16[192,256]{1,0:T(8,128)(2,1)S(1)} collective-permute-done((bf16[192,256]{1,0:T(8,128)(2,1)S(1)}, bf16[192,256]{1,0:T(8,128)(2,1)S(1)}, u32[]{:S(2)}, u32[]{:S(2)}) %collective-permute-start.8) | collective-permute-done | bytes 98336 | tf_op jit(solution)/shard_map/ppermute | solution.py:203
  37.4 2.8 %collective-permute-start.9 = (bf16[192,256]{1,0:T(8,128)(2,1)S(1)}, bf16[192,256]{1,0:T(8,128)(2,1)S(1)}, u32[]{:S(2)}, u32[]{:S(2)}) collective-permute-start(bf16[192,256]{1,0:T(8,128)(2,1)S(1)} %collective-permute-done.8.refs_7_), channel_id=1, source_target_pairs={{0,8},{8,0},{1,9},{9,1},{2,10},{10,2},{3,11},{11,3},{4,12},{12,4},... | collective-permute-start | bytes 294920 | tf_op jit(solution)/shard_map/ppermute | solution.py:196
  40.1 0.1 pad_add_fusion.pos_ref
  40.2 0.9 collective-permute-done.9.refs_8_
  41.1 0.0 collective-permute-done.5.refs_4_
  41.1 0.0 collective-permute-done.3.refs_2_
  41.1 0.0 collective-permute-done.7.refs_6_
  41.1 8.9 %first_affinity.1 = (bf16[8,4096,256]{2,1,0:T(8,128)(2,1)}, f32[8,256]{1,0:T(8,128)S(1)}, bf16[16,256,192]{2,1,0:T(8,128)(2,1)S(1)}) custom-call(s32[4]{0:T(128)S(1)} %pad_add_fusion.pos_ref, bf16[8,224,256]{2,1,0:T(8,128)(2,1)S(1)} %all-to-all-done.1.t_ref.refs_0_, bf16[2,192,256]{2,1,0:T(8,128)(2,1)S(1)} %pad_maximum_fusion.refs_0_, ...), custom_call_target="tpu_custom_call" | custom-call | flops 4294967296 | bytes 16777216 | tf_op jit(solution)/shard_map/first_affinity/pallas_call | solution.py:230
  50.0 0.0 copy-start.1
  50.0 1.3 %copy-done.1 = bf16[16,256,192]{2,1,0:T(8,128)(2,1)} copy-done((bf16[16,256,192]{2,1,0:T(8,128)(2,1)}, bf16[16,256,192]{2,1,0:T(8,128)(2,1)S(1)}, u32[]{:S(2)}) %copy-start.1) | copy-done | bytes 1572888
  51.4 0.0 all-to-all-done.t_ref.refs_1_
  51.4 0.0 copy-start.2
  51.4 1.6 %copy-done.2 = bf16[16,256,192]{2,1,0:T(8,128)(2,1)S(1)} copy-done((bf16[16,256,192]{2,1,0:T(8,128)(2,1)S(1)}, bf16[16,256,192]{2,1,0:T(8,128)(2,1)}, u32[]{:S(2)}) %copy-start.2) | copy-done | bytes 1572888
  53.0 8.3 %second_affinity.1 = (bf16[8,4096,256]{2,1,0:T(8,128)(2,1)}, f32[16,16,256]{2,1,0:T(8,128)S(1)}) custom-call(s32[4]{0:T(128)S(1)} %pad_add_fusion.pos_ref, bf16[8,224,256]{2,1,0:T(8,128)(2,1)S(1)} %all-to-all-done.t_ref.refs_1_, bf16[16,256,192]{2,1,0:T(8,128)(2,1)S(1)} %copy-done.2, f32[8,256]{1,0:T(8,128)S(1)} %get-tuple-element.21.first_ref), custom_call_target="tpu_custom_call" | custom-call | flops 4294967296 | bytes 16777216 | tf_op jit(solution)/shard_map/second_affinity/pallas_call | solution.py:240
  61.3 13.6 %all_to_all.25.deg_ref = f32[16,16,256]{2,1,0:T(8,128)S(1)} all-to-all(f32[16,16,256]{2,1,0:T(8,128)S(1)} %get-tuple-element.22), channel_id=1, replica_groups=mesh['xl'=2,'z'=8,'core'=2,'y'=4,'xh'=2] {'xl','y','xh'}, dimensions={0} | all-to-all | bytes 524288 | tf_op jit(solution)/shard_map/all_to_all | solution.py:188
  74.9 12.1 %apply.1 = (f32[8,16,256]{2,1,0:T(8,128)S(1)}, f32[8,16,256]{2,1,0:T(8,128)S(1)}, f32[1,256]{1,0:T(1,128)S(1)}) custom-call(s32[4]{0:T(128)S(1)} %pad_add_fusion.pos_ref, f32[16,16,256]{2,1,0:T(8,128)S(1)} %all_to_all.25.deg_ref, bf16[8,224,256]{2,1,0:T(8,128)(2,1)S(1)} %all-to-all-done.1.t_ref.refs_0_, bf16[8,224,256]{2,1,0:T(8,128)(2,1)S(1)} %all-to-all-done.t_ref.refs_1_, ...), custom_call_target="tpu_custom_call" | custom-call | tf_op jit(solution)/shard_map/apply/pallas_call | solution.py:251
  87.0 0.0 copy-start
  87.0 1.9 %collective-permute-start.10 = (f32[8,16,256]{2,1,0:T(8,128)S(1)}, f32[8,16,256]{2,1,0:T(8,128)S(1)}, u32[]{:S(2)}, u32[]{:S(2)}) collective-permute-start(f32[8,16,256]{2,1,0:T(8,128)S(1)} %get-tuple-element.26), channel_id=1, source_target_pairs={{0,8},{8,0},{1,9},{9,1},{2,10},{10,2},{3,11},{11,3},{4,12},{12,4},... | collective-permute-start | bytes 393224 | tf_op jit(solution)/shard_map/ppermute | solution.py:196
  88.9 1.0 collective-permute-done.10
  89.9 0.0 copy-done
  90.0 14.6 %all_to_all.26.p_ref = f32[8,16,256]{2,1,0:T(8,128)} all-to-all(f32[8,16,256]{2,1,0:T(8,128)S(1)} %add.14), channel_id=1, replica_groups=mesh['xl'=2,'z'=8,'core'=2,'y'=4,'xh'=2] {'z'}, dimensions={0} | all-to-all | bytes 262144 | tf_op jit(solution)/shard_map/all_to_all | solution.py:188
  104.5 1.8 %project.1 = (f32[16,256]{1,0:T(8,128)}, f32[2,128]{1,0:T(2,128)}) custom-call(f32[8,16,256]{2,1,0:T(8,128)} %all_to_all.26.p_ref, f32[1,256]{1,0:T(1,128)} %copy-done), custom_call_target="tpu_custom_call" | custom-call | tf_op jit(solution)/shard_map/project/pallas_call | solution.py:265
  106.3 2.1 %collective-permute-start.11 = (f32[2,128]{1,0:T(2,128)}, f32[2,128]{1,0:T(2,128)S(1)}, u32[]{:S(2)}, u32[]{:S(2)}) collective-permute-start(f32[2,128]{1,0:T(2,128)} %get-tuple-element.28), channel_id=1, source_target_pairs={{0,8},{8,0},{1,9},{9,1},{2,10},{10,2},{3,11},{11,3},{4,12},{12,4},... | collective-permute-start | bytes 3080 | tf_op jit(solution)/shard_map/ppermute | solution.py:196
  108.4 1.0 collective-permute-done.11
  109.5 0.7 add.15
  110.2 17.3 %all_to_all.27.gram_ref = f32[128,2,128]{2,1,0:T(2,128)} all-to-all(f32[128,2,128]{2,1,0:T(2,128)S(1)} %broadcast_in_dim.7), channel_id=1, replica_groups=mesh['xl'=2,'z'=8,'core'=2,'y'=4,'xh'=2] {'xl','z','y','xh'}, dimensions={0} | all-to-all | bytes 262144 | tf_op jit(solution)/shard_map/all_to_all | solution.py:188
  127.5 3.2 %finish.1 = (f32[16,256]{1,0:T(8,128)}, f32[16,16]{1,0:T(8,128)}) custom-call(f32[128,2,128]{2,1,0:T(2,128)} %all_to_all.27.gram_ref, f32[16,256]{1,0:T(8,128)} %get-tuple-element.29.q_ref), custom_call_target="tpu_custom_call" | custom-call | tf_op jit(solution)/shard_map/finish/pallas_call | solution.py:272
  (3 shorter events, 0.1 us)
Async XLA Ops:
  2.7 22.1 %all-to-all-start.1 = ((bf16[8,224,256]{2,1,0:T(8,128)(2,1)}), bf16[8,224,256]{2,1,0:T(8,128)(2,1)S(1)}, u32[]{:S(2)}, u32[]{:S(2)}) async-start(bf16[8,224,256]{2,1,0:T(8,128)(2,1)} %get-tuple-element.18), calls=%async_computation.1 | async-start | bytes 1835008 | tf_op jit(solution)/shard_map/all_to_all | solution.py:188
  8.6 2.1 %collective-permute-start.1 = (bf16[192,256]{1,0:T(8,128)(2,1)}, bf16[192,256]{1,0:T(8,128)(2,1)S(1)}, u32[]{:S(2)}, u32[]{:S(2)}) collective-permute-start(bf16[192,256]{1,0:T(8,128)(2,1)} %get-tuple-element.19), channel_id=1, source_target_pairs={{0,8},{8,0},{1,9},{9,1},{2,10},{10,2},{3,11},{11,3},{4,12},{12,4},... | collective-permute-start | bytes 294920 | tf_op jit(solution)/shard_map/ppermute | solution.py:196
  11.7 10.8 %collective-permute-start.4 = (bf16[2,192,256]{2,1,0:T(8,128)(2,1)S(1)}, bf16[2,192,256]{2,1,0:T(8,128)(2,1)S(1)}, u32[]{:S(2)}, u32[]{:S(2)}) collective-permute-start(bf16[2,192,256]{2,1,0:T(8,128)(2,1)S(1)} %pad_maximum_fusion.refs_0_), channel_id=1, source_target_pairs={{0,32},{8,104},{16,48},{24,120},{32,64},{40,8},{48,80},{56,24},{64... | collective-permute-start | bytes 589832 | tf_op jit(solution)/shard_map/ppermute | solution.py:203
  17.7 7.0 %collective-permute-start = (bf16[224,256]{1,0:T(8,128)(2,1)}, bf16[224,256]{1,0:T(8,128)(2,1)S(1)}, u32[]{:S(2)}, u32[]{:S(2)}) collective-permute-start(bf16[224,256]{1,0:T(8,128)(2,1)} %get-tuple-element.17), channel_id=1, source_target_pairs={{0,1},{1,0},{2,3},{3,2},{4,5},{5,4},{6,7},{7,6},{8,9},{9,8},{10,11... | collective-permute-start | bytes 344072 | tf_op jit(solution)/shard_map/ppermute | solution.py:219
  20.2 14.6 %collective-permute-start.2 = (bf16[2,192,256]{2,1,0:T(8,128)(2,1)S(1)}, bf16[2,192,256]{2,1,0:T(8,128)(2,1)S(1)}, u32[]{:S(2)}, u32[]{:S(2)}) collective-permute-start(bf16[2,192,256]{2,1,0:T(8,128)(2,1)S(1)} %pad_maximum_fusion.refs_0_), channel_id=1, source_target_pairs={{0,16},{8,120},{16,32},{24,8},{32,48},{40,24},{48,64},{56,40},{64,... | collective-permute-start | bytes 589832 | tf_op jit(solution)/shard_map/ppermute | solution.py:203
  22.4 12.8 %collective-permute-start.6 = (bf16[2,192,256]{2,1,0:T(8,128)(2,1)S(1)}, bf16[2,192,256]{2,1,0:T(8,128)(2,1)S(1)}, u32[]{:S(2)}, u32[]{:S(2)}) collective-permute-start(bf16[2,192,256]{2,1,0:T(8,128)(2,1)S(1)} %collective-permute-done.4.refs_3_), channel_id=1, source_target_pairs={{0,16},{8,120},{16,32},{24,8},{32,48},{40,24},{48,64},{56,40},{64,... | collective-permute-start | bytes 589832 | tf_op jit(solution)/shard_map/ppermute | solution.py:203
  25.7 25.7 %all-to-all-start = ((bf16[8,224,256]{2,1,0:T(8,128)(2,1)}), bf16[8,224,256]{2,1,0:T(8,128)(2,1)S(1)}, u32[]{:S(2)}, u32[]{:S(2)}) async-start(bf16[8,224,256]{2,1,0:T(8,128)(2,1)} %broadcast_in_dim.6), calls=%async_computation | async-start | bytes 1835008 | tf_op jit(solution)/shard_map/all_to_all | solution.py:188
  30.9 6.5 %collective-permute-start.8 = (bf16[192,256]{1,0:T(8,128)(2,1)S(1)}, bf16[192,256]{1,0:T(8,128)(2,1)S(1)}, u32[]{:S(2)}, u32[]{:S(2)}) collective-permute-start(bf16[192,256]{1,0:T(8,128)(2,1)S(1)} %slice_bitcast_fusion), channel_id=1, source_target_pairs={{0,32},{8,104},{16,48},{24,120},{32,64},{40,8},{48,80},{56,24},{64... | collective-permute-start | bytes 294920 | tf_op jit(solution)/shard_map/ppermute | solution.py:203
  34.8 6.3 %collective-permute-start.5 = (bf16[2,192,256]{2,1,0:T(8,128)(2,1)S(1)}, bf16[2,192,256]{2,1,0:T(8,128)(2,1)S(1)}, u32[]{:S(2)}, u32[]{:S(2)}) collective-permute-start(bf16[2,192,256]{2,1,0:T(8,128)(2,1)S(1)} %collective-permute-done.4.refs_3_), channel_id=1, source_target_pairs={{0,8},{8,0},{1,9},{9,1},{2,10},{10,2},{3,11},{11,3},{4,12},{12,4},... | collective-permute-start | bytes 589832 | tf_op jit(solution)/shard_map/ppermute | solution.py:196
  34.8 6.3 %collective-permute-start.3 = (bf16[2,192,256]{2,1,0:T(8,128)(2,1)S(1)}, bf16[2,192,256]{2,1,0:T(8,128)(2,1)S(1)}, u32[]{:S(2)}, u32[]{:S(2)}) collective-permute-start(bf16[2,192,256]{2,1,0:T(8,128)(2,1)S(1)} %collective-permute-done.2.refs_1_), channel_id=1, source_target_pairs={{0,8},{8,0},{1,9},{9,1},{2,10},{10,2},{3,11},{11,3},{4,12},{12,4},... | collective-permute-start | bytes 589832 | tf_op jit(solution)/shard_map/ppermute | solution.py:196
  35.3 5.8 %collective-permute-start.7 = (bf16[2,192,256]{2,1,0:T(8,128)(2,1)S(1)}, bf16[2,192,256]{2,1,0:T(8,128)(2,1)S(1)}, u32[]{:S(2)}, u32[]{:S(2)}) collective-permute-start(bf16[2,192,256]{2,1,0:T(8,128)(2,1)S(1)} %collective-permute-done.6.refs_5_), channel_id=1, source_target_pairs={{0,8},{8,0},{1,9},{9,1},{2,10},{10,2},{3,11},{11,3},{4,12},{12,4},... | collective-permute-start | bytes 589832 | tf_op jit(solution)/shard_map/ppermute | solution.py:196
  37.4 3.7 %collective-permute-start.9 = (bf16[192,256]{1,0:T(8,128)(2,1)S(1)}, bf16[192,256]{1,0:T(8,128)(2,1)S(1)}, u32[]{:S(2)}, u32[]{:S(2)}) collective-permute-start(bf16[192,256]{1,0:T(8,128)(2,1)S(1)} %collective-permute-done.8.refs_7_), channel_id=1, source_target_pairs={{0,8},{8,0},{1,9},{9,1},{2,10},{10,2},{3,11},{11,3},{4,12},{12,4},... | collective-permute-start | bytes 294920 | tf_op jit(solution)/shard_map/ppermute | solution.py:196
  50.0 1.3 %copy-start.1 = (bf16[16,256,192]{2,1,0:T(8,128)(2,1)}, bf16[16,256,192]{2,1,0:T(8,128)(2,1)S(1)}, u32[]{:S(2)}) copy-start(bf16[16,256,192]{2,1,0:T(8,128)(2,1)S(1)} %get-tuple-element.20.s_ref) | copy-start | bytes 4718596
  51.4 1.6 %copy-start.2 = (bf16[16,256,192]{2,1,0:T(8,128)(2,1)S(1)}, bf16[16,256,192]{2,1,0:T(8,128)(2,1)}, u32[]{:S(2)}) copy-start(bf16[16,256,192]{2,1,0:T(8,128)(2,1)} %copy-done.1) | copy-start | bytes 4718596
  87.0 2.9 %copy-start = (f32[1,256]{1,0:T(1,128)}, f32[1,256]{1,0:T(1,128)S(1)}, u32[]{:S(2)}) copy-start(f32[1,256]{1,0:T(1,128)S(1)} %get-tuple-element.27.own_ref) | copy-start | bytes 3076
  87.0 2.9 %collective-permute-start.10 = (f32[8,16,256]{2,1,0:T(8,128)S(1)}, f32[8,16,256]{2,1,0:T(8,128)S(1)}, u32[]{:S(2)}, u32[]{:S(2)}) collective-permute-start(f32[8,16,256]{2,1,0:T(8,128)S(1)} %get-tuple-element.26), channel_id=1, source_target_pairs={{0,8},{8,0},{1,9},{9,1},{2,10},{10,2},{3,11},{11,3},{4,12},{12,4},... | collective-permute-start | bytes 393224 | tf_op jit(solution)/shard_map/ppermute | solution.py:196
  106.3 3.2 %collective-permute-start.11 = (f32[2,128]{1,0:T(2,128)}, f32[2,128]{1,0:T(2,128)S(1)}, u32[]{:S(2)}, u32[]{:S(2)}) collective-permute-start(f32[2,128]{1,0:T(2,128)} %get-tuple-element.28), channel_id=1, source_target_pairs={{0,8},{8,0},{1,9},{9,1},{2,10},{10,2},{3,11},{11,3},{4,12},{12,4},... | collective-permute-start | bytes 3080 | tf_op jit(solution)/shard_map/ppermute | solution.py:196

commit v5 on v3

v5 whole, which is shorter than its diff:
```python
import jax
import jax.numpy as jnp
from jax import lax
from jax.experimental import pallas as pl
from jax.experimental.pallas import tpu as pltpu
from jax.sharding import Mesh
from jax.sharding import PartitionSpec as P

AXES = ("xl", "z", "core", "y", "xh")
SIZES = (2, 8, 2, 4, 2)
ROWS = ("z", "core")
COLS = ("xl", "y", "xh")
CHIPS = 128
HALF = 8
NR = 16
NC = 16
SEG = 256
DIM = 192
VEC = 16
DEPTH = 6
SCALE = 14.426950408889634
UNSCALE = 4.5399929762484854e-05
EPS = 1e-6
NEAR = [(2 * k + j, chip, flip) for k, (chip, flip) in enumerate(((0, 0), (-1, 0), (1, 1), (-2, 0), (2, 1))) for j in range(2)]
FAR = [(2 * k + j, chip, flip) for k, (chip, flip) in enumerate(((-3, 0), (3, 1))) for j in range(2)]
MIB = 1 << 20
F32 = jnp.float32
BF16 = jnp.bfloat16
HI = lax.Precision.HIGHEST


def params(mib):
    return pltpu.CompilerParams(vmem_limit_bytes=mib * MIB)


def vmem():
    return pl.BlockSpec(memory_space=pltpu.VMEM)


def smem():
    return pl.BlockSpec(memory_space=pltpu.SMEM)


def nt(a, b, **kw):
    return lax.dot_general(a, b, (((1,), (1,)), ((), ())), preferred_element_type=F32, **kw)


def unit_kernel(e_ref, u_ref, many_ref):
    e = e_ref[...].astype(F32)
    u_ref[...] = (e * lax.rsqrt(jnp.sum(e * e, axis=0, keepdims=True) + EPS)).astype(BF16)
    for k in range(NC):
        many_ref[k] = u_ref[...]


def score_pieces(step, t_ref, s_ref, b_ref, keep):
    for j in range(2):
        t = step * 2 + j
        piece = t_ref[t]
        total = jnp.zeros((8, SEG), F32)
        for r in range(s_ref.shape[0]):
            score = jnp.dot(s_ref[r], piece, preferred_element_type=F32)
            tile = jnp.exp2(score * SCALE)
            total = total + jnp.sum(tile.reshape(SEG // 8, 8, SEG), axis=0)
            b_ref[j, r * SEG : (r + 1) * SEG, :] = tile.astype(BF16)
        keep(t, jnp.sum(total, axis=0, keepdims=True) * UNSCALE)


def near_kernel(t_ref, *refs):
    pairs = refs[0:5]
    b_ref, deg_ref, s_ref = refs[5:8]
    step = pl.program_id(0)

    @pl.when(step == 0)
    def _():
        for k in range(5):
            for j in range(2):
                s_ref[2 * k + j] = pairs[k][j].T

    def keep(t, sums):
        deg_ref[pl.ds(t, 1), :] = sums

    score_pieces(step, t_ref, s_ref, b_ref, keep)


def far_kernel(t_ref, near_deg_ref, v_ref, *refs):
    pairs, lone = refs[0:2], refs[2:4]
    b_ref, deg_ref, s_ref = refs[4:7]
    step = pl.program_id(0)

    @pl.when(step == 0)
    def _():
        for k in range(2):
            for j in range(2):
                s_ref[2 * k + j] = pairs[k][j].T
            s_ref[4 + k] = lone[k][...].T
        for k in range(NC):
            deg_ref[k, NC : NC + VEC, :] = v_ref[...]

    def keep(t, sums):
        sums = sums + near_deg_ref[pl.ds(t, 1), :]
        for k in range(NC):
            deg_ref[k, pl.ds(t, 1), :] = sums

    score_pieces(step, t_ref, s_ref, b_ref, keep)


def apply_kernel(pos_ref, deg_ref, near_ref, far_ref, *refs):
    mine_ref, other_ref, own_ref, root_ref, near_held, far_held, sem_ref = refs
    z, core = pos_ref[0], pos_ref[1]
    sign = 1 - 2 * core

    def fetch(t):
        slot = t % DEPTH
        return (
            pltpu.make_async_copy(near_ref.at[t], near_held.at[slot], sem_ref.at[0, slot]),
            pltpu.make_async_copy(far_ref.at[t], far_held.at[slot], sem_ref.at[1, slot]),
        )

    for t in range(DEPTH):
        for copy in fetch(t):
            copy.start()
    degree = deg_ref[0, 0:NC, :]
    for k in range(1, NC):
        degree = degree + deg_ref[k, 0:NC, :]
    root_ref[...] = lax.rsqrt(degree)
    own_ref[...] = root_ref[pl.ds(pos_ref[2], 1), :] * UNSCALE
    places = [(near_held, r, chip, r % 2 == flip) for r, chip, flip in NEAR]
    places += [(far_held, r, chip, r % 2 == flip) for r, chip, flip in FAR]
    places += [(far_held, 4, 4, True), (far_held, 5, 4, False)]
    for t in range(NC):
        w = (deg_ref[t, NC : NC + VEC, :] * root_ref[t : t + 1, :]).astype(BF16)
        for copy in fetch(t):
            copy.wait()
        for held, r, chip, same in places:
            part = nt(w, held[t % DEPTH, r * SEG : (r + 1) * SEG, :])
            p_ref = mine_ref if same else other_ref
            place = lax.rem(z + chip * sign + 16, 8)
            p_ref[place] = part if t == 0 else p_ref[place] + part
        if t + DEPTH < NC:
            for copy in fetch(t + DEPTH):
                copy.start()


def project_kernel(p_ref, own_ref, q_ref, gram_ref):
    q = jnp.sum(p_ref[...], axis=0) * own_ref[...]
    q_ref[...] = q
    down = jnp.concatenate([jnp.broadcast_to(q[a : a + 1], (VEC, SEG)) for a in range(VEC)], axis=0)
    pairs = down * jnp.concatenate([q] * VEC, axis=0)
    gram = nt(jnp.ones((8, SEG), F32), pairs, precision=HI)[0:1]
    flat = jnp.concatenate([gram[:, 0:128], gram[:, 128:256]], axis=0)
    gram_ref[...] = flat


def finish_kernel(gram_ref, q_ref, basis_ref, triangle_ref):
    flat = jnp.sum(gram_ref[...], axis=0)
    row = lax.broadcasted_iota(jnp.int32, (VEC, 128), 0)
    lane = lax.broadcasted_iota(jnp.int32, (VEC, 128), 1)
    low = jnp.where(lane // VEC == row, flat[0:1], 0.0)
    high = jnp.where(lane // VEC == row - 8, flat[1:2], 0.0)
    pick = jnp.where(
        lax.broadcasted_iota(jnp.int32, (128, 128), 0) % VEC
        == lax.broadcasted_iota(jnp.int32, (128, 128), 1),
        1.0,
        0.0,
    )
    g = jnp.dot(low + high, pick, preferred_element_type=F32, precision=HI)
    q = q_ref[...]
    wide = lax.broadcasted_iota(jnp.int32, (VEC, SEG), 0)
    for k in range(VEC):
        column = jnp.sum(jnp.where(lane == k, g, 0.0), axis=1, keepdims=True)
        inverse = lax.rsqrt(column[k : k + 1, :])
        factor = column * inverse
        top_g = g[k : k + 1, :] * inverse
        top_q = q[k : k + 1, :] * inverse
        g = jnp.where(row == k, top_g, jnp.where(row > k, g - factor * top_g, g))
        q = jnp.where(wide == k, top_q, jnp.where(wide > k, q - factor * top_q, q))
    basis_ref[...] = q
    triangle_ref[...] = jnp.where(lane >= row, g, 0.0)[:, 0:VEC]


def to_all(copies, axes):
    return lax.all_to_all(copies, axes, split_axis=0, concat_axis=0, tiled=True)


def shape(*dims, dtype=F32):
    return jax.ShapeDtypeStruct(dims, dtype)


def across(a):
    return lax.ppermute(a, "core", [(0, 1), (1, 0)])


def along(a, hops):
    turns = []
    for z in range(8):
        turns += [(z * 2, (z + hops) % 8 * 2), (z * 2 + 1, (z - hops) % 8 * 2 + 1)]
    return lax.ppermute(a, ROWS, turns)


def per_device(embeddings, vectors):
    position = jnp.stack([lax.axis_index("z"), lax.axis_index("core"), lax.axis_index(COLS)])
    unit, copies = pl.pallas_call(
        unit_kernel,
        out_shape=(shape(DIM, SEG, dtype=BF16), shape(NC, DIM, SEG, dtype=BF16)),
        name="unit",
    )(embeddings.T)
    columns = to_all(copies, COLS)
    pair = jnp.stack([unit, across(unit)])
    one, two = along(pair, 1), along(pair, 2)
    three, four = along(two, 1), along(two[0], 2)

    def affinity(kernel, name, count, operands, out_degree):
        return pl.pallas_call(
            kernel,
            grid=(NC // 2,),
            out_shape=(pltpu.HBM((NC, count * SEG, SEG), BF16), out_degree),
            in_specs=[vmem()] * len(operands),
            out_specs=(pl.BlockSpec((2, count * SEG, SEG), lambda i: (i, 0, 0)), vmem()),
            scratch_shapes=[pltpu.VMEM((count, SEG, DIM), BF16)],
            compiler_params=params(32),
            cost_estimate=pl.CostEstimate(
                flops=2 * 256 * 4096 * SEG * count,
                transcendentals=4096 * SEG * count,
                bytes_accessed=2 * 4096 * SEG * count,
            ),
            name=name,
        )(*operands)

    near = (columns, pair, one, across(one), two, across(two))
    near_block, near_degree = affinity(near_kernel, "near_affinity", 10, near, shape(NC, SEG))
    far = (columns, near_degree, vectors.T, three, across(three), four, across(four))
    far_block, degree = affinity(far_kernel, "far_affinity", 6, far, shape(NC, NC + VEC, SEG))
    degree = to_all(degree, COLS)
    mine, other, own = pl.pallas_call(
        apply_kernel,
        out_shape=(shape(HALF, VEC, SEG), shape(HALF, VEC, SEG), shape(1, SEG)),
        in_specs=[smem(), vmem()] + [pl.BlockSpec(memory_space=pl.ANY)] * 2,
        out_specs=(vmem(), vmem(), vmem()),
        scratch_shapes=[
            pltpu.VMEM((NC, SEG), F32),
            pltpu.VMEM((DEPTH, 10 * SEG, SEG), BF16),
            pltpu.VMEM((DEPTH, 6 * SEG, SEG), BF16),
            pltpu.SemaphoreType.DMA((2, DEPTH)),
        ],
        compiler_params=params(48),
        name="apply",
    )(position, degree, near_block, far_block)
    product = to_all(mine + across(other), "z")
    projected, gram = pl.pallas_call(
        project_kernel,
        out_shape=(shape(VEC, SEG), shape(2, 128)),
        name="project",
    )(product, own)
    gram = jnp.broadcast_to(gram + across(gram), (CHIPS, 2, 128))
    gram = to_all(gram, ("xl", "z", "y", "xh"))
    basis, triangle = pl.pallas_call(
        finish_kernel,
        out_shape=(shape(VEC, SEG), shape(VEC, VEC)),
        name="finish",
    )(gram, projected)
    return basis.T, triangle


def solution(mesh):
    torus = Mesh(mesh.devices.reshape(SIZES), AXES)
    placed = (P(AXES, None), P(AXES, None))
    return jax.shard_map(
        per_device, mesh=torus, in_specs=placed, out_specs=(P(AXES, None), P()), check_vma=False
    )
```

time: 124 us -> 128 us (1.032)
  blocking collectives: 39.5 us -> 30.9 us
  starting transfers between devices: 29.9 us -> 36.1 us
  Pallas kernels: 34.4 us -> 38.9 us
    all_to_all x2, blocking collectives: 39.5 us -> 30.9 us  [to_all(): return lax.all_to_all(copies, axes, split_axis=0, concat_axis=0, tiled=True)]
    pallas_call x2 -> x3, Pallas kernels: 27 us -> 31.7 us  [the longest x2 18.9 us: affinity(): pl.pallas_call(kernel, grid=(NC // 2,), out_shape=(pltpu.HBM((NC, count *...]
    all_to_all x2, starting transfers between devices: 12.1 us -> 14.6 us  [to_all(): return lax.all_to_all(copies, axes, split_axis=0, concat_axis=0, tiled=True)]
    ppermute x6 -> x7, starting transfers between devices: 6.82 us -> 8.79 us  [across(): return lax.ppermute(a, 'core', [(0, 1), (1, 0)])]
    ppermute x4, waiting for transfers between devices: 4.65 us -> 6.32 us  [along(): return lax.ppermute(a, ROWS, turns)]
    ppermute x4, starting transfers between devices: 11 us -> 12.7 us  [along(): return lax.ppermute(a, ROWS, turns)]
    ppermute x6 -> x7, waiting for transfers between devices: 3.17 us -> 3.18 us  [across(): return lax.ppermute(a, 'core', [(0, 1), (1, 0)])]
  transfers between devices with their start and end apart: 12 -> 13, of which waited for: 8 -> 6; matrix products, arithmetic and copies ran while one was open for 0% -> 1% of each run, Pallas kernels for 0% -> 8%
where the time goes in v5:
time: 128 us; the launch traced here: 127 us
  Pallas kernels  38.9 us (30%)
  starting transfers between devices  36.1 us (28%)
  blocking collectives  30.9 us (24%)
  waiting for transfers between devices  18.8 us (15%)
  other arithmetic  1.69 us (1%)
    all_to_all x2, blocking collectives, to_all(): return lax.all_to_all(copies, axes, split_axis=0, concat_axis=0, tiled=True)  30.9 us
    pallas_call x2, Pallas kernels, affinity(): pl.pallas_call(kernel, grid=(NC // 2,), out_shape=(pltpu.HBM((NC, count *...  18.9 us
    all_to_all x2, starting transfers between devices, to_all(): return lax.all_to_all(copies, axes, split_axis=0, concat_axis=0, tiled=True)  14.6 us
    pallas_call x1, Pallas kernels, per_device(): pl.pallas_call(apply_kernel, out_shape=(shape(HALF, VEC, SEG), shape(HALF...  12.8 us
    ppermute x4, starting transfers between devices, along(): return lax.ppermute(a, ROWS, turns)  12.7 us
    all_to_all x2, waiting for transfers between devices, to_all(): return lax.all_to_all(copies, axes, split_axis=0, concat_axis=0, tiled=True)  9.3 us
    ppermute x7, starting transfers between devices, across(): return lax.ppermute(a, 'core', [(0, 1), (1, 0)])  8.79 us
    ppermute x4, waiting for transfers between devices, along(): return lax.ppermute(a, ROWS, turns)  6.32 us
  transfers between devices with their start and end apart: 13, of which 6 were waited for; matrix products, arithmetic and copies ran while one was open for 1% of the time, Pallas kernels for 8%

profile of v5, /device:TPU:1, one launch (start us, length us, event | category | flops | bytes accessed | tf_op | source)
XLA Modules:
  0.0 127.2 jit_solution(3887317859597807062)
XLA Ops:
  0.6 0.0 copy-start.1
  0.6 2.2 %unit.1 = (bf16[192,256]{1,0:T(8,128)(2,1)}, bf16[16,192,256]{2,1,0:T(8,128)(2,1)}) custom-call(bf16[192,256]{1,0:T(8,128)(2,1)} %bitcast.11), custom_call_target="tpu_custom_call" | custom-call | tf_op jit(solution)/shard_map/unit/pallas_call | solution.py:202
  2.9 7.6 %all-to-all-start = ((bf16[16,192,256]{2,1,0:T(8,128)(2,1)}), bf16[16,192,256]{2,1,0:T(8,128)(2,1)S(1)}, u32[]{:S(2)}, u32[]{:S(2)}) async-start(bf16[16,192,256]{2,1,0:T(8,128)(2,1)} %get-tuple-element.15), calls=%async_computation | async-start | bytes 3145728 | tf_op jit(solution)/shard_map/all_to_all | solution.py:182
  10.4 1.0 collective-permute-start
  11.5 1.2 collective-permute-done
  12.6 0.9 pad_maximum_fusion.refs_0_
  13.6 6.1 %collective-permute-start.3 = (bf16[2,192,256]{2,1,0:T(8,128)(2,1)S(1)}, bf16[2,192,256]{2,1,0:T(8,128)(2,1)S(1)}, u32[]{:S(2)}, u32[]{:S(2)}) collective-permute-start(bf16[2,192,256]{2,1,0:T(8,128)(2,1)S(1)} %pad_maximum_fusion.refs_0_), channel_id=1, source_target_pairs={{0,32},{8,104},{16,48},{24,120},{32,64},{40,8},{48,80},{56,24},{64... | collective-permute-start | bytes 589832 | tf_op jit(solution)/shard_map/ppermute | solution.py:197
  19.7 0.7 collective-permute-start.1
  20.4 4.0 %collective-permute-done.3.refs_3_ = bf16[2,192,256]{2,1,0:T(8,128)(2,1)S(1)} collective-permute-done((bf16[2,192,256]{2,1,0:T(8,128)(2,1)S(1)}, bf16[2,192,256]{2,1,0:T(8,128)(2,1)S(1)}, u32[]{:S(2)}, u32[]{:S(2)}) %collective-permute-start.3) | collective-permute-done | bytes 196640 | tf_op jit(solution)/shard_map/ppermute | solution.py:197
  24.4 0.2 collective-permute-start.4
  24.5 3.4 %collective-permute-start.5 = (bf16[2,192,256]{2,1,0:T(8,128)(2,1)S(1)}, bf16[2,192,256]{2,1,0:T(8,128)(2,1)S(1)}, u32[]{:S(2)}, u32[]{:S(2)}) collective-permute-start(bf16[2,192,256]{2,1,0:T(8,128)(2,1)S(1)} %collective-permute-done.3.refs_3_), channel_id=1, source_target_pairs={{0,16},{8,120},{16,32},{24,8},{32,48},{40,24},{48,64},{56,40},{64,... | collective-permute-start | bytes 589832 | tf_op jit(solution)/shard_map/ppermute | solution.py:197
  28.0 0.0 collective-permute-done.1.refs_1_
  28.0 0.0 collective-permute-start.2
  28.0 2.4 %collective-permute-start.7 = (bf16[192,256]{1,0:T(8,128)(2,1)S(1)}, bf16[192,256]{1,0:T(8,128)(2,1)S(1)}, u32[]{:S(2)}, u32[]{:S(2)}) collective-permute-start(bf16[192,256]{1,0:T(8,128)(2,1)S(1)} %slice_bitcast_fusion), channel_id=1, source_target_pairs={{0,32},{8,104},{16,48},{24,120},{32,64},{40,8},{48,80},{56,24},{64... | collective-permute-start | bytes 294920 | tf_op jit(solution)/shard_map/ppermute | solution.py:197
  30.4 2.3 %collective-permute-done.7.refs_2_ = bf16[192,256]{1,0:T(8,128)(2,1)S(1)} collective-permute-done((bf16[192,256]{1,0:T(8,128)(2,1)S(1)}, bf16[192,256]{1,0:T(8,128)(2,1)S(1)}, u32[]{:S(2)}, u32[]{:S(2)}) %collective-permute-start.7) | collective-permute-done | bytes 98336 | tf_op jit(solution)/shard_map/ppermute | solution.py:197
  32.8 2.7 %collective-permute-start.8 = (bf16[192,256]{1,0:T(8,128)(2,1)S(1)}, bf16[192,256]{1,0:T(8,128)(2,1)S(1)}, u32[]{:S(2)}, u32[]{:S(2)}) collective-permute-start(bf16[192,256]{1,0:T(8,128)(2,1)S(1)} %collective-permute-done.7.refs_2_), channel_id=1, source_target_pairs={{0,8},{8,0},{1,9},{9,1},{2,10},{10,2},{3,11},{11,3},{4,12},{12,4},... | collective-permute-start | bytes 294920 | tf_op jit(solution)/shard_map/ppermute | solution.py:190
  35.5 0.0 collective-permute-done.5.refs_0_
  35.5 0.0 collective-permute-start.6
  35.5 0.0 collective-permute-done.4.refs_4_
  35.5 0.0 collective-permute-done.2.refs_2_
  35.5 0.0 all-to-all-done.t_ref
  35.5 10.7 %near_affinity.1 = (bf16[16,2560,256]{2,1,0:T(8,128)(2,1)}, f32[16,256]{1,0:T(8,128)S(1)}) custom-call(bf16[16,192,256]{2,1,0:T(8,128)(2,1)S(1)} %all-to-all-done.t_ref, bf16[2,192,256]{2,1,0:T(8,128)(2,1)S(1)} %pad_maximum_fusion.refs_0_, bf16[2,192,256]{2,1,0:T(8,128)(2,1)S(1)} %collective-permute-done.1.refs_1_, ...), custom_call_target="tpu_custom_call" | custom-call | flops 5368709120 | bytes 20971520 | tf_op jit(solution)/shard_map/near_affinity/pallas_call | solution.py:213
  46.2 0.0 collective-permute-done.8.refs_3_
  46.2 0.0 collective-permute-done.6.refs_1_
  46.2 0.0 copy-done.1
  46.2 8.2 %far_affinity.1 = (bf16[16,1536,256]{2,1,0:T(8,128)(2,1)}, f32[16,32,256]{2,1,0:T(8,128)}) custom-call(bf16[16,192,256]{2,1,0:T(8,128)(2,1)S(1)} %all-to-all-done.t_ref, f32[16,256]{1,0:T(8,128)S(1)} %get-tuple-element.17.near_deg_ref, f32[16,256]{1,0:T(8,128)S(1)} %bitcast.10, bf16[2,192,256]{2,1,0:T(8,128)(2,1)S(1)} %collective-permute-done.5.refs_0_, ...), custom_call_target="tpu_custom_call" | custom-call | flops 3221225472 | bytes 12582912 | tf_op jit(solution)/shard_map/far_affinity/pallas_call | solution.py:213
  54.4 7.0 %all-to-all-start.1 = ((f32[16,32,256]{2,1,0:T(8,128)}), f32[16,32,256]{2,1,0:T(8,128)S(1)}, u32[]{:S(2)}, u32[]{:S(2)}) async-start(f32[16,32,256]{2,1,0:T(8,128)} %get-tuple-element.18), calls=%async_computation.1 | async-start | bytes 1048576 | tf_op jit(solution)/shard_map/all_to_all | solution.py:182
  61.4 0.1 pad_add_fusion.pos_ref
  61.5 9.3 %all-to-all-done.1.deg_ref = f32[16,32,256]{2,1,0:T(8,128)S(1)} async-done(((f32[16,32,256]{2,1,0:T(8,128)}), f32[16,32,256]{2,1,0:T(8,128)S(1)}, u32[]{:S(2)}, u32[]{:S(2)}) %all-to-all-start.1) | async-done | bytes 524320 | tf_op jit(solution)/shard_map/all_to_all | solution.py:182
  70.8 12.8 %apply.1 = (f32[8,16,256]{2,1,0:T(8,128)S(1)}, f32[8,16,256]{2,1,0:T(8,128)S(1)}, f32[1,256]{1,0:T(1,128)S(1)}) custom-call(s32[3]{0:T(128)S(1)} %pad_add_fusion.pos_ref, f32[16,32,256]{2,1,0:T(8,128)S(1)} %all-to-all-done.1.deg_ref, bf16[16,2560,256]{2,1,0:T(8,128)(2,1)} %get-tuple-element.19.near_ref, bf16[16,1536,256]{2,1,0:T(8,128)(2,1)} %get-tuple-element.20.far_ref), custom_call_target="tpu_custom_call" | custom-call | tf_op jit(solution)/shard_map/apply/pallas_call | solution.py:234
  83.6 0.0 copy-start
  83.6 2.7 %collective-permute-start.9 = (f32[8,16,256]{2,1,0:T(8,128)S(1)}, f32[8,16,256]{2,1,0:T(8,128)S(1)}, u32[]{:S(2)}, u32[]{:S(2)}) collective-permute-start(f32[8,16,256]{2,1,0:T(8,128)S(1)} %get-tuple-element.22), channel_id=1, source_target_pairs={{0,8},{8,0},{1,9},{9,1},{2,10},{10,2},{3,11},{11,3},{4,12},{12,4},... | collective-permute-start | bytes 393224 | tf_op jit(solution)/shard_map/ppermute | solution.py:190
  86.4 1.0 collective-permute-done.9
  87.4 0.0 copy-done
  87.4 13.6 %all_to_all.20.p_ref = f32[8,16,256]{2,1,0:T(8,128)} all-to-all(f32[8,16,256]{2,1,0:T(8,128)S(1)} %add.14), channel_id=1, replica_groups=mesh['xl'=2,'z'=8,'core'=2,'y'=4,'xh'=2] {'z'}, dimensions={0} | all-to-all | bytes 262144 | tf_op jit(solution)/shard_map/all_to_all | solution.py:182
  101.0 1.8 %project.1 = (f32[16,256]{1,0:T(8,128)}, f32[2,128]{1,0:T(2,128)}) custom-call(f32[8,16,256]{2,1,0:T(8,128)} %all_to_all.20.p_ref, f32[1,256]{1,0:T(1,128)} %copy-done), custom_call_target="tpu_custom_call" | custom-call | tf_op jit(solution)/shard_map/project/pallas_call | solution.py:249
  102.8 2.1 %collective-permute-start.10 = (f32[2,128]{1,0:T(2,128)}, f32[2,128]{1,0:T(2,128)S(1)}, u32[]{:S(2)}, u32[]{:S(2)}) collective-permute-start(f32[2,128]{1,0:T(2,128)} %get-tuple-element.24), channel_id=1, source_target_pairs={{0,8},{8,0},{1,9},{9,1},{2,10},{10,2},{3,11},{11,3},{4,12},{12,4},... | collective-permute-start | bytes 3080 | tf_op jit(solution)/shard_map/ppermute | solution.py:190
  104.9 1.0 collective-permute-done.10
  105.9 0.7 add.15
  106.6 17.4 %all_to_all.21.gram_ref = f32[128,2,128]{2,1,0:T(2,128)} all-to-all(f32[128,2,128]{2,1,0:T(2,128)S(1)} %broadcast_in_dim.3), channel_id=1, replica_groups=mesh['xl'=2,'z'=8,'core'=2,'y'=4,'xh'=2] {'xl','z','y','xh'}, dimensions={0} | all-to-all | bytes 262144 | tf_op jit(solution)/shard_map/all_to_all | solution.py:182
  124.0 3.2 %finish.1 = (f32[16,256]{1,0:T(8,128)}, f32[16,16]{1,0:T(8,128)}) custom-call(f32[128,2,128]{2,1,0:T(2,128)} %all_to_all.21.gram_ref, f32[16,256]{1,0:T(8,128)} %get-tuple-element.25.q_ref), custom_call_target="tpu_custom_call" | custom-call | tf_op jit(solution)/shard_map/finish/pallas_call | solution.py:256
  (3 shorter events, 0.1 us)
Async XLA Ops:
  0.6 45.6 %copy-start.1 = (f32[256,16]{0,1:T(8,128)S(1)}, f32[256,16]{0,1:T(8,128)}, u32[]{:S(2)}) copy-start(f32[256,16]{0,1:T(8,128)} %param.3) | copy-start | bytes 49156
  2.9 32.7 %all-to-all-start = ((bf16[16,192,256]{2,1,0:T(8,128)(2,1)}), bf16[16,192,256]{2,1,0:T(8,128)(2,1)S(1)}, u32[]{:S(2)}, u32[]{:S(2)}) async-start(bf16[16,192,256]{2,1,0:T(8,128)(2,1)} %get-tuple-element.15), calls=%async_computation | async-start | bytes 3145728 | tf_op jit(solution)/shard_map/all_to_all | solution.py:182
  10.4 2.2 %collective-permute-start = (bf16[192,256]{1,0:T(8,128)(2,1)}, bf16[192,256]{1,0:T(8,128)(2,1)S(1)}, u32[]{:S(2)}, u32[]{:S(2)}) collective-permute-start(bf16[192,256]{1,0:T(8,128)(2,1)} %get-tuple-element.16), channel_id=1, source_target_pairs={{0,8},{8,0},{1,9},{9,1},{2,10},{10,2},{3,11},{11,3},{4,12},{12,4},... | collective-permute-start | bytes 294920 | tf_op jit(solution)/shard_map/ppermute | solution.py:190
  13.6 10.8 %collective-permute-start.3 = (bf16[2,192,256]{2,1,0:T(8,128)(2,1)S(1)}, bf16[2,192,256]{2,1,0:T(8,128)(2,1)S(1)}, u32[]{:S(2)}, u32[]{:S(2)}) collective-permute-start(bf16[2,192,256]{2,1,0:T(8,128)(2,1)S(1)} %pad_maximum_fusion.refs_0_), channel_id=1, source_target_pairs={{0,32},{8,104},{16,48},{24,120},{32,64},{40,8},{48,80},{56,24},{64... | collective-permute-start | bytes 589832 | tf_op jit(solution)/shard_map/ppermute | solution.py:197
  19.7 8.3 %collective-permute-start.1 = (bf16[2,192,256]{2,1,0:T(8,128)(2,1)S(1)}, bf16[2,192,256]{2,1,0:T(8,128)(2,1)S(1)}, u32[]{:S(2)}, u32[]{:S(2)}) collective-permute-start(bf16[2,192,256]{2,1,0:T(8,128)(2,1)S(1)} %pad_maximum_fusion.refs_0_), channel_id=1, source_target_pairs={{0,16},{8,120},{16,32},{24,8},{32,48},{40,24},{48,64},{56,40},{64,... | collective-permute-start | bytes 589832 | tf_op jit(solution)/shard_map/ppermute | solution.py:197
  24.4 11.1 %collective-permute-start.4 = (bf16[2,192,256]{2,1,0:T(8,128)(2,1)S(1)}, bf16[2,192,256]{2,1,0:T(8,128)(2,1)S(1)}, u32[]{:S(2)}, u32[]{:S(2)}) collective-permute-start(bf16[2,192,256]{2,1,0:T(8,128)(2,1)S(1)} %collective-permute-done.3.refs_3_), channel_id=1, source_target_pairs={{0,8},{8,0},{1,9},{9,1},{2,10},{10,2},{3,11},{11,3},{4,12},{12,4},... | collective-permute-start | bytes 589832 | tf_op jit(solution)/shard_map/ppermute | solution.py:190
  24.5 10.9 %collective-permute-start.5 = (bf16[2,192,256]{2,1,0:T(8,128)(2,1)S(1)}, bf16[2,192,256]{2,1,0:T(8,128)(2,1)S(1)}, u32[]{:S(2)}, u32[]{:S(2)}) collective-permute-start(bf16[2,192,256]{2,1,0:T(8,128)(2,1)S(1)} %collective-permute-done.3.refs_3_), channel_id=1, source_target_pairs={{0,16},{8,120},{16,32},{24,8},{32,48},{40,24},{48,64},{56,40},{64,... | collective-permute-start | bytes 589832 | tf_op jit(solution)/shard_map/ppermute | solution.py:197
  28.0 7.5 %collective-permute-start.2 = (bf16[2,192,256]{2,1,0:T(8,128)(2,1)S(1)}, bf16[2,192,256]{2,1,0:T(8,128)(2,1)S(1)}, u32[]{:S(2)}, u32[]{:S(2)}) collective-permute-start(bf16[2,192,256]{2,1,0:T(8,128)(2,1)S(1)} %collective-permute-done.1.refs_1_), channel_id=1, source_target_pairs={{0,8},{8,0},{1,9},{9,1},{2,10},{10,2},{3,11},{11,3},{4,12},{12,4},... | collective-permute-start | bytes 589832 | tf_op jit(solution)/shard_map/ppermute | solution.py:190
  28.0 4.8 %collective-permute-start.7 = (bf16[192,256]{1,0:T(8,128)(2,1)S(1)}, bf16[192,256]{1,0:T(8,128)(2,1)S(1)}, u32[]{:S(2)}, u32[]{:S(2)}) collective-permute-start(bf16[192,256]{1,0:T(8,128)(2,1)S(1)} %slice_bitcast_fusion), channel_id=1, source_target_pairs={{0,32},{8,104},{16,48},{24,120},{32,64},{40,8},{48,80},{56,24},{64... | collective-permute-start | bytes 294920 | tf_op jit(solution)/shard_map/ppermute | solution.py:197
  32.8 13.5 %collective-permute-start.8 = (bf16[192,256]{1,0:T(8,128)(2,1)S(1)}, bf16[192,256]{1,0:T(8,128)(2,1)S(1)}, u32[]{:S(2)}, u32[]{:S(2)}) collective-permute-start(bf16[192,256]{1,0:T(8,128)(2,1)S(1)} %collective-permute-done.7.refs_2_), channel_id=1, source_target_pairs={{0,8},{8,0},{1,9},{9,1},{2,10},{10,2},{3,11},{11,3},{4,12},{12,4},... | collective-permute-start | bytes 294920 | tf_op jit(solution)/shard_map/ppermute | solution.py:190
  35.5 10.7 %collective-permute-start.6 = (bf16[2,192,256]{2,1,0:T(8,128)(2,1)S(1)}, bf16[2,192,256]{2,1,0:T(8,128)(2,1)S(1)}, u32[]{:S(2)}, u32[]{:S(2)}) collective-permute-start(bf16[2,192,256]{2,1,0:T(8,128)(2,1)S(1)} %collective-permute-done.5.refs_0_), channel_id=1, source_target_pairs={{0,8},{8,0},{1,9},{9,1},{2,10},{10,2},{3,11},{11,3},{4,12},{12,4},... | collective-permute-start | bytes 589832 | tf_op jit(solution)/shard_map/ppermute | solution.py:190
  54.4 16.4 %all-to-all-start.1 = ((f32[16,32,256]{2,1,0:T(8,128)}), f32[16,32,256]{2,1,0:T(8,128)S(1)}, u32[]{:S(2)}, u32[]{:S(2)}) async-start(f32[16,32,256]{2,1,0:T(8,128)} %get-tuple-element.18), calls=%async_computation.1 | async-start | bytes 1048576 | tf_op jit(solution)/shard_map/all_to_all | solution.py:182
  83.6 3.8 %copy-start = (f32[1,256]{1,0:T(1,128)}, f32[1,256]{1,0:T(1,128)S(1)}, u32[]{:S(2)}) copy-start(f32[1,256]{1,0:T(1,128)S(1)} %get-tuple-element.23.own_ref) | copy-start | bytes 3076
  83.6 3.7 %collective-permute-start.9 = (f32[8,16,256]{2,1,0:T(8,128)S(1)}, f32[8,16,256]{2,1,0:T(8,128)S(1)}, u32[]{:S(2)}, u32[]{:S(2)}) collective-permute-start(f32[8,16,256]{2,1,0:T(8,128)S(1)} %get-tuple-element.22), channel_id=1, source_target_pairs={{0,8},{8,0},{1,9},{9,1},{2,10},{10,2},{3,11},{11,3},{4,12},{12,4},... | collective-permute-start | bytes 393224 | tf_op jit(solution)/shard_map/ppermute | solution.py:190
  102.8 3.2 %collective-permute-start.10 = (f32[2,128]{1,0:T(2,128)}, f32[2,128]{1,0:T(2,128)S(1)}, u32[]{:S(2)}, u32[]{:S(2)}) collective-permute-start(f32[2,128]{1,0:T(2,128)} %get-tuple-element.24), channel_id=1, source_target_pairs={{0,8},{8,0},{1,9},{9,1},{2,10},{10,2},{3,11},{11,3},{4,12},{12,4},... | collective-permute-start | bytes 3080 | tf_op jit(solution)/shard_map/ppermute | solution.py:190

commit v6 on v3

--- a/solution.py
+++ b/solution.py
@@ -11,6 +11,7 @@
 ROWS = ("z", "core")
 COLS = ("xl", "y", "xh")
 CHIPS = 128
+HALF = 8
 NR = 16
 NC = 16
 SEG = 256
@@ -91,7 +92,7 @@
             deg_ref[k, pl.ds(step * 2 + j, 1), :] = sums
 
 
-def apply_kernel(pos_ref, deg_ref, t_ref, b_ref, p_ref, own_ref, root_ref, held_ref, sem_ref):
+def apply_kernel(pos_ref, deg_ref, t_ref, b_ref, mine_ref, other_ref, own_ref, root_ref, held_ref, sem_ref):
     def fetch(t):
         slot = t % DEPTH
         return pltpu.make_async_copy(b_ref.at[t], held_ref.at[slot], sem_ref.at[slot])
@@ -99,14 +100,17 @@
     for t in range(DEPTH):
         fetch(t).start()
     root_ref[...] = lax.rsqrt(jnp.sum(deg_ref[...], axis=0))
-    own_ref[...] = root_ref[pl.ds(pos_ref[0], 1), :] * UNSCALE
+    core = pos_ref[0]
+    own_ref[...] = root_ref[pl.ds(pos_ref[1], 1), :] * UNSCALE
     for t in range(NC):
         v = t_ref[t, DIM : DIM + VEC, :].astype(F32) + t_ref[t, DIM + VEC : WIDE, :].astype(F32)
         w = (v * root_ref[t : t + 1, :]).astype(BF16)
         fetch(t).wait()
-        for r in range(NR):
-            part = nt(w, held_ref[t % DEPTH, r * SEG : (r + 1) * SEG, :])
-            p_ref[r] = part if t == 0 else p_ref[r] + part
+        for r in range(NR // 2):
+            for side, p_ref in ((core, mine_ref), (1 - core, other_ref)):
+                rows = pl.ds(pl.multiple_of((r * 2 + side) * SEG, SEG), SEG)
+                part = nt(w, held_ref[t % DEPTH, rows, :])
+                p_ref[r] = part if t == 0 else p_ref[r] + part
         if t + DEPTH < NC:
             fetch(t + DEPTH).start()
 
@@ -194,11 +198,11 @@
         name="affinity",
     )(jnp.stack([z, core]), columns, *pairs, four, across(four))
     degree = to_all(degree, COLS)
-    product, own = pl.pallas_call(
+    mine, other, own = pl.pallas_call(
         apply_kernel,
-        out_shape=(shape(NR, VEC, SEG), shape(1, SEG)),
+        out_shape=(shape(HALF, VEC, SEG), shape(HALF, VEC, SEG), shape(1, SEG)),
         in_specs=[smem(), vmem(), vmem(), pl.BlockSpec(memory_space=pl.ANY)],
-        out_specs=(vmem(), vmem()),
+        out_specs=(vmem(), vmem(), vmem()),
         scratch_shapes=[
             pltpu.VMEM((NC, SEG), F32),
             pltpu.VMEM((DEPTH, NR * SEG, SEG), BF16),
@@ -206,8 +210,8 @@
         ],
         compiler_params=params(44),
         name="apply",
-    )(jnp.stack([column]), degree, columns, block)
-    product = to_all(product, ROWS)
+    )(jnp.stack([core, column]), degree, columns, block)
+    product = to_all(mine + across(other), "z")
     projected, gram = pl.pallas_call(
         project_kernel,
         out_shape=(shape(VEC, SEG), shape(2, 128)),

time: 124 us -> 123 us (level)
  blocking collectives: 39.5 us -> 33.3 us
  starting transfers between devices: 29.9 us -> 34.1 us
    all_to_all x2, blocking collectives: 39.5 us -> 33.3 us  [to_all(): return lax.all_to_all(copies, axes, split_axis=0, concat_axis=0, tiled=True)]
    ppermute x6 -> x7, starting transfers between devices: 6.82 us -> 11 us  [across(): return lax.ppermute(a, 'core', [(0, 1), (1, 0)])]
    ppermute x6 -> x7, waiting for transfers between devices: 3.17 us -> 3.84 us  [across(): return lax.ppermute(a, 'core', [(0, 1), (1, 0)])]
  transfers between devices with their start and end apart: 12 -> 13, of which waited for: 8 -> 9; matrix products, arithmetic and copies ran while one was open for 0% -> 0% of each run, Pallas kernels for 0% -> 0%
where the time goes in v6:
time: 123 us
  Pallas kernels  34.9 us (28%)
  starting transfers between devices  34.1 us (28%)
  blocking collectives  33.3 us (27%)
  waiting for transfers between devices  18.7 us (15%)
    all_to_all x2, blocking collectives, to_all(): return lax.all_to_all(copies, axes, split_axis=0, concat_axis=0, tiled=True)  33.3 us
    pallas_call x1, Pallas kernels, per_device(): pl.pallas_call(affinity_kernel, grid=(NC // 2,), out_shape=(shape(NC, NR...  15.5 us
    pallas_call x1, Pallas kernels, per_device(): pl.pallas_call(apply_kernel, out_shape=(shape(HALF, VEC, SEG), shape(HALF...  12.1 us
    all_to_all x2, starting transfers between devices, to_all(): return lax.all_to_all(copies, axes, split_axis=0, concat_axis=0, tiled=True)  12.1 us
    ppermute x4, starting transfers between devices, along(): return lax.ppermute(a, ROWS, turns)  11 us
    ppermute x7, starting transfers between devices, across(): return lax.ppermute(a, 'core', [(0, 1), (1, 0)])  11 us
    all_to_all x2, waiting for transfers between devices, to_all(): return lax.all_to_all(copies, axes, split_axis=0, concat_axis=0, tiled=True)  10.2 us
    ppermute x4, waiting for transfers between devices, along(): return lax.ppermute(a, ROWS, turns)  4.65 us
  transfers between devices with their start and end apart: 13, of which 9 were waited for; matrix products, arithmetic and copies ran while one was open for 0% of the time, Pallas kernels for 0%

profile of v6, /device:TPU:1, one launch (start us, length us, event | category | flops | bytes accessed | tf_op | source)
XLA Modules:
  0.0 122.7 jit_solution(6045200067141759996)
XLA Ops:
  0.6 2.3 %unit.1 = (bf16[192,256]{1,0:T(8,128)(2,1)}, bf16[16,224,256]{2,1,0:T(8,128)(2,1)}) custom-call(bf16[192,256]{1,0:T(8,128)(2,1)} %bitcast.10, f32[16,256]{1,0:T(8,128)} %bitcast.13), custom_call_target="tpu_custom_call" | custom-call | tf_op jit(solution)/shard_map/unit/pallas_call | solution.py:177
  3.0 0.0 copy-start.1
  3.0 7.7 %all-to-all-start = ((bf16[16,224,256]{2,1,0:T(8,128)(2,1)}), bf16[16,224,256]{2,1,0:T(8,128)(2,1)S(1)}, u32[]{:S(2)}, u32[]{:S(2)}) async-start(bf16[16,224,256]{2,1,0:T(8,128)(2,1)} %get-tuple-element.13), calls=%async_computation | async-start | bytes 3670016 | tf_op jit(solution)/shard_map/all_to_all | solution.py:156
  10.7 0.0 copy-done.1
  10.7 1.0 collective-permute-start
  11.7 0.9 collective-permute-done
  12.7 6.1 %collective-permute-start.3 = (bf16[2,192,256]{2,1,0:T(8,128)(2,1)S(1)}, bf16[2,192,256]{2,1,0:T(8,128)(2,1)S(1)}, u32[]{:S(2)}, u32[]{:S(2)}) collective-permute-start(bf16[2,192,256]{2,1,0:T(8,128)(2,1)S(1)} %pad_maximum_fusion.refs_0_), channel_id=1, source_target_pairs={{0,32},{8,104},{16,48},{24,120},{32,64},{40,8},{48,80},{56,24},{64... | collective-permute-start | bytes 589832 | tf_op jit(solution)/shard_map/ppermute | solution.py:171
  18.8 0.7 collective-permute-start.1
  19.5 4.0 %collective-permute-done.3.refs_3_ = bf16[2,192,256]{2,1,0:T(8,128)(2,1)S(1)} collective-permute-done((bf16[2,192,256]{2,1,0:T(8,128)(2,1)S(1)}, bf16[2,192,256]{2,1,0:T(8,128)(2,1)S(1)}, u32[]{:S(2)}, u32[]{:S(2)}) %collective-permute-start.3) | collective-permute-done | bytes 196640 | tf_op jit(solution)/shard_map/ppermute | solution.py:171
  23.5 2.3 %collective-permute-start.5 = (bf16[2,192,256]{2,1,0:T(8,128)(2,1)S(1)}, bf16[2,192,256]{2,1,0:T(8,128)(2,1)S(1)}, u32[]{:S(2)}, u32[]{:S(2)}) collective-permute-start(bf16[2,192,256]{2,1,0:T(8,128)(2,1)S(1)} %collective-permute-done.3.refs_3_), channel_id=1, source_target_pairs={{0,16},{8,120},{16,32},{24,8},{32,48},{40,24},{48,64},{56,40},{64,... | collective-permute-start | bytes 589832 | tf_op jit(solution)/shard_map/ppermute | solution.py:171
  25.8 1.9 %collective-permute-start.7 = (bf16[192,256]{1,0:T(8,128)(2,1)S(1)}, bf16[192,256]{1,0:T(8,128)(2,1)S(1)}, u32[]{:S(2)}, u32[]{:S(2)}) collective-permute-start(bf16[192,256]{1,0:T(8,128)(2,1)S(1)} %slice_bitcast_fusion), channel_id=1, source_target_pairs={{0,32},{8,104},{16,48},{24,120},{32,64},{40,8},{48,80},{56,24},{64... | collective-permute-start | bytes 294920 | tf_op jit(solution)/shard_map/ppermute | solution.py:171
  27.7 0.0 collective-permute-start.4
  27.7 0.0 collective-permute-done.1.refs_1_
  27.7 0.5 collective-permute-start.2
  28.2 0.1 collective-permute-done.5.refs_5_
  28.4 2.7 %collective-permute-start.6 = (bf16[2,192,256]{2,1,0:T(8,128)(2,1)S(1)}, bf16[2,192,256]{2,1,0:T(8,128)(2,1)S(1)}, u32[]{:S(2)}, u32[]{:S(2)}) collective-permute-start(bf16[2,192,256]{2,1,0:T(8,128)(2,1)S(1)} %collective-permute-done.5.refs_5_), channel_id=1, source_target_pairs={{0,8},{8,0},{1,9},{9,1},{2,10},{10,2},{3,11},{11,3},{4,12},{12,4},... | collective-permute-start | bytes 589832 | tf_op jit(solution)/shard_map/ppermute | solution.py:164
  31.1 0.5 collective-permute-done.7.refs_7_
  31.6 2.6 %collective-permute-start.8 = (bf16[192,256]{1,0:T(8,128)(2,1)S(1)}, bf16[192,256]{1,0:T(8,128)(2,1)S(1)}, u32[]{:S(2)}, u32[]{:S(2)}) collective-permute-start(bf16[192,256]{1,0:T(8,128)(2,1)S(1)} %collective-permute-done.7.refs_7_), channel_id=1, source_target_pairs={{0,8},{8,0},{1,9},{9,1},{2,10},{10,2},{3,11},{11,3},{4,12},{12,4},... | collective-permute-start | bytes 294920 | tf_op jit(solution)/shard_map/ppermute | solution.py:164
  34.2 0.1 pad_add_fusion.1.pos_ref
  34.2 0.9 collective-permute-done.8.refs_8_
  35.1 0.0 collective-permute-done.4.refs_4_
  35.1 0.0 collective-permute-done.2.refs_2_
  35.1 0.0 collective-permute-done.6.refs_6_
  35.1 2.6 %all-to-all-done.t_ref = bf16[16,224,256]{2,1,0:T(8,128)(2,1)S(1)} async-done(((bf16[16,224,256]{2,1,0:T(8,128)(2,1)}), bf16[16,224,256]{2,1,0:T(8,128)(2,1)S(1)}, u32[]{:S(2)}, u32[]{:S(2)}) %all-to-all-start) | async-done | bytes 1835040 | tf_op jit(solution)/shard_map/all_to_all | solution.py:156
  37.8 15.5 %affinity.1 = (bf16[16,4096,256]{2,1,0:T(8,128)(2,1)}, f32[16,16,256]{2,1,0:T(8,128)}) custom-call(s32[2]{0:T(128)S(1)} %pad_add_fusion.1.pos_ref, bf16[16,224,256]{2,1,0:T(8,128)(2,1)S(1)} %all-to-all-done.t_ref, bf16[2,192,256]{2,1,0:T(8,128)(2,1)S(1)} %pad_maximum_fusion.refs_0_, bf16[2,192,256]{2,1,0:T(8,128)(2,1)S(1)} %collective-permute-done.1.refs_1_, ...), custom_call_target="tpu_custom_call" | custom-call | flops 8589934592 | bytes 33554432 | tf_op jit(solution)/shard_map/affinity/pallas_call | solution.py:187
  53.2 4.3 %all-to-all-start.1 = ((f32[16,16,256]{2,1,0:T(8,128)}), f32[16,16,256]{2,1,0:T(8,128)S(1)}, u32[]{:S(2)}, u32[]{:S(2)}) async-start(f32[16,16,256]{2,1,0:T(8,128)} %get-tuple-element.15), calls=%async_computation.1 | async-start | bytes 524288 | tf_op jit(solution)/shard_map/all_to_all | solution.py:156
  57.6 0.1 pad_add_fusion.pos_ref
  57.7 7.6 %all-to-all-done.1.deg_ref = f32[16,16,256]{2,1,0:T(8,128)S(1)} async-done(((f32[16,16,256]{2,1,0:T(8,128)}), f32[16,16,256]{2,1,0:T(8,128)S(1)}, u32[]{:S(2)}, u32[]{:S(2)}) %all-to-all-start.1) | async-done | bytes 262176 | tf_op jit(solution)/shard_map/all_to_all | solution.py:156
  65.3 12.1 %apply.1 = (f32[8,16,256]{2,1,0:T(8,128)S(1)}, f32[8,16,256]{2,1,0:T(8,128)S(1)}, f32[1,256]{1,0:T(1,128)S(1)}) custom-call(s32[2]{0:T(128)S(1)} %pad_add_fusion.pos_ref, f32[16,16,256]{2,1,0:T(8,128)S(1)} %all-to-all-done.1.deg_ref, bf16[16,224,256]{2,1,0:T(8,128)(2,1)S(1)} %all-to-all-done.t_ref, bf16[16,4096,256]{2,1,0:T(8,128)(2,1)} %get-tuple-element.16.b_ref), custom_call_target="tpu_custom_call" | custom-call | tf_op jit(solution)/shard_map/apply/pallas_call | solution.py:201
  77.4 0.0 copy-start
  77.4 2.1 %collective-permute-start.9 = (f32[8,16,256]{2,1,0:T(8,128)S(1)}, f32[8,16,256]{2,1,0:T(8,128)S(1)}, u32[]{:S(2)}, u32[]{:S(2)}) collective-permute-start(f32[8,16,256]{2,1,0:T(8,128)S(1)} %get-tuple-element.18), channel_id=1, source_target_pairs={{0,8},{8,0},{1,9},{9,1},{2,10},{10,2},{3,11},{11,3},{4,12},{12,4},... | collective-permute-start | bytes 393224 | tf_op jit(solution)/shard_map/ppermute | solution.py:164
  79.5 1.0 collective-permute-done.9
  80.5 0.0 copy-done
  80.5 16.0 %all_to_all.20.p_ref = f32[8,16,256]{2,1,0:T(8,128)} all-to-all(f32[8,16,256]{2,1,0:T(8,128)S(1)} %add.14), channel_id=1, replica_groups=mesh['xl'=2,'z'=8,'core'=2,'y'=4,'xh'=2] {'z'}, dimensions={0} | all-to-all | bytes 262144 | tf_op jit(solution)/shard_map/all_to_all | solution.py:156
  96.5 1.8 %project.1 = (f32[16,256]{1,0:T(8,128)}, f32[2,128]{1,0:T(2,128)}) custom-call(f32[8,16,256]{2,1,0:T(8,128)} %all_to_all.20.p_ref, f32[1,256]{1,0:T(1,128)} %copy-done), custom_call_target="tpu_custom_call" | custom-call | tf_op jit(solution)/shard_map/project/pallas_call | solution.py:215
  98.3 2.1 %collective-permute-start.10 = (f32[2,128]{1,0:T(2,128)}, f32[2,128]{1,0:T(2,128)S(1)}, u32[]{:S(2)}, u32[]{:S(2)}) collective-permute-start(f32[2,128]{1,0:T(2,128)} %get-tuple-element.20), channel_id=1, source_target_pairs={{0,8},{8,0},{1,9},{9,1},{2,10},{10,2},{3,11},{11,3},{4,12},{12,4},... | collective-permute-start | bytes 3080 | tf_op jit(solution)/shard_map/ppermute | solution.py:164
  100.4 1.0 collective-permute-done.10
  101.4 0.7 add.15
  102.2 17.3 %all_to_all.21.gram_ref = f32[128,2,128]{2,1,0:T(2,128)} all-to-all(f32[128,2,128]{2,1,0:T(2,128)S(1)} %broadcast_in_dim.3), channel_id=1, replica_groups=mesh['xl'=2,'z'=8,'core'=2,'y'=4,'xh'=2] {'xl','z','y','xh'}, dimensions={0} | all-to-all | bytes 262144 | tf_op jit(solution)/shard_map/all_to_all | solution.py:156
  119.5 3.2 %finish.1 = (f32[16,256]{1,0:T(8,128)}, f32[16,16]{1,0:T(8,128)}) custom-call(f32[128,2,128]{2,1,0:T(2,128)} %all_to_all.21.gram_ref, f32[16,256]{1,0:T(8,128)} %get-tuple-element.21.q_ref), custom_call_target="tpu_custom_call" | custom-call | tf_op jit(solution)/shard_map/finish/pallas_call | solution.py:222
  (4 shorter events, 0.1 us)
Async XLA Ops:
  3.0 7.7 %copy-start.1 = (bf16[192,256]{1,0:T(8,128)(2,1)S(1)}, bf16[192,256]{1,0:T(8,128)(2,1)}, u32[]{:S(2)}) copy-start(bf16[192,256]{1,0:T(8,128)(2,1)} %get-tuple-element.14) | copy-start | bytes 294916
  3.0 34.8 %all-to-all-start = ((bf16[16,224,256]{2,1,0:T(8,128)(2,1)}), bf16[16,224,256]{2,1,0:T(8,128)(2,1)S(1)}, u32[]{:S(2)}, u32[]{:S(2)}) async-start(bf16[16,224,256]{2,1,0:T(8,128)(2,1)} %get-tuple-element.13), calls=%async_computation | async-start | bytes 3670016 | tf_op jit(solution)/shard_map/all_to_all | solution.py:156
  10.7 2.0 %collective-permute-start = (bf16[192,256]{1,0:T(8,128)(2,1)S(1)}, bf16[192,256]{1,0:T(8,128)(2,1)S(1)}, u32[]{:S(2)}, u32[]{:S(2)}) collective-permute-start(bf16[192,256]{1,0:T(8,128)(2,1)S(1)} %copy-done.1), channel_id=1, source_target_pairs={{0,8},{8,0},{1,9},{9,1},{2,10},{10,2},{3,11},{11,3},{4,12},{12,4},... | collective-permute-start | bytes 294920 | tf_op jit(solution)/shard_map/ppermute | solution.py:164
  12.7 10.8 %collective-permute-start.3 = (bf16[2,192,256]{2,1,0:T(8,128)(2,1)S(1)}, bf16[2,192,256]{2,1,0:T(8,128)(2,1)S(1)}, u32[]{:S(2)}, u32[]{:S(2)}) collective-permute-start(bf16[2,192,256]{2,1,0:T(8,128)(2,1)S(1)} %pad_maximum_fusion.refs_0_), channel_id=1, source_target_pairs={{0,32},{8,104},{16,48},{24,120},{32,64},{40,8},{48,80},{56,24},{64... | collective-permute-start | bytes 589832 | tf_op jit(solution)/shard_map/ppermute | solution.py:171
  18.8 8.9 %collective-permute-start.1 = (bf16[2,192,256]{2,1,0:T(8,128)(2,1)S(1)}, bf16[2,192,256]{2,1,0:T(8,128)(2,1)S(1)}, u32[]{:S(2)}, u32[]{:S(2)}) collective-permute-start(bf16[2,192,256]{2,1,0:T(8,128)(2,1)S(1)} %pad_maximum_fusion.refs_0_), channel_id=1, source_target_pairs={{0,16},{8,120},{16,32},{24,8},{32,48},{40,24},{48,64},{56,40},{64,... | collective-permute-start | bytes 589832 | tf_op jit(solution)/shard_map/ppermute | solution.py:171
  23.5 4.9 %collective-permute-start.5 = (bf16[2,192,256]{2,1,0:T(8,128)(2,1)S(1)}, bf16[2,192,256]{2,1,0:T(8,128)(2,1)S(1)}, u32[]{:S(2)}, u32[]{:S(2)}) collective-permute-start(bf16[2,192,256]{2,1,0:T(8,128)(2,1)S(1)} %collective-permute-done.3.refs_3_), channel_id=1, source_target_pairs={{0,16},{8,120},{16,32},{24,8},{32,48},{40,24},{48,64},{56,40},{64,... | collective-permute-start | bytes 589832 | tf_op jit(solution)/shard_map/ppermute | solution.py:171
  25.8 5.8 %collective-permute-start.7 = (bf16[192,256]{1,0:T(8,128)(2,1)S(1)}, bf16[192,256]{1,0:T(8,128)(2,1)S(1)}, u32[]{:S(2)}, u32[]{:S(2)}) collective-permute-start(bf16[192,256]{1,0:T(8,128)(2,1)S(1)} %slice_bitcast_fusion), channel_id=1, source_target_pairs={{0,32},{8,104},{16,48},{24,120},{32,64},{40,8},{48,80},{56,24},{64... | collective-permute-start | bytes 294920 | tf_op jit(solution)/shard_map/ppermute | solution.py:171
  27.7 7.4 %collective-permute-start.4 = (bf16[2,192,256]{2,1,0:T(8,128)(2,1)S(1)}, bf16[2,192,256]{2,1,0:T(8,128)(2,1)S(1)}, u32[]{:S(2)}, u32[]{:S(2)}) collective-permute-start(bf16[2,192,256]{2,1,0:T(8,128)(2,1)S(1)} %collective-permute-done.3.refs_3_), channel_id=1, source_target_pairs={{0,8},{8,0},{1,9},{9,1},{2,10},{10,2},{3,11},{11,3},{4,12},{12,4},... | collective-permute-start | bytes 589832 | tf_op jit(solution)/shard_map/ppermute | solution.py:164
  27.7 7.4 %collective-permute-start.2 = (bf16[2,192,256]{2,1,0:T(8,128)(2,1)S(1)}, bf16[2,192,256]{2,1,0:T(8,128)(2,1)S(1)}, u32[]{:S(2)}, u32[]{:S(2)}) collective-permute-start(bf16[2,192,256]{2,1,0:T(8,128)(2,1)S(1)} %collective-permute-done.1.refs_1_), channel_id=1, source_target_pairs={{0,8},{8,0},{1,9},{9,1},{2,10},{10,2},{3,11},{11,3},{4,12},{12,4},... | collective-permute-start | bytes 589832 | tf_op jit(solution)/shard_map/ppermute | solution.py:164
  28.4 6.7 %collective-permute-start.6 = (bf16[2,192,256]{2,1,0:T(8,128)(2,1)S(1)}, bf16[2,192,256]{2,1,0:T(8,128)(2,1)S(1)}, u32[]{:S(2)}, u32[]{:S(2)}) collective-permute-start(bf16[2,192,256]{2,1,0:T(8,128)(2,1)S(1)} %collective-permute-done.5.refs_5_), channel_id=1, source_target_pairs={{0,8},{8,0},{1,9},{9,1},{2,10},{10,2},{3,11},{11,3},{4,12},{12,4},... | collective-permute-start | bytes 589832 | tf_op jit(solution)/shard_map/ppermute | solution.py:164
  31.6 3.5 %collective-permute-start.8 = (bf16[192,256]{1,0:T(8,128)(2,1)S(1)}, bf16[192,256]{1,0:T(8,128)(2,1)S(1)}, u32[]{:S(2)}, u32[]{:S(2)}) collective-permute-start(bf16[192,256]{1,0:T(8,128)(2,1)S(1)} %collective-permute-done.7.refs_7_), channel_id=1, source_target_pairs={{0,8},{8,0},{1,9},{9,1},{2,10},{10,2},{3,11},{11,3},{4,12},{12,4},... | collective-permute-start | bytes 294920 | tf_op jit(solution)/shard_map/ppermute | solution.py:164
  53.2 12.0 %all-to-all-start.1 = ((f32[16,16,256]{2,1,0:T(8,128)}), f32[16,16,256]{2,1,0:T(8,128)S(1)}, u32[]{:S(2)}, u32[]{:S(2)}) async-start(f32[16,16,256]{2,1,0:T(8,128)} %get-tuple-element.15), calls=%async_computation.1 | async-start | bytes 524288 | tf_op jit(solution)/shard_map/all_to_all | solution.py:156
  77.4 3.1 %copy-start = (f32[1,256]{1,0:T(1,128)}, f32[1,256]{1,0:T(1,128)S(1)}, u32[]{:S(2)}) copy-start(f32[1,256]{1,0:T(1,128)S(1)} %get-tuple-element.19.own_ref) | copy-start | bytes 3076
  77.4 3.1 %collective-permute-start.9 = (f32[8,16,256]{2,1,0:T(8,128)S(1)}, f32[8,16,256]{2,1,0:T(8,128)S(1)}, u32[]{:S(2)}, u32[]{:S(2)}) collective-permute-start(f32[8,16,256]{2,1,0:T(8,128)S(1)} %get-tuple-element.18), channel_id=1, source_target_pairs={{0,8},{8,0},{1,9},{9,1},{2,10},{10,2},{3,11},{11,3},{4,12},{12,4},... | collective-permute-start | bytes 393224 | tf_op jit(solution)/shard_map/ppermute | solution.py:164
  98.3 3.2 %collective-permute-start.10 = (f32[2,128]{1,0:T(2,128)}, f32[2,128]{1,0:T(2,128)S(1)}, u32[]{:S(2)}, u32[]{:S(2)}) collective-permute-start(f32[2,128]{1,0:T(2,128)} %get-tuple-element.20), channel_id=1, source_target_pairs={{0,8},{8,0},{1,9},{9,1},{2,10},{10,2},{3,11},{11,3},{4,12},{12,4},... | collective-permute-start | bytes 3080 | tf_op jit(solution)/shard_map/ppermute | solution.py:164

commit v7 on v6

--- a/solution.py
+++ b/solution.py
@@ -12,6 +12,7 @@
 COLS = ("xl", "y", "xh")
 CHIPS = 128
 HALF = 8
+KEPT = 13
 NR = 16
 NC = 16
 SEG = 256
@@ -22,6 +23,10 @@
 SCALE = 14.426950408889634
 UNSCALE = 4.5399929762484854e-05
 EPS = 1e-6
+SLOTS = [(0, True), (0, False)]
+for _hops in (1, 2, 3):
+    SLOTS += [(-_hops, True), (-_hops, False), (_hops, False), (_hops, True)]
+SLOTS += [(4, True), (4, False)]
 MIB = 1 << 20
 F32 = jnp.float32
 BF16 = jnp.bfloat16
@@ -57,42 +62,40 @@
         many_ref[k, DIM + VEC : WIDE, :] = low
 
 
-def affinity_kernel(pos_ref, t_ref, *refs):
-    pairs, lone = refs[0:7], refs[7:9]
-    b_ref, deg_ref, s_ref = refs[9:12]
-    z, core = pos_ref[0], pos_ref[1]
+def turn_kernel(*refs):
+    pairs, lone, rows_ref = refs[0:7], refs[7:9], refs[9]
+    for k in range(7):
+        for j in range(2):
+            rows_ref[2 * k + j] = pairs[k][j].T
+    for k in range(2):
+        rows_ref[14 + k] = lone[k][...].T
+
+
+def affinity_kernel(t_ref, s_ref, b_ref, deg_ref):
     step = pl.program_id(0)
 
-    def place(chip, side, rows):
-        s_ref[lax.rem(chip + 16, 8) * 2 + side] = rows.T
-
-    @pl.when(step == 0)
-    def _():
-        sign = 1 - 2 * core
-        place(z, core, pairs[0][0])
-        place(z, 1 - core, pairs[0][1])
-        for k in range(1, 4):
-            place(z - k * sign, core, pairs[2 * k - 1][0])
-            place(z - k * sign, 1 - core, pairs[2 * k - 1][1])
-            place(z + k * sign, 1 - core, pairs[2 * k][0])
-            place(z + k * sign, core, pairs[2 * k][1])
-        place(z + 4, core, lone[0][...])
-        place(z + 4, 1 - core, lone[1][...])
-
-    for j in range(2):
-        piece = t_ref[step * 2 + j, 0:DIM, :]
+    def score_piece(keep):
+        piece = t_ref[step, 0:DIM, :]
         total = jnp.zeros((8, SEG), F32)
         for r in range(NR):
             score = jnp.dot(s_ref[r], piece, preferred_element_type=F32)
             tile = jnp.exp2(score * SCALE)
             total = total + jnp.sum(tile.reshape(SEG // 8, 8, SEG), axis=0)
-            b_ref[j, r * SEG : (r + 1) * SEG, :] = tile.astype(BF16)
+            if keep:
+                b_ref[0, r * SEG : (r + 1) * SEG, :] = tile.astype(BF16)
         sums = jnp.sum(total, axis=0, keepdims=True) * UNSCALE
         for k in range(NC):
-            deg_ref[k, pl.ds(step * 2 + j, 1), :] = sums
-
-
-def apply_kernel(pos_ref, deg_ref, t_ref, b_ref, mine_ref, other_ref, own_ref, root_ref, held_ref, sem_ref):
+            deg_ref[k, pl.ds(step, 1), :] = sums
+
+    pl.when(step < KEPT)(lambda: score_piece(True))
+    pl.when(step >= KEPT)(lambda: score_piece(False))
+
+
+def apply_kernel(pos_ref, deg_ref, t_ref, s_ref, b_ref, *refs):
+    mine_ref, other_ref, own_ref, root_ref, held_ref, sem_ref = refs
+    z, core = pos_ref[0], pos_ref[1]
+    sign = 1 - 2 * core
+
     def fetch(t):
         slot = t % DEPTH
         return pltpu.make_async_copy(b_ref.at[t], held_ref.at[slot], sem_ref.at[slot])
@@ -100,18 +103,29 @@
     for t in range(DEPTH):
         fetch(t).start()
     root_ref[...] = lax.rsqrt(jnp.sum(deg_ref[...], axis=0))
-    core = pos_ref[0]
-    own_ref[...] = root_ref[pl.ds(pos_ref[1], 1), :] * UNSCALE
-    for t in range(NC):
+    own_ref[...] = root_ref[pl.ds(pos_ref[2], 1), :] * UNSCALE
+    mine_ref[...] = jnp.zeros_like(mine_ref)
+    other_ref[...] = jnp.zeros_like(other_ref)
+
+    def column_piece(t, tile_of):
         v = t_ref[t, DIM : DIM + VEC, :].astype(F32) + t_ref[t, DIM + VEC : WIDE, :].astype(F32)
         w = (v * root_ref[t : t + 1, :]).astype(BF16)
+        for r, (chip, same) in enumerate(SLOTS):
+            p_ref = mine_ref if same else other_ref
+            place = lax.rem(z + chip * sign + 16, 8)
+            p_ref[place] = p_ref[place] + nt(w, tile_of(r))
+
+    for t in range(KEPT, NC):
+
+        def again(r):
+            score = jnp.dot(s_ref[r], t_ref[t, 0:DIM, :], preferred_element_type=F32)
+            return jnp.exp2(score * SCALE).astype(BF16)
+
+        column_piece(t, again)
+    for t in range(KEPT):
         fetch(t).wait()
-        for r in range(NR // 2):
-            for side, p_ref in ((core, mine_ref), (1 - core, other_ref)):
-                rows = pl.ds(pl.multiple_of((r * 2 + side) * SEG, SEG), SEG)
-                part = nt(w, held_ref[t % DEPTH, rows, :])
-                p_ref[r] = part if t == 0 else p_ref[r] + part
-        if t + DEPTH < NC:
+        column_piece(t, lambda r: held_ref[t % DEPTH, r * SEG : (r + 1) * SEG, :])
+        if t + DEPTH < KEPT:
             fetch(t + DEPTH).start()
 
 
@@ -177,6 +191,7 @@
     unit, unit_copies = pl.pallas_call(
         unit_kernel,
         out_shape=(shape(DIM, SEG, dtype=BF16), shape(NC, WIDE, SEG, dtype=BF16)),
+        compiler_params=params(8),
         name="unit",
     )(embeddings.T, vectors.T)
     columns = to_all(unit_copies, COLS)
@@ -184,24 +199,32 @@
     one, two = along(pair, 1), along(pair, 2)
     three, four = along(two, 1), along(two[0], 2)
     pairs = (pair, one, across(one), two, across(two), three, across(three))
+    rows = pl.pallas_call(
+        turn_kernel,
+        out_shape=shape(NR, SEG, DIM, dtype=BF16),
+        compiler_params=params(8),
+        name="turn",
+    )(*pairs, four, across(four))
     block, degree = pl.pallas_call(
         affinity_kernel,
-        grid=(NC // 2,),
-        out_shape=(shape(NC, NR * SEG, SEG, dtype=BF16), shape(NC, NC, SEG)),
-        in_specs=[smem()] + [vmem()] * 10,
-        out_specs=(pl.BlockSpec((2, NR * SEG, SEG), lambda i: (i, 0, 0)), vmem()),
-        scratch_shapes=[pltpu.VMEM((NR, SEG, DIM), BF16)],
+        grid=(NC,),
+        out_shape=(pltpu.HBM((KEPT, NR * SEG, SEG), BF16), shape(NC, NC, SEG)),
+        in_specs=[vmem()] * 2,
+        out_specs=(
+            pl.BlockSpec((1, NR * SEG, SEG), lambda i: (jnp.minimum(i, KEPT - 1), 0, 0)),
+            vmem(),
+        ),
         compiler_params=params(32),
         cost_estimate=pl.CostEstimate(
             flops=2 * 256 * 4096 * 4096, transcendentals=4096 * 4096, bytes_accessed=1 << 25
         ),
         name="affinity",
-    )(jnp.stack([z, core]), columns, *pairs, four, across(four))
+    )(columns, rows)
     degree = to_all(degree, COLS)
     mine, other, own = pl.pallas_call(
         apply_kernel,
         out_shape=(shape(HALF, VEC, SEG), shape(HALF, VEC, SEG), shape(1, SEG)),
-        in_specs=[smem(), vmem(), vmem(), pl.BlockSpec(memory_space=pl.ANY)],
+        in_specs=[smem()] + [vmem()] * 3 + [pl.BlockSpec(memory_space=pl.ANY)],
         out_specs=(vmem(), vmem(), vmem()),
         scratch_shapes=[
             pltpu.VMEM((NC, SEG), F32),
@@ -210,11 +233,12 @@
         ],
         compiler_params=params(44),
         name="apply",
-    )(jnp.stack([core, column]), degree, columns, block)
+    )(jnp.stack([z, core, column]), degree, columns, rows, block)
     product = to_all(mine + across(other), "z")
     projected, gram = pl.pallas_call(
         project_kernel,
         out_shape=(shape(VEC, SEG), shape(2, 128)),
+        compiler_params=params(8),
         name="project",
     )(product, own)
     gram = jnp.broadcast_to(gram + across(gram), (CHIPS, 2, 128))
@@ -222,6 +246,7 @@
     basis, triangle = pl.pallas_call(
         finish_kernel,
         out_shape=(shape(VEC, SEG), shape(VEC, VEC)),
+        compiler_params=params(8),
         name="finish",
     )(gram, projected)
     return basis.T, triangle

time: 123 us -> 126 us (1.024)
  Pallas kernels: 34.9 us -> 38.2 us
  local copies, waits for them, and re-layouts: 0.06 us -> 1.65 us
    pallas_call x1 -> x2, Pallas kernels: 15.5 us -> 19 us  [the longest x1 18.4 us: per_device(): pl.pallas_call(affinity_kernel, grid=(NC,), out_shape=(pltpu.HBM((KEPT, N...]
    pallas_call x1, Pallas kernels: 12.1 us -> 15.2 us  [per_device(): pl.pallas_call(apply_kernel, out_shape=(shape(HALF, VEC, SEG), shape(HALF...]
    unnamed x4, local copies, waits for them, and re-layouts: 0.01 us -> 1.6 us
    pallas_call x1, Pallas kernels: 1.8 us -> 0.31 us  [per_device(): pl.pallas_call(project_kernel, out_shape=(shape(VEC, SEG), shape(2, 128))...]
where the time goes in v7:
time: 126 us; the launch traced here: 125 us
  Pallas kernels  38.2 us (30%)
  starting transfers between devices  34 us (27%)
  blocking collectives  32.3 us (26%)
  waiting for transfers between devices  18.4 us (15%)
  local copies, waits for them, and re-layouts  1.65 us (1%)
    all_to_all x2, blocking collectives, to_all(): return lax.all_to_all(copies, axes, split_axis=0, concat_axis=0, tiled=True)  32.3 us
    pallas_call x1, Pallas kernels, per_device(): pl.pallas_call(affinity_kernel, grid=(NC,), out_shape=(pltpu.HBM((KEPT, N...  18.4 us
    pallas_call x1, Pallas kernels, per_device(): pl.pallas_call(apply_kernel, out_shape=(shape(HALF, VEC, SEG), shape(HALF...  15.2 us
    all_to_all x2, starting transfers between devices, to_all(): return lax.all_to_all(copies, axes, split_axis=0, concat_axis=0, tiled=True)  12.4 us
    ppermute x4, starting transfers between devices, along(): return lax.ppermute(a, ROWS, turns)  11 us
    ppermute x7, starting transfers between devices, across(): return lax.ppermute(a, 'core', [(0, 1), (1, 0)])  10.6 us
    all_to_all x2, waiting for transfers between devices, to_all(): return lax.all_to_all(copies, axes, split_axis=0, concat_axis=0, tiled=True)  9.75 us
    ppermute x4, waiting for transfers between devices, along(): return lax.ppermute(a, ROWS, turns)  4.97 us
  transfers between devices with their start and end apart: 13, of which 9 were waited for; matrix products, arithmetic and copies ran while one was open for 0% of the time, Pallas kernels for 0%

profile of v7, /device:TPU:1, one launch (start us, length us, event | category | flops | bytes accessed | tf_op | source)
XLA Modules:
  0.0 125.3 jit_solution(6940555186242919029)
XLA Ops:
  0.6 0.0 copy-start
  0.6 0.9 copy-done
  1.5 0.0 copy-start.1
  1.5 0.7 copy-done.1
  2.2 1.4 %unit.1 = (bf16[192,256]{1,0:T(8,128)(2,1)S(1)}, bf16[16,224,256]{2,1,0:T(8,128)(2,1)}) custom-call(bf16[192,256]{1,0:T(8,128)(2,1)S(1)} %bitcast.10, f32[16,256]{1,0:T(8,128)S(1)} %bitcast.12), custom_call_target="tpu_custom_call" | custom-call | tf_op jit(solution)/shard_map/unit/pallas_call | solution.py:191
  3.6 7.6 %all-to-all-start = ((bf16[16,224,256]{2,1,0:T(8,128)(2,1)}), bf16[16,224,256]{2,1,0:T(8,128)(2,1)}, u32[]{:S(2)}, u32[]{:S(2)}) async-start(bf16[16,224,256]{2,1,0:T(8,128)(2,1)} %get-tuple-element.13), calls=%async_computation | async-start | bytes 3670016 | tf_op jit(solution)/shard_map/all_to_all | solution.py:170
  11.3 1.0 collective-permute-start
  12.3 0.9 collective-permute-done
  13.3 6.1 %collective-permute-start.3 = (bf16[2,192,256]{2,1,0:T(8,128)(2,1)S(1)}, bf16[2,192,256]{2,1,0:T(8,128)(2,1)S(1)}, u32[]{:S(2)}, u32[]{:S(2)}) collective-permute-start(bf16[2,192,256]{2,1,0:T(8,128)(2,1)S(1)} %pad_maximum_fusion.refs_0_), channel_id=1, source_target_pairs={{0,32},{8,104},{16,48},{24,120},{32,64},{40,8},{48,80},{56,24},{64... | collective-permute-start | bytes 589832 | tf_op jit(solution)/shard_map/ppermute | solution.py:185
  19.4 0.7 collective-permute-start.1
  20.1 4.0 %collective-permute-done.3.refs_3_ = bf16[2,192,256]{2,1,0:T(8,128)(2,1)S(1)} collective-permute-done((bf16[2,192,256]{2,1,0:T(8,128)(2,1)S(1)}, bf16[2,192,256]{2,1,0:T(8,128)(2,1)S(1)}, u32[]{:S(2)}, u32[]{:S(2)}) %collective-permute-start.3) | collective-permute-done | bytes 196640 | tf_op jit(solution)/shard_map/ppermute | solution.py:185
  24.1 2.4 %collective-permute-start.5 = (bf16[2,192,256]{2,1,0:T(8,128)(2,1)S(1)}, bf16[2,192,256]{2,1,0:T(8,128)(2,1)S(1)}, u32[]{:S(2)}, u32[]{:S(2)}) collective-permute-start(bf16[2,192,256]{2,1,0:T(8,128)(2,1)S(1)} %collective-permute-done.3.refs_3_), channel_id=1, source_target_pairs={{0,16},{8,120},{16,32},{24,8},{32,48},{40,24},{48,64},{56,40},{64,... | collective-permute-start | bytes 589832 | tf_op jit(solution)/shard_map/ppermute | solution.py:185
  26.5 1.8 %collective-permute-start.7 = (bf16[192,256]{1,0:T(8,128)(2,1)S(1)}, bf16[192,256]{1,0:T(8,128)(2,1)S(1)}, u32[]{:S(2)}, u32[]{:S(2)}) collective-permute-start(bf16[192,256]{1,0:T(8,128)(2,1)S(1)} %slice_bitcast_fusion), channel_id=1, source_target_pairs={{0,32},{8,104},{16,48},{24,120},{32,64},{40,8},{48,80},{56,24},{64... | collective-permute-start | bytes 294920 | tf_op jit(solution)/shard_map/ppermute | solution.py:185
  28.3 0.0 collective-permute-start.4
  28.3 0.0 collective-permute-done.1.refs_1_
  28.3 0.5 collective-permute-start.2
  28.8 0.2 collective-permute-done.5.refs_5_
  29.1 2.6 %collective-permute-start.6 = (bf16[2,192,256]{2,1,0:T(8,128)(2,1)S(1)}, bf16[2,192,256]{2,1,0:T(8,128)(2,1)S(1)}, u32[]{:S(2)}, u32[]{:S(2)}) collective-permute-start(bf16[2,192,256]{2,1,0:T(8,128)(2,1)S(1)} %collective-permute-done.5.refs_5_), channel_id=1, source_target_pairs={{0,8},{8,0},{1,9},{9,1},{2,10},{10,2},{3,11},{11,3},{4,12},{12,4},... | collective-permute-start | bytes 589832 | tf_op jit(solution)/shard_map/ppermute | solution.py:178
  31.7 0.7 collective-permute-done.7.refs_7_
  32.4 2.4 %collective-permute-start.8 = (bf16[192,256]{1,0:T(8,128)(2,1)S(1)}, bf16[192,256]{1,0:T(8,128)(2,1)S(1)}, u32[]{:S(2)}, u32[]{:S(2)}) collective-permute-start(bf16[192,256]{1,0:T(8,128)(2,1)S(1)} %collective-permute-done.7.refs_7_), channel_id=1, source_target_pairs={{0,8},{8,0},{1,9},{9,1},{2,10},{10,2},{3,11},{11,3},{4,12},{12,4},... | collective-permute-start | bytes 294920 | tf_op jit(solution)/shard_map/ppermute | solution.py:178
  34.8 0.9 collective-permute-done.8.refs_8_
  35.7 0.0 collective-permute-done.4.refs_4_
  35.7 0.0 collective-permute-done.2.refs_2_
  35.7 0.0 collective-permute-done.6.refs_6_
  35.7 0.6 turn.1.s_ref
  36.3 2.1 %all-to-all-done.t_ref = bf16[16,224,256]{2,1,0:T(8,128)(2,1)} async-done(((bf16[16,224,256]{2,1,0:T(8,128)(2,1)}), bf16[16,224,256]{2,1,0:T(8,128)(2,1)}, u32[]{:S(2)}, u32[]{:S(2)}) %all-to-all-start) | async-done | bytes 1835040 | tf_op jit(solution)/shard_map/all_to_all | solution.py:170
  38.5 18.4 %affinity.1 = (bf16[13,4096,256]{2,1,0:T(8,128)(2,1)}, f32[16,16,256]{2,1,0:T(8,128)}) custom-call(bf16[16,224,256]{2,1,0:T(8,128)(2,1)} %all-to-all-done.t_ref, bf16[16,256,192]{2,1,0:T(8,128)(2,1)S(1)} %turn.1.s_ref), custom_call_target="tpu_custom_call" | custom-call | flops 8589934592 | bytes 33554432 | tf_op jit(solution)/shard_map/affinity/pallas_call | solution.py:208
  56.8 4.7 %all-to-all-start.1 = ((f32[16,16,256]{2,1,0:T(8,128)}), f32[16,16,256]{2,1,0:T(8,128)S(1)}, u32[]{:S(2)}, u32[]{:S(2)}) async-start(f32[16,16,256]{2,1,0:T(8,128)} %get-tuple-element.15), calls=%async_computation.1 | async-start | bytes 524288 | tf_op jit(solution)/shard_map/all_to_all | solution.py:170
  61.6 0.1 pad_add_fusion.pos_ref
  61.7 7.6 %all-to-all-done.1.deg_ref = f32[16,16,256]{2,1,0:T(8,128)S(1)} async-done(((f32[16,16,256]{2,1,0:T(8,128)}), f32[16,16,256]{2,1,0:T(8,128)S(1)}, u32[]{:S(2)}, u32[]{:S(2)}) %all-to-all-start.1) | async-done | bytes 262176 | tf_op jit(solution)/shard_map/all_to_all | solution.py:170
  69.3 15.2 %apply.1 = (f32[8,16,256]{2,1,0:T(8,128)S(1)}, f32[8,16,256]{2,1,0:T(8,128)S(1)}, f32[1,256]{1,0:T(1,128)S(1)}) custom-call(s32[3]{0:T(128)S(1)} %pad_add_fusion.pos_ref, f32[16,16,256]{2,1,0:T(8,128)S(1)} %all-to-all-done.1.deg_ref, bf16[16,224,256]{2,1,0:T(8,128)(2,1)} %all-to-all-done.t_ref, bf16[16,256,192]{2,1,0:T(8,128)(2,1)S(1)} %turn.1.s_ref, ...), custom_call_target="tpu_custom_call" | custom-call | tf_op jit(solution)/shard_map/apply/pallas_call | solution.py:224
  84.5 1.9 %collective-permute-start.9 = (f32[8,16,256]{2,1,0:T(8,128)S(1)}, f32[8,16,256]{2,1,0:T(8,128)S(1)}, u32[]{:S(2)}, u32[]{:S(2)}) collective-permute-start(f32[8,16,256]{2,1,0:T(8,128)S(1)} %get-tuple-element.18), channel_id=1, source_target_pairs={{0,8},{8,0},{1,9},{9,1},{2,10},{10,2},{3,11},{11,3},{4,12},{12,4},... | collective-permute-start | bytes 393224 | tf_op jit(solution)/shard_map/ppermute | solution.py:178
  86.4 1.0 collective-permute-done.9
  87.4 15.6 %all_to_all.20.p_ref = f32[8,16,256]{2,1,0:T(8,128)S(1)} all-to-all(f32[8,16,256]{2,1,0:T(8,128)S(1)} %add.14), channel_id=1, replica_groups=mesh['xl'=2,'z'=8,'core'=2,'y'=4,'xh'=2] {'z'}, dimensions={0} | all-to-all | bytes 262144 | tf_op jit(solution)/shard_map/all_to_all | solution.py:170
  103.1 0.3 project.1
  103.4 2.1 %collective-permute-start.10 = (f32[2,128]{1,0:T(2,128)S(1)}, f32[2,128]{1,0:T(2,128)S(1)}, u32[]{:S(2)}, u32[]{:S(2)}) collective-permute-start(f32[2,128]{1,0:T(2,128)S(1)} %get-tuple-element.20), channel_id=1, source_target_pairs={{0,8},{8,0},{1,9},{9,1},{2,10},{10,2},{3,11},{11,3},{4,12},{12,4},... | collective-permute-start | bytes 3080 | tf_op jit(solution)/shard_map/ppermute | solution.py:178
  105.5 0.8 collective-permute-done.10
  106.4 16.7 %all_to_all.21.gram_ref = f32[128,2,128]{2,1,0:T(2,128)S(1)} all-to-all(f32[128,2,128]{2,1,0:T(2,128)S(1)} %broadcast_in_dim.3), channel_id=1, replica_groups=mesh['xl'=2,'z'=8,'core'=2,'y'=4,'xh'=2] {'xl','z','y','xh'}, dimensions={0} | all-to-all | bytes 262144 | tf_op jit(solution)/shard_map/all_to_all | solution.py:170
  123.0 2.3 %finish.1 = (f32[16,256]{1,0:T(8,128)}, f32[16,16]{1,0:T(8,128)}) custom-call(f32[128,2,128]{2,1,0:T(2,128)S(1)} %all_to_all.21.gram_ref, f32[16,256]{1,0:T(8,128)S(1)} %get-tuple-element.21.q_ref), custom_call_target="tpu_custom_call" | custom-call | tf_op jit(solution)/shard_map/finish/pallas_call | solution.py:246
  (5 shorter events, 0.1 us)
Async XLA Ops:
  0.6 0.9 copy-start
  1.5 0.7 copy-start.1
  3.6 34.8 %all-to-all-start = ((bf16[16,224,256]{2,1,0:T(8,128)(2,1)}), bf16[16,224,256]{2,1,0:T(8,128)(2,1)}, u32[]{:S(2)}, u32[]{:S(2)}) async-start(bf16[16,224,256]{2,1,0:T(8,128)(2,1)} %get-tuple-element.13), calls=%async_computation | async-start | bytes 3670016 | tf_op jit(solution)/shard_map/all_to_all | solution.py:170
  11.3 2.0 %collective-permute-start = (bf16[192,256]{1,0:T(8,128)(2,1)S(1)}, bf16[192,256]{1,0:T(8,128)(2,1)S(1)}, u32[]{:S(2)}, u32[]{:S(2)}) collective-permute-start(bf16[192,256]{1,0:T(8,128)(2,1)S(1)} %get-tuple-element.14), channel_id=1, source_target_pairs={{0,8},{8,0},{1,9},{9,1},{2,10},{10,2},{3,11},{11,3},{4,12},{12,4},... | collective-permute-start | bytes 294920 | tf_op jit(solution)/shard_map/ppermute | solution.py:178
  13.3 10.8 %collective-permute-start.3 = (bf16[2,192,256]{2,1,0:T(8,128)(2,1)S(1)}, bf16[2,192,256]{2,1,0:T(8,128)(2,1)S(1)}, u32[]{:S(2)}, u32[]{:S(2)}) collective-permute-start(bf16[2,192,256]{2,1,0:T(8,128)(2,1)S(1)} %pad_maximum_fusion.refs_0_), channel_id=1, source_target_pairs={{0,32},{8,104},{16,48},{24,120},{32,64},{40,8},{48,80},{56,24},{64... | collective-permute-start | bytes 589832 | tf_op jit(solution)/shard_map/ppermute | solution.py:185
  19.4 8.9 %collective-permute-start.1 = (bf16[2,192,256]{2,1,0:T(8,128)(2,1)S(1)}, bf16[2,192,256]{2,1,0:T(8,128)(2,1)S(1)}, u32[]{:S(2)}, u32[]{:S(2)}) collective-permute-start(bf16[2,192,256]{2,1,0:T(8,128)(2,1)S(1)} %pad_maximum_fusion.refs_0_), channel_id=1, source_target_pairs={{0,16},{8,120},{16,32},{24,8},{32,48},{40,24},{48,64},{56,40},{64,... | collective-permute-start | bytes 589832 | tf_op jit(solution)/shard_map/ppermute | solution.py:185
  24.1 5.0 %collective-permute-start.5 = (bf16[2,192,256]{2,1,0:T(8,128)(2,1)S(1)}, bf16[2,192,256]{2,1,0:T(8,128)(2,1)S(1)}, u32[]{:S(2)}, u32[]{:S(2)}) collective-permute-start(bf16[2,192,256]{2,1,0:T(8,128)(2,1)S(1)} %collective-permute-done.3.refs_3_), channel_id=1, source_target_pairs={{0,16},{8,120},{16,32},{24,8},{32,48},{40,24},{48,64},{56,40},{64,... | collective-permute-start | bytes 589832 | tf_op jit(solution)/shard_map/ppermute | solution.py:185
  26.5 5.9 %collective-permute-start.7 = (bf16[192,256]{1,0:T(8,128)(2,1)S(1)}, bf16[192,256]{1,0:T(8,128)(2,1)S(1)}, u32[]{:S(2)}, u32[]{:S(2)}) collective-permute-start(bf16[192,256]{1,0:T(8,128)(2,1)S(1)} %slice_bitcast_fusion), channel_id=1, source_target_pairs={{0,32},{8,104},{16,48},{24,120},{32,64},{40,8},{48,80},{56,24},{64... | collective-permute-start | bytes 294920 | tf_op jit(solution)/shard_map/ppermute | solution.py:185
  28.3 7.4 %collective-permute-start.4 = (bf16[2,192,256]{2,1,0:T(8,128)(2,1)S(1)}, bf16[2,192,256]{2,1,0:T(8,128)(2,1)S(1)}, u32[]{:S(2)}, u32[]{:S(2)}) collective-permute-start(bf16[2,192,256]{2,1,0:T(8,128)(2,1)S(1)} %collective-permute-done.3.refs_3_), channel_id=1, source_target_pairs={{0,8},{8,0},{1,9},{9,1},{2,10},{10,2},{3,11},{11,3},{4,12},{12,4},... | collective-permute-start | bytes 589832 | tf_op jit(solution)/shard_map/ppermute | solution.py:178
  28.3 7.4 %collective-permute-start.2 = (bf16[2,192,256]{2,1,0:T(8,128)(2,1)S(1)}, bf16[2,192,256]{2,1,0:T(8,128)(2,1)S(1)}, u32[]{:S(2)}, u32[]{:S(2)}) collective-permute-start(bf16[2,192,256]{2,1,0:T(8,128)(2,1)S(1)} %collective-permute-done.1.refs_1_), channel_id=1, source_target_pairs={{0,8},{8,0},{1,9},{9,1},{2,10},{10,2},{3,11},{11,3},{4,12},{12,4},... | collective-permute-start | bytes 589832 | tf_op jit(solution)/shard_map/ppermute | solution.py:178
  29.1 6.6 %collective-permute-start.6 = (bf16[2,192,256]{2,1,0:T(8,128)(2,1)S(1)}, bf16[2,192,256]{2,1,0:T(8,128)(2,1)S(1)}, u32[]{:S(2)}, u32[]{:S(2)}) collective-permute-start(bf16[2,192,256]{2,1,0:T(8,128)(2,1)S(1)} %collective-permute-done.5.refs_5_), channel_id=1, source_target_pairs={{0,8},{8,0},{1,9},{9,1},{2,10},{10,2},{3,11},{11,3},{4,12},{12,4},... | collective-permute-start | bytes 589832 | tf_op jit(solution)/shard_map/ppermute | solution.py:178
  32.4 3.3 %collective-permute-start.8 = (bf16[192,256]{1,0:T(8,128)(2,1)S(1)}, bf16[192,256]{1,0:T(8,128)(2,1)S(1)}, u32[]{:S(2)}, u32[]{:S(2)}) collective-permute-start(bf16[192,256]{1,0:T(8,128)(2,1)S(1)} %collective-permute-done.7.refs_7_), channel_id=1, source_target_pairs={{0,8},{8,0},{1,9},{9,1},{2,10},{10,2},{3,11},{11,3},{4,12},{12,4},... | collective-permute-start | bytes 294920 | tf_op jit(solution)/shard_map/ppermute | solution.py:178
  56.8 12.5 %all-to-all-start.1 = ((f32[16,16,256]{2,1,0:T(8,128)}), f32[16,16,256]{2,1,0:T(8,128)S(1)}, u32[]{:S(2)}, u32[]{:S(2)}) async-start(f32[16,16,256]{2,1,0:T(8,128)} %get-tuple-element.15), calls=%async_computation.1 | async-start | bytes 524288 | tf_op jit(solution)/shard_map/all_to_all | solution.py:170
  84.5 2.9 %collective-permute-start.9 = (f32[8,16,256]{2,1,0:T(8,128)S(1)}, f32[8,16,256]{2,1,0:T(8,128)S(1)}, u32[]{:S(2)}, u32[]{:S(2)}) collective-permute-start(f32[8,16,256]{2,1,0:T(8,128)S(1)} %get-tuple-element.18), channel_id=1, source_target_pairs={{0,8},{8,0},{1,9},{9,1},{2,10},{10,2},{3,11},{11,3},{4,12},{12,4},... | collective-permute-start | bytes 393224 | tf_op jit(solution)/shard_map/ppermute | solution.py:178
  103.4 3.0 %collective-permute-start.10 = (f32[2,128]{1,0:T(2,128)S(1)}, f32[2,128]{1,0:T(2,128)S(1)}, u32[]{:S(2)}, u32[]{:S(2)}) collective-permute-start(f32[2,128]{1,0:T(2,128)S(1)} %get-tuple-element.20), channel_id=1, source_target_pairs={{0,8},{8,0},{1,9},{9,1},{2,10},{10,2},{3,11},{11,3},{4,12},{12,4},... | collective-permute-start | bytes 3080 | tf_op jit(solution)/shard_map/ppermute | solution.py:178

commit v8 on v7

--- a/solution.py
+++ b/solution.py
@@ -12,7 +12,7 @@
 COLS = ("xl", "y", "xh")
 CHIPS = 128
 HALF = 8
-KEPT = 13
+KEPT = 14
 NR = 16
 NC = 16
 SEG = 256
@@ -74,25 +74,30 @@
 def affinity_kernel(t_ref, s_ref, b_ref, deg_ref):
     step = pl.program_id(0)
 
-    def score_piece(keep):
-        piece = t_ref[step, 0:DIM, :]
-        total = jnp.zeros((8, SEG), F32)
-        for r in range(NR):
-            score = jnp.dot(s_ref[r], piece, preferred_element_type=F32)
-            tile = jnp.exp2(score * SCALE)
-            total = total + jnp.sum(tile.reshape(SEG // 8, 8, SEG), axis=0)
-            if keep:
-                b_ref[0, r * SEG : (r + 1) * SEG, :] = tile.astype(BF16)
-        sums = jnp.sum(total, axis=0, keepdims=True) * UNSCALE
-        for k in range(NC):
-            deg_ref[k, pl.ds(step, 1), :] = sums
-
-    pl.when(step < KEPT)(lambda: score_piece(True))
-    pl.when(step >= KEPT)(lambda: score_piece(False))
+    def score_pieces(keep):
+        for j in range(2):
+            t = step * 2 + j
+            piece = t_ref[t, 0:DIM, :]
+            total = jnp.zeros((8, SEG), F32)
+            for r in range(NR):
+                score = jnp.dot(s_ref[r], piece, preferred_element_type=F32)
+                tile = jnp.exp2(score * SCALE)
+                total = total + jnp.sum(tile.reshape(SEG // 8, 8, SEG), axis=0)
+                if keep:
+                    b_ref[j, r * SEG : (r + 1) * SEG, :] = tile.astype(BF16)
+            sums = jnp.sum(total, axis=0, keepdims=True) * UNSCALE
+            for k in range(NC):
+                deg_ref[k, pl.ds(t, 1), :] = sums
+
+    if KEPT == NC:
+        score_pieces(True)
+    else:
+        pl.when(step < KEPT // 2)(lambda: score_pieces(True))
+        pl.when(step >= KEPT // 2)(lambda: score_pieces(False))
 
 
 def apply_kernel(pos_ref, deg_ref, t_ref, s_ref, b_ref, *refs):
-    mine_ref, other_ref, own_ref, root_ref, held_ref, sem_ref = refs
+    mine_ref, other_ref, own_ref, root_ref, held_ref, acc_ref, sem_ref = refs
     z, core = pos_ref[0], pos_ref[1]
     sign = 1 - 2 * core
 
@@ -104,16 +109,13 @@
         fetch(t).start()
     root_ref[...] = lax.rsqrt(jnp.sum(deg_ref[...], axis=0))
     own_ref[...] = root_ref[pl.ds(pos_ref[2], 1), :] * UNSCALE
-    mine_ref[...] = jnp.zeros_like(mine_ref)
-    other_ref[...] = jnp.zeros_like(other_ref)
-
-    def column_piece(t, tile_of):
+
+    def column_piece(t, first, tile_of):
         v = t_ref[t, DIM : DIM + VEC, :].astype(F32) + t_ref[t, DIM + VEC : WIDE, :].astype(F32)
         w = (v * root_ref[t : t + 1, :]).astype(BF16)
-        for r, (chip, same) in enumerate(SLOTS):
-            p_ref = mine_ref if same else other_ref
-            place = lax.rem(z + chip * sign + 16, 8)
-            p_ref[place] = p_ref[place] + nt(w, tile_of(r))
+        for r in range(NR):
+            part = nt(w, tile_of(r))
+            acc_ref[r] = part if first else acc_ref[r] + part
 
     for t in range(KEPT, NC):
 
@@ -121,12 +123,19 @@
             score = jnp.dot(s_ref[r], t_ref[t, 0:DIM, :], preferred_element_type=F32)
             return jnp.exp2(score * SCALE).astype(BF16)
 
-        column_piece(t, again)
+        column_piece(t, t == KEPT, again)
     for t in range(KEPT):
         fetch(t).wait()
-        column_piece(t, lambda r: held_ref[t % DEPTH, r * SEG : (r + 1) * SEG, :])
+        column_piece(
+            t,
+            KEPT == NC and t == 0,
+            lambda r: held_ref[t % DEPTH, r * SEG : (r + 1) * SEG, :],
+        )
         if t + DEPTH < KEPT:
             fetch(t + DEPTH).start()
+    for r, (chip, same) in enumerate(SLOTS):
+        p_ref = mine_ref if same else other_ref
+        p_ref[lax.rem(z + chip * sign + 16, 8)] = acc_ref[r]
 
 
 def project_kernel(p_ref, own_ref, q_ref, gram_ref):
@@ -191,7 +200,6 @@
     unit, unit_copies = pl.pallas_call(
         unit_kernel,
         out_shape=(shape(DIM, SEG, dtype=BF16), shape(NC, WIDE, SEG, dtype=BF16)),
-        compiler_params=params(8),
         name="unit",
     )(embeddings.T, vectors.T)
     columns = to_all(unit_copies, COLS)
@@ -207,11 +215,11 @@
     )(*pairs, four, across(four))
     block, degree = pl.pallas_call(
         affinity_kernel,
-        grid=(NC,),
+        grid=(NC // 2,),
         out_shape=(pltpu.HBM((KEPT, NR * SEG, SEG), BF16), shape(NC, NC, SEG)),
         in_specs=[vmem()] * 2,
         out_specs=(
-            pl.BlockSpec((1, NR * SEG, SEG), lambda i: (jnp.minimum(i, KEPT - 1), 0, 0)),
+            pl.BlockSpec((2, NR * SEG, SEG), lambda i: (jnp.minimum(i, KEPT // 2 - 1), 0, 0)),
             vmem(),
         ),
         compiler_params=params(32),
@@ -229,6 +237,7 @@
         scratch_shapes=[
             pltpu.VMEM((NC, SEG), F32),
             pltpu.VMEM((DEPTH, NR * SEG, SEG), BF16),
+            pltpu.VMEM((NR, VEC, SEG), F32),
             pltpu.SemaphoreType.DMA((DEPTH,)),
         ],
         compiler_params=params(44),

time: 126 us -> 131 us (1.040)
  Pallas kernels: 38.2 us -> 45 us
  local copies, waits for them, and re-layouts: 1.65 us -> 0.05 us
    pallas_call x1, Pallas kernels: 15.2 us -> 23.6 us  [per_device(): pl.pallas_call(apply_kernel, out_shape=(shape(HALF, VEC, SEG), shape(HALF...]
    pallas_call x1, Pallas kernels: 18.4 us -> 15.9 us  [per_device(): pl.pallas_call(affinity_kernel, grid=(NC // 2,), out_shape=(pltpu.HBM((KE...]
    unnamed x4 -> x2, local copies, waits for them, and re-layouts: 1.6 us -> 0.01 us
where the time goes in v8:
time: 131 us
  Pallas kernels  45 us (34%)
  starting transfers between devices  34.2 us (26%)
  blocking collectives  32.2 us (25%)
  waiting for transfers between devices  18.4 us (14%)
    all_to_all x2, blocking collectives, to_all(): return lax.all_to_all(copies, axes, split_axis=0, concat_axis=0, tiled=True)  32.2 us
    pallas_call x1, Pallas kernels, per_device(): pl.pallas_call(apply_kernel, out_shape=(shape(HALF, VEC, SEG), shape(HALF...  23.6 us
    pallas_call x1, Pallas kernels, per_device(): pl.pallas_call(affinity_kernel, grid=(NC // 2,), out_shape=(pltpu.HBM((KE...  15.9 us
    all_to_all x2, starting transfers between devices, to_all(): return lax.all_to_all(copies, axes, split_axis=0, concat_axis=0, tiled=True)  12.6 us
    ppermute x4, starting transfers between devices, along(): return lax.ppermute(a, ROWS, turns)  11 us
    ppermute x7, starting transfers between devices, across(): return lax.ppermute(a, 'core', [(0, 1), (1, 0)])  10.6 us
    all_to_all x2, waiting for transfers between devices, to_all(): return lax.all_to_all(copies, axes, split_axis=0, concat_axis=0, tiled=True)  9.74 us
    ppermute x4, waiting for transfers between devices, along(): return lax.ppermute(a, ROWS, turns)  4.97 us
  transfers between devices with their start and end apart: 13, of which 9 were waited for; matrix products, arithmetic and copies ran while one was open for 0% of the time, Pallas kernels for 0%

profile of v8, /device:TPU:1, one launch (start us, length us, event | category | flops | bytes accessed | tf_op | source)
XLA Modules:
  0.0 130.7 jit_solution(1407658213118710552)
XLA Ops:
  0.6 2.3 %unit.1 = (bf16[192,256]{1,0:T(8,128)(2,1)}, bf16[16,224,256]{2,1,0:T(8,128)(2,1)}) custom-call(bf16[192,256]{1,0:T(8,128)(2,1)} %bitcast.10, f32[16,256]{1,0:T(8,128)} %bitcast.13), custom_call_target="tpu_custom_call" | custom-call | tf_op jit(solution)/shard_map/unit/pallas_call | solution.py:200
  2.9 0.0 copy-start
  2.9 7.8 %all-to-all-start = ((bf16[16,224,256]{2,1,0:T(8,128)(2,1)}), bf16[16,224,256]{2,1,0:T(8,128)(2,1)}, u32[]{:S(2)}, u32[]{:S(2)}) async-start(bf16[16,224,256]{2,1,0:T(8,128)(2,1)} %get-tuple-element.13), calls=%async_computation | async-start | bytes 3670016 | tf_op jit(solution)/shard_map/all_to_all | solution.py:179
  10.7 0.0 copy-done
  10.7 1.0 collective-permute-start
  11.8 0.9 collective-permute-done
  12.7 6.1 %collective-permute-start.3 = (bf16[2,192,256]{2,1,0:T(8,128)(2,1)S(1)}, bf16[2,192,256]{2,1,0:T(8,128)(2,1)S(1)}, u32[]{:S(2)}, u32[]{:S(2)}) collective-permute-start(bf16[2,192,256]{2,1,0:T(8,128)(2,1)S(1)} %pad_maximum_fusion.refs_0_), channel_id=1, source_target_pairs={{0,32},{8,104},{16,48},{24,120},{32,64},{40,8},{48,80},{56,24},{64... | collective-permute-start | bytes 589832 | tf_op jit(solution)/shard_map/ppermute | solution.py:194
  18.8 0.7 collective-permute-start.1
  19.6 4.0 %collective-permute-done.3.refs_3_ = bf16[2,192,256]{2,1,0:T(8,128)(2,1)S(1)} collective-permute-done((bf16[2,192,256]{2,1,0:T(8,128)(2,1)S(1)}, bf16[2,192,256]{2,1,0:T(8,128)(2,1)S(1)}, u32[]{:S(2)}, u32[]{:S(2)}) %collective-permute-start.3) | collective-permute-done | bytes 196640 | tf_op jit(solution)/shard_map/ppermute | solution.py:194
  23.6 2.4 %collective-permute-start.5 = (bf16[2,192,256]{2,1,0:T(8,128)(2,1)S(1)}, bf16[2,192,256]{2,1,0:T(8,128)(2,1)S(1)}, u32[]{:S(2)}, u32[]{:S(2)}) collective-permute-start(bf16[2,192,256]{2,1,0:T(8,128)(2,1)S(1)} %collective-permute-done.3.refs_3_), channel_id=1, source_target_pairs={{0,16},{8,120},{16,32},{24,8},{32,48},{40,24},{48,64},{56,40},{64,... | collective-permute-start | bytes 589832 | tf_op jit(solution)/shard_map/ppermute | solution.py:194
  25.9 1.8 %collective-permute-start.7 = (bf16[192,256]{1,0:T(8,128)(2,1)S(1)}, bf16[192,256]{1,0:T(8,128)(2,1)S(1)}, u32[]{:S(2)}, u32[]{:S(2)}) collective-permute-start(bf16[192,256]{1,0:T(8,128)(2,1)S(1)} %slice_bitcast_fusion), channel_id=1, source_target_pairs={{0,32},{8,104},{16,48},{24,120},{32,64},{40,8},{48,80},{56,24},{64... | collective-permute-start | bytes 294920 | tf_op jit(solution)/shard_map/ppermute | solution.py:194
  27.8 0.0 collective-permute-start.4
  27.8 0.0 collective-permute-done.1.refs_1_
  27.8 0.5 collective-permute-start.2
  28.3 0.2 collective-permute-done.5.refs_5_
  28.5 2.6 %collective-permute-start.6 = (bf16[2,192,256]{2,1,0:T(8,128)(2,1)S(1)}, bf16[2,192,256]{2,1,0:T(8,128)(2,1)S(1)}, u32[]{:S(2)}, u32[]{:S(2)}) collective-permute-start(bf16[2,192,256]{2,1,0:T(8,128)(2,1)S(1)} %collective-permute-done.5.refs_5_), channel_id=1, source_target_pairs={{0,8},{8,0},{1,9},{9,1},{2,10},{10,2},{3,11},{11,3},{4,12},{12,4},... | collective-permute-start | bytes 589832 | tf_op jit(solution)/shard_map/ppermute | solution.py:187
  31.1 0.7 collective-permute-done.7.refs_7_
  31.8 2.4 %collective-permute-start.8 = (bf16[192,256]{1,0:T(8,128)(2,1)S(1)}, bf16[192,256]{1,0:T(8,128)(2,1)S(1)}, u32[]{:S(2)}, u32[]{:S(2)}) collective-permute-start(bf16[192,256]{1,0:T(8,128)(2,1)S(1)} %collective-permute-done.7.refs_7_), channel_id=1, source_target_pairs={{0,8},{8,0},{1,9},{9,1},{2,10},{10,2},{3,11},{11,3},{4,12},{12,4},... | collective-permute-start | bytes 294920 | tf_op jit(solution)/shard_map/ppermute | solution.py:187
  34.2 0.9 collective-permute-done.8.refs_8_
  35.1 0.0 collective-permute-done.4.refs_4_
  35.1 0.0 collective-permute-done.2.refs_2_
  35.2 0.0 collective-permute-done.6.refs_6_
  35.2 0.6 turn.1.s_ref
  35.8 2.1 %all-to-all-done.t_ref = bf16[16,224,256]{2,1,0:T(8,128)(2,1)} async-done(((bf16[16,224,256]{2,1,0:T(8,128)(2,1)}), bf16[16,224,256]{2,1,0:T(8,128)(2,1)}, u32[]{:S(2)}, u32[]{:S(2)}) %all-to-all-start) | async-done | bytes 1835040 | tf_op jit(solution)/shard_map/all_to_all | solution.py:179
  37.9 15.9 %affinity.1 = (bf16[14,4096,256]{2,1,0:T(8,128)(2,1)}, f32[16,16,256]{2,1,0:T(8,128)}) custom-call(bf16[16,224,256]{2,1,0:T(8,128)(2,1)} %all-to-all-done.t_ref, bf16[16,256,192]{2,1,0:T(8,128)(2,1)S(1)} %turn.1.s_ref), custom_call_target="tpu_custom_call" | custom-call | flops 8589934592 | bytes 33554432 | tf_op jit(solution)/shard_map/affinity/pallas_call | solution.py:216
  53.7 4.8 %all-to-all-start.1 = ((f32[16,16,256]{2,1,0:T(8,128)}), f32[16,16,256]{2,1,0:T(8,128)S(1)}, u32[]{:S(2)}, u32[]{:S(2)}) async-start(f32[16,16,256]{2,1,0:T(8,128)} %get-tuple-element.15), calls=%async_computation.1 | async-start | bytes 524288 | tf_op jit(solution)/shard_map/all_to_all | solution.py:179
  58.6 0.1 pad_add_fusion.pos_ref
  58.7 7.6 %all-to-all-done.1.deg_ref = f32[16,16,256]{2,1,0:T(8,128)S(1)} async-done(((f32[16,16,256]{2,1,0:T(8,128)}), f32[16,16,256]{2,1,0:T(8,128)S(1)}, u32[]{:S(2)}, u32[]{:S(2)}) %all-to-all-start.1) | async-done | bytes 262176 | tf_op jit(solution)/shard_map/all_to_all | solution.py:179
  66.3 23.6 %apply.1 = (f32[8,16,256]{2,1,0:T(8,128)S(1)}, f32[8,16,256]{2,1,0:T(8,128)S(1)}, f32[1,256]{1,0:T(1,128)S(1)}) custom-call(s32[3]{0:T(128)S(1)} %pad_add_fusion.pos_ref, f32[16,16,256]{2,1,0:T(8,128)S(1)} %all-to-all-done.1.deg_ref, bf16[16,224,256]{2,1,0:T(8,128)(2,1)} %all-to-all-done.t_ref, bf16[16,256,192]{2,1,0:T(8,128)(2,1)S(1)} %turn.1.s_ref, ...), custom_call_target="tpu_custom_call" | custom-call | tf_op jit(solution)/shard_map/apply/pallas_call | solution.py:232
  89.9 1.9 %collective-permute-start.9 = (f32[8,16,256]{2,1,0:T(8,128)S(1)}, f32[8,16,256]{2,1,0:T(8,128)S(1)}, u32[]{:S(2)}, u32[]{:S(2)}) collective-permute-start(f32[8,16,256]{2,1,0:T(8,128)S(1)} %get-tuple-element.18), channel_id=1, source_target_pairs={{0,8},{8,0},{1,9},{9,1},{2,10},{10,2},{3,11},{11,3},{4,12},{12,4},... | collective-permute-start | bytes 393224 | tf_op jit(solution)/shard_map/ppermute | solution.py:187
  91.8 1.0 collective-permute-done.9
  92.9 15.5 %all_to_all.20.p_ref = f32[8,16,256]{2,1,0:T(8,128)S(1)} all-to-all(f32[8,16,256]{2,1,0:T(8,128)S(1)} %add.14), channel_id=1, replica_groups=mesh['xl'=2,'z'=8,'core'=2,'y'=4,'xh'=2] {'z'}, dimensions={0} | all-to-all | bytes 262144 | tf_op jit(solution)/shard_map/all_to_all | solution.py:179
  108.4 0.3 project.1
  108.7 2.1 %collective-permute-start.10 = (f32[2,128]{1,0:T(2,128)S(1)}, f32[2,128]{1,0:T(2,128)S(1)}, u32[]{:S(2)}, u32[]{:S(2)}) collective-permute-start(f32[2,128]{1,0:T(2,128)S(1)} %get-tuple-element.20), channel_id=1, source_target_pairs={{0,8},{8,0},{1,9},{9,1},{2,10},{10,2},{3,11},{11,3},{4,12},{12,4},... | collective-permute-start | bytes 3080 | tf_op jit(solution)/shard_map/ppermute | solution.py:187
  110.8 0.8 collective-permute-done.10
  111.7 16.7 %all_to_all.21.gram_ref = f32[128,2,128]{2,1,0:T(2,128)S(1)} all-to-all(f32[128,2,128]{2,1,0:T(2,128)S(1)} %broadcast_in_dim.3), channel_id=1, replica_groups=mesh['xl'=2,'z'=8,'core'=2,'y'=4,'xh'=2] {'xl','z','y','xh'}, dimensions={0} | all-to-all | bytes 262144 | tf_op jit(solution)/shard_map/all_to_all | solution.py:179
  128.4 2.3 %finish.1 = (f32[16,256]{1,0:T(8,128)}, f32[16,16]{1,0:T(8,128)}) custom-call(f32[128,2,128]{2,1,0:T(2,128)S(1)} %all_to_all.21.gram_ref, f32[16,256]{1,0:T(8,128)S(1)} %get-tuple-element.21.q_ref), custom_call_target="tpu_custom_call" | custom-call | tf_op jit(solution)/shard_map/finish/pallas_call | solution.py:255
  (5 shorter events, 0.1 us)
Async XLA Ops:
  2.9 7.8 %copy-start = (bf16[192,256]{1,0:T(8,128)(2,1)S(1)}, bf16[192,256]{1,0:T(8,128)(2,1)}, u32[]{:S(2)}) copy-start(bf16[192,256]{1,0:T(8,128)(2,1)} %get-tuple-element.14) | copy-start | bytes 294916
  2.9 34.9 %all-to-all-start = ((bf16[16,224,256]{2,1,0:T(8,128)(2,1)}), bf16[16,224,256]{2,1,0:T(8,128)(2,1)}, u32[]{:S(2)}, u32[]{:S(2)}) async-start(bf16[16,224,256]{2,1,0:T(8,128)(2,1)} %get-tuple-element.13), calls=%async_computation | async-start | bytes 3670016 | tf_op jit(solution)/shard_map/all_to_all | solution.py:179
  10.7 2.0 %collective-permute-start = (bf16[192,256]{1,0:T(8,128)(2,1)S(1)}, bf16[192,256]{1,0:T(8,128)(2,1)S(1)}, u32[]{:S(2)}, u32[]{:S(2)}) collective-permute-start(bf16[192,256]{1,0:T(8,128)(2,1)S(1)} %copy-done), channel_id=1, source_target_pairs={{0,8},{8,0},{1,9},{9,1},{2,10},{10,2},{3,11},{11,3},{4,12},{12,4},... | collective-permute-start | bytes 294920 | tf_op jit(solution)/shard_map/ppermute | solution.py:187
  12.7 10.8 %collective-permute-start.3 = (bf16[2,192,256]{2,1,0:T(8,128)(2,1)S(1)}, bf16[2,192,256]{2,1,0:T(8,128)(2,1)S(1)}, u32[]{:S(2)}, u32[]{:S(2)}) collective-permute-start(bf16[2,192,256]{2,1,0:T(8,128)(2,1)S(1)} %pad_maximum_fusion.refs_0_), channel_id=1, source_target_pairs={{0,32},{8,104},{16,48},{24,120},{32,64},{40,8},{48,80},{56,24},{64... | collective-permute-start | bytes 589832 | tf_op jit(solution)/shard_map/ppermute | solution.py:194
  18.8 8.9 %collective-permute-start.1 = (bf16[2,192,256]{2,1,0:T(8,128)(2,1)S(1)}, bf16[2,192,256]{2,1,0:T(8,128)(2,1)S(1)}, u32[]{:S(2)}, u32[]{:S(2)}) collective-permute-start(bf16[2,192,256]{2,1,0:T(8,128)(2,1)S(1)} %pad_maximum_fusion.refs_0_), channel_id=1, source_target_pairs={{0,16},{8,120},{16,32},{24,8},{32,48},{40,24},{48,64},{56,40},{64,... | collective-permute-start | bytes 589832 | tf_op jit(solution)/shard_map/ppermute | solution.py:194
  23.6 5.0 %collective-permute-start.5 = (bf16[2,192,256]{2,1,0:T(8,128)(2,1)S(1)}, bf16[2,192,256]{2,1,0:T(8,128)(2,1)S(1)}, u32[]{:S(2)}, u32[]{:S(2)}) collective-permute-start(bf16[2,192,256]{2,1,0:T(8,128)(2,1)S(1)} %collective-permute-done.3.refs_3_), channel_id=1, source_target_pairs={{0,16},{8,120},{16,32},{24,8},{32,48},{40,24},{48,64},{56,40},{64,... | collective-permute-start | bytes 589832 | tf_op jit(solution)/shard_map/ppermute | solution.py:194
  25.9 5.9 %collective-permute-start.7 = (bf16[192,256]{1,0:T(8,128)(2,1)S(1)}, bf16[192,256]{1,0:T(8,128)(2,1)S(1)}, u32[]{:S(2)}, u32[]{:S(2)}) collective-permute-start(bf16[192,256]{1,0:T(8,128)(2,1)S(1)} %slice_bitcast_fusion), channel_id=1, source_target_pairs={{0,32},{8,104},{16,48},{24,120},{32,64},{40,8},{48,80},{56,24},{64... | collective-permute-start | bytes 294920 | tf_op jit(solution)/shard_map/ppermute | solution.py:194
  27.8 7.4 %collective-permute-start.4 = (bf16[2,192,256]{2,1,0:T(8,128)(2,1)S(1)}, bf16[2,192,256]{2,1,0:T(8,128)(2,1)S(1)}, u32[]{:S(2)}, u32[]{:S(2)}) collective-permute-start(bf16[2,192,256]{2,1,0:T(8,128)(2,1)S(1)} %collective-permute-done.3.refs_3_), channel_id=1, source_target_pairs={{0,8},{8,0},{1,9},{9,1},{2,10},{10,2},{3,11},{11,3},{4,12},{12,4},... | collective-permute-start | bytes 589832 | tf_op jit(solution)/shard_map/ppermute | solution.py:187
  27.8 7.4 %collective-permute-start.2 = (bf16[2,192,256]{2,1,0:T(8,128)(2,1)S(1)}, bf16[2,192,256]{2,1,0:T(8,128)(2,1)S(1)}, u32[]{:S(2)}, u32[]{:S(2)}) collective-permute-start(bf16[2,192,256]{2,1,0:T(8,128)(2,1)S(1)} %collective-permute-done.1.refs_1_), channel_id=1, source_target_pairs={{0,8},{8,0},{1,9},{9,1},{2,10},{10,2},{3,11},{11,3},{4,12},{12,4},... | collective-permute-start | bytes 589832 | tf_op jit(solution)/shard_map/ppermute | solution.py:187
  28.5 6.6 %collective-permute-start.6 = (bf16[2,192,256]{2,1,0:T(8,128)(2,1)S(1)}, bf16[2,192,256]{2,1,0:T(8,128)(2,1)S(1)}, u32[]{:S(2)}, u32[]{:S(2)}) collective-permute-start(bf16[2,192,256]{2,1,0:T(8,128)(2,1)S(1)} %collective-permute-done.5.refs_5_), channel_id=1, source_target_pairs={{0,8},{8,0},{1,9},{9,1},{2,10},{10,2},{3,11},{11,3},{4,12},{12,4},... | collective-permute-start | bytes 589832 | tf_op jit(solution)/shard_map/ppermute | solution.py:187
  31.8 3.3 %collective-permute-start.8 = (bf16[192,256]{1,0:T(8,128)(2,1)S(1)}, bf16[192,256]{1,0:T(8,128)(2,1)S(1)}, u32[]{:S(2)}, u32[]{:S(2)}) collective-permute-start(bf16[192,256]{1,0:T(8,128)(2,1)S(1)} %collective-permute-done.7.refs_7_), channel_id=1, source_target_pairs={{0,8},{8,0},{1,9},{9,1},{2,10},{10,2},{3,11},{11,3},{4,12},{12,4},... | collective-permute-start | bytes 294920 | tf_op jit(solution)/shard_map/ppermute | solution.py:187
  53.7 12.6 %all-to-all-start.1 = ((f32[16,16,256]{2,1,0:T(8,128)}), f32[16,16,256]{2,1,0:T(8,128)S(1)}, u32[]{:S(2)}, u32[]{:S(2)}) async-start(f32[16,16,256]{2,1,0:T(8,128)} %get-tuple-element.15), calls=%async_computation.1 | async-start | bytes 524288 | tf_op jit(solution)/shard_map/all_to_all | solution.py:179
  89.9 2.9 %collective-permute-start.9 = (f32[8,16,256]{2,1,0:T(8,128)S(1)}, f32[8,16,256]{2,1,0:T(8,128)S(1)}, u32[]{:S(2)}, u32[]{:S(2)}) collective-permute-start(f32[8,16,256]{2,1,0:T(8,128)S(1)} %get-tuple-element.18), channel_id=1, source_target_pairs={{0,8},{8,0},{1,9},{9,1},{2,10},{10,2},{3,11},{11,3},{4,12},{12,4},... | collective-permute-start | bytes 393224 | tf_op jit(solution)/shard_map/ppermute | solution.py:187
  108.7 3.0 %collective-permute-start.10 = (f32[2,128]{1,0:T(2,128)S(1)}, f32[2,128]{1,0:T(2,128)S(1)}, u32[]{:S(2)}, u32[]{:S(2)}) collective-permute-start(f32[2,128]{1,0:T(2,128)S(1)} %get-tuple-element.20), channel_id=1, source_target_pairs={{0,8},{8,0},{1,9},{9,1},{2,10},{10,2},{3,11},{11,3},{4,12},{12,4},... | collective-permute-start | bytes 3080 | tf_op jit(solution)/shard_map/ppermute | solution.py:187

commit v9 on v6

--- a/solution.py
+++ b/solution.py
@@ -215,6 +215,7 @@
     projected, gram = pl.pallas_call(
         project_kernel,
         out_shape=(shape(VEC, SEG), shape(2, 128)),
+        compiler_params=params(8),
         name="project",
     )(product, own)
     gram = jnp.broadcast_to(gram + across(gram), (CHIPS, 2, 128))
@@ -222,6 +223,7 @@
     basis, triangle = pl.pallas_call(
         finish_kernel,
         out_shape=(shape(VEC, SEG), shape(VEC, VEC)),
+        compiler_params=params(8),
         name="finish",
     )(gram, projected)
     return basis.T, triangle

time: 123 us -> 119 us (0.967)
  Pallas kernels: 34.9 us -> 32.5 us
    pallas_call x1, Pallas kernels: 1.8 us -> 0.31 us  [per_device(): pl.pallas_call(project_kernel, out_shape=(shape(VEC, SEG), shape(2, 128))...]
where the time goes in v9:
time: 119 us
  starting transfers between devices  34.1 us (29%)
  blocking collectives  32.6 us (27%)
  Pallas kernels  32.5 us (27%)
  waiting for transfers between devices  18.5 us (16%)
    all_to_all x2, blocking collectives, to_all(): return lax.all_to_all(copies, axes, split_axis=0, concat_axis=0, tiled=True)  32.6 us
    pallas_call x1, Pallas kernels, per_device(): pl.pallas_call(affinity_kernel, grid=(NC // 2,), out_shape=(shape(NC, NR...  15.4 us
    pallas_call x1, Pallas kernels, per_device(): pl.pallas_call(apply_kernel, out_shape=(shape(HALF, VEC, SEG), shape(HALF...  12.1 us
    all_to_all x2, starting transfers between devices, to_all(): return lax.all_to_all(copies, axes, split_axis=0, concat_axis=0, tiled=True)  12.1 us
    ppermute x4, starting transfers between devices, along(): return lax.ppermute(a, ROWS, turns)  11 us
    ppermute x7, starting transfers between devices, across(): return lax.ppermute(a, 'core', [(0, 1), (1, 0)])  11 us
    all_to_all x2, waiting for transfers between devices, to_all(): return lax.all_to_all(copies, axes, split_axis=0, concat_axis=0, tiled=True)  10.2 us
    ppermute x4, waiting for transfers between devices, along(): return lax.ppermute(a, ROWS, turns)  4.65 us
  transfers between devices with their start and end apart: 13, of which 9 were waited for; matrix products, arithmetic and copies ran while one was open for 0% of the time, Pallas kernels for 0%

profile of v9, /device:TPU:1, one launch (start us, length us, event | category | flops | bytes accessed | tf_op | source)
XLA Modules:
  0.0 118.6 jit_solution(5475771381247087788)
XLA Ops:
  0.6 2.3 %unit.1 = (bf16[192,256]{1,0:T(8,128)(2,1)}, bf16[16,224,256]{2,1,0:T(8,128)(2,1)}) custom-call(bf16[192,256]{1,0:T(8,128)(2,1)} %bitcast.10, f32[16,256]{1,0:T(8,128)} %bitcast.13), custom_call_target="tpu_custom_call" | custom-call | tf_op jit(solution)/shard_map/unit/pallas_call | solution.py:177
  2.9 0.0 copy-start
  2.9 7.7 %all-to-all-start = ((bf16[16,224,256]{2,1,0:T(8,128)(2,1)}), bf16[16,224,256]{2,1,0:T(8,128)(2,1)S(1)}, u32[]{:S(2)}, u32[]{:S(2)}) async-start(bf16[16,224,256]{2,1,0:T(8,128)(2,1)} %get-tuple-element.13), calls=%async_computation | async-start | bytes 3670016 | tf_op jit(solution)/shard_map/all_to_all | solution.py:156
  10.7 0.0 copy-done
  10.7 1.0 collective-permute-start
  11.7 0.9 collective-permute-done
  12.7 6.1 %collective-permute-start.3 = (bf16[2,192,256]{2,1,0:T(8,128)(2,1)S(1)}, bf16[2,192,256]{2,1,0:T(8,128)(2,1)S(1)}, u32[]{:S(2)}, u32[]{:S(2)}) collective-permute-start(bf16[2,192,256]{2,1,0:T(8,128)(2,1)S(1)} %pad_maximum_fusion.refs_0_), channel_id=1, source_target_pairs={{0,32},{8,104},{16,48},{24,120},{32,64},{40,8},{48,80},{56,24},{64... | collective-permute-start | bytes 589832 | tf_op jit(solution)/shard_map/ppermute | solution.py:171
  18.8 0.7 collective-permute-start.1
  19.5 4.0 %collective-permute-done.3.refs_3_ = bf16[2,192,256]{2,1,0:T(8,128)(2,1)S(1)} collective-permute-done((bf16[2,192,256]{2,1,0:T(8,128)(2,1)S(1)}, bf16[2,192,256]{2,1,0:T(8,128)(2,1)S(1)}, u32[]{:S(2)}, u32[]{:S(2)}) %collective-permute-start.3) | collective-permute-done | bytes 196640 | tf_op jit(solution)/shard_map/ppermute | solution.py:171
  23.5 2.3 %collective-permute-start.5 = (bf16[2,192,256]{2,1,0:T(8,128)(2,1)S(1)}, bf16[2,192,256]{2,1,0:T(8,128)(2,1)S(1)}, u32[]{:S(2)}, u32[]{:S(2)}) collective-permute-start(bf16[2,192,256]{2,1,0:T(8,128)(2,1)S(1)} %collective-permute-done.3.refs_3_), channel_id=1, source_target_pairs={{0,16},{8,120},{16,32},{24,8},{32,48},{40,24},{48,64},{56,40},{64,... | collective-permute-start | bytes 589832 | tf_op jit(solution)/shard_map/ppermute | solution.py:171
  25.8 1.9 %collective-permute-start.7 = (bf16[192,256]{1,0:T(8,128)(2,1)S(1)}, bf16[192,256]{1,0:T(8,128)(2,1)S(1)}, u32[]{:S(2)}, u32[]{:S(2)}) collective-permute-start(bf16[192,256]{1,0:T(8,128)(2,1)S(1)} %slice_bitcast_fusion), channel_id=1, source_target_pairs={{0,32},{8,104},{16,48},{24,120},{32,64},{40,8},{48,80},{56,24},{64... | collective-permute-start | bytes 294920 | tf_op jit(solution)/shard_map/ppermute | solution.py:171
  27.7 0.0 collective-permute-start.4
  27.7 0.0 collective-permute-done.1.refs_1_
  27.7 0.5 collective-permute-start.2
  28.2 0.1 collective-permute-done.5.refs_5_
  28.4 2.7 %collective-permute-start.6 = (bf16[2,192,256]{2,1,0:T(8,128)(2,1)S(1)}, bf16[2,192,256]{2,1,0:T(8,128)(2,1)S(1)}, u32[]{:S(2)}, u32[]{:S(2)}) collective-permute-start(bf16[2,192,256]{2,1,0:T(8,128)(2,1)S(1)} %collective-permute-done.5.refs_5_), channel_id=1, source_target_pairs={{0,8},{8,0},{1,9},{9,1},{2,10},{10,2},{3,11},{11,3},{4,12},{12,4},... | collective-permute-start | bytes 589832 | tf_op jit(solution)/shard_map/ppermute | solution.py:164
  31.0 0.5 collective-permute-done.7.refs_7_
  31.6 2.6 %collective-permute-start.8 = (bf16[192,256]{1,0:T(8,128)(2,1)S(1)}, bf16[192,256]{1,0:T(8,128)(2,1)S(1)}, u32[]{:S(2)}, u32[]{:S(2)}) collective-permute-start(bf16[192,256]{1,0:T(8,128)(2,1)S(1)} %collective-permute-done.7.refs_7_), channel_id=1, source_target_pairs={{0,8},{8,0},{1,9},{9,1},{2,10},{10,2},{3,11},{11,3},{4,12},{12,4},... | collective-permute-start | bytes 294920 | tf_op jit(solution)/shard_map/ppermute | solution.py:164
  34.2 0.1 pad_add_fusion.1.pos_ref
  34.2 0.9 collective-permute-done.8.refs_8_
  35.1 0.0 collective-permute-done.4.refs_4_
  35.1 0.0 collective-permute-done.2.refs_2_
  35.1 0.0 collective-permute-done.6.refs_6_
  35.1 2.6 %all-to-all-done.t_ref = bf16[16,224,256]{2,1,0:T(8,128)(2,1)S(1)} async-done(((bf16[16,224,256]{2,1,0:T(8,128)(2,1)}), bf16[16,224,256]{2,1,0:T(8,128)(2,1)S(1)}, u32[]{:S(2)}, u32[]{:S(2)}) %all-to-all-start) | async-done | bytes 1835040 | tf_op jit(solution)/shard_map/all_to_all | solution.py:156
  37.8 15.4 %affinity.1 = (bf16[16,4096,256]{2,1,0:T(8,128)(2,1)}, f32[16,16,256]{2,1,0:T(8,128)}) custom-call(s32[2]{0:T(128)S(1)} %pad_add_fusion.1.pos_ref, bf16[16,224,256]{2,1,0:T(8,128)(2,1)S(1)} %all-to-all-done.t_ref, bf16[2,192,256]{2,1,0:T(8,128)(2,1)S(1)} %pad_maximum_fusion.refs_0_, bf16[2,192,256]{2,1,0:T(8,128)(2,1)S(1)} %collective-permute-done.1.refs_1_, ...), custom_call_target="tpu_custom_call" | custom-call | flops 8589934592 | bytes 33554432 | tf_op jit(solution)/shard_map/affinity/pallas_call | solution.py:187
  53.2 4.4 %all-to-all-start.1 = ((f32[16,16,256]{2,1,0:T(8,128)}), f32[16,16,256]{2,1,0:T(8,128)S(1)}, u32[]{:S(2)}, u32[]{:S(2)}) async-start(f32[16,16,256]{2,1,0:T(8,128)} %get-tuple-element.15), calls=%async_computation.1 | async-start | bytes 524288 | tf_op jit(solution)/shard_map/all_to_all | solution.py:156
  57.6 0.1 pad_add_fusion.pos_ref
  57.6 7.6 %all-to-all-done.1.deg_ref = f32[16,16,256]{2,1,0:T(8,128)S(1)} async-done(((f32[16,16,256]{2,1,0:T(8,128)}), f32[16,16,256]{2,1,0:T(8,128)S(1)}, u32[]{:S(2)}, u32[]{:S(2)}) %all-to-all-start.1) | async-done | bytes 262176 | tf_op jit(solution)/shard_map/all_to_all | solution.py:156
  65.3 12.1 %apply.1 = (f32[8,16,256]{2,1,0:T(8,128)S(1)}, f32[8,16,256]{2,1,0:T(8,128)S(1)}, f32[1,256]{1,0:T(1,128)S(1)}) custom-call(s32[2]{0:T(128)S(1)} %pad_add_fusion.pos_ref, f32[16,16,256]{2,1,0:T(8,128)S(1)} %all-to-all-done.1.deg_ref, bf16[16,224,256]{2,1,0:T(8,128)(2,1)S(1)} %all-to-all-done.t_ref, bf16[16,4096,256]{2,1,0:T(8,128)(2,1)} %get-tuple-element.16.b_ref), custom_call_target="tpu_custom_call" | custom-call | tf_op jit(solution)/shard_map/apply/pallas_call | solution.py:201
  77.4 2.1 %collective-permute-start.9 = (f32[8,16,256]{2,1,0:T(8,128)S(1)}, f32[8,16,256]{2,1,0:T(8,128)S(1)}, u32[]{:S(2)}, u32[]{:S(2)}) collective-permute-start(f32[8,16,256]{2,1,0:T(8,128)S(1)} %get-tuple-element.18), channel_id=1, source_target_pairs={{0,8},{8,0},{1,9},{9,1},{2,10},{10,2},{3,11},{11,3},{4,12},{12,4},... | collective-permute-start | bytes 393224 | tf_op jit(solution)/shard_map/ppermute | solution.py:164
  79.4 1.0 collective-permute-done.9
  80.4 15.9 %all_to_all.20.p_ref = f32[8,16,256]{2,1,0:T(8,128)S(1)} all-to-all(f32[8,16,256]{2,1,0:T(8,128)S(1)} %add.14), channel_id=1, replica_groups=mesh['xl'=2,'z'=8,'core'=2,'y'=4,'xh'=2] {'z'}, dimensions={0} | all-to-all | bytes 262144 | tf_op jit(solution)/shard_map/all_to_all | solution.py:156
  96.3 0.3 project.1
  96.6 2.1 %collective-permute-start.10 = (f32[2,128]{1,0:T(2,128)S(1)}, f32[2,128]{1,0:T(2,128)S(1)}, u32[]{:S(2)}, u32[]{:S(2)}) collective-permute-start(f32[2,128]{1,0:T(2,128)S(1)} %get-tuple-element.20), channel_id=1, source_target_pairs={{0,8},{8,0},{1,9},{9,1},{2,10},{10,2},{3,11},{11,3},{4,12},{12,4},... | collective-permute-start | bytes 3080 | tf_op jit(solution)/shard_map/ppermute | solution.py:164
  98.8 0.8 collective-permute-done.10
  99.6 16.7 %all_to_all.21.gram_ref = f32[128,2,128]{2,1,0:T(2,128)S(1)} all-to-all(f32[128,2,128]{2,1,0:T(2,128)S(1)} %broadcast_in_dim.3), channel_id=1, replica_groups=mesh['xl'=2,'z'=8,'core'=2,'y'=4,'xh'=2] {'xl','z','y','xh'}, dimensions={0} | all-to-all | bytes 262144 | tf_op jit(solution)/shard_map/all_to_all | solution.py:156
  116.3 2.3 %finish.1 = (f32[16,256]{1,0:T(8,128)}, f32[16,16]{1,0:T(8,128)}) custom-call(f32[128,2,128]{2,1,0:T(2,128)S(1)} %all_to_all.21.gram_ref, f32[16,256]{1,0:T(8,128)S(1)} %get-tuple-element.21.q_ref), custom_call_target="tpu_custom_call" | custom-call | tf_op jit(solution)/shard_map/finish/pallas_call | solution.py:223
  (5 shorter events, 0.1 us)
Async XLA Ops:
  2.9 7.7 %copy-start = (bf16[192,256]{1,0:T(8,128)(2,1)S(1)}, bf16[192,256]{1,0:T(8,128)(2,1)}, u32[]{:S(2)}) copy-start(bf16[192,256]{1,0:T(8,128)(2,1)} %get-tuple-element.14) | copy-start | bytes 294916
  2.9 34.8 %all-to-all-start = ((bf16[16,224,256]{2,1,0:T(8,128)(2,1)}), bf16[16,224,256]{2,1,0:T(8,128)(2,1)S(1)}, u32[]{:S(2)}, u32[]{:S(2)}) async-start(bf16[16,224,256]{2,1,0:T(8,128)(2,1)} %get-tuple-element.13), calls=%async_computation | async-start | bytes 3670016 | tf_op jit(solution)/shard_map/all_to_all | solution.py:156
  10.7 2.0 %collective-permute-start = (bf16[192,256]{1,0:T(8,128)(2,1)S(1)}, bf16[192,256]{1,0:T(8,128)(2,1)S(1)}, u32[]{:S(2)}, u32[]{:S(2)}) collective-permute-start(bf16[192,256]{1,0:T(8,128)(2,1)S(1)} %copy-done), channel_id=1, source_target_pairs={{0,8},{8,0},{1,9},{9,1},{2,10},{10,2},{3,11},{11,3},{4,12},{12,4},... | collective-permute-start | bytes 294920 | tf_op jit(solution)/shard_map/ppermute | solution.py:164
  12.7 10.8 %collective-permute-start.3 = (bf16[2,192,256]{2,1,0:T(8,128)(2,1)S(1)}, bf16[2,192,256]{2,1,0:T(8,128)(2,1)S(1)}, u32[]{:S(2)}, u32[]{:S(2)}) collective-permute-start(bf16[2,192,256]{2,1,0:T(8,128)(2,1)S(1)} %pad_maximum_fusion.refs_0_), channel_id=1, source_target_pairs={{0,32},{8,104},{16,48},{24,120},{32,64},{40,8},{48,80},{56,24},{64... | collective-permute-start | bytes 589832 | tf_op jit(solution)/shard_map/ppermute | solution.py:171
  18.8 8.9 %collective-permute-start.1 = (bf16[2,192,256]{2,1,0:T(8,128)(2,1)S(1)}, bf16[2,192,256]{2,1,0:T(8,128)(2,1)S(1)}, u32[]{:S(2)}, u32[]{:S(2)}) collective-permute-start(bf16[2,192,256]{2,1,0:T(8,128)(2,1)S(1)} %pad_maximum_fusion.refs_0_), channel_id=1, source_target_pairs={{0,16},{8,120},{16,32},{24,8},{32,48},{40,24},{48,64},{56,40},{64,... | collective-permute-start | bytes 589832 | tf_op jit(solution)/shard_map/ppermute | solution.py:171
  23.5 4.9 %collective-permute-start.5 = (bf16[2,192,256]{2,1,0:T(8,128)(2,1)S(1)}, bf16[2,192,256]{2,1,0:T(8,128)(2,1)S(1)}, u32[]{:S(2)}, u32[]{:S(2)}) collective-permute-start(bf16[2,192,256]{2,1,0:T(8,128)(2,1)S(1)} %collective-permute-done.3.refs_3_), channel_id=1, source_target_pairs={{0,16},{8,120},{16,32},{24,8},{32,48},{40,24},{48,64},{56,40},{64,... | collective-permute-start | bytes 589832 | tf_op jit(solution)/shard_map/ppermute | solution.py:171
  25.8 5.8 %collective-permute-start.7 = (bf16[192,256]{1,0:T(8,128)(2,1)S(1)}, bf16[192,256]{1,0:T(8,128)(2,1)S(1)}, u32[]{:S(2)}, u32[]{:S(2)}) collective-permute-start(bf16[192,256]{1,0:T(8,128)(2,1)S(1)} %slice_bitcast_fusion), channel_id=1, source_target_pairs={{0,32},{8,104},{16,48},{24,120},{32,64},{40,8},{48,80},{56,24},{64... | collective-permute-start | bytes 294920 | tf_op jit(solution)/shard_map/ppermute | solution.py:171
  27.7 7.4 %collective-permute-start.4 = (bf16[2,192,256]{2,1,0:T(8,128)(2,1)S(1)}, bf16[2,192,256]{2,1,0:T(8,128)(2,1)S(1)}, u32[]{:S(2)}, u32[]{:S(2)}) collective-permute-start(bf16[2,192,256]{2,1,0:T(8,128)(2,1)S(1)} %collective-permute-done.3.refs_3_), channel_id=1, source_target_pairs={{0,8},{8,0},{1,9},{9,1},{2,10},{10,2},{3,11},{11,3},{4,12},{12,4},... | collective-permute-start | bytes 589832 | tf_op jit(solution)/shard_map/ppermute | solution.py:164
  27.7 7.4 %collective-permute-start.2 = (bf16[2,192,256]{2,1,0:T(8,128)(2,1)S(1)}, bf16[2,192,256]{2,1,0:T(8,128)(2,1)S(1)}, u32[]{:S(2)}, u32[]{:S(2)}) collective-permute-start(bf16[2,192,256]{2,1,0:T(8,128)(2,1)S(1)} %collective-permute-done.1.refs_1_), channel_id=1, source_target_pairs={{0,8},{8,0},{1,9},{9,1},{2,10},{10,2},{3,11},{11,3},{4,12},{12,4},... | collective-permute-start | bytes 589832 | tf_op jit(solution)/shard_map/ppermute | solution.py:164
  28.4 6.7 %collective-permute-start.6 = (bf16[2,192,256]{2,1,0:T(8,128)(2,1)S(1)}, bf16[2,192,256]{2,1,0:T(8,128)(2,1)S(1)}, u32[]{:S(2)}, u32[]{:S(2)}) collective-permute-start(bf16[2,192,256]{2,1,0:T(8,128)(2,1)S(1)} %collective-permute-done.5.refs_5_), channel_id=1, source_target_pairs={{0,8},{8,0},{1,9},{9,1},{2,10},{10,2},{3,11},{11,3},{4,12},{12,4},... | collective-permute-start | bytes 589832 | tf_op jit(solution)/shard_map/ppermute | solution.py:164
  31.6 3.5 %collective-permute-start.8 = (bf16[192,256]{1,0:T(8,128)(2,1)S(1)}, bf16[192,256]{1,0:T(8,128)(2,1)S(1)}, u32[]{:S(2)}, u32[]{:S(2)}) collective-permute-start(bf16[192,256]{1,0:T(8,128)(2,1)S(1)} %collective-permute-done.7.refs_7_), channel_id=1, source_target_pairs={{0,8},{8,0},{1,9},{9,1},{2,10},{10,2},{3,11},{11,3},{4,12},{12,4},... | collective-permute-start | bytes 294920 | tf_op jit(solution)/shard_map/ppermute | solution.py:164
  53.2 12.0 %all-to-all-start.1 = ((f32[16,16,256]{2,1,0:T(8,128)}), f32[16,16,256]{2,1,0:T(8,128)S(1)}, u32[]{:S(2)}, u32[]{:S(2)}) async-start(f32[16,16,256]{2,1,0:T(8,128)} %get-tuple-element.15), calls=%async_computation.1 | async-start | bytes 524288 | tf_op jit(solution)/shard_map/all_to_all | solution.py:156
  77.4 3.1 %collective-permute-start.9 = (f32[8,16,256]{2,1,0:T(8,128)S(1)}, f32[8,16,256]{2,1,0:T(8,128)S(1)}, u32[]{:S(2)}, u32[]{:S(2)}) collective-permute-start(f32[8,16,256]{2,1,0:T(8,128)S(1)} %get-tuple-element.18), channel_id=1, source_target_pairs={{0,8},{8,0},{1,9},{9,1},{2,10},{10,2},{3,11},{11,3},{4,12},{12,4},... | collective-permute-start | bytes 393224 | tf_op jit(solution)/shard_map/ppermute | solution.py:164
  96.6 3.0 %collective-permute-start.10 = (f32[2,128]{1,0:T(2,128)S(1)}, f32[2,128]{1,0:T(2,128)S(1)}, u32[]{:S(2)}, u32[]{:S(2)}) collective-permute-start(f32[2,128]{1,0:T(2,128)S(1)} %get-tuple-element.20), channel_id=1, source_target_pairs={{0,8},{8,0},{1,9},{9,1},{2,10},{10,2},{3,11},{11,3},{4,12},{12,4},... | collective-permute-start | bytes 3080 | tf_op jit(solution)/shard_map/ppermute | solution.py:164

commit v10 on v9

--- a/solution.py
+++ b/solution.py
@@ -18,7 +18,6 @@
 DIM = 192
 VEC = 16
 WIDE = DIM + 2 * VEC
-DEPTH = 6
 SCALE = 14.426950408889634
 UNSCALE = 4.5399929762484854e-05
 EPS = 1e-6
@@ -60,7 +59,7 @@
 def affinity_kernel(pos_ref, t_ref, *refs):
     pairs, lone = refs[0:7], refs[7:9]
     b_ref, deg_ref, s_ref = refs[9:12]
-    z, core = pos_ref[0], pos_ref[1]
+    z, core = pos_ref[2], pos_ref[0]
     step = pl.program_id(0)
 
     def place(chip, side, rows):
@@ -86,33 +85,23 @@
             score = jnp.dot(s_ref[r], piece, preferred_element_type=F32)
             tile = jnp.exp2(score * SCALE)
             total = total + jnp.sum(tile.reshape(SEG // 8, 8, SEG), axis=0)
-            b_ref[j, r * SEG : (r + 1) * SEG, :] = tile.astype(BF16)
+            b_ref[step * 2 + j, r * SEG : (r + 1) * SEG, :] = tile.astype(BF16)
         sums = jnp.sum(total, axis=0, keepdims=True) * UNSCALE
-        for k in range(NC):
-            deg_ref[k, pl.ds(step * 2 + j, 1), :] = sums
-
-
-def apply_kernel(pos_ref, deg_ref, t_ref, b_ref, mine_ref, other_ref, own_ref, root_ref, held_ref, sem_ref):
-    def fetch(t):
-        slot = t % DEPTH
-        return pltpu.make_async_copy(b_ref.at[t], held_ref.at[slot], sem_ref.at[slot])
-
-    for t in range(DEPTH):
-        fetch(t).start()
-    root_ref[...] = lax.rsqrt(jnp.sum(deg_ref[...], axis=0))
+        deg_ref[pl.ds(step * 2 + j, 1), :] = sums
+
+
+def apply_kernel(pos_ref, d0_ref, d1_ref, d2_ref, d3_ref, t_ref, b_ref, mine_ref, other_ref, own_ref, root_ref):
+    root_ref[...] = lax.rsqrt((d0_ref[...] + d2_ref[...]) + (d1_ref[...] + d3_ref[...]))
     core = pos_ref[0]
     own_ref[...] = root_ref[pl.ds(pos_ref[1], 1), :] * UNSCALE
     for t in range(NC):
         v = t_ref[t, DIM : DIM + VEC, :].astype(F32) + t_ref[t, DIM + VEC : WIDE, :].astype(F32)
         w = (v * root_ref[t : t + 1, :]).astype(BF16)
-        fetch(t).wait()
         for r in range(NR // 2):
             for side, p_ref in ((core, mine_ref), (1 - core, other_ref)):
                 rows = pl.ds(pl.multiple_of((r * 2 + side) * SEG, SEG), SEG)
-                part = nt(w, held_ref[t % DEPTH, rows, :])
+                part = nt(w, b_ref[t, rows, :])
                 p_ref[r] = part if t == 0 else p_ref[r] + part
-        if t + DEPTH < NC:
-            fetch(t + DEPTH).start()
 
 
 def project_kernel(p_ref, own_ref, q_ref, gram_ref):
@@ -171,9 +160,19 @@
     return lax.ppermute(a, ROWS, turns)
 
 
+def ring_copies(a, axes, crossed):
+    def place(k):
+        return k % 4 % 2 * 2 + k % 4 // 2 if crossed else k % 4
+
+    turned = [
+        lax.ppermute(a, axes, [(place(k), place(k + hops)) for k in range(4)]) for hops in (1, 2, 3)
+    ]
+    return [a, *turned]
+
+
 def per_device(embeddings, vectors):
     z, core = lax.axis_index("z"), lax.axis_index("core")
-    column = lax.axis_index(COLS)
+    position = jnp.stack([core, lax.axis_index(COLS), z])
     unit, unit_copies = pl.pallas_call(
         unit_kernel,
         out_shape=(shape(DIM, SEG, dtype=BF16), shape(NC, WIDE, SEG, dtype=BF16)),
@@ -187,30 +186,29 @@
     block, degree = pl.pallas_call(
         affinity_kernel,
         grid=(NC // 2,),
-        out_shape=(shape(NC, NR * SEG, SEG, dtype=BF16), shape(NC, NC, SEG)),
+        out_shape=(pltpu.VMEM((NC, NR * SEG, SEG), BF16), shape(NC, SEG)),
         in_specs=[smem()] + [vmem()] * 10,
-        out_specs=(pl.BlockSpec((2, NR * SEG, SEG), lambda i: (i, 0, 0)), vmem()),
+        out_specs=(vmem(), vmem()),
         scratch_shapes=[pltpu.VMEM((NR, SEG, DIM), BF16)],
-        compiler_params=params(32),
+        compiler_params=params(24),
         cost_estimate=pl.CostEstimate(
             flops=2 * 256 * 4096 * 4096, transcendentals=4096 * 4096, bytes_accessed=1 << 25
         ),
         name="affinity",
-    )(jnp.stack([z, core]), columns, *pairs, four, across(four))
-    degree = to_all(degree, COLS)
+    )(position, columns, *pairs, four, across(four))
+    degree = sum(ring_copies(degree, "y", False))
+    degrees = ring_copies(degree, ("xl", "xh"), True)
     mine, other, own = pl.pallas_call(
         apply_kernel,
         out_shape=(shape(HALF, VEC, SEG), shape(HALF, VEC, SEG), shape(1, SEG)),
-        in_specs=[smem(), vmem(), vmem(), pl.BlockSpec(memory_space=pl.ANY)],
+        in_specs=[smem()] + [vmem()] * 6,
         out_specs=(vmem(), vmem(), vmem()),
         scratch_shapes=[
             pltpu.VMEM((NC, SEG), F32),
-            pltpu.VMEM((DEPTH, NR * SEG, SEG), BF16),
-            pltpu.SemaphoreType.DMA((DEPTH,)),
         ],
-        compiler_params=params(44),
+        compiler_params=params(24),
         name="apply",
-    )(jnp.stack([core, column]), degree, columns, block)
+    )(position, *degrees, columns, pltpu.with_memory_space_constraint(block, pltpu.VMEM))
     product = to_all(mine + across(other), "z")
     projected, gram = pl.pallas_call(
         project_kernel,

time: 119 us -> 123 us (1.034)
  starting transfers between devices: 34.1 us -> 37.3 us
  Pallas kernels: 32.5 us -> 29.5 us
  local copies, waits for them, and re-layouts: 0.05 us -> 2.61 us
  other arithmetic: 0.19 us -> 2.32 us
    all_to_all x2 -> x1, waiting for transfers between devices: 10.2 us -> 2.59 us  [to_all(): return lax.all_to_all(copies, axes, split_axis=0, concat_axis=0, tiled=True)]
    ppermute x0 -> x6, waiting for transfers between devices: none -> 6.86 us  [ring_copies(): lax.ppermute(a, axes, [(place(k), place(k + hops)) for k in range(4)])]
    ppermute x0 -> x6, starting transfers between devices: none -> 5.56 us  [ring_copies(): lax.ppermute(a, axes, [(place(k), place(k + hops)) for k in range(4)])]
    all_to_all x2 -> x1, starting transfers between devices: 12.1 us -> 7.72 us  [to_all(): return lax.all_to_all(copies, axes, split_axis=0, concat_axis=0, tiled=True)]
    unnamed x2 -> x32, local copies, waits for them, and re-layouts: 0.01 us -> 2.56 us
    ppermute x7, starting transfers between devices: 11 us -> 13 us  [across(): return lax.ppermute(a, 'core', [(0, 1), (1, 0)])]
    pallas_call x1, Pallas kernels: 15.4 us -> 13.6 us  [per_device(): pl.pallas_call(affinity_kernel, grid=(NC // 2,), out_shape=(pltpu.VMEM((N...]
  transfers between devices with their start and end apart: 13 -> 18, of which waited for: 9 -> 13; matrix products, arithmetic and copies ran while one was open for 0% -> 1% of each run, Pallas kernels for 0% -> 0%
where the time goes in v10:
time: 123 us; the launch traced here: 122 us
  starting transfers between devices  37.3 us (30%)
  blocking collectives  32.4 us (26%)
  Pallas kernels  29.5 us (24%)
  waiting for transfers between devices  17.4 us (14%)
  local copies, waits for them, and re-layouts  2.61 us (2%)
  other arithmetic  2.32 us (2%)
    all_to_all x2, blocking collectives, to_all(): return lax.all_to_all(copies, axes, split_axis=0, concat_axis=0, tiled=True)  32.4 us
    pallas_call x1, Pallas kernels, per_device(): pl.pallas_call(affinity_kernel, grid=(NC // 2,), out_shape=(pltpu.VMEM((N...  13.6 us
    ppermute x7, starting transfers between devices, across(): return lax.ppermute(a, 'core', [(0, 1), (1, 0)])  13 us
    pallas_call x1, Pallas kernels, per_device(): pl.pallas_call(apply_kernel, out_shape=(shape(HALF, VEC, SEG), shape(HALF...  11 us
    ppermute x4, starting transfers between devices, along(): return lax.ppermute(a, ROWS, turns)  11 us
    all_to_all x1, starting transfers between devices, to_all(): return lax.all_to_all(copies, axes, split_axis=0, concat_axis=0, tiled=True)  7.72 us
    ppermute x6, waiting for transfers between devices, ring_copies(): lax.ppermute(a, axes, [(place(k), place(k + hops)) for k in range(4)])  6.86 us
    ppermute x6, starting transfers between devices, ring_copies(): lax.ppermute(a, axes, [(place(k), place(k + hops)) for k in range(4)])  5.56 us
  transfers between devices with their start and end apart: 18, of which 13 were waited for; matrix products, arithmetic and copies ran while one was open for 1% of the time, Pallas kernels for 0%

profile of v10, /device:TPU:1, one launch (start us, length us, event | category | flops | bytes accessed | tf_op | source)
XLA Modules:
  0.0 122.4 jit_solution(10871658602462018559)
XLA Ops:
  0.6 2.3 %unit.1 = (bf16[192,256]{1,0:T(8,128)(2,1)}, bf16[16,224,256]{2,1,0:T(8,128)(2,1)}) custom-call(bf16[192,256]{1,0:T(8,128)(2,1)} %bitcast.10, f32[16,256]{1,0:T(8,128)} %bitcast.13), custom_call_target="tpu_custom_call" | custom-call | tf_op jit(solution)/shard_map/unit/pallas_call | solution.py:176
  2.9 7.7 %all-to-all-start = ((bf16[16,224,256]{2,1,0:T(8,128)(2,1)}), bf16[16,224,256]{2,1,0:T(8,128)(2,1)S(1)}, u32[]{:S(2)}, u32[]{:S(2)}) async-start(bf16[16,224,256]{2,1,0:T(8,128)(2,1)} %get-tuple-element.13), calls=%async_computation | async-start | bytes 3670016 | tf_op jit(solution)/shard_map/all_to_all | solution.py:145
  10.7 0.0 copy-done.3
  10.7 1.0 collective-permute-start
  11.7 0.9 collective-permute-done
  12.7 0.0 copy-start.2
  12.7 6.1 %collective-permute-start.3 = (bf16[2,192,256]{2,1,0:T(8,128)(2,1)S(1)}, bf16[2,192,256]{2,1,0:T(8,128)(2,1)S(1)}, u32[]{:S(2)}, u32[]{:S(2)}) collective-permute-start(bf16[2,192,256]{2,1,0:T(8,128)(2,1)S(1)} %pad_maximum_fusion.refs_0_), channel_id=1, source_target_pairs={{0,32},{8,104},{16,48},{24,120},{32,64},{40,8},{48,80},{56,24},{64... | collective-permute-start | bytes 589832 | tf_op jit(solution)/shard_map/ppermute | solution.py:160
  18.8 0.7 collective-permute-start.1
  19.5 4.0 %collective-permute-done.3.refs_3_ = bf16[2,192,256]{2,1,0:T(8,128)(2,1)S(1)} collective-permute-done((bf16[2,192,256]{2,1,0:T(8,128)(2,1)S(1)}, bf16[2,192,256]{2,1,0:T(8,128)(2,1)S(1)}, u32[]{:S(2)}, u32[]{:S(2)}) %collective-permute-start.3) | collective-permute-done | bytes 196640 | tf_op jit(solution)/shard_map/ppermute | solution.py:160
  23.5 2.3 %collective-permute-start.5 = (bf16[2,192,256]{2,1,0:T(8,128)(2,1)S(1)}, bf16[2,192,256]{2,1,0:T(8,128)(2,1)S(1)}, u32[]{:S(2)}, u32[]{:S(2)}) collective-permute-start(bf16[2,192,256]{2,1,0:T(8,128)(2,1)S(1)} %collective-permute-done.3.refs_3_), channel_id=1, source_target_pairs={{0,16},{8,120},{16,32},{24,8},{32,48},{40,24},{48,64},{56,40},{64,... | collective-permute-start | bytes 589832 | tf_op jit(solution)/shard_map/ppermute | solution.py:160
  25.8 1.9 %collective-permute-start.7 = (bf16[192,256]{1,0:T(8,128)(2,1)S(1)}, bf16[192,256]{1,0:T(8,128)(2,1)S(1)}, u32[]{:S(2)}, u32[]{:S(2)}) collective-permute-start(bf16[192,256]{1,0:T(8,128)(2,1)S(1)} %slice_bitcast_fusion), channel_id=1, source_target_pairs={{0,32},{8,104},{16,48},{24,120},{32,64},{40,8},{48,80},{56,24},{64... | collective-permute-start | bytes 294920 | tf_op jit(solution)/shard_map/ppermute | solution.py:160
  27.7 0.0 collective-permute-start.4
  27.7 0.0 collective-permute-done.1.refs_1_
  27.7 0.5 collective-permute-start.2
  28.2 0.1 collective-permute-done.5.refs_5_
  28.4 2.7 %collective-permute-start.6 = (bf16[2,192,256]{2,1,0:T(8,128)(2,1)S(1)}, bf16[2,192,256]{2,1,0:T(8,128)(2,1)S(1)}, u32[]{:S(2)}, u32[]{:S(2)}) collective-permute-start(bf16[2,192,256]{2,1,0:T(8,128)(2,1)S(1)} %collective-permute-done.5.refs_5_), channel_id=1, source_target_pairs={{0,8},{8,0},{1,9},{9,1},{2,10},{10,2},{3,11},{11,3},{4,12},{12,4},... | collective-permute-start | bytes 589832 | tf_op jit(solution)/shard_map/ppermute | solution.py:153
  31.1 0.5 collective-permute-done.7.refs_7_
  31.6 2.6 %collective-permute-start.8 = (bf16[192,256]{1,0:T(8,128)(2,1)S(1)}, bf16[192,256]{1,0:T(8,128)(2,1)S(1)}, u32[]{:S(2)}, u32[]{:S(2)}) collective-permute-start(bf16[192,256]{1,0:T(8,128)(2,1)S(1)} %collective-permute-done.7.refs_7_), channel_id=1, source_target_pairs={{0,8},{8,0},{1,9},{9,1},{2,10},{10,2},{3,11},{11,3},{4,12},{12,4},... | collective-permute-start | bytes 294920 | tf_op jit(solution)/shard_map/ppermute | solution.py:153
  34.2 0.7 pad_add_fusion.pos_ref
  34.8 0.3 collective-permute-done.8.refs_8_
  35.1 0.0 collective-permute-done.4.refs_4_
  35.1 0.0 collective-permute-done.2.refs_2_
  35.1 0.0 copy-start.12
  35.1 0.0 collective-permute-done.6.refs_6_
  35.1 0.0 copy-start.13
  35.2 2.6 %all-to-all-done.t_ref = bf16[16,224,256]{2,1,0:T(8,128)(2,1)S(1)} async-done(((bf16[16,224,256]{2,1,0:T(8,128)(2,1)}), bf16[16,224,256]{2,1,0:T(8,128)(2,1)S(1)}, u32[]{:S(2)}, u32[]{:S(2)}) %all-to-all-start) | async-done | bytes 1835040 | tf_op jit(solution)/shard_map/all_to_all | solution.py:145
  37.8 0.0 copy-done.2
  37.8 0.0 copy-done.5
  37.8 0.0 copy-done.9
  37.8 0.0 copy-done.10
  37.8 0.0 copy-done.14
  37.8 0.0 copy-done.15
  37.8 0.0 copy-done.11
  37.8 0.0 copy-done.12
  37.8 0.0 copy-done.13
  37.8 1.2 %copy-done.1 = bf16[16,224,256]{2,1,0:T(8,128)(2,1)} copy-done((bf16[16,224,256]{2,1,0:T(8,128)(2,1)}, bf16[16,224,256]{2,1,0:T(8,128)(2,1)S(1)}, u32[]{:S(2)}) %copy-start.1) | copy-done | bytes 1835032
  39.1 13.6 %affinity.1 = (bf16[16,4096,256]{2,1,0:T(8,128)(2,1)S(1)}, f32[16,256]{1,0:T(8,128)}) custom-call(s32[3]{0:T(128)} %pad_add_fusion.pos_ref, bf16[16,224,256]{2,1,0:T(8,128)(2,1)} %copy-done.1, bf16[2,192,256]{2,1,0:T(8,128)(2,1)} %copy-done.2, bf16[2,192,256]{2,1,0:T(8,128)(2,1)} %copy-done.9, bf16[2,192,256]{2,1,0:T(8,128)(2,1)} %copy-done.12, ...), custom_call_target="tpu_custom_call" | custom-call | flops 8589934592 | bytes 33554432 | tf_op jit(solution)/shard_map/affinity/pallas_call | solution.py:186
  52.6 1.0 collective-permute-start.11
  53.7 1.1 collective-permute-start.10
  54.7 0.4 collective-permute-start.9
  55.1 0.3 collective-permute-done.11
  55.4 2.5 %collective-permute-done.10 = f32[16,256]{1,0:T(8,128)S(1)} collective-permute-done((f32[16,256]{1,0:T(8,128)}, f32[16,256]{1,0:T(8,128)S(1)}, u32[]{:S(2)}, u32[]{:S(2)}) %collective-permute-start.10) | collective-permute-done | bytes 16416 | tf_op jit(solution)/shard_map/ppermute | solution.py:168
  58.0 0.8 collective-permute-done.9
  58.7 0.7 add_add_fusion.d0_ref
  59.5 2.0 %collective-permute-start.14 = (f32[16,256]{1,0:T(8,128)S(1)}, f32[16,256]{1,0:T(8,128)S(1)}, u32[]{:S(2)}, u32[]{:S(2)}) collective-permute-start(f32[16,256]{1,0:T(8,128)S(1)} %add_add_fusion.d0_ref), channel_id=1, source_target_pairs={{0,129},{128,0},{1,128},{129,1},{2,131},{130,2},{3,130},{131,3},{4... | collective-permute-start | bytes 49160 | tf_op jit(solution)/shard_map/ppermute | solution.py:168
  61.4 0.6 collective-permute-start.13
  62.0 0.6 collective-permute-start.12
  62.6 0.0 collective-permute-done.14.d3_ref
  62.6 3.0 %collective-permute-done.13.d2_ref = f32[16,256]{1,0:T(8,128)S(1)} collective-permute-done((f32[16,256]{1,0:T(8,128)S(1)}, f32[16,256]{1,0:T(8,128)S(1)}, u32[]{:S(2)}, u32[]{:S(2)}) %collective-permute-start.13) | collective-permute-done | bytes 16416 | tf_op jit(solution)/shard_map/ppermute | solution.py:168
  65.5 0.3 collective-permute-done.12.d1_ref
  65.8 0.0 copy-done.6
  65.8 0.3 copy-done.7
  66.1 0.3 copy-done.8
  66.4 11.0 %apply.1 = (f32[8,16,256]{2,1,0:T(8,128)}, f32[8,16,256]{2,1,0:T(8,128)}, f32[1,256]{1,0:T(1,128)}) custom-call(s32[3]{0:T(128)} %pad_add_fusion.pos_ref, f32[16,256]{1,0:T(8,128)} %copy-done.4, f32[16,256]{1,0:T(8,128)} %copy-done.8, f32[16,256]{1,0:T(8,128)} %copy-done.7, f32[16,256]{1,0:T(8,128)} %copy-done.6, bf16[16,224,256]{2,1,0:T(8,128)(2,1)} %copy-done.1, ...), custom_call_target="tpu_custom_call" | custom-call | tf_op jit(solution)/shard_map/apply/pallas_call | solution.py:201
  77.4 4.1 %collective-permute-start.15 = (f32[8,16,256]{2,1,0:T(8,128)}, f32[8,16,256]{2,1,0:T(8,128)S(1)}, u32[]{:S(2)}, u32[]{:S(2)}) collective-permute-start(f32[8,16,256]{2,1,0:T(8,128)} %get-tuple-element.18), channel_id=1, source_target_pairs={{0,8},{8,0},{1,9},{9,1},{2,10},{10,2},{3,11},{11,3},{4,12},{12,4},... | collective-permute-start | bytes 393224 | tf_op jit(solution)/shard_map/ppermute | solution.py:153
  81.5 1.2 collective-permute-done.15
  82.7 0.9 add.26
  83.7 15.9 %all_to_all.15.p_ref = f32[8,16,256]{2,1,0:T(8,128)S(1)} all-to-all(f32[8,16,256]{2,1,0:T(8,128)S(1)} %add.26), channel_id=1, replica_groups=mesh['xl'=2,'z'=8,'core'=2,'y'=4,'xh'=2] {'z'}, dimensions={0} | all-to-all | bytes 262144 | tf_op jit(solution)/shard_map/all_to_all | solution.py:145
  99.5 0.7 copy-done
  100.2 0.3 project.1
  100.5 2.1 %collective-permute-start.16 = (f32[2,128]{1,0:T(2,128)S(1)}, f32[2,128]{1,0:T(2,128)S(1)}, u32[]{:S(2)}, u32[]{:S(2)}) collective-permute-start(f32[2,128]{1,0:T(2,128)S(1)} %get-tuple-element.20), channel_id=1, source_target_pairs={{0,8},{8,0},{1,9},{9,1},{2,10},{10,2},{3,11},{11,3},{4,12},{12,4},... | collective-permute-start | bytes 3080 | tf_op jit(solution)/shard_map/ppermute | solution.py:153
  102.7 0.8 collective-permute-done.16
  103.5 16.5 %all_to_all.16.gram_ref = f32[128,2,128]{2,1,0:T(2,128)S(1)} all-to-all(f32[128,2,128]{2,1,0:T(2,128)S(1)} %broadcast_in_dim.3), channel_id=1, replica_groups=mesh['xl'=2,'z'=8,'core'=2,'y'=4,'xh'=2] {'xl','z','y','xh'}, dimensions={0} | all-to-all | bytes 262144 | tf_op jit(solution)/shard_map/all_to_all | solution.py:145
  120.1 2.3 %finish.1 = (f32[16,256]{1,0:T(8,128)}, f32[16,16]{1,0:T(8,128)}) custom-call(f32[128,2,128]{2,1,0:T(2,128)S(1)} %all_to_all.16.gram_ref, f32[16,256]{1,0:T(8,128)S(1)} %get-tuple-element.21.q_ref), custom_call_target="tpu_custom_call" | custom-call | tf_op jit(solution)/shard_map/finish/pallas_call | solution.py:221
  (18 shorter events, 0.1 us)
Async XLA Ops:
  2.9 7.7 %copy-start.3 = (bf16[192,256]{1,0:T(8,128)(2,1)S(1)}, bf16[192,256]{1,0:T(8,128)(2,1)}, u32[]{:S(2)}) copy-start(bf16[192,256]{1,0:T(8,128)(2,1)} %get-tuple-element.14) | copy-start | bytes 294916
  2.9 34.8 %all-to-all-start = ((bf16[16,224,256]{2,1,0:T(8,128)(2,1)}), bf16[16,224,256]{2,1,0:T(8,128)(2,1)S(1)}, u32[]{:S(2)}, u32[]{:S(2)}) async-start(bf16[16,224,256]{2,1,0:T(8,128)(2,1)} %get-tuple-element.13), calls=%async_computation | async-start | bytes 3670016 | tf_op jit(solution)/shard_map/all_to_all | solution.py:145
  10.7 2.0 %collective-permute-start = (bf16[192,256]{1,0:T(8,128)(2,1)S(1)}, bf16[192,256]{1,0:T(8,128)(2,1)S(1)}, u32[]{:S(2)}, u32[]{:S(2)}) collective-permute-start(bf16[192,256]{1,0:T(8,128)(2,1)S(1)} %copy-done.3), channel_id=1, source_target_pairs={{0,8},{8,0},{1,9},{9,1},{2,10},{10,2},{3,11},{11,3},{4,12},{12,4},... | collective-permute-start | bytes 294920 | tf_op jit(solution)/shard_map/ppermute | solution.py:153
  12.7 25.1 %copy-start.2 = (bf16[2,192,256]{2,1,0:T(8,128)(2,1)}, bf16[2,192,256]{2,1,0:T(8,128)(2,1)S(1)}, u32[]{:S(2)}) copy-start(bf16[2,192,256]{2,1,0:T(8,128)(2,1)S(1)} %pad_maximum_fusion.refs_0_) | copy-start | bytes 589828
  12.7 10.8 %collective-permute-start.3 = (bf16[2,192,256]{2,1,0:T(8,128)(2,1)S(1)}, bf16[2,192,256]{2,1,0:T(8,128)(2,1)S(1)}, u32[]{:S(2)}, u32[]{:S(2)}) collective-permute-start(bf16[2,192,256]{2,1,0:T(8,128)(2,1)S(1)} %pad_maximum_fusion.refs_0_), channel_id=1, source_target_pairs={{0,32},{8,104},{16,48},{24,120},{32,64},{40,8},{48,80},{56,24},{64... | collective-permute-start | bytes 589832 | tf_op jit(solution)/shard_map/ppermute | solution.py:160
  18.8 8.9 %collective-permute-start.1 = (bf16[2,192,256]{2,1,0:T(8,128)(2,1)S(1)}, bf16[2,192,256]{2,1,0:T(8,128)(2,1)S(1)}, u32[]{:S(2)}, u32[]{:S(2)}) collective-permute-start(bf16[2,192,256]{2,1,0:T(8,128)(2,1)S(1)} %pad_maximum_fusion.refs_0_), channel_id=1, source_target_pairs={{0,16},{8,120},{16,32},{24,8},{32,48},{40,24},{48,64},{56,40},{64,... | collective-permute-start | bytes 589832 | tf_op jit(solution)/shard_map/ppermute | solution.py:160
  23.5 14.2 %copy-start.5 = (bf16[2,192,256]{2,1,0:T(8,128)(2,1)}, bf16[2,192,256]{2,1,0:T(8,128)(2,1)S(1)}, u32[]{:S(2)}) copy-start(bf16[2,192,256]{2,1,0:T(8,128)(2,1)S(1)} %collective-permute-done.3.refs_3_) | copy-start | bytes 589828
  23.5 4.9 %collective-permute-start.5 = (bf16[2,192,256]{2,1,0:T(8,128)(2,1)S(1)}, bf16[2,192,256]{2,1,0:T(8,128)(2,1)S(1)}, u32[]{:S(2)}, u32[]{:S(2)}) collective-permute-start(bf16[2,192,256]{2,1,0:T(8,128)(2,1)S(1)} %collective-permute-done.3.refs_3_), channel_id=1, source_target_pairs={{0,16},{8,120},{16,32},{24,8},{32,48},{40,24},{48,64},{56,40},{64,... | collective-permute-start | bytes 589832 | tf_op jit(solution)/shard_map/ppermute | solution.py:160
  25.8 5.8 %collective-permute-start.7 = (bf16[192,256]{1,0:T(8,128)(2,1)S(1)}, bf16[192,256]{1,0:T(8,128)(2,1)S(1)}, u32[]{:S(2)}, u32[]{:S(2)}) collective-permute-start(bf16[192,256]{1,0:T(8,128)(2,1)S(1)} %slice_bitcast_fusion), channel_id=1, source_target_pairs={{0,32},{8,104},{16,48},{24,120},{32,64},{40,8},{48,80},{56,24},{64... | collective-permute-start | bytes 294920 | tf_op jit(solution)/shard_map/ppermute | solution.py:160
  27.7 7.4 %collective-permute-start.4 = (bf16[2,192,256]{2,1,0:T(8,128)(2,1)S(1)}, bf16[2,192,256]{2,1,0:T(8,128)(2,1)S(1)}, u32[]{:S(2)}, u32[]{:S(2)}) collective-permute-start(bf16[2,192,256]{2,1,0:T(8,128)(2,1)S(1)} %collective-permute-done.3.refs_3_), channel_id=1, source_target_pairs={{0,8},{8,0},{1,9},{9,1},{2,10},{10,2},{3,11},{11,3},{4,12},{12,4},... | collective-permute-start | bytes 589832 | tf_op jit(solution)/shard_map/ppermute | solution.py:153
  27.7 10.0 %copy-start.9 = (bf16[2,192,256]{2,1,0:T(8,128)(2,1)}, bf16[2,192,256]{2,1,0:T(8,128)(2,1)S(1)}, u32[]{:S(2)}) copy-start(bf16[2,192,256]{2,1,0:T(8,128)(2,1)S(1)} %collective-permute-done.1.refs_1_) | copy-start | bytes 589828
  27.7 7.4 %collective-permute-start.2 = (bf16[2,192,256]{2,1,0:T(8,128)(2,1)S(1)}, bf16[2,192,256]{2,1,0:T(8,128)(2,1)S(1)}, u32[]{:S(2)}, u32[]{:S(2)}) collective-permute-start(bf16[2,192,256]{2,1,0:T(8,128)(2,1)S(1)} %collective-permute-done.1.refs_1_), channel_id=1, source_target_pairs={{0,8},{8,0},{1,9},{9,1},{2,10},{10,2},{3,11},{11,3},{4,12},{12,4},... | collective-permute-start | bytes 589832 | tf_op jit(solution)/shard_map/ppermute | solution.py:153
  28.4 9.4 %copy-start.10 = (bf16[2,192,256]{2,1,0:T(8,128)(2,1)}, bf16[2,192,256]{2,1,0:T(8,128)(2,1)S(1)}, u32[]{:S(2)}) copy-start(bf16[2,192,256]{2,1,0:T(8,128)(2,1)S(1)} %collective-permute-done.5.refs_5_) | copy-start | bytes 589828
  28.4 6.7 %collective-permute-start.6 = (bf16[2,192,256]{2,1,0:T(8,128)(2,1)S(1)}, bf16[2,192,256]{2,1,0:T(8,128)(2,1)S(1)}, u32[]{:S(2)}, u32[]{:S(2)}) collective-permute-start(bf16[2,192,256]{2,1,0:T(8,128)(2,1)S(1)} %collective-permute-done.5.refs_5_), channel_id=1, source_target_pairs={{0,8},{8,0},{1,9},{9,1},{2,10},{10,2},{3,11},{11,3},{4,12},{12,4},... | collective-permute-start | bytes 589832 | tf_op jit(solution)/shard_map/ppermute | solution.py:153
  31.6 6.2 %copy-start.14 = (bf16[192,256]{1,0:T(8,128)(2,1)}, bf16[192,256]{1,0:T(8,128)(2,1)S(1)}, u32[]{:S(2)}) copy-start(bf16[192,256]{1,0:T(8,128)(2,1)S(1)} %collective-permute-done.7.refs_7_) | copy-start | bytes 294916
  31.6 3.5 %collective-permute-start.8 = (bf16[192,256]{1,0:T(8,128)(2,1)S(1)}, bf16[192,256]{1,0:T(8,128)(2,1)S(1)}, u32[]{:S(2)}, u32[]{:S(2)}) collective-permute-start(bf16[192,256]{1,0:T(8,128)(2,1)S(1)} %collective-permute-done.7.refs_7_), channel_id=1, source_target_pairs={{0,8},{8,0},{1,9},{9,1},{2,10},{10,2},{3,11},{11,3},{4,12},{12,4},... | collective-permute-start | bytes 294920 | tf_op jit(solution)/shard_map/ppermute | solution.py:153
  35.1 2.7 %copy-start.15 = (bf16[192,256]{1,0:T(8,128)(2,1)}, bf16[192,256]{1,0:T(8,128)(2,1)S(1)}, u32[]{:S(2)}) copy-start(bf16[192,256]{1,0:T(8,128)(2,1)S(1)} %collective-permute-done.8.refs_8_) | copy-start | bytes 294916
  35.1 2.7 %copy-start.11 = (bf16[2,192,256]{2,1,0:T(8,128)(2,1)}, bf16[2,192,256]{2,1,0:T(8,128)(2,1)S(1)}, u32[]{:S(2)}) copy-start(bf16[2,192,256]{2,1,0:T(8,128)(2,1)S(1)} %collective-permute-done.4.refs_4_) | copy-start | bytes 589828
  35.1 2.7 %copy-start.12 = (bf16[2,192,256]{2,1,0:T(8,128)(2,1)}, bf16[2,192,256]{2,1,0:T(8,128)(2,1)S(1)}, u32[]{:S(2)}) copy-start(bf16[2,192,256]{2,1,0:T(8,128)(2,1)S(1)} %collective-permute-done.2.refs_2_) | copy-start | bytes 589828
  35.1 2.7 %copy-start.13 = (bf16[2,192,256]{2,1,0:T(8,128)(2,1)}, bf16[2,192,256]{2,1,0:T(8,128)(2,1)S(1)}, u32[]{:S(2)}) copy-start(bf16[2,192,256]{2,1,0:T(8,128)(2,1)S(1)} %collective-permute-done.6.refs_6_) | copy-start | bytes 589828
  37.8 1.2 %copy-start.1 = (bf16[16,224,256]{2,1,0:T(8,128)(2,1)}, bf16[16,224,256]{2,1,0:T(8,128)(2,1)S(1)}, u32[]{:S(2)}) copy-start(bf16[16,224,256]{2,1,0:T(8,128)(2,1)S(1)} %all-to-all-done.t_ref) | copy-start | bytes 5505028
  52.6 2.8 %collective-permute-start.11 = (f32[16,256]{1,0:T(8,128)}, f32[16,256]{1,0:T(8,128)S(1)}, u32[]{:S(2)}, u32[]{:S(2)}) collective-permute-start(f32[16,256]{1,0:T(8,128)} %get-tuple-element.15), channel_id=1, source_target_pairs={{0,6},{2,0},{4,2},{6,4},{1,7},{3,1},{5,3},{7,5},{8,14},{10,8},{12,... | collective-permute-start | bytes 49160 | tf_op jit(solution)/shard_map/ppermute | solution.py:168
  53.7 4.3 %collective-permute-start.10 = (f32[16,256]{1,0:T(8,128)}, f32[16,256]{1,0:T(8,128)S(1)}, u32[]{:S(2)}, u32[]{:S(2)}) collective-permute-start(f32[16,256]{1,0:T(8,128)} %get-tuple-element.15), channel_id=1, source_target_pairs={{0,4},{2,6},{4,0},{6,2},{1,5},{3,7},{5,1},{7,3},{8,12},{10,14},{12... | collective-permute-start | bytes 49160 | tf_op jit(solution)/shard_map/ppermute | solution.py:168
  54.7 4.0 %collective-permute-start.9 = (f32[16,256]{1,0:T(8,128)}, f32[16,256]{1,0:T(8,128)S(1)}, u32[]{:S(2)}, u32[]{:S(2)}) collective-permute-start(f32[16,256]{1,0:T(8,128)} %get-tuple-element.15), channel_id=1, source_target_pairs={{0,2},{2,4},{4,6},{6,0},{1,3},{3,5},{5,7},{7,1},{8,10},{10,12},{12... | collective-permute-start | bytes 49160 | tf_op jit(solution)/shard_map/ppermute | solution.py:168
  59.5 6.3 %copy-start.4 = (f32[16,256]{1,0:T(8,128)}, f32[16,256]{1,0:T(8,128)S(1)}, u32[]{:S(2)}) copy-start(f32[16,256]{1,0:T(8,128)S(1)} %add_add_fusion.d0_ref) | copy-start | bytes 49156
  59.5 3.1 %collective-permute-start.14 = (f32[16,256]{1,0:T(8,128)S(1)}, f32[16,256]{1,0:T(8,128)S(1)}, u32[]{:S(2)}, u32[]{:S(2)}) collective-permute-start(f32[16,256]{1,0:T(8,128)S(1)} %add_add_fusion.d0_ref), channel_id=1, source_target_pairs={{0,129},{128,0},{1,128},{129,1},{2,131},{130,2},{3,130},{131,3},{4... | collective-permute-start | bytes 49160 | tf_op jit(solution)/shard_map/ppermute | solution.py:168
  61.4 4.1 %collective-permute-start.13 = (f32[16,256]{1,0:T(8,128)S(1)}, f32[16,256]{1,0:T(8,128)S(1)}, u32[]{:S(2)}, u32[]{:S(2)}) collective-permute-start(f32[16,256]{1,0:T(8,128)S(1)} %add_add_fusion.d0_ref), channel_id=1, source_target_pairs={{0,1},{128,129},{1,0},{129,128},{2,3},{130,131},{3,2},{131,130},{4... | collective-permute-start | bytes 49160 | tf_op jit(solution)/shard_map/ppermute | solution.py:168
  62.0 3.8 %collective-permute-start.12 = (f32[16,256]{1,0:T(8,128)S(1)}, f32[16,256]{1,0:T(8,128)S(1)}, u32[]{:S(2)}, u32[]{:S(2)}) collective-permute-start(f32[16,256]{1,0:T(8,128)S(1)} %add_add_fusion.d0_ref), channel_id=1, source_target_pairs={{0,128},{128,1},{1,129},{129,0},{2,130},{130,3},{3,131},{131,2},{4... | collective-permute-start | bytes 49160 | tf_op jit(solution)/shard_map/ppermute | solution.py:168
  62.6 3.2 %copy-start.6 = (f32[16,256]{1,0:T(8,128)}, f32[16,256]{1,0:T(8,128)S(1)}, u32[]{:S(2)}) copy-start(f32[16,256]{1,0:T(8,128)S(1)} %collective-permute-done.14.d3_ref) | copy-start | bytes 49156
  65.5 0.6 copy-start.7
  65.8 0.6 copy-start.8
  77.4 5.3 %collective-permute-start.15 = (f32[8,16,256]{2,1,0:T(8,128)}, f32[8,16,256]{2,1,0:T(8,128)S(1)}, u32[]{:S(2)}, u32[]{:S(2)}) collective-permute-start(f32[8,16,256]{2,1,0:T(8,128)} %get-tuple-element.18), channel_id=1, source_target_pairs={{0,8},{8,0},{1,9},{9,1},{2,10},{10,2},{3,11},{11,3},{4,12},{12,4},... | collective-permute-start | bytes 393224 | tf_op jit(solution)/shard_map/ppermute | solution.py:153
  99.5 0.7 copy-start
  100.5 3.0 %collective-permute-start.16 = (f32[2,128]{1,0:T(2,128)S(1)}, f32[2,128]{1,0:T(2,128)S(1)}, u32[]{:S(2)}, u32[]{:S(2)}) collective-permute-start(f32[2,128]{1,0:T(2,128)S(1)} %get-tuple-element.20), channel_id=1, source_target_pairs={{0,8},{8,0},{1,9},{9,1},{2,10},{10,2},{3,11},{11,3},{4,12},{12,4},... | collective-permute-start | bytes 3080 | tf_op jit(solution)/shard_map/ppermute | solution.py:153

commit v11 on v10

--- a/solution.py
+++ b/solution.py
@@ -17,7 +17,7 @@
 SEG = 256
 DIM = 192
 VEC = 16
-WIDE = DIM + 2 * VEC
+WIDE = DIM + VEC
 SCALE = 14.426950408889634
 UNSCALE = 4.5399929762484854e-05
 EPS = 1e-6
@@ -47,23 +47,20 @@
     e = e_ref[...].astype(F32)
     u = (e * lax.rsqrt(jnp.sum(e * e, axis=0, keepdims=True) + EPS)).astype(BF16)
     u_ref[...] = u
-    v = v_ref[...]
-    high = v.astype(BF16)
-    low = (v - high.astype(F32)).astype(BF16)
+    v = v_ref[...].astype(BF16)
     for k in range(NC):
         many_ref[k, 0:DIM, :] = u
-        many_ref[k, DIM : DIM + VEC, :] = high
-        many_ref[k, DIM + VEC : WIDE, :] = low
+        many_ref[k, DIM:WIDE, :] = v
 
 
 def affinity_kernel(pos_ref, t_ref, *refs):
     pairs, lone = refs[0:7], refs[7:9]
-    b_ref, deg_ref, s_ref = refs[9:12]
+    b_ref, deg_ref, v_ref, s_ref, c_ref, acc_ref = refs[9:15]
     z, core = pos_ref[2], pos_ref[0]
     step = pl.program_id(0)
 
     def place(chip, side, rows):
-        s_ref[lax.rem(chip + 16, 8) * 2 + side] = rows.T
+        s_ref[lax.rem(chip + 16, 8) * 2 + side] = rows
 
     @pl.when(step == 0)
     def _():
@@ -77,31 +74,38 @@
             place(z + k * sign, core, pairs[2 * k][1])
         place(z + 4, core, lone[0][...])
         place(z + 4, 1 - core, lone[1][...])
-
-    for j in range(2):
-        piece = t_ref[step * 2 + j, 0:DIM, :]
-        total = jnp.zeros((8, SEG), F32)
-        for r in range(NR):
-            score = jnp.dot(s_ref[r], piece, preferred_element_type=F32)
+        for t in range(NC):
+            c_ref[t] = t_ref[t, 0:DIM, :].T
+            v_ref[t] = t_ref[t, DIM:WIDE, :]
+        acc_ref[...] = jnp.zeros_like(acc_ref)
+
+    for t in range(NC):
+        total = acc_ref[t]
+        for j in range(2):
+            score = jnp.dot(c_ref[t], s_ref[step * 2 + j], preferred_element_type=F32)
             tile = jnp.exp2(score * SCALE)
-            total = total + jnp.sum(tile.reshape(SEG // 8, 8, SEG), axis=0)
-            b_ref[step * 2 + j, r * SEG : (r + 1) * SEG, :] = tile.astype(BF16)
-        sums = jnp.sum(total, axis=0, keepdims=True) * UNSCALE
-        deg_ref[pl.ds(step * 2 + j, 1), :] = sums
-
-
-def apply_kernel(pos_ref, d0_ref, d1_ref, d2_ref, d3_ref, t_ref, b_ref, mine_ref, other_ref, own_ref, root_ref):
+            total = total + (tile[:, 0:128] + tile[:, 128:256])
+            b_ref[step * 2 + j, t * SEG : (t + 1) * SEG, :] = tile.astype(BF16)
+        acc_ref[t] = total
+
+    @pl.when(step == NR // 2 - 1)
+    def _():
+        for t in range(NC):
+            sums = nt(jnp.ones((8, 128), F32), acc_ref[t], precision=HI)
+            deg_ref[t : t + 1, :] = sums[0:1, :] * UNSCALE
+
+
+def apply_kernel(pos_ref, d0_ref, d1_ref, d2_ref, d3_ref, v_ref, b_ref, *refs):
+    mine_ref, other_ref, own_ref, root_ref, w_ref = refs
+    core = pos_ref[0]
     root_ref[...] = lax.rsqrt((d0_ref[...] + d2_ref[...]) + (d1_ref[...] + d3_ref[...]))
-    core = pos_ref[0]
     own_ref[...] = root_ref[pl.ds(pos_ref[1], 1), :] * UNSCALE
     for t in range(NC):
-        v = t_ref[t, DIM : DIM + VEC, :].astype(F32) + t_ref[t, DIM + VEC : WIDE, :].astype(F32)
-        w = (v * root_ref[t : t + 1, :]).astype(BF16)
-        for r in range(NR // 2):
-            for side, p_ref in ((core, mine_ref), (1 - core, other_ref)):
-                rows = pl.ds(pl.multiple_of((r * 2 + side) * SEG, SEG), SEG)
-                part = nt(w, b_ref[t, rows, :])
-                p_ref[r] = part if t == 0 else p_ref[r] + part
+        w = v_ref[t].astype(F32) * root_ref[t : t + 1, :]
+        w_ref[:, t * SEG : (t + 1) * SEG] = w.astype(BF16)
+    for r in range(NR // 2):
+        for side, p_ref in ((core, mine_ref), (1 - core, other_ref)):
+            p_ref[r] = jnp.dot(w_ref[...], b_ref[r * 2 + side], preferred_element_type=F32)
 
 
 def project_kernel(p_ref, own_ref, q_ref, gram_ref):
@@ -178,18 +182,26 @@
         out_shape=(shape(DIM, SEG, dtype=BF16), shape(NC, WIDE, SEG, dtype=BF16)),
         name="unit",
     )(embeddings.T, vectors.T)
-    columns = to_all(unit_copies, COLS)
+    columns = pltpu.with_memory_space_constraint(to_all(unit_copies, COLS), pltpu.HBM)
     pair = jnp.stack([unit, across(unit)])
     one, two = along(pair, 1), along(pair, 2)
     three, four = along(two, 1), along(two[0], 2)
     pairs = (pair, one, across(one), two, across(two), three, across(three))
-    block, degree = pl.pallas_call(
+    block, degree, vector_columns = pl.pallas_call(
         affinity_kernel,
         grid=(NC // 2,),
-        out_shape=(pltpu.VMEM((NC, NR * SEG, SEG), BF16), shape(NC, SEG)),
+        out_shape=(
+            pltpu.VMEM((NR, NC * SEG, SEG), BF16),
+            shape(NC, SEG),
+            shape(NC, VEC, SEG, dtype=BF16),
+        ),
         in_specs=[smem()] + [vmem()] * 10,
-        out_specs=(vmem(), vmem()),
-        scratch_shapes=[pltpu.VMEM((NR, SEG, DIM), BF16)],
+        out_specs=(vmem(), vmem(), vmem()),
+        scratch_shapes=[
+            pltpu.VMEM((NR, DIM, SEG), BF16),
+            pltpu.VMEM((NC, SEG, DIM), BF16),
+            pltpu.VMEM((NC, SEG, 128), F32),
+        ],
         compiler_params=params(24),
         cost_estimate=pl.CostEstimate(
             flops=2 * 256 * 4096 * 4096, transcendentals=4096 * 4096, bytes_accessed=1 << 25
@@ -205,10 +217,11 @@
         out_specs=(vmem(), vmem(), vmem()),
         scratch_shapes=[
             pltpu.VMEM((NC, SEG), F32),
+            pltpu.VMEM((VEC, NC * SEG), BF16),
         ],
         compiler_params=params(24),
         name="apply",
-    )(position, *degrees, columns, pltpu.with_memory_space_constraint(block, pltpu.VMEM))
+    )(position, *degrees, vector_columns, pltpu.with_memory_space_constraint(block, pltpu.VMEM))
     product = to_all(mine + across(other), "z")
     projected, gram = pl.pallas_call(
         project_kernel,

time: 123 us -> 119 us (0.967)
  Pallas kernels: 29.5 us -> 26.7 us
  waiting for transfers between devices: 17.4 us -> 14.6 us
  starting transfers between devices: 37.3 us -> 39.3 us
    pallas_call x1, Pallas kernels: 11 us -> 6.12 us  [per_device(): pl.pallas_call(apply_kernel, out_shape=(shape(HALF, VEC, SEG), shape(HALF...]
    all_to_all x1, waiting for transfers between devices: 2.59 us -> 0.02 us  [to_all(): return lax.all_to_all(copies, axes, split_axis=0, concat_axis=0, tiled=True)]
    ppermute x6, starting transfers between devices: 5.56 us -> 7.81 us  [ring_copies(): lax.ppermute(a, axes, [(place(k), place(k + hops)) for k in range(4)])]
    pallas_call x1, Pallas kernels: 13.6 us -> 15.7 us  [per_device(): pl.pallas_call(affinity_kernel, grid=(NC // 2,), out_shape=(pltpu.VMEM((N...]
  transfers between devices with their start and end apart: 18 -> 18, of which waited for: 13 -> 11; matrix products, arithmetic and copies ran while one was open for 1% -> 1% of each run, Pallas kernels for 0% -> 0%
where the time goes in v11:
time: 119 us; the launch traced here: 118 us
  starting transfers between devices  39.3 us (33%)
  blocking collectives  31.3 us (26%)
  Pallas kernels  26.7 us (22%)
  waiting for transfers between devices  14.6 us (12%)
  local copies, waits for them, and re-layouts  3.33 us (3%)
  other arithmetic  2.32 us (2%)
    all_to_all x2, blocking collectives, to_all(): return lax.all_to_all(copies, axes, split_axis=0, concat_axis=0, tiled=True)  31.3 us
    pallas_call x1, Pallas kernels, per_device(): pl.pallas_call(affinity_kernel, grid=(NC // 2,), out_shape=(pltpu.VMEM((N...  15.7 us
    ppermute x7, starting transfers between devices, across(): return lax.ppermute(a, 'core', [(0, 1), (1, 0)])  12.7 us
    ppermute x4, starting transfers between devices, along(): return lax.ppermute(a, ROWS, turns)  11 us
    ppermute x6, starting transfers between devices, ring_copies(): lax.ppermute(a, axes, [(place(k), place(k + hops)) for k in range(4)])  7.81 us
    all_to_all x1, starting transfers between devices, to_all(): return lax.all_to_all(copies, axes, split_axis=0, concat_axis=0, tiled=True)  7.72 us
    ppermute x6, waiting for transfers between devices, ring_copies(): lax.ppermute(a, axes, [(place(k), place(k + hops)) for k in range(4)])  6.65 us
    pallas_call x1, Pallas kernels, per_device(): pl.pallas_call(apply_kernel, out_shape=(shape(HALF, VEC, SEG), shape(HALF...  6.12 us
  transfers between devices with their start and end apart: 18, of which 11 were waited for; matrix products, arithmetic and copies ran while one was open for 1% of the time, Pallas kernels for 0%

profile of v11, /device:TPU:1, one launch (start us, length us, event | category | flops | bytes accessed | tf_op | source)
XLA Modules:
  0.0 118.2 jit_solution(11085153586027479653)
XLA Ops:
  0.6 2.3 %unit.1 = (bf16[192,256]{1,0:T(8,128)(2,1)}, bf16[16,208,256]{2,1,0:T(8,128)(2,1)}) custom-call(bf16[192,256]{1,0:T(8,128)(2,1)} %bitcast.10, f32[16,256]{1,0:T(8,128)} %bitcast.13), custom_call_target="tpu_custom_call" | custom-call | tf_op jit(solution)/shard_map/unit/pallas_call | solution.py:180
  2.9 7.7 %all-to-all-start = ((bf16[16,208,256]{2,1,0:T(8,128)(2,1)}), bf16[16,208,256]{2,1,0:T(8,128)(2,1)S(1)}, u32[]{:S(2)}, u32[]{:S(2)}) async-start(bf16[16,208,256]{2,1,0:T(8,128)(2,1)} %get-tuple-element.14), calls=%async_computation | async-start | bytes 3407872 | tf_op jit(solution)/shard_map/all_to_all | solution.py:149
  10.6 0.0 copy-done.3
  10.6 1.0 collective-permute-start
  11.7 0.9 collective-permute-done
  12.6 0.0 copy-start.2
  12.7 6.1 %collective-permute-start.3 = (bf16[2,192,256]{2,1,0:T(8,128)(2,1)S(1)}, bf16[2,192,256]{2,1,0:T(8,128)(2,1)S(1)}, u32[]{:S(2)}, u32[]{:S(2)}) collective-permute-start(bf16[2,192,256]{2,1,0:T(8,128)(2,1)S(1)} %pad_maximum_fusion.refs_0_), channel_id=1, source_target_pairs={{0,32},{8,104},{16,48},{24,120},{32,64},{40,8},{48,80},{56,24},{64... | collective-permute-start | bytes 589832 | tf_op jit(solution)/shard_map/ppermute | solution.py:164
  18.8 0.7 collective-permute-start.1
  19.5 4.0 %collective-permute-done.3.refs_3_ = bf16[2,192,256]{2,1,0:T(8,128)(2,1)S(1)} collective-permute-done((bf16[2,192,256]{2,1,0:T(8,128)(2,1)S(1)}, bf16[2,192,256]{2,1,0:T(8,128)(2,1)S(1)}, u32[]{:S(2)}, u32[]{:S(2)}) %collective-permute-start.3) | collective-permute-done | bytes 196640 | tf_op jit(solution)/shard_map/ppermute | solution.py:164
  23.5 2.3 %collective-permute-start.5 = (bf16[2,192,256]{2,1,0:T(8,128)(2,1)S(1)}, bf16[2,192,256]{2,1,0:T(8,128)(2,1)S(1)}, u32[]{:S(2)}, u32[]{:S(2)}) collective-permute-start(bf16[2,192,256]{2,1,0:T(8,128)(2,1)S(1)} %collective-permute-done.3.refs_3_), channel_id=1, source_target_pairs={{0,16},{8,120},{16,32},{24,8},{32,48},{40,24},{48,64},{56,40},{64,... | collective-permute-start | bytes 589832 | tf_op jit(solution)/shard_map/ppermute | solution.py:164
  25.7 1.9 %collective-permute-start.7 = (bf16[192,256]{1,0:T(8,128)(2,1)S(1)}, bf16[192,256]{1,0:T(8,128)(2,1)S(1)}, u32[]{:S(2)}, u32[]{:S(2)}) collective-permute-start(bf16[192,256]{1,0:T(8,128)(2,1)S(1)} %slice_bitcast_fusion), channel_id=1, source_target_pairs={{0,32},{8,104},{16,48},{24,120},{32,64},{40,8},{48,80},{56,24},{64... | collective-permute-start | bytes 294920 | tf_op jit(solution)/shard_map/ppermute | solution.py:164
  27.7 0.0 collective-permute-start.4
  27.7 0.0 collective-permute-done.1.refs_1_
  27.7 0.5 collective-permute-start.2
  28.2 0.1 collective-permute-done.5.refs_5_
  28.4 2.7 %collective-permute-start.6 = (bf16[2,192,256]{2,1,0:T(8,128)(2,1)S(1)}, bf16[2,192,256]{2,1,0:T(8,128)(2,1)S(1)}, u32[]{:S(2)}, u32[]{:S(2)}) collective-permute-start(bf16[2,192,256]{2,1,0:T(8,128)(2,1)S(1)} %collective-permute-done.5.refs_5_), channel_id=1, source_target_pairs={{0,8},{8,0},{1,9},{9,1},{2,10},{10,2},{3,11},{11,3},{4,12},{12,4},... | collective-permute-start | bytes 589832 | tf_op jit(solution)/shard_map/ppermute | solution.py:157
  31.0 0.5 collective-permute-done.7.refs_7_
  31.5 2.6 %collective-permute-start.8 = (bf16[192,256]{1,0:T(8,128)(2,1)S(1)}, bf16[192,256]{1,0:T(8,128)(2,1)S(1)}, u32[]{:S(2)}, u32[]{:S(2)}) collective-permute-start(bf16[192,256]{1,0:T(8,128)(2,1)S(1)} %collective-permute-done.7.refs_7_), channel_id=1, source_target_pairs={{0,8},{8,0},{1,9},{9,1},{2,10},{10,2},{3,11},{11,3},{4,12},{12,4},... | collective-permute-start | bytes 294920 | tf_op jit(solution)/shard_map/ppermute | solution.py:157
  34.1 0.7 pad_add_fusion.pos_ref
  34.8 0.3 collective-permute-done.8.refs_8_
  35.1 0.0 collective-permute-done.4.refs_4_
  35.1 0.0 collective-permute-done.2.refs_2_
  35.1 0.0 copy-start.12
  35.1 0.0 collective-permute-done.6.refs_6_
  35.1 0.0 copy-start.13
  35.1 0.0 all-to-all-done.t_ref
  35.1 0.0 copy-done.2
  35.1 0.0 copy-done.5
  35.1 0.0 copy-done.9
  35.2 0.0 copy-done.10
  35.2 0.0 copy-done.14
  35.2 0.5 copy-done.15
  35.7 0.1 copy-done.11
  35.8 0.1 copy-done.12
  35.9 0.1 copy-done.13
  35.9 1.2 %copy-done.1 = bf16[16,208,256]{2,1,0:T(8,128)(2,1)} copy-done((bf16[16,208,256]{2,1,0:T(8,128)(2,1)}, bf16[16,208,256]{2,1,0:T(8,128)(2,1)S(1)}, u32[]{:S(2)}) %copy-start.1) | copy-done | bytes 1703960
  37.2 15.7 %affinity.1 = (bf16[16,4096,256]{2,1,0:T(8,128)(2,1)S(1)}, f32[16,256]{1,0:T(8,128)}, bf16[16,16,256]{2,1,0:T(8,128)(2,1)}) custom-call(s32[3]{0:T(128)} %pad_add_fusion.pos_ref, bf16[16,208,256]{2,1,0:T(8,128)(2,1)} %copy-done.1, bf16[2,192,256]{2,1,0:T(8,128)(2,1)} %copy-done.2, bf16[2,192,256]{2,1,0:T(8,128)(2,1)} %copy-done.9, ...), custom_call_target="tpu_custom_call" | custom-call | flops 8589934592 | bytes 33554432 | tf_op jit(solution)/shard_map/affinity/pallas_call | solution.py:190
  52.8 2.9 %collective-permute-start.11 = (f32[16,256]{1,0:T(8,128)}, f32[16,256]{1,0:T(8,128)S(1)}, u32[]{:S(2)}, u32[]{:S(2)}) collective-permute-start(f32[16,256]{1,0:T(8,128)} %get-tuple-element.16), channel_id=1, source_target_pairs={{0,6},{2,0},{4,2},{6,4},{1,7},{3,1},{5,3},{7,5},{8,14},{10,8},{12,... | collective-permute-start | bytes 49160 | tf_op jit(solution)/shard_map/ppermute | solution.py:172
  55.7 0.6 collective-permute-start.10
  56.3 0.6 collective-permute-start.9
  56.8 0.0 collective-permute-done.11
  56.8 3.1 %collective-permute-done.10 = f32[16,256]{1,0:T(8,128)S(1)} collective-permute-done((f32[16,256]{1,0:T(8,128)}, f32[16,256]{1,0:T(8,128)S(1)}, u32[]{:S(2)}, u32[]{:S(2)}) %collective-permute-start.10) | collective-permute-done | bytes 16416 | tf_op jit(solution)/shard_map/ppermute | solution.py:172
  60.0 0.3 collective-permute-done.9
  60.3 0.7 add_add_fusion.d0_ref
  61.0 2.7 %collective-permute-start.14 = (f32[16,256]{1,0:T(8,128)S(1)}, f32[16,256]{1,0:T(8,128)S(1)}, u32[]{:S(2)}, u32[]{:S(2)}) collective-permute-start(f32[16,256]{1,0:T(8,128)S(1)} %add_add_fusion.d0_ref), channel_id=1, source_target_pairs={{0,129},{128,0},{1,128},{129,1},{2,131},{130,2},{3,130},{131,3},{4... | collective-permute-start | bytes 49160 | tf_op jit(solution)/shard_map/ppermute | solution.py:172
  63.7 0.6 collective-permute-start.13
  64.2 0.6 collective-permute-start.12
  64.8 0.0 collective-permute-done.14.d3_ref
  64.8 2.9 %collective-permute-done.13.d2_ref = f32[16,256]{1,0:T(8,128)S(1)} collective-permute-done((f32[16,256]{1,0:T(8,128)S(1)}, f32[16,256]{1,0:T(8,128)S(1)}, u32[]{:S(2)}, u32[]{:S(2)}) %collective-permute-start.13) | collective-permute-done | bytes 16416 | tf_op jit(solution)/shard_map/ppermute | solution.py:172
  67.7 0.3 collective-permute-done.12.d1_ref
  68.0 0.0 copy-done.4
  68.0 0.3 copy-done.7
  68.3 0.3 copy-done.8
  68.6 6.1 %apply.1 = (f32[8,16,256]{2,1,0:T(8,128)}, f32[8,16,256]{2,1,0:T(8,128)}, f32[1,256]{1,0:T(1,128)}) custom-call(s32[3]{0:T(128)} %pad_add_fusion.pos_ref, f32[16,256]{1,0:T(8,128)} %copy-done.4, f32[16,256]{1,0:T(8,128)} %copy-done.8, f32[16,256]{1,0:T(8,128)} %copy-done.7, f32[16,256]{1,0:T(8,128)} %copy-done.6, ...), custom_call_target="tpu_custom_call" | custom-call | tf_op jit(solution)/shard_map/apply/pallas_call | solution.py:213
  74.8 3.8 %collective-permute-start.15 = (f32[8,16,256]{2,1,0:T(8,128)}, f32[8,16,256]{2,1,0:T(8,128)S(1)}, u32[]{:S(2)}, u32[]{:S(2)}) collective-permute-start(f32[8,16,256]{2,1,0:T(8,128)} %get-tuple-element.20), channel_id=1, source_target_pairs={{0,8},{8,0},{1,9},{9,1},{2,10},{10,2},{3,11},{11,3},{4,12},{12,4},... | collective-permute-start | bytes 393224 | tf_op jit(solution)/shard_map/ppermute | solution.py:157
  78.5 1.2 %collective-permute-done.15 = f32[8,16,256]{2,1,0:T(8,128)S(1)} collective-permute-done((f32[8,16,256]{2,1,0:T(8,128)}, f32[8,16,256]{2,1,0:T(8,128)S(1)}, u32[]{:S(2)}, u32[]{:S(2)}) %collective-permute-start.15) | collective-permute-done | bytes 131104 | tf_op jit(solution)/shard_map/ppermute | solution.py:157
  79.7 0.9 add.26
  80.6 14.1 %all_to_all.15.p_ref = f32[8,16,256]{2,1,0:T(8,128)S(1)} all-to-all(f32[8,16,256]{2,1,0:T(8,128)S(1)} %add.26), channel_id=1, replica_groups=mesh['xl'=2,'z'=8,'core'=2,'y'=4,'xh'=2] {'z'}, dimensions={0} | all-to-all | bytes 262144 | tf_op jit(solution)/shard_map/all_to_all | solution.py:149
  94.7 0.7 copy-done
  95.4 0.3 project.1
  95.7 2.1 %collective-permute-start.16 = (f32[2,128]{1,0:T(2,128)S(1)}, f32[2,128]{1,0:T(2,128)S(1)}, u32[]{:S(2)}, u32[]{:S(2)}) collective-permute-start(f32[2,128]{1,0:T(2,128)S(1)} %get-tuple-element.22), channel_id=1, source_target_pairs={{0,8},{8,0},{1,9},{9,1},{2,10},{10,2},{3,11},{11,3},{4,12},{12,4},... | collective-permute-start | bytes 3080 | tf_op jit(solution)/shard_map/ppermute | solution.py:157
  97.9 0.8 collective-permute-done.16
  98.7 17.2 %all_to_all.16.gram_ref = f32[128,2,128]{2,1,0:T(2,128)S(1)} all-to-all(f32[128,2,128]{2,1,0:T(2,128)S(1)} %broadcast_in_dim.3), channel_id=1, replica_groups=mesh['xl'=2,'z'=8,'core'=2,'y'=4,'xh'=2] {'xl','z','y','xh'}, dimensions={0} | all-to-all | bytes 262144 | tf_op jit(solution)/shard_map/all_to_all | solution.py:149
  115.9 2.3 %finish.1 = (f32[16,256]{1,0:T(8,128)}, f32[16,16]{1,0:T(8,128)}) custom-call(f32[128,2,128]{2,1,0:T(2,128)S(1)} %all_to_all.16.gram_ref, f32[16,256]{1,0:T(8,128)S(1)} %get-tuple-element.23.q_ref), custom_call_target="tpu_custom_call" | custom-call | tf_op jit(solution)/shard_map/finish/pallas_call | solution.py:234
  (18 shorter events, 0.1 us)
Async XLA Ops:
  2.9 7.7 %copy-start.3 = (bf16[192,256]{1,0:T(8,128)(2,1)S(1)}, bf16[192,256]{1,0:T(8,128)(2,1)}, u32[]{:S(2)}) copy-start(bf16[192,256]{1,0:T(8,128)(2,1)} %get-tuple-element.15) | copy-start | bytes 294916
  2.9 32.2 %all-to-all-start = ((bf16[16,208,256]{2,1,0:T(8,128)(2,1)}), bf16[16,208,256]{2,1,0:T(8,128)(2,1)S(1)}, u32[]{:S(2)}, u32[]{:S(2)}) async-start(bf16[16,208,256]{2,1,0:T(8,128)(2,1)} %get-tuple-element.14), calls=%async_computation | async-start | bytes 3407872 | tf_op jit(solution)/shard_map/all_to_all | solution.py:149
  10.6 2.0 %collective-permute-start = (bf16[192,256]{1,0:T(8,128)(2,1)S(1)}, bf16[192,256]{1,0:T(8,128)(2,1)S(1)}, u32[]{:S(2)}, u32[]{:S(2)}) collective-permute-start(bf16[192,256]{1,0:T(8,128)(2,1)S(1)} %copy-done.3), channel_id=1, source_target_pairs={{0,8},{8,0},{1,9},{9,1},{2,10},{10,2},{3,11},{11,3},{4,12},{12,4},... | collective-permute-start | bytes 294920 | tf_op jit(solution)/shard_map/ppermute | solution.py:157
  12.6 22.5 %copy-start.2 = (bf16[2,192,256]{2,1,0:T(8,128)(2,1)}, bf16[2,192,256]{2,1,0:T(8,128)(2,1)S(1)}, u32[]{:S(2)}) copy-start(bf16[2,192,256]{2,1,0:T(8,128)(2,1)S(1)} %pad_maximum_fusion.refs_0_) | copy-start | bytes 589828
  12.7 10.8 %collective-permute-start.3 = (bf16[2,192,256]{2,1,0:T(8,128)(2,1)S(1)}, bf16[2,192,256]{2,1,0:T(8,128)(2,1)S(1)}, u32[]{:S(2)}, u32[]{:S(2)}) collective-permute-start(bf16[2,192,256]{2,1,0:T(8,128)(2,1)S(1)} %pad_maximum_fusion.refs_0_), channel_id=1, source_target_pairs={{0,32},{8,104},{16,48},{24,120},{32,64},{40,8},{48,80},{56,24},{64... | collective-permute-start | bytes 589832 | tf_op jit(solution)/shard_map/ppermute | solution.py:164
  18.8 8.9 %collective-permute-start.1 = (bf16[2,192,256]{2,1,0:T(8,128)(2,1)S(1)}, bf16[2,192,256]{2,1,0:T(8,128)(2,1)S(1)}, u32[]{:S(2)}, u32[]{:S(2)}) collective-permute-start(bf16[2,192,256]{2,1,0:T(8,128)(2,1)S(1)} %pad_maximum_fusion.refs_0_), channel_id=1, source_target_pairs={{0,16},{8,120},{16,32},{24,8},{32,48},{40,24},{48,64},{56,40},{64,... | collective-permute-start | bytes 589832 | tf_op jit(solution)/shard_map/ppermute | solution.py:164
  23.5 11.7 %copy-start.5 = (bf16[2,192,256]{2,1,0:T(8,128)(2,1)}, bf16[2,192,256]{2,1,0:T(8,128)(2,1)S(1)}, u32[]{:S(2)}) copy-start(bf16[2,192,256]{2,1,0:T(8,128)(2,1)S(1)} %collective-permute-done.3.refs_3_) | copy-start | bytes 589828
  23.5 4.9 %collective-permute-start.5 = (bf16[2,192,256]{2,1,0:T(8,128)(2,1)S(1)}, bf16[2,192,256]{2,1,0:T(8,128)(2,1)S(1)}, u32[]{:S(2)}, u32[]{:S(2)}) collective-permute-start(bf16[2,192,256]{2,1,0:T(8,128)(2,1)S(1)} %collective-permute-done.3.refs_3_), channel_id=1, source_target_pairs={{0,16},{8,120},{16,32},{24,8},{32,48},{40,24},{48,64},{56,40},{64,... | collective-permute-start | bytes 589832 | tf_op jit(solution)/shard_map/ppermute | solution.py:164
  25.7 5.8 %collective-permute-start.7 = (bf16[192,256]{1,0:T(8,128)(2,1)S(1)}, bf16[192,256]{1,0:T(8,128)(2,1)S(1)}, u32[]{:S(2)}, u32[]{:S(2)}) collective-permute-start(bf16[192,256]{1,0:T(8,128)(2,1)S(1)} %slice_bitcast_fusion), channel_id=1, source_target_pairs={{0,32},{8,104},{16,48},{24,120},{32,64},{40,8},{48,80},{56,24},{64... | collective-permute-start | bytes 294920 | tf_op jit(solution)/shard_map/ppermute | solution.py:164
  27.7 7.4 %collective-permute-start.4 = (bf16[2,192,256]{2,1,0:T(8,128)(2,1)S(1)}, bf16[2,192,256]{2,1,0:T(8,128)(2,1)S(1)}, u32[]{:S(2)}, u32[]{:S(2)}) collective-permute-start(bf16[2,192,256]{2,1,0:T(8,128)(2,1)S(1)} %collective-permute-done.3.refs_3_), channel_id=1, source_target_pairs={{0,8},{8,0},{1,9},{9,1},{2,10},{10,2},{3,11},{11,3},{4,12},{12,4},... | collective-permute-start | bytes 589832 | tf_op jit(solution)/shard_map/ppermute | solution.py:157
  27.7 7.5 %copy-start.9 = (bf16[2,192,256]{2,1,0:T(8,128)(2,1)}, bf16[2,192,256]{2,1,0:T(8,128)(2,1)S(1)}, u32[]{:S(2)}) copy-start(bf16[2,192,256]{2,1,0:T(8,128)(2,1)S(1)} %collective-permute-done.1.refs_1_) | copy-start | bytes 589828
  27.7 7.4 %collective-permute-start.2 = (bf16[2,192,256]{2,1,0:T(8,128)(2,1)S(1)}, bf16[2,192,256]{2,1,0:T(8,128)(2,1)S(1)}, u32[]{:S(2)}, u32[]{:S(2)}) collective-permute-start(bf16[2,192,256]{2,1,0:T(8,128)(2,1)S(1)} %collective-permute-done.1.refs_1_), channel_id=1, source_target_pairs={{0,8},{8,0},{1,9},{9,1},{2,10},{10,2},{3,11},{11,3},{4,12},{12,4},... | collective-permute-start | bytes 589832 | tf_op jit(solution)/shard_map/ppermute | solution.py:157
  28.3 6.8 %copy-start.10 = (bf16[2,192,256]{2,1,0:T(8,128)(2,1)}, bf16[2,192,256]{2,1,0:T(8,128)(2,1)S(1)}, u32[]{:S(2)}) copy-start(bf16[2,192,256]{2,1,0:T(8,128)(2,1)S(1)} %collective-permute-done.5.refs_5_) | copy-start | bytes 589828
  28.4 6.7 %collective-permute-start.6 = (bf16[2,192,256]{2,1,0:T(8,128)(2,1)S(1)}, bf16[2,192,256]{2,1,0:T(8,128)(2,1)S(1)}, u32[]{:S(2)}, u32[]{:S(2)}) collective-permute-start(bf16[2,192,256]{2,1,0:T(8,128)(2,1)S(1)} %collective-permute-done.5.refs_5_), channel_id=1, source_target_pairs={{0,8},{8,0},{1,9},{9,1},{2,10},{10,2},{3,11},{11,3},{4,12},{12,4},... | collective-permute-start | bytes 589832 | tf_op jit(solution)/shard_map/ppermute | solution.py:157
  31.5 3.6 %copy-start.14 = (bf16[192,256]{1,0:T(8,128)(2,1)}, bf16[192,256]{1,0:T(8,128)(2,1)S(1)}, u32[]{:S(2)}) copy-start(bf16[192,256]{1,0:T(8,128)(2,1)S(1)} %collective-permute-done.7.refs_7_) | copy-start | bytes 294916
  31.5 3.5 %collective-permute-start.8 = (bf16[192,256]{1,0:T(8,128)(2,1)S(1)}, bf16[192,256]{1,0:T(8,128)(2,1)S(1)}, u32[]{:S(2)}, u32[]{:S(2)}) collective-permute-start(bf16[192,256]{1,0:T(8,128)(2,1)S(1)} %collective-permute-done.7.refs_7_), channel_id=1, source_target_pairs={{0,8},{8,0},{1,9},{9,1},{2,10},{10,2},{3,11},{11,3},{4,12},{12,4},... | collective-permute-start | bytes 294920 | tf_op jit(solution)/shard_map/ppermute | solution.py:157
  35.1 0.6 copy-start.15
  35.1 0.7 copy-start.11
  35.1 0.8 copy-start.12
  35.1 0.8 copy-start.13
  35.9 1.2 %copy-start.1 = (bf16[16,208,256]{2,1,0:T(8,128)(2,1)}, bf16[16,208,256]{2,1,0:T(8,128)(2,1)S(1)}, u32[]{:S(2)}) copy-start(bf16[16,208,256]{2,1,0:T(8,128)(2,1)S(1)} %all-to-all-done.t_ref) | copy-start | bytes 5111812
  52.8 4.0 %collective-permute-start.11 = (f32[16,256]{1,0:T(8,128)}, f32[16,256]{1,0:T(8,128)S(1)}, u32[]{:S(2)}, u32[]{:S(2)}) collective-permute-start(f32[16,256]{1,0:T(8,128)} %get-tuple-element.16), channel_id=1, source_target_pairs={{0,6},{2,0},{4,2},{6,4},{1,7},{3,1},{5,3},{7,5},{8,14},{10,8},{12,... | collective-permute-start | bytes 49160 | tf_op jit(solution)/shard_map/ppermute | solution.py:172
  55.7 4.3 %collective-permute-start.10 = (f32[16,256]{1,0:T(8,128)}, f32[16,256]{1,0:T(8,128)S(1)}, u32[]{:S(2)}, u32[]{:S(2)}) collective-permute-start(f32[16,256]{1,0:T(8,128)} %get-tuple-element.16), channel_id=1, source_target_pairs={{0,4},{2,6},{4,0},{6,2},{1,5},{3,7},{5,1},{7,3},{8,12},{10,14},{12... | collective-permute-start | bytes 49160 | tf_op jit(solution)/shard_map/ppermute | solution.py:172
  56.3 4.0 %collective-permute-start.9 = (f32[16,256]{1,0:T(8,128)}, f32[16,256]{1,0:T(8,128)S(1)}, u32[]{:S(2)}, u32[]{:S(2)}) collective-permute-start(f32[16,256]{1,0:T(8,128)} %get-tuple-element.16), channel_id=1, source_target_pairs={{0,2},{2,4},{4,6},{6,0},{1,3},{3,5},{5,7},{7,1},{8,10},{10,12},{12... | collective-permute-start | bytes 49160 | tf_op jit(solution)/shard_map/ppermute | solution.py:172
  61.0 7.0 %copy-start.4 = (f32[16,256]{1,0:T(8,128)}, f32[16,256]{1,0:T(8,128)S(1)}, u32[]{:S(2)}) copy-start(f32[16,256]{1,0:T(8,128)S(1)} %add_add_fusion.d0_ref) | copy-start | bytes 49156
  61.0 3.8 %collective-permute-start.14 = (f32[16,256]{1,0:T(8,128)S(1)}, f32[16,256]{1,0:T(8,128)S(1)}, u32[]{:S(2)}, u32[]{:S(2)}) collective-permute-start(f32[16,256]{1,0:T(8,128)S(1)} %add_add_fusion.d0_ref), channel_id=1, source_target_pairs={{0,129},{128,0},{1,128},{129,1},{2,131},{130,2},{3,130},{131,3},{4... | collective-permute-start | bytes 49160 | tf_op jit(solution)/shard_map/ppermute | solution.py:172
  63.7 4.1 %collective-permute-start.13 = (f32[16,256]{1,0:T(8,128)S(1)}, f32[16,256]{1,0:T(8,128)S(1)}, u32[]{:S(2)}, u32[]{:S(2)}) collective-permute-start(f32[16,256]{1,0:T(8,128)S(1)} %add_add_fusion.d0_ref), channel_id=1, source_target_pairs={{0,1},{128,129},{1,0},{129,128},{2,3},{130,131},{3,2},{131,130},{4... | collective-permute-start | bytes 49160 | tf_op jit(solution)/shard_map/ppermute | solution.py:172
  64.2 3.8 %collective-permute-start.12 = (f32[16,256]{1,0:T(8,128)S(1)}, f32[16,256]{1,0:T(8,128)S(1)}, u32[]{:S(2)}, u32[]{:S(2)}) collective-permute-start(f32[16,256]{1,0:T(8,128)S(1)} %add_add_fusion.d0_ref), channel_id=1, source_target_pairs={{0,128},{128,1},{1,129},{129,0},{2,130},{130,3},{3,131},{131,2},{4... | collective-permute-start | bytes 49160 | tf_op jit(solution)/shard_map/ppermute | solution.py:172
  64.8 3.2 %copy-start.6 = (f32[16,256]{1,0:T(8,128)}, f32[16,256]{1,0:T(8,128)S(1)}, u32[]{:S(2)}) copy-start(f32[16,256]{1,0:T(8,128)S(1)} %collective-permute-done.14.d3_ref) | copy-start | bytes 49156
  67.7 0.6 copy-start.7
  68.0 0.6 copy-start.8
  74.8 5.0 %collective-permute-start.15 = (f32[8,16,256]{2,1,0:T(8,128)}, f32[8,16,256]{2,1,0:T(8,128)S(1)}, u32[]{:S(2)}, u32[]{:S(2)}) collective-permute-start(f32[8,16,256]{2,1,0:T(8,128)} %get-tuple-element.20), channel_id=1, source_target_pairs={{0,8},{8,0},{1,9},{9,1},{2,10},{10,2},{3,11},{11,3},{4,12},{12,4},... | collective-permute-start | bytes 393224 | tf_op jit(solution)/shard_map/ppermute | solution.py:157
  94.7 0.7 copy-start
  95.7 3.0 %collective-permute-start.16 = (f32[2,128]{1,0:T(2,128)S(1)}, f32[2,128]{1,0:T(2,128)S(1)}, u32[]{:S(2)}, u32[]{:S(2)}) collective-permute-start(f32[2,128]{1,0:T(2,128)S(1)} %get-tuple-element.22), channel_id=1, source_target_pairs={{0,8},{8,0},{1,9},{9,1},{2,10},{10,2},{3,11},{11,3},{4,12},{12,4},... | collective-permute-start | bytes 3080 | tf_op jit(solution)/shard_map/ppermute | solution.py:157

commit v12 on v11

--- a/solution.py
+++ b/solution.py
@@ -6,18 +6,18 @@
 from jax.sharding import Mesh
 from jax.sharding import PartitionSpec as P
 
-AXES = ("xl", "z", "core", "y", "xh")
-SIZES = (2, 8, 2, 4, 2)
-ROWS = ("z", "core")
+AXES = ("xl", "zh", "zl", "core", "y", "xh")
+SIZES = (2, 4, 2, 2, 4, 2)
+ROWS = ("zh", "zl", "core")
 COLS = ("xl", "y", "xh")
 CHIPS = 128
-HALF = 8
+QUARTER = 4
 NR = 16
 NC = 16
 SEG = 256
 DIM = 192
 VEC = 16
-WIDE = DIM + VEC
+WIDE = DIM + 2 * VEC
 SCALE = 14.426950408889634
 UNSCALE = 4.5399929762484854e-05
 EPS = 1e-6
@@ -47,10 +47,13 @@
     e = e_ref[...].astype(F32)
     u = (e * lax.rsqrt(jnp.sum(e * e, axis=0, keepdims=True) + EPS)).astype(BF16)
     u_ref[...] = u
-    v = v_ref[...].astype(BF16)
+    v = v_ref[...]
+    high = v.astype(BF16)
+    low = (v - high.astype(F32)).astype(BF16)
     for k in range(NC):
         many_ref[k, 0:DIM, :] = u
-        many_ref[k, DIM:WIDE, :] = v
+        many_ref[k, DIM : DIM + VEC, :] = high
+        many_ref[k, DIM + VEC : WIDE, :] = low
 
 
 def affinity_kernel(pos_ref, t_ref, *refs):
@@ -76,7 +79,8 @@
         place(z + 4, 1 - core, lone[1][...])
         for t in range(NC):
             c_ref[t] = t_ref[t, 0:DIM, :].T
-            v_ref[t] = t_ref[t, DIM:WIDE, :]
+            high = t_ref[t, DIM : DIM + VEC, :].astype(F32)
+            v_ref[t] = high + t_ref[t, DIM + VEC : WIDE, :].astype(F32)
         acc_ref[...] = jnp.zeros_like(acc_ref)
 
     for t in range(NC):
@@ -96,16 +100,19 @@
 
 
 def apply_kernel(pos_ref, d0_ref, d1_ref, d2_ref, d3_ref, v_ref, b_ref, *refs):
-    mine_ref, other_ref, own_ref, root_ref, w_ref = refs
-    core = pos_ref[0]
+    p_refs, (own_ref, root_ref, w_ref) = refs[0:4], refs[4:7]
+    core, low = pos_ref[0], lax.rem(pos_ref[2], 2)
     root_ref[...] = lax.rsqrt((d0_ref[...] + d2_ref[...]) + (d1_ref[...] + d3_ref[...]))
     own_ref[...] = root_ref[pl.ds(pos_ref[1], 1), :] * UNSCALE
     for t in range(NC):
-        w = v_ref[t].astype(F32) * root_ref[t : t + 1, :]
+        w = v_ref[t] * root_ref[t : t + 1, :]
         w_ref[:, t * SEG : (t + 1) * SEG] = w.astype(BF16)
-    for r in range(NR // 2):
-        for side, p_ref in ((core, mine_ref), (1 - core, other_ref)):
-            p_ref[r] = jnp.dot(w_ref[...], b_ref[r * 2 + side], preferred_element_type=F32)
+    for k, p_ref in enumerate(p_refs):
+        side = core if k % 2 == 0 else 1 - core
+        chip = low if k < 2 else 1 - low
+        for high in range(QUARTER):
+            rows = b_ref[high * 4 + chip * 2 + side]
+            p_ref[high] = jnp.dot(w_ref[...], rows, preferred_element_type=F32)
 
 
 def project_kernel(p_ref, own_ref, q_ref, gram_ref):
@@ -175,7 +182,7 @@
 
 
 def per_device(embeddings, vectors):
-    z, core = lax.axis_index("z"), lax.axis_index("core")
+    z, core = lax.axis_index(("zh", "zl")), lax.axis_index("core")
     position = jnp.stack([core, lax.axis_index(COLS), z])
     unit, unit_copies = pl.pallas_call(
         unit_kernel,
@@ -193,7 +200,7 @@
         out_shape=(
             pltpu.VMEM((NR, NC * SEG, SEG), BF16),
             shape(NC, SEG),
-            shape(NC, VEC, SEG, dtype=BF16),
+            shape(NC, VEC, SEG),
         ),
         in_specs=[smem()] + [vmem()] * 10,
         out_specs=(vmem(), vmem(), vmem()),
@@ -210,11 +217,11 @@
     )(position, columns, *pairs, four, across(four))
     degree = sum(ring_copies(degree, "y", False))
     degrees = ring_copies(degree, ("xl", "xh"), True)
-    mine, other, own = pl.pallas_call(
+    *parts, own = pl.pallas_call(
         apply_kernel,
-        out_shape=(shape(HALF, VEC, SEG), shape(HALF, VEC, SEG), shape(1, SEG)),
+        out_shape=(*[shape(QUARTER, VEC, SEG)] * 4, shape(1, SEG)),
         in_specs=[smem()] + [vmem()] * 6,
-        out_specs=(vmem(), vmem(), vmem()),
+        out_specs=(vmem(),) * 5,
         scratch_shapes=[
             pltpu.VMEM((NC, SEG), F32),
             pltpu.VMEM((VEC, NC * SEG), BF16),
@@ -222,7 +229,10 @@
         compiler_params=params(24),
         name="apply",
     )(position, *degrees, vector_columns, pltpu.with_memory_space_constraint(block, pltpu.VMEM))
-    product = to_all(mine + across(other), "z")
+    beside = lax.ppermute(parts[2], "zl", [(0, 1), (1, 0)])
+    corner = lax.ppermute(parts[3], ("zl", "core"), [(k, 3 - k) for k in range(4)])
+    product = (parts[0] + across(parts[1])) + (beside + corner)
+    product = to_all(product, "zh")
     projected, gram = pl.pallas_call(
         project_kernel,
         out_shape=(shape(VEC, SEG), shape(2, 128)),
@@ -230,7 +240,7 @@
         name="project",
     )(product, own)
     gram = jnp.broadcast_to(gram + across(gram), (CHIPS, 2, 128))
-    gram = to_all(gram, ("xl", "z", "y", "xh"))
+    gram = to_all(gram, ("xl", "zh", "zl", "y", "xh"))
     basis, triangle = pl.pallas_call(
         finish_kernel,
         out_shape=(shape(VEC, SEG), shape(VEC, VEC)),

time: 119 us -> 123 us (1.034)
  waiting for transfers between devices: 14.6 us -> 20.4 us
    ppermute x0 -> x2, waiting for transfers between devices: none -> 4.16 us  [the longest x1 2.53 us: per_device(): beside = lax.ppermute(parts[2], 'zl', [(0, 1), (1, 0)])]
    all_to_all x1, waiting for transfers between devices: 0.02 us -> 2.59 us  [to_all(): return lax.all_to_all(copies, axes, split_axis=0, concat_axis=0, tiled=True)]
    ppermute x6, starting transfers between devices: 7.81 us -> 5.76 us  [ring_copies(): lax.ppermute(a, axes, [(place(k), place(k + hops)) for k in range(4)])]
    ppermute x0 -> x2, starting transfers between devices: none -> 1.67 us  [the longest x1 1.67 us: per_device(): beside = lax.ppermute(parts[2], 'zl', [(0, 1), (1, 0)])]
  transfers between devices with their start and end apart: 18 -> 20, of which waited for: 11 -> 14; matrix products, arithmetic and copies ran while one was open for 1% -> 0% of each run, Pallas kernels for 0% -> 0%
where the time goes in v12:
time: 123 us
  starting transfers between devices  39 us (32%)
  blocking collectives  31.2 us (25%)
  Pallas kernels  26.8 us (22%)
  waiting for transfers between devices  20.4 us (17%)
  local copies, waits for them, and re-layouts  2.61 us (2%)
  other arithmetic  2.19 us (2%)
    all_to_all x2, blocking collectives, to_all(): return lax.all_to_all(copies, axes, split_axis=0, concat_axis=0, tiled=True)  31.2 us
    pallas_call x1, Pallas kernels, per_device(): pl.pallas_call(affinity_kernel, grid=(NC // 2,), out_shape=(pltpu.VMEM((N...  15.8 us
    ppermute x7, starting transfers between devices, across(): return lax.ppermute(a, 'core', [(0, 1), (1, 0)])  12.8 us
    ppermute x4, starting transfers between devices, along(): return lax.ppermute(a, ROWS, turns)  11 us
    all_to_all x1, starting transfers between devices, to_all(): return lax.all_to_all(copies, axes, split_axis=0, concat_axis=0, tiled=True)  7.72 us
    ppermute x6, waiting for transfers between devices, ring_copies(): lax.ppermute(a, axes, [(place(k), place(k + hops)) for k in range(4)])  6.85 us
    pallas_call x1, Pallas kernels, per_device(): pl.pallas_call(apply_kernel, out_shape=(*[shape(QUARTER, VEC, SEG)] * 4,...  6.1 us
    ppermute x6, starting transfers between devices, ring_copies(): lax.ppermute(a, axes, [(place(k), place(k + hops)) for k in range(4)])  5.76 us
  transfers between devices with their start and end apart: 20, of which 14 were waited for; matrix products, arithmetic and copies ran while one was open for 0% of the time, Pallas kernels for 0%

profile of v12, /device:TPU:1, one launch (start us, length us, event | category | flops | bytes accessed | tf_op | source)
XLA Modules:
  0.0 123.0 jit_solution(11559279081489134673)
XLA Ops:
  0.6 2.3 %unit.1 = (bf16[192,256]{1,0:T(8,128)(2,1)}, bf16[16,224,256]{2,1,0:T(8,128)(2,1)}) custom-call(bf16[192,256]{1,0:T(8,128)(2,1)} %bitcast.10, f32[16,256]{1,0:T(8,128)} %bitcast.13), custom_call_target="tpu_custom_call" | custom-call | tf_op jit(solution)/shard_map/unit/pallas_call | solution.py:187
  2.9 7.7 %all-to-all-start = ((bf16[16,224,256]{2,1,0:T(8,128)(2,1)}), bf16[16,224,256]{2,1,0:T(8,128)(2,1)S(1)}, u32[]{:S(2)}, u32[]{:S(2)}) async-start(bf16[16,224,256]{2,1,0:T(8,128)(2,1)} %get-tuple-element.16), calls=%async_computation | async-start | bytes 3670016 | tf_op jit(solution)/shard_map/all_to_all | solution.py:156
  10.7 0.0 copy-done.3
  10.7 1.0 collective-permute-start
  11.7 0.9 collective-permute-done
  12.7 6.1 %collective-permute-start.3 = (bf16[2,192,256]{2,1,0:T(8,128)(2,1)S(1)}, bf16[2,192,256]{2,1,0:T(8,128)(2,1)S(1)}, u32[]{:S(2)}, u32[]{:S(2)}) collective-permute-start(bf16[2,192,256]{2,1,0:T(8,128)(2,1)S(1)} %pad_maximum_fusion.refs_0_), channel_id=1, source_target_pairs={{0,32},{8,104},{16,48},{24,120},{32,64},{40,8},{48,80},{56,24},{64... | collective-permute-start | bytes 589832 | tf_op jit(solution)/shard_map/ppermute | solution.py:171
  18.8 0.7 collective-permute-start.1
  19.5 4.0 %collective-permute-done.3.refs_3_ = bf16[2,192,256]{2,1,0:T(8,128)(2,1)S(1)} collective-permute-done((bf16[2,192,256]{2,1,0:T(8,128)(2,1)S(1)}, bf16[2,192,256]{2,1,0:T(8,128)(2,1)S(1)}, u32[]{:S(2)}, u32[]{:S(2)}) %collective-permute-start.3) | collective-permute-done | bytes 196640 | tf_op jit(solution)/shard_map/ppermute | solution.py:171
  23.5 2.3 %collective-permute-start.5 = (bf16[2,192,256]{2,1,0:T(8,128)(2,1)S(1)}, bf16[2,192,256]{2,1,0:T(8,128)(2,1)S(1)}, u32[]{:S(2)}, u32[]{:S(2)}) collective-permute-start(bf16[2,192,256]{2,1,0:T(8,128)(2,1)S(1)} %collective-permute-done.3.refs_3_), channel_id=1, source_target_pairs={{0,16},{8,120},{16,32},{24,8},{32,48},{40,24},{48,64},{56,40},{64,... | collective-permute-start | bytes 589832 | tf_op jit(solution)/shard_map/ppermute | solution.py:171
  25.8 1.9 %collective-permute-start.7 = (bf16[192,256]{1,0:T(8,128)(2,1)S(1)}, bf16[192,256]{1,0:T(8,128)(2,1)S(1)}, u32[]{:S(2)}, u32[]{:S(2)}) collective-permute-start(bf16[192,256]{1,0:T(8,128)(2,1)S(1)} %slice_bitcast_fusion), channel_id=1, source_target_pairs={{0,32},{8,104},{16,48},{24,120},{32,64},{40,8},{48,80},{56,24},{64... | collective-permute-start | bytes 294920 | tf_op jit(solution)/shard_map/ppermute | solution.py:171
  27.7 0.0 collective-permute-start.4
  27.7 0.0 collective-permute-done.1.refs_1_
  27.8 0.5 collective-permute-start.2
  28.3 0.1 collective-permute-done.5.refs_5_
  28.4 2.7 %collective-permute-start.6 = (bf16[2,192,256]{2,1,0:T(8,128)(2,1)S(1)}, bf16[2,192,256]{2,1,0:T(8,128)(2,1)S(1)}, u32[]{:S(2)}, u32[]{:S(2)}) collective-permute-start(bf16[2,192,256]{2,1,0:T(8,128)(2,1)S(1)} %collective-permute-done.5.refs_5_), channel_id=1, source_target_pairs={{0,8},{8,0},{1,9},{9,1},{2,10},{10,2},{3,11},{11,3},{4,12},{12,4},... | collective-permute-start | bytes 589832 | tf_op jit(solution)/shard_map/ppermute | solution.py:164
  31.1 0.5 collective-permute-done.7.refs_7_
  31.6 2.6 %collective-permute-start.8 = (bf16[192,256]{1,0:T(8,128)(2,1)S(1)}, bf16[192,256]{1,0:T(8,128)(2,1)S(1)}, u32[]{:S(2)}, u32[]{:S(2)}) collective-permute-start(bf16[192,256]{1,0:T(8,128)(2,1)S(1)} %collective-permute-done.7.refs_7_), channel_id=1, source_target_pairs={{0,8},{8,0},{1,9},{9,1},{2,10},{10,2},{3,11},{11,3},{4,12},{12,4},... | collective-permute-start | bytes 294920 | tf_op jit(solution)/shard_map/ppermute | solution.py:164
  34.2 0.6 pad_add_fusion.pos_ref
  34.8 0.4 collective-permute-done.8.refs_8_
  35.1 0.0 collective-permute-done.4.refs_4_
  35.1 0.0 collective-permute-done.2.refs_2_
  35.1 0.0 copy-start.12
  35.1 0.0 collective-permute-done.6.refs_6_
  35.2 2.6 %all-to-all-done.t_ref = bf16[16,224,256]{2,1,0:T(8,128)(2,1)S(1)} async-done(((bf16[16,224,256]{2,1,0:T(8,128)(2,1)}), bf16[16,224,256]{2,1,0:T(8,128)(2,1)S(1)}, u32[]{:S(2)}, u32[]{:S(2)}) %all-to-all-start) | async-done | bytes 1835040 | tf_op jit(solution)/shard_map/all_to_all | solution.py:156
  37.8 0.0 copy-done.10
  37.8 0.0 copy-done.14
  37.8 0.0 copy-done.15
  37.8 0.0 copy-done.11
  37.8 0.0 copy-done.12
  37.8 0.0 copy-done.13
  37.8 0.0 copy-start.1
  37.8 1.2 %copy-done.1 = bf16[16,224,256]{2,1,0:T(8,128)(2,1)} copy-done((bf16[16,224,256]{2,1,0:T(8,128)(2,1)}, bf16[16,224,256]{2,1,0:T(8,128)(2,1)S(1)}, u32[]{:S(2)}) %copy-start.1) | copy-done | bytes 1835032
  39.1 15.8 %affinity.1 = (bf16[16,4096,256]{2,1,0:T(8,128)(2,1)S(1)}, f32[16,256]{1,0:T(8,128)}, f32[16,16,256]{2,1,0:T(8,128)}) custom-call(s32[3]{0:T(128)} %pad_add_fusion.pos_ref, bf16[16,224,256]{2,1,0:T(8,128)(2,1)} %copy-done.1, bf16[2,192,256]{2,1,0:T(8,128)(2,1)} %copy-done.2, bf16[2,192,256]{2,1,0:T(8,128)(2,1)} %copy-done.9, ...), custom_call_target="tpu_custom_call" | custom-call | flops 8589934592 | bytes 33554432 | tf_op jit(solution)/shard_map/affinity/pallas_call | solution.py:197
  54.9 1.0 collective-permute-start.11
  55.9 1.1 collective-permute-start.10
  56.9 0.4 collective-permute-start.9
  57.3 0.3 collective-permute-done.11
  57.7 2.5 %collective-permute-done.10 = f32[16,256]{1,0:T(8,128)S(1)} collective-permute-done((f32[16,256]{1,0:T(8,128)}, f32[16,256]{1,0:T(8,128)S(1)}, u32[]{:S(2)}, u32[]{:S(2)}) %collective-permute-start.10) | collective-permute-done | bytes 16416 | tf_op jit(solution)/shard_map/ppermute | solution.py:179
  60.2 0.8 collective-permute-done.9
  60.9 0.7 add_add_fusion.1.d0_ref
  61.7 2.2 %collective-permute-start.14 = (f32[16,256]{1,0:T(8,128)S(1)}, f32[16,256]{1,0:T(8,128)S(1)}, u32[]{:S(2)}, u32[]{:S(2)}) collective-permute-start(f32[16,256]{1,0:T(8,128)S(1)} %add_add_fusion.1.d0_ref), channel_id=1, source_target_pairs={{0,129},{128,0},{1,128},{129,1},{2,131},{130,2},{3,130},{131,3},{4... | collective-permute-start | bytes 49160 | tf_op jit(solution)/shard_map/ppermute | solution.py:179
  63.8 0.6 collective-permute-start.13
  64.4 0.6 collective-permute-start.12
  65.0 0.0 collective-permute-done.14.d3_ref
  65.0 2.9 %collective-permute-done.13.d2_ref = f32[16,256]{1,0:T(8,128)S(1)} collective-permute-done((f32[16,256]{1,0:T(8,128)S(1)}, f32[16,256]{1,0:T(8,128)S(1)}, u32[]{:S(2)}, u32[]{:S(2)}) %collective-permute-start.13) | collective-permute-done | bytes 16416 | tf_op jit(solution)/shard_map/ppermute | solution.py:179
  67.9 0.3 collective-permute-done.12.d1_ref
  68.2 0.0 copy-done.6
  68.2 0.3 copy-done.7
  68.5 0.3 copy-done.8
  68.8 6.1 %apply.1 = (f32[4,16,256]{2,1,0:T(8,128)}, f32[4,16,256]{2,1,0:T(8,128)}, f32[4,16,256]{2,1,0:T(8,128)}, f32[4,16,256]{2,1,0:T(8,128)}, f32[1,256]{1,0:T(1,128)}) custom-call(s32[3]{0:T(128)} %pad_add_fusion.pos_ref, f32[16,256]{1,0:T(8,128)} %copy-done.4, f32[16,256]{1,0:T(8,128)} %copy-done.8, f32[16,256]{1,0:T(8,128)} %copy-done.7, f32[16,256]{1,0:T(8,128)} %copy-done.6, ...), custom_call_target="tpu_custom_call" | custom-call | tf_op jit(solution)/shard_map/apply/pallas_call | solution.py:220
  74.9 4.1 %collective-permute-start.15 = (f32[4,16,256]{2,1,0:T(8,128)}, f32[4,16,256]{2,1,0:T(8,128)S(1)}, u32[]{:S(2)}, u32[]{:S(2)}) collective-permute-start(f32[4,16,256]{2,1,0:T(8,128)} %get-tuple-element.22), channel_id=1, source_target_pairs={{0,8},{8,0},{1,9},{9,1},{2,10},{10,2},{3,11},{11,3},{4,12},{12,4},... | collective-permute-start | bytes 196616 | tf_op jit(solution)/shard_map/ppermute | solution.py:164
  79.0 1.7 %collective-permute-start.16 = (f32[4,16,256]{2,1,0:T(8,128)}, f32[4,16,256]{2,1,0:T(8,128)S(1)}, u32[]{:S(2)}, u32[]{:S(2)}) collective-permute-start(f32[4,16,256]{2,1,0:T(8,128)} %get-tuple-element.23), channel_id=1, source_target_pairs={{0,16},{16,0},{1,17},{17,1},{2,18},{18,2},{3,19},{19,3},{4,20},{20... | collective-permute-start | bytes 196616 | tf_op jit(solution)/shard_map/ppermute | solution.py:232
  80.7 0.0 collective-permute-start.17
  80.7 0.0 collective-permute-done.15
  80.7 2.5 %collective-permute-done.16 = f32[4,16,256]{2,1,0:T(8,128)S(1)} collective-permute-done((f32[4,16,256]{2,1,0:T(8,128)}, f32[4,16,256]{2,1,0:T(8,128)S(1)}, u32[]{:S(2)}, u32[]{:S(2)}) %collective-permute-start.16) | collective-permute-done | bytes 65568 | tf_op jit(solution)/shard_map/ppermute | solution.py:232
  83.2 1.6 %collective-permute-done.17 = f32[4,16,256]{2,1,0:T(8,128)S(1)} collective-permute-done((f32[4,16,256]{2,1,0:T(8,128)}, f32[4,16,256]{2,1,0:T(8,128)S(1)}, u32[]{:S(2)}, u32[]{:S(2)}) %collective-permute-start.17) | collective-permute-done | bytes 65568 | tf_op jit(solution)/shard_map/ppermute | solution.py:233
  84.8 0.9 add_add_fusion
  85.7 14.5 %all_to_all.15.p_ref = f32[4,16,256]{2,1,0:T(8,128)S(1)} all-to-all(f32[4,16,256]{2,1,0:T(8,128)S(1)} %add_add_fusion), channel_id=1, replica_groups=mesh['xl'=2,'zh'=4,'zl'=2,'core'=2,'y'=4,'xh'=2] {'zh'}, dimensions={0} | all-to-all | bytes 131072 | tf_op jit(solution)/shard_map/all_to_all | solution.py:156
  100.1 0.7 copy-done
  100.8 0.3 project.1
  101.1 1.9 %collective-permute-start.18 = (f32[2,128]{1,0:T(2,128)S(1)}, f32[2,128]{1,0:T(2,128)S(1)}, u32[]{:S(2)}, u32[]{:S(2)}) collective-permute-start(f32[2,128]{1,0:T(2,128)S(1)} %get-tuple-element.26), channel_id=1, source_target_pairs={{0,8},{8,0},{1,9},{9,1},{2,10},{10,2},{3,11},{11,3},{4,12},{12,4},... | collective-permute-start | bytes 3080 | tf_op jit(solution)/shard_map/ppermute | solution.py:164
  103.1 0.8 collective-permute-done.18
  103.9 16.8 %all_to_all.16.gram_ref = f32[128,2,128]{2,1,0:T(2,128)S(1)} all-to-all(f32[128,2,128]{2,1,0:T(2,128)S(1)} %broadcast_in_dim.3), channel_id=1, replica_groups=mesh['xl'=2,'zh'=4,'zl'=2,'core'=2,'y'=4,'xh'=2] {'xl','zh','zl','y','xh'}, dimensions={0} | all-to-all | bytes 262144 | tf_op jit(solution)/shard_map/all_to_all | solution.py:156
  120.7 2.3 %finish.1 = (f32[16,256]{1,0:T(8,128)}, f32[16,16]{1,0:T(8,128)}) custom-call(f32[128,2,128]{2,1,0:T(2,128)S(1)} %all_to_all.16.gram_ref, f32[16,256]{1,0:T(8,128)S(1)} %get-tuple-element.27.q_ref), custom_call_target="tpu_custom_call" | custom-call | tf_op jit(solution)/shard_map/finish/pallas_call | solution.py:244
  (22 shorter events, 0.1 us)
Async XLA Ops:
  2.9 7.7 %copy-start.3 = (bf16[192,256]{1,0:T(8,128)(2,1)S(1)}, bf16[192,256]{1,0:T(8,128)(2,1)}, u32[]{:S(2)}) copy-start(bf16[192,256]{1,0:T(8,128)(2,1)} %get-tuple-element.17) | copy-start | bytes 294916
  2.9 34.8 %all-to-all-start = ((bf16[16,224,256]{2,1,0:T(8,128)(2,1)}), bf16[16,224,256]{2,1,0:T(8,128)(2,1)S(1)}, u32[]{:S(2)}, u32[]{:S(2)}) async-start(bf16[16,224,256]{2,1,0:T(8,128)(2,1)} %get-tuple-element.16), calls=%async_computation | async-start | bytes 3670016 | tf_op jit(solution)/shard_map/all_to_all | solution.py:156
  10.7 2.0 %collective-permute-start = (bf16[192,256]{1,0:T(8,128)(2,1)S(1)}, bf16[192,256]{1,0:T(8,128)(2,1)S(1)}, u32[]{:S(2)}, u32[]{:S(2)}) collective-permute-start(bf16[192,256]{1,0:T(8,128)(2,1)S(1)} %copy-done.3), channel_id=1, source_target_pairs={{0,8},{8,0},{1,9},{9,1},{2,10},{10,2},{3,11},{11,3},{4,12},{12,4},... | collective-permute-start | bytes 294920 | tf_op jit(solution)/shard_map/ppermute | solution.py:164
  12.7 25.1 %copy-start.2 = (bf16[2,192,256]{2,1,0:T(8,128)(2,1)}, bf16[2,192,256]{2,1,0:T(8,128)(2,1)S(1)}, u32[]{:S(2)}) copy-start(bf16[2,192,256]{2,1,0:T(8,128)(2,1)S(1)} %pad_maximum_fusion.refs_0_) | copy-start | bytes 589828
  12.7 10.8 %collective-permute-start.3 = (bf16[2,192,256]{2,1,0:T(8,128)(2,1)S(1)}, bf16[2,192,256]{2,1,0:T(8,128)(2,1)S(1)}, u32[]{:S(2)}, u32[]{:S(2)}) collective-permute-start(bf16[2,192,256]{2,1,0:T(8,128)(2,1)S(1)} %pad_maximum_fusion.refs_0_), channel_id=1, source_target_pairs={{0,32},{8,104},{16,48},{24,120},{32,64},{40,8},{48,80},{56,24},{64... | collective-permute-start | bytes 589832 | tf_op jit(solution)/shard_map/ppermute | solution.py:171
  18.8 8.9 %collective-permute-start.1 = (bf16[2,192,256]{2,1,0:T(8,128)(2,1)S(1)}, bf16[2,192,256]{2,1,0:T(8,128)(2,1)S(1)}, u32[]{:S(2)}, u32[]{:S(2)}) collective-permute-start(bf16[2,192,256]{2,1,0:T(8,128)(2,1)S(1)} %pad_maximum_fusion.refs_0_), channel_id=1, source_target_pairs={{0,16},{8,120},{16,32},{24,8},{32,48},{40,24},{48,64},{56,40},{64,... | collective-permute-start | bytes 589832 | tf_op jit(solution)/shard_map/ppermute | solution.py:171
  23.5 14.2 %copy-start.5 = (bf16[2,192,256]{2,1,0:T(8,128)(2,1)}, bf16[2,192,256]{2,1,0:T(8,128)(2,1)S(1)}, u32[]{:S(2)}) copy-start(bf16[2,192,256]{2,1,0:T(8,128)(2,1)S(1)} %collective-permute-done.3.refs_3_) | copy-start | bytes 589828
  23.5 4.9 %collective-permute-start.5 = (bf16[2,192,256]{2,1,0:T(8,128)(2,1)S(1)}, bf16[2,192,256]{2,1,0:T(8,128)(2,1)S(1)}, u32[]{:S(2)}, u32[]{:S(2)}) collective-permute-start(bf16[2,192,256]{2,1,0:T(8,128)(2,1)S(1)} %collective-permute-done.3.refs_3_), channel_id=1, source_target_pairs={{0,16},{8,120},{16,32},{24,8},{32,48},{40,24},{48,64},{56,40},{64,... | collective-permute-start | bytes 589832 | tf_op jit(solution)/shard_map/ppermute | solution.py:171
  25.8 5.8 %collective-permute-start.7 = (bf16[192,256]{1,0:T(8,128)(2,1)S(1)}, bf16[192,256]{1,0:T(8,128)(2,1)S(1)}, u32[]{:S(2)}, u32[]{:S(2)}) collective-permute-start(bf16[192,256]{1,0:T(8,128)(2,1)S(1)} %slice_bitcast_fusion), channel_id=1, source_target_pairs={{0,32},{8,104},{16,48},{24,120},{32,64},{40,8},{48,80},{56,24},{64... | collective-permute-start | bytes 294920 | tf_op jit(solution)/shard_map/ppermute | solution.py:171
  27.7 7.4 %collective-permute-start.4 = (bf16[2,192,256]{2,1,0:T(8,128)(2,1)S(1)}, bf16[2,192,256]{2,1,0:T(8,128)(2,1)S(1)}, u32[]{:S(2)}, u32[]{:S(2)}) collective-permute-start(bf16[2,192,256]{2,1,0:T(8,128)(2,1)S(1)} %collective-permute-done.3.refs_3_), channel_id=1, source_target_pairs={{0,8},{8,0},{1,9},{9,1},{2,10},{10,2},{3,11},{11,3},{4,12},{12,4},... | collective-permute-start | bytes 589832 | tf_op jit(solution)/shard_map/ppermute | solution.py:164
  27.7 10.0 %copy-start.9 = (bf16[2,192,256]{2,1,0:T(8,128)(2,1)}, bf16[2,192,256]{2,1,0:T(8,128)(2,1)S(1)}, u32[]{:S(2)}) copy-start(bf16[2,192,256]{2,1,0:T(8,128)(2,1)S(1)} %collective-permute-done.1.refs_1_) | copy-start | bytes 589828
  27.8 7.4 %collective-permute-start.2 = (bf16[2,192,256]{2,1,0:T(8,128)(2,1)S(1)}, bf16[2,192,256]{2,1,0:T(8,128)(2,1)S(1)}, u32[]{:S(2)}, u32[]{:S(2)}) collective-permute-start(bf16[2,192,256]{2,1,0:T(8,128)(2,1)S(1)} %collective-permute-done.1.refs_1_), channel_id=1, source_target_pairs={{0,8},{8,0},{1,9},{9,1},{2,10},{10,2},{3,11},{11,3},{4,12},{12,4},... | collective-permute-start | bytes 589832 | tf_op jit(solution)/shard_map/ppermute | solution.py:164
  28.4 9.4 %copy-start.10 = (bf16[2,192,256]{2,1,0:T(8,128)(2,1)}, bf16[2,192,256]{2,1,0:T(8,128)(2,1)S(1)}, u32[]{:S(2)}) copy-start(bf16[2,192,256]{2,1,0:T(8,128)(2,1)S(1)} %collective-permute-done.5.refs_5_) | copy-start | bytes 589828
  28.4 6.7 %collective-permute-start.6 = (bf16[2,192,256]{2,1,0:T(8,128)(2,1)S(1)}, bf16[2,192,256]{2,1,0:T(8,128)(2,1)S(1)}, u32[]{:S(2)}, u32[]{:S(2)}) collective-permute-start(bf16[2,192,256]{2,1,0:T(8,128)(2,1)S(1)} %collective-permute-done.5.refs_5_), channel_id=1, source_target_pairs={{0,8},{8,0},{1,9},{9,1},{2,10},{10,2},{3,11},{11,3},{4,12},{12,4},... | collective-permute-start | bytes 589832 | tf_op jit(solution)/shard_map/ppermute | solution.py:164
  31.6 6.2 %copy-start.14 = (bf16[192,256]{1,0:T(8,128)(2,1)}, bf16[192,256]{1,0:T(8,128)(2,1)S(1)}, u32[]{:S(2)}) copy-start(bf16[192,256]{1,0:T(8,128)(2,1)S(1)} %collective-permute-done.7.refs_7_) | copy-start | bytes 294916
  31.6 3.5 %collective-permute-start.8 = (bf16[192,256]{1,0:T(8,128)(2,1)S(1)}, bf16[192,256]{1,0:T(8,128)(2,1)S(1)}, u32[]{:S(2)}, u32[]{:S(2)}) collective-permute-start(bf16[192,256]{1,0:T(8,128)(2,1)S(1)} %collective-permute-done.7.refs_7_), channel_id=1, source_target_pairs={{0,8},{8,0},{1,9},{9,1},{2,10},{10,2},{3,11},{11,3},{4,12},{12,4},... | collective-permute-start | bytes 294920 | tf_op jit(solution)/shard_map/ppermute | solution.py:164
  35.1 2.7 %copy-start.15 = (bf16[192,256]{1,0:T(8,128)(2,1)}, bf16[192,256]{1,0:T(8,128)(2,1)S(1)}, u32[]{:S(2)}) copy-start(bf16[192,256]{1,0:T(8,128)(2,1)S(1)} %collective-permute-done.8.refs_8_) | copy-start | bytes 294916
  35.1 2.7 %copy-start.11 = (bf16[2,192,256]{2,1,0:T(8,128)(2,1)}, bf16[2,192,256]{2,1,0:T(8,128)(2,1)S(1)}, u32[]{:S(2)}) copy-start(bf16[2,192,256]{2,1,0:T(8,128)(2,1)S(1)} %collective-permute-done.4.refs_4_) | copy-start | bytes 589828
  35.1 2.7 %copy-start.12 = (bf16[2,192,256]{2,1,0:T(8,128)(2,1)}, bf16[2,192,256]{2,1,0:T(8,128)(2,1)S(1)}, u32[]{:S(2)}) copy-start(bf16[2,192,256]{2,1,0:T(8,128)(2,1)S(1)} %collective-permute-done.2.refs_2_) | copy-start | bytes 589828
  35.2 2.7 %copy-start.13 = (bf16[2,192,256]{2,1,0:T(8,128)(2,1)}, bf16[2,192,256]{2,1,0:T(8,128)(2,1)S(1)}, u32[]{:S(2)}) copy-start(bf16[2,192,256]{2,1,0:T(8,128)(2,1)S(1)} %collective-permute-done.6.refs_6_) | copy-start | bytes 589828
  37.8 1.3 %copy-start.1 = (bf16[16,224,256]{2,1,0:T(8,128)(2,1)}, bf16[16,224,256]{2,1,0:T(8,128)(2,1)S(1)}, u32[]{:S(2)}) copy-start(bf16[16,224,256]{2,1,0:T(8,128)(2,1)S(1)} %all-to-all-done.t_ref) | copy-start | bytes 5505028
  54.9 2.8 %collective-permute-start.11 = (f32[16,256]{1,0:T(8,128)}, f32[16,256]{1,0:T(8,128)S(1)}, u32[]{:S(2)}, u32[]{:S(2)}) collective-permute-start(f32[16,256]{1,0:T(8,128)} %get-tuple-element.18), channel_id=1, source_target_pairs={{0,6},{2,0},{4,2},{6,4},{1,7},{3,1},{5,3},{7,5},{8,14},{10,8},{12,... | collective-permute-start | bytes 49160 | tf_op jit(solution)/shard_map/ppermute | solution.py:179
  55.9 4.3 %collective-permute-start.10 = (f32[16,256]{1,0:T(8,128)}, f32[16,256]{1,0:T(8,128)S(1)}, u32[]{:S(2)}, u32[]{:S(2)}) collective-permute-start(f32[16,256]{1,0:T(8,128)} %get-tuple-element.18), channel_id=1, source_target_pairs={{0,4},{2,6},{4,0},{6,2},{1,5},{3,7},{5,1},{7,3},{8,12},{10,14},{12... | collective-permute-start | bytes 49160 | tf_op jit(solution)/shard_map/ppermute | solution.py:179
  56.9 4.0 %collective-permute-start.9 = (f32[16,256]{1,0:T(8,128)}, f32[16,256]{1,0:T(8,128)S(1)}, u32[]{:S(2)}, u32[]{:S(2)}) collective-permute-start(f32[16,256]{1,0:T(8,128)} %get-tuple-element.18), channel_id=1, source_target_pairs={{0,2},{2,4},{4,6},{6,0},{1,3},{3,5},{5,7},{7,1},{8,10},{10,12},{12... | collective-permute-start | bytes 49160 | tf_op jit(solution)/shard_map/ppermute | solution.py:179
  61.7 6.5 %copy-start.4 = (f32[16,256]{1,0:T(8,128)}, f32[16,256]{1,0:T(8,128)S(1)}, u32[]{:S(2)}) copy-start(f32[16,256]{1,0:T(8,128)S(1)} %add_add_fusion.1.d0_ref) | copy-start | bytes 49156
  61.7 3.3 %collective-permute-start.14 = (f32[16,256]{1,0:T(8,128)S(1)}, f32[16,256]{1,0:T(8,128)S(1)}, u32[]{:S(2)}, u32[]{:S(2)}) collective-permute-start(f32[16,256]{1,0:T(8,128)S(1)} %add_add_fusion.1.d0_ref), channel_id=1, source_target_pairs={{0,129},{128,0},{1,128},{129,1},{2,131},{130,2},{3,130},{131,3},{4... | collective-permute-start | bytes 49160 | tf_op jit(solution)/shard_map/ppermute | solution.py:179
  63.8 4.1 %collective-permute-start.13 = (f32[16,256]{1,0:T(8,128)S(1)}, f32[16,256]{1,0:T(8,128)S(1)}, u32[]{:S(2)}, u32[]{:S(2)}) collective-permute-start(f32[16,256]{1,0:T(8,128)S(1)} %add_add_fusion.1.d0_ref), channel_id=1, source_target_pairs={{0,1},{128,129},{1,0},{129,128},{2,3},{130,131},{3,2},{131,130},{4... | collective-permute-start | bytes 49160 | tf_op jit(solution)/shard_map/ppermute | solution.py:179
  64.4 3.8 %collective-permute-start.12 = (f32[16,256]{1,0:T(8,128)S(1)}, f32[16,256]{1,0:T(8,128)S(1)}, u32[]{:S(2)}, u32[]{:S(2)}) collective-permute-start(f32[16,256]{1,0:T(8,128)S(1)} %add_add_fusion.1.d0_ref), channel_id=1, source_target_pairs={{0,128},{128,1},{1,129},{129,0},{2,130},{130,3},{3,131},{131,2},{4... | collective-permute-start | bytes 49160 | tf_op jit(solution)/shard_map/ppermute | solution.py:179
  65.0 3.2 %copy-start.6 = (f32[16,256]{1,0:T(8,128)}, f32[16,256]{1,0:T(8,128)S(1)}, u32[]{:S(2)}) copy-start(f32[16,256]{1,0:T(8,128)S(1)} %collective-permute-done.14.d3_ref) | copy-start | bytes 49156
  67.9 0.6 copy-start.7
  68.2 0.6 copy-start.8
  74.9 5.8 %collective-permute-start.15 = (f32[4,16,256]{2,1,0:T(8,128)}, f32[4,16,256]{2,1,0:T(8,128)S(1)}, u32[]{:S(2)}, u32[]{:S(2)}) collective-permute-start(f32[4,16,256]{2,1,0:T(8,128)} %get-tuple-element.22), channel_id=1, source_target_pairs={{0,8},{8,0},{1,9},{9,1},{2,10},{10,2},{3,11},{11,3},{4,12},{12,4},... | collective-permute-start | bytes 196616 | tf_op jit(solution)/shard_map/ppermute | solution.py:164
  79.0 4.2 %collective-permute-start.16 = (f32[4,16,256]{2,1,0:T(8,128)}, f32[4,16,256]{2,1,0:T(8,128)S(1)}, u32[]{:S(2)}, u32[]{:S(2)}) collective-permute-start(f32[4,16,256]{2,1,0:T(8,128)} %get-tuple-element.23), channel_id=1, source_target_pairs={{0,16},{16,0},{1,17},{17,1},{2,18},{18,2},{3,19},{19,3},{4,20},{20... | collective-permute-start | bytes 196616 | tf_op jit(solution)/shard_map/ppermute | solution.py:232
  80.7 4.2 %collective-permute-start.17 = (f32[4,16,256]{2,1,0:T(8,128)}, f32[4,16,256]{2,1,0:T(8,128)S(1)}, u32[]{:S(2)}, u32[]{:S(2)}) collective-permute-start(f32[4,16,256]{2,1,0:T(8,128)} %get-tuple-element.24), channel_id=1, source_target_pairs={{0,24},{8,16},{16,8},{24,0},{1,25},{9,17},{17,9},{25,1},{2,26},{10... | collective-permute-start | bytes 196616 | tf_op jit(solution)/shard_map/ppermute | solution.py:233
  100.1 0.7 copy-start
  101.1 2.7 %collective-permute-start.18 = (f32[2,128]{1,0:T(2,128)S(1)}, f32[2,128]{1,0:T(2,128)S(1)}, u32[]{:S(2)}, u32[]{:S(2)}) collective-permute-start(f32[2,128]{1,0:T(2,128)S(1)} %get-tuple-element.26), channel_id=1, source_target_pairs={{0,8},{8,0},{1,9},{9,1},{2,10},{10,2},{3,11},{11,3},{4,12},{12,4},... | collective-permute-start | bytes 3080 | tf_op jit(solution)/shard_map/ppermute | solution.py:164

commit v13 on v9

--- a/solution.py
+++ b/solution.py
@@ -17,7 +17,7 @@
 SEG = 256
 DIM = 192
 VEC = 16
-WIDE = DIM + 2 * VEC
+WIDE = DIM + VEC
 DEPTH = 6
 SCALE = 14.426950408889634
 UNSCALE = 4.5399929762484854e-05
@@ -48,13 +48,10 @@
     e = e_ref[...].astype(F32)
     u = (e * lax.rsqrt(jnp.sum(e * e, axis=0, keepdims=True) + EPS)).astype(BF16)
     u_ref[...] = u
-    v = v_ref[...]
-    high = v.astype(BF16)
-    low = (v - high.astype(F32)).astype(BF16)
+    v = v_ref[...].astype(BF16)
     for k in range(NC):
         many_ref[k, 0:DIM, :] = u
-        many_ref[k, DIM : DIM + VEC, :] = high
-        many_ref[k, DIM + VEC : WIDE, :] = low
+        many_ref[k, DIM:WIDE, :] = v
 
 
 def affinity_kernel(pos_ref, t_ref, *refs):
@@ -103,7 +100,7 @@
     core = pos_ref[0]
     own_ref[...] = root_ref[pl.ds(pos_ref[1], 1), :] * UNSCALE
     for t in range(NC):
-        v = t_ref[t, DIM : DIM + VEC, :].astype(F32) + t_ref[t, DIM + VEC : WIDE, :].astype(F32)
+        v = t_ref[t, DIM:WIDE, :].astype(F32)
         w = (v * root_ref[t : t + 1, :]).astype(BF16)
         fetch(t).wait()
         for r in range(NR // 2):

time: 119 us -> 117 us (0.983)
  starting transfers between devices: 34.1 us -> 36.7 us
  waiting for transfers between devices: 18.5 us -> 16 us
  blocking collectives: 32.6 us -> 30.8 us
    all_to_all x2, starting transfers between devices: 12.1 us -> 14.6 us  [to_all(): return lax.all_to_all(copies, axes, split_axis=0, concat_axis=0, tiled=True)]
    all_to_all x2, waiting for transfers between devices: 10.2 us -> 7.72 us  [to_all(): return lax.all_to_all(copies, axes, split_axis=0, concat_axis=0, tiled=True)]
    all_to_all x2, blocking collectives: 32.6 us -> 30.8 us  [to_all(): return lax.all_to_all(copies, axes, split_axis=0, concat_axis=0, tiled=True)]
where the time goes in v13:
time: 117 us
  starting transfers between devices  36.7 us (31%)
  Pallas kernels  32.4 us (28%)
  blocking collectives  30.8 us (26%)
  waiting for transfers between devices  16 us (14%)
    all_to_all x2, blocking collectives, to_all(): return lax.all_to_all(copies, axes, split_axis=0, concat_axis=0, tiled=True)  30.8 us
    pallas_call x1, Pallas kernels, per_device(): pl.pallas_call(affinity_kernel, grid=(NC // 2,), out_shape=(shape(NC, NR...  15.4 us
    all_to_all x2, starting transfers between devices, to_all(): return lax.all_to_all(copies, axes, split_axis=0, concat_axis=0, tiled=True)  14.6 us
    pallas_call x1, Pallas kernels, per_device(): pl.pallas_call(apply_kernel, out_shape=(shape(HALF, VEC, SEG), shape(HALF...  12.1 us
    ppermute x7, starting transfers between devices, across(): return lax.ppermute(a, 'core', [(0, 1), (1, 0)])  11.1 us
    ppermute x4, starting transfers between devices, along(): return lax.ppermute(a, ROWS, turns)  11 us
    all_to_all x2, waiting for transfers between devices, to_all(): return lax.all_to_all(copies, axes, split_axis=0, concat_axis=0, tiled=True)  7.72 us
    ppermute x4, waiting for transfers between devices, along(): return lax.ppermute(a, ROWS, turns)  4.65 us
  transfers between devices with their start and end apart: 13, of which 9 were waited for; matrix products, arithmetic and copies ran while one was open for 0% of the time, Pallas kernels for 0%

profile of v13, /device:TPU:1, one launch (start us, length us, event | category | flops | bytes accessed | tf_op | source)
XLA Modules:
  0.0 116.9 jit_solution(6179825244688264754)
XLA Ops:
  0.6 2.3 %unit.1 = (bf16[192,256]{1,0:T(8,128)(2,1)}, bf16[16,208,256]{2,1,0:T(8,128)(2,1)}) custom-call(bf16[192,256]{1,0:T(8,128)(2,1)} %bitcast.10, f32[16,256]{1,0:T(8,128)} %bitcast.13), custom_call_target="tpu_custom_call" | custom-call | tf_op jit(solution)/shard_map/unit/pallas_call | solution.py:174
  2.9 0.0 copy-start
  2.9 7.7 %all-to-all-start = ((bf16[16,208,256]{2,1,0:T(8,128)(2,1)}), bf16[16,208,256]{2,1,0:T(8,128)(2,1)S(1)}, u32[]{:S(2)}, u32[]{:S(2)}) async-start(bf16[16,208,256]{2,1,0:T(8,128)(2,1)} %get-tuple-element.13), calls=%async_computation | async-start | bytes 3407872 | tf_op jit(solution)/shard_map/all_to_all | solution.py:153
  10.6 0.0 copy-done
  10.6 1.0 collective-permute-start
  11.7 0.9 collective-permute-done
  12.6 6.1 %collective-permute-start.3 = (bf16[2,192,256]{2,1,0:T(8,128)(2,1)S(1)}, bf16[2,192,256]{2,1,0:T(8,128)(2,1)S(1)}, u32[]{:S(2)}, u32[]{:S(2)}) collective-permute-start(bf16[2,192,256]{2,1,0:T(8,128)(2,1)S(1)} %pad_maximum_fusion.refs_0_), channel_id=1, source_target_pairs={{0,32},{8,104},{16,48},{24,120},{32,64},{40,8},{48,80},{56,24},{64... | collective-permute-start | bytes 589832 | tf_op jit(solution)/shard_map/ppermute | solution.py:168
  18.7 0.7 collective-permute-start.1
  19.5 4.0 %collective-permute-done.3.refs_3_ = bf16[2,192,256]{2,1,0:T(8,128)(2,1)S(1)} collective-permute-done((bf16[2,192,256]{2,1,0:T(8,128)(2,1)S(1)}, bf16[2,192,256]{2,1,0:T(8,128)(2,1)S(1)}, u32[]{:S(2)}, u32[]{:S(2)}) %collective-permute-start.3) | collective-permute-done | bytes 196640 | tf_op jit(solution)/shard_map/ppermute | solution.py:168
  23.5 2.3 %collective-permute-start.5 = (bf16[2,192,256]{2,1,0:T(8,128)(2,1)S(1)}, bf16[2,192,256]{2,1,0:T(8,128)(2,1)S(1)}, u32[]{:S(2)}, u32[]{:S(2)}) collective-permute-start(bf16[2,192,256]{2,1,0:T(8,128)(2,1)S(1)} %collective-permute-done.3.refs_3_), channel_id=1, source_target_pairs={{0,16},{8,120},{16,32},{24,8},{32,48},{40,24},{48,64},{56,40},{64,... | collective-permute-start | bytes 589832 | tf_op jit(solution)/shard_map/ppermute | solution.py:168
  25.7 1.9 %collective-permute-start.7 = (bf16[192,256]{1,0:T(8,128)(2,1)S(1)}, bf16[192,256]{1,0:T(8,128)(2,1)S(1)}, u32[]{:S(2)}, u32[]{:S(2)}) collective-permute-start(bf16[192,256]{1,0:T(8,128)(2,1)S(1)} %slice_bitcast_fusion), channel_id=1, source_target_pairs={{0,32},{8,104},{16,48},{24,120},{32,64},{40,8},{48,80},{56,24},{64... | collective-permute-start | bytes 294920 | tf_op jit(solution)/shard_map/ppermute | solution.py:168
  27.7 0.0 collective-permute-start.4
  27.7 0.0 collective-permute-done.1.refs_1_
  27.7 0.5 collective-permute-start.2
  28.2 0.1 collective-permute-done.5.refs_5_
  28.3 2.7 %collective-permute-start.6 = (bf16[2,192,256]{2,1,0:T(8,128)(2,1)S(1)}, bf16[2,192,256]{2,1,0:T(8,128)(2,1)S(1)}, u32[]{:S(2)}, u32[]{:S(2)}) collective-permute-start(bf16[2,192,256]{2,1,0:T(8,128)(2,1)S(1)} %collective-permute-done.5.refs_5_), channel_id=1, source_target_pairs={{0,8},{8,0},{1,9},{9,1},{2,10},{10,2},{3,11},{11,3},{4,12},{12,4},... | collective-permute-start | bytes 589832 | tf_op jit(solution)/shard_map/ppermute | solution.py:161
  31.0 0.5 collective-permute-done.7.refs_7_
  31.5 2.6 %collective-permute-start.8 = (bf16[192,256]{1,0:T(8,128)(2,1)S(1)}, bf16[192,256]{1,0:T(8,128)(2,1)S(1)}, u32[]{:S(2)}, u32[]{:S(2)}) collective-permute-start(bf16[192,256]{1,0:T(8,128)(2,1)S(1)} %collective-permute-done.7.refs_7_), channel_id=1, source_target_pairs={{0,8},{8,0},{1,9},{9,1},{2,10},{10,2},{3,11},{11,3},{4,12},{12,4},... | collective-permute-start | bytes 294920 | tf_op jit(solution)/shard_map/ppermute | solution.py:161
  34.1 0.1 pad_add_fusion.1.pos_ref
  34.2 0.9 collective-permute-done.8.refs_8_
  35.1 0.0 collective-permute-done.4.refs_4_
  35.1 0.0 collective-permute-done.2.refs_2_
  35.1 0.0 collective-permute-done.6.refs_6_
  35.1 0.1 all-to-all-done.t_ref
  35.1 15.4 %affinity.1 = (bf16[16,4096,256]{2,1,0:T(8,128)(2,1)}, f32[16,16,256]{2,1,0:T(8,128)}) custom-call(s32[2]{0:T(128)S(1)} %pad_add_fusion.1.pos_ref, bf16[16,208,256]{2,1,0:T(8,128)(2,1)S(1)} %all-to-all-done.t_ref, bf16[2,192,256]{2,1,0:T(8,128)(2,1)S(1)} %pad_maximum_fusion.refs_0_, bf16[2,192,256]{2,1,0:T(8,128)(2,1)S(1)} %collective-permute-done.1.refs_1_, ...), custom_call_target="tpu_custom_call" | custom-call | flops 8589934592 | bytes 33554432 | tf_op jit(solution)/shard_map/affinity/pallas_call | solution.py:184
  50.6 6.9 %all-to-all-start.1 = ((f32[16,16,256]{2,1,0:T(8,128)}), f32[16,16,256]{2,1,0:T(8,128)S(1)}, u32[]{:S(2)}, u32[]{:S(2)}) async-start(f32[16,16,256]{2,1,0:T(8,128)} %get-tuple-element.15), calls=%async_computation.1 | async-start | bytes 524288 | tf_op jit(solution)/shard_map/all_to_all | solution.py:153
  57.5 0.1 pad_add_fusion.pos_ref
  57.6 7.7 %all-to-all-done.1.deg_ref = f32[16,16,256]{2,1,0:T(8,128)S(1)} async-done(((f32[16,16,256]{2,1,0:T(8,128)}), f32[16,16,256]{2,1,0:T(8,128)S(1)}, u32[]{:S(2)}, u32[]{:S(2)}) %all-to-all-start.1) | async-done | bytes 262176 | tf_op jit(solution)/shard_map/all_to_all | solution.py:153
  65.2 12.1 %apply.1 = (f32[8,16,256]{2,1,0:T(8,128)S(1)}, f32[8,16,256]{2,1,0:T(8,128)S(1)}, f32[1,256]{1,0:T(1,128)S(1)}) custom-call(s32[2]{0:T(128)S(1)} %pad_add_fusion.pos_ref, f32[16,16,256]{2,1,0:T(8,128)S(1)} %all-to-all-done.1.deg_ref, bf16[16,208,256]{2,1,0:T(8,128)(2,1)S(1)} %all-to-all-done.t_ref, bf16[16,4096,256]{2,1,0:T(8,128)(2,1)} %get-tuple-element.16.b_ref), custom_call_target="tpu_custom_call" | custom-call | tf_op jit(solution)/shard_map/apply/pallas_call | solution.py:198
  77.3 2.1 %collective-permute-start.9 = (f32[8,16,256]{2,1,0:T(8,128)S(1)}, f32[8,16,256]{2,1,0:T(8,128)S(1)}, u32[]{:S(2)}, u32[]{:S(2)}) collective-permute-start(f32[8,16,256]{2,1,0:T(8,128)S(1)} %get-tuple-element.18), channel_id=1, source_target_pairs={{0,8},{8,0},{1,9},{9,1},{2,10},{10,2},{3,11},{11,3},{4,12},{12,4},... | collective-permute-start | bytes 393224 | tf_op jit(solution)/shard_map/ppermute | solution.py:161
  79.5 1.0 collective-permute-done.9
  80.5 14.1 %all_to_all.20.p_ref = f32[8,16,256]{2,1,0:T(8,128)S(1)} all-to-all(f32[8,16,256]{2,1,0:T(8,128)S(1)} %add.14), channel_id=1, replica_groups=mesh['xl'=2,'z'=8,'core'=2,'y'=4,'xh'=2] {'z'}, dimensions={0} | all-to-all | bytes 262144 | tf_op jit(solution)/shard_map/all_to_all | solution.py:153
  94.6 0.3 project.1
  94.9 2.1 %collective-permute-start.10 = (f32[2,128]{1,0:T(2,128)S(1)}, f32[2,128]{1,0:T(2,128)S(1)}, u32[]{:S(2)}, u32[]{:S(2)}) collective-permute-start(f32[2,128]{1,0:T(2,128)S(1)} %get-tuple-element.20), channel_id=1, source_target_pairs={{0,8},{8,0},{1,9},{9,1},{2,10},{10,2},{3,11},{11,3},{4,12},{12,4},... | collective-permute-start | bytes 3080 | tf_op jit(solution)/shard_map/ppermute | solution.py:161
  97.0 0.8 collective-permute-done.10
  97.9 16.7 %all_to_all.21.gram_ref = f32[128,2,128]{2,1,0:T(2,128)S(1)} all-to-all(f32[128,2,128]{2,1,0:T(2,128)S(1)} %broadcast_in_dim.3), channel_id=1, replica_groups=mesh['xl'=2,'z'=8,'core'=2,'y'=4,'xh'=2] {'xl','z','y','xh'}, dimensions={0} | all-to-all | bytes 262144 | tf_op jit(solution)/shard_map/all_to_all | solution.py:153
  114.6 2.3 %finish.1 = (f32[16,256]{1,0:T(8,128)}, f32[16,16]{1,0:T(8,128)}) custom-call(f32[128,2,128]{2,1,0:T(2,128)S(1)} %all_to_all.21.gram_ref, f32[16,256]{1,0:T(8,128)S(1)} %get-tuple-element.21.q_ref), custom_call_target="tpu_custom_call" | custom-call | tf_op jit(solution)/shard_map/finish/pallas_call | solution.py:220
  (5 shorter events, 0.1 us)
Async XLA Ops:
  2.9 7.7 %copy-start = (bf16[192,256]{1,0:T(8,128)(2,1)S(1)}, bf16[192,256]{1,0:T(8,128)(2,1)}, u32[]{:S(2)}) copy-start(bf16[192,256]{1,0:T(8,128)(2,1)} %get-tuple-element.14) | copy-start | bytes 294916
  2.9 32.2 %all-to-all-start = ((bf16[16,208,256]{2,1,0:T(8,128)(2,1)}), bf16[16,208,256]{2,1,0:T(8,128)(2,1)S(1)}, u32[]{:S(2)}, u32[]{:S(2)}) async-start(bf16[16,208,256]{2,1,0:T(8,128)(2,1)} %get-tuple-element.13), calls=%async_computation | async-start | bytes 3407872 | tf_op jit(solution)/shard_map/all_to_all | solution.py:153
  10.6 2.0 %collective-permute-start = (bf16[192,256]{1,0:T(8,128)(2,1)S(1)}, bf16[192,256]{1,0:T(8,128)(2,1)S(1)}, u32[]{:S(2)}, u32[]{:S(2)}) collective-permute-start(bf16[192,256]{1,0:T(8,128)(2,1)S(1)} %copy-done), channel_id=1, source_target_pairs={{0,8},{8,0},{1,9},{9,1},{2,10},{10,2},{3,11},{11,3},{4,12},{12,4},... | collective-permute-start | bytes 294920 | tf_op jit(solution)/shard_map/ppermute | solution.py:161
  12.6 10.8 %collective-permute-start.3 = (bf16[2,192,256]{2,1,0:T(8,128)(2,1)S(1)}, bf16[2,192,256]{2,1,0:T(8,128)(2,1)S(1)}, u32[]{:S(2)}, u32[]{:S(2)}) collective-permute-start(bf16[2,192,256]{2,1,0:T(8,128)(2,1)S(1)} %pad_maximum_fusion.refs_0_), channel_id=1, source_target_pairs={{0,32},{8,104},{16,48},{24,120},{32,64},{40,8},{48,80},{56,24},{64... | collective-permute-start | bytes 589832 | tf_op jit(solution)/shard_map/ppermute | solution.py:168
  18.7 8.9 %collective-permute-start.1 = (bf16[2,192,256]{2,1,0:T(8,128)(2,1)S(1)}, bf16[2,192,256]{2,1,0:T(8,128)(2,1)S(1)}, u32[]{:S(2)}, u32[]{:S(2)}) collective-permute-start(bf16[2,192,256]{2,1,0:T(8,128)(2,1)S(1)} %pad_maximum_fusion.refs_0_), channel_id=1, source_target_pairs={{0,16},{8,120},{16,32},{24,8},{32,48},{40,24},{48,64},{56,40},{64,... | collective-permute-start | bytes 589832 | tf_op jit(solution)/shard_map/ppermute | solution.py:168
  23.5 4.9 %collective-permute-start.5 = (bf16[2,192,256]{2,1,0:T(8,128)(2,1)S(1)}, bf16[2,192,256]{2,1,0:T(8,128)(2,1)S(1)}, u32[]{:S(2)}, u32[]{:S(2)}) collective-permute-start(bf16[2,192,256]{2,1,0:T(8,128)(2,1)S(1)} %collective-permute-done.3.refs_3_), channel_id=1, source_target_pairs={{0,16},{8,120},{16,32},{24,8},{32,48},{40,24},{48,64},{56,40},{64,... | collective-permute-start | bytes 589832 | tf_op jit(solution)/shard_map/ppermute | solution.py:168
  25.7 5.8 %collective-permute-start.7 = (bf16[192,256]{1,0:T(8,128)(2,1)S(1)}, bf16[192,256]{1,0:T(8,128)(2,1)S(1)}, u32[]{:S(2)}, u32[]{:S(2)}) collective-permute-start(bf16[192,256]{1,0:T(8,128)(2,1)S(1)} %slice_bitcast_fusion), channel_id=1, source_target_pairs={{0,32},{8,104},{16,48},{24,120},{32,64},{40,8},{48,80},{56,24},{64... | collective-permute-start | bytes 294920 | tf_op jit(solution)/shard_map/ppermute | solution.py:168
  27.7 7.4 %collective-permute-start.4 = (bf16[2,192,256]{2,1,0:T(8,128)(2,1)S(1)}, bf16[2,192,256]{2,1,0:T(8,128)(2,1)S(1)}, u32[]{:S(2)}, u32[]{:S(2)}) collective-permute-start(bf16[2,192,256]{2,1,0:T(8,128)(2,1)S(1)} %collective-permute-done.3.refs_3_), channel_id=1, source_target_pairs={{0,8},{8,0},{1,9},{9,1},{2,10},{10,2},{3,11},{11,3},{4,12},{12,4},... | collective-permute-start | bytes 589832 | tf_op jit(solution)/shard_map/ppermute | solution.py:161
  27.7 7.4 %collective-permute-start.2 = (bf16[2,192,256]{2,1,0:T(8,128)(2,1)S(1)}, bf16[2,192,256]{2,1,0:T(8,128)(2,1)S(1)}, u32[]{:S(2)}, u32[]{:S(2)}) collective-permute-start(bf16[2,192,256]{2,1,0:T(8,128)(2,1)S(1)} %collective-permute-done.1.refs_1_), channel_id=1, source_target_pairs={{0,8},{8,0},{1,9},{9,1},{2,10},{10,2},{3,11},{11,3},{4,12},{12,4},... | collective-permute-start | bytes 589832 | tf_op jit(solution)/shard_map/ppermute | solution.py:161
  28.3 6.7 %collective-permute-start.6 = (bf16[2,192,256]{2,1,0:T(8,128)(2,1)S(1)}, bf16[2,192,256]{2,1,0:T(8,128)(2,1)S(1)}, u32[]{:S(2)}, u32[]{:S(2)}) collective-permute-start(bf16[2,192,256]{2,1,0:T(8,128)(2,1)S(1)} %collective-permute-done.5.refs_5_), channel_id=1, source_target_pairs={{0,8},{8,0},{1,9},{9,1},{2,10},{10,2},{3,11},{11,3},{4,12},{12,4},... | collective-permute-start | bytes 589832 | tf_op jit(solution)/shard_map/ppermute | solution.py:161
  31.5 3.5 %collective-permute-start.8 = (bf16[192,256]{1,0:T(8,128)(2,1)S(1)}, bf16[192,256]{1,0:T(8,128)(2,1)S(1)}, u32[]{:S(2)}, u32[]{:S(2)}) collective-permute-start(bf16[192,256]{1,0:T(8,128)(2,1)S(1)} %collective-permute-done.7.refs_7_), channel_id=1, source_target_pairs={{0,8},{8,0},{1,9},{9,1},{2,10},{10,2},{3,11},{11,3},{4,12},{12,4},... | collective-permute-start | bytes 294920 | tf_op jit(solution)/shard_map/ppermute | solution.py:161
  50.6 14.7 %all-to-all-start.1 = ((f32[16,16,256]{2,1,0:T(8,128)}), f32[16,16,256]{2,1,0:T(8,128)S(1)}, u32[]{:S(2)}, u32[]{:S(2)}) async-start(f32[16,16,256]{2,1,0:T(8,128)} %get-tuple-element.15), calls=%async_computation.1 | async-start | bytes 524288 | tf_op jit(solution)/shard_map/all_to_all | solution.py:153
  77.3 3.1 %collective-permute-start.9 = (f32[8,16,256]{2,1,0:T(8,128)S(1)}, f32[8,16,256]{2,1,0:T(8,128)S(1)}, u32[]{:S(2)}, u32[]{:S(2)}) collective-permute-start(f32[8,16,256]{2,1,0:T(8,128)S(1)} %get-tuple-element.18), channel_id=1, source_target_pairs={{0,8},{8,0},{1,9},{9,1},{2,10},{10,2},{3,11},{11,3},{4,12},{12,4},... | collective-permute-start | bytes 393224 | tf_op jit(solution)/shard_map/ppermute | solution.py:161
  94.9 3.0 %collective-permute-start.10 = (f32[2,128]{1,0:T(2,128)S(1)}, f32[2,128]{1,0:T(2,128)S(1)}, u32[]{:S(2)}, u32[]{:S(2)}) collective-permute-start(f32[2,128]{1,0:T(2,128)S(1)} %get-tuple-element.20), channel_id=1, source_target_pairs={{0,8},{8,0},{1,9},{9,1},{2,10},{10,2},{3,11},{11,3},{4,12},{12,4},... | collective-permute-start | bytes 3080 | tf_op jit(solution)/shard_map/ppermute | solution.py:161

commit v14 on v13

--- a/solution.py
+++ b/solution.py
@@ -56,7 +56,7 @@
 
 def affinity_kernel(pos_ref, t_ref, *refs):
     pairs, lone = refs[0:7], refs[7:9]
-    b_ref, deg_ref, s_ref = refs[9:12]
+    b_ref, deg_ref, s_ref, sum_ref = refs[9:13]
     z, core = pos_ref[0], pos_ref[1]
     step = pl.program_id(0)
 
@@ -85,8 +85,12 @@
             total = total + jnp.sum(tile.reshape(SEG // 8, 8, SEG), axis=0)
             b_ref[j, r * SEG : (r + 1) * SEG, :] = tile.astype(BF16)
         sums = jnp.sum(total, axis=0, keepdims=True) * UNSCALE
+        sum_ref[pl.ds(step * 2 + j, 1), :] = sums
+
+    @pl.when(step == NC // 2 - 1)
+    def _():
         for k in range(NC):
-            deg_ref[k, pl.ds(step * 2 + j, 1), :] = sums
+            deg_ref[k] = sum_ref[...].astype(BF16)
 
 
 def apply_kernel(pos_ref, deg_ref, t_ref, b_ref, mine_ref, other_ref, own_ref, root_ref, held_ref, sem_ref):
@@ -96,7 +100,7 @@
 
     for t in range(DEPTH):
         fetch(t).start()
-    root_ref[...] = lax.rsqrt(jnp.sum(deg_ref[...], axis=0))
+    root_ref[...] = lax.rsqrt(jnp.sum(deg_ref[...].astype(F32), axis=0))
     core = pos_ref[0]
     own_ref[...] = root_ref[pl.ds(pos_ref[1], 1), :] * UNSCALE
     for t in range(NC):
@@ -184,10 +188,10 @@
     block, degree = pl.pallas_call(
         affinity_kernel,
         grid=(NC // 2,),
-        out_shape=(shape(NC, NR * SEG, SEG, dtype=BF16), shape(NC, NC, SEG)),
+        out_shape=(shape(NC, NR * SEG, SEG, dtype=BF16), shape(NC, NC, SEG, dtype=BF16)),
         in_specs=[smem()] + [vmem()] * 10,
         out_specs=(pl.BlockSpec((2, NR * SEG, SEG), lambda i: (i, 0, 0)), vmem()),
-        scratch_shapes=[pltpu.VMEM((NR, SEG, DIM), BF16)],
+        scratch_shapes=[pltpu.VMEM((NR, SEG, DIM), BF16), pltpu.VMEM((NC, SEG), F32)],
         compiler_params=params(32),
         cost_estimate=pl.CostEstimate(
             flops=2 * 256 * 4096 * 4096, transcendentals=4096 * 4096, bytes_accessed=1 << 25

time: 117 us -> 117 us (level)
  no operation moved by 1% of the time
where the time goes in v14:
time: 117 us; the launch traced here: 116 us
  starting transfers between devices  36.5 us (31%)
  Pallas kernels  32.4 us (28%)
  blocking collectives  31.1 us (27%)
  waiting for transfers between devices  15.2 us (13%)
    all_to_all x2, blocking collectives, to_all(): return lax.all_to_all(copies, axes, split_axis=0, concat_axis=0, tiled=True)  31.1 us
    pallas_call x1, Pallas kernels, per_device(): pl.pallas_call(affinity_kernel, grid=(NC // 2,), out_shape=(shape(NC, NR...  15.5 us
    all_to_all x2, starting transfers between devices, to_all(): return lax.all_to_all(copies, axes, split_axis=0, concat_axis=0, tiled=True)  14.6 us
    pallas_call x1, Pallas kernels, per_device(): pl.pallas_call(apply_kernel, out_shape=(shape(HALF, VEC, SEG), shape(HALF...  12.1 us
    ppermute x4, starting transfers between devices, along(): return lax.ppermute(a, ROWS, turns)  11 us
    ppermute x7, starting transfers between devices, across(): return lax.ppermute(a, 'core', [(0, 1), (1, 0)])  10.8 us
    all_to_all x2, waiting for transfers between devices, to_all(): return lax.all_to_all(copies, axes, split_axis=0, concat_axis=0, tiled=True)  6.92 us
    ppermute x4, waiting for transfers between devices, along(): return lax.ppermute(a, ROWS, turns)  4.65 us
  transfers between devices with their start and end apart: 13, of which 9 were waited for; matrix products, arithmetic and copies ran while one was open for 0% of the time, Pallas kernels for 0%

profile of v14, /device:TPU:1, one launch (start us, length us, event | category | flops | bytes accessed | tf_op | source)
XLA Modules:
  0.0 116.2 jit_solution(4788844582212854220)
XLA Ops:
  0.6 2.3 %unit.1 = (bf16[192,256]{1,0:T(8,128)(2,1)}, bf16[16,208,256]{2,1,0:T(8,128)(2,1)}) custom-call(bf16[192,256]{1,0:T(8,128)(2,1)} %bitcast.10, f32[16,256]{1,0:T(8,128)} %bitcast.13), custom_call_target="tpu_custom_call" | custom-call | tf_op jit(solution)/shard_map/unit/pallas_call | solution.py:178
  2.9 0.0 copy-start
  2.9 7.7 %all-to-all-start = ((bf16[16,208,256]{2,1,0:T(8,128)(2,1)}), bf16[16,208,256]{2,1,0:T(8,128)(2,1)S(1)}, u32[]{:S(2)}, u32[]{:S(2)}) async-start(bf16[16,208,256]{2,1,0:T(8,128)(2,1)} %get-tuple-element.13), calls=%async_computation | async-start | bytes 3407872 | tf_op jit(solution)/shard_map/all_to_all | solution.py:157
  10.6 0.0 copy-done
  10.6 1.0 collective-permute-start
  11.7 0.9 collective-permute-done
  12.6 6.1 %collective-permute-start.3 = (bf16[2,192,256]{2,1,0:T(8,128)(2,1)S(1)}, bf16[2,192,256]{2,1,0:T(8,128)(2,1)S(1)}, u32[]{:S(2)}, u32[]{:S(2)}) collective-permute-start(bf16[2,192,256]{2,1,0:T(8,128)(2,1)S(1)} %pad_maximum_fusion.refs_0_), channel_id=1, source_target_pairs={{0,32},{8,104},{16,48},{24,120},{32,64},{40,8},{48,80},{56,24},{64... | collective-permute-start | bytes 589832 | tf_op jit(solution)/shard_map/ppermute | solution.py:172
  18.7 0.7 collective-permute-start.1
  19.5 4.0 %collective-permute-done.3.refs_3_ = bf16[2,192,256]{2,1,0:T(8,128)(2,1)S(1)} collective-permute-done((bf16[2,192,256]{2,1,0:T(8,128)(2,1)S(1)}, bf16[2,192,256]{2,1,0:T(8,128)(2,1)S(1)}, u32[]{:S(2)}, u32[]{:S(2)}) %collective-permute-start.3) | collective-permute-done | bytes 196640 | tf_op jit(solution)/shard_map/ppermute | solution.py:172
  23.5 2.3 %collective-permute-start.5 = (bf16[2,192,256]{2,1,0:T(8,128)(2,1)S(1)}, bf16[2,192,256]{2,1,0:T(8,128)(2,1)S(1)}, u32[]{:S(2)}, u32[]{:S(2)}) collective-permute-start(bf16[2,192,256]{2,1,0:T(8,128)(2,1)S(1)} %collective-permute-done.3.refs_3_), channel_id=1, source_target_pairs={{0,16},{8,120},{16,32},{24,8},{32,48},{40,24},{48,64},{56,40},{64,... | collective-permute-start | bytes 589832 | tf_op jit(solution)/shard_map/ppermute | solution.py:172
  25.7 1.9 %collective-permute-start.7 = (bf16[192,256]{1,0:T(8,128)(2,1)S(1)}, bf16[192,256]{1,0:T(8,128)(2,1)S(1)}, u32[]{:S(2)}, u32[]{:S(2)}) collective-permute-start(bf16[192,256]{1,0:T(8,128)(2,1)S(1)} %slice_bitcast_fusion), channel_id=1, source_target_pairs={{0,32},{8,104},{16,48},{24,120},{32,64},{40,8},{48,80},{56,24},{64... | collective-permute-start | bytes 294920 | tf_op jit(solution)/shard_map/ppermute | solution.py:172
  27.7 0.0 collective-permute-start.4
  27.7 0.0 collective-permute-done.1.refs_1_
  27.7 0.5 collective-permute-start.2
  28.2 0.1 collective-permute-done.5.refs_5_
  28.3 2.7 %collective-permute-start.6 = (bf16[2,192,256]{2,1,0:T(8,128)(2,1)S(1)}, bf16[2,192,256]{2,1,0:T(8,128)(2,1)S(1)}, u32[]{:S(2)}, u32[]{:S(2)}) collective-permute-start(bf16[2,192,256]{2,1,0:T(8,128)(2,1)S(1)} %collective-permute-done.5.refs_5_), channel_id=1, source_target_pairs={{0,8},{8,0},{1,9},{9,1},{2,10},{10,2},{3,11},{11,3},{4,12},{12,4},... | collective-permute-start | bytes 589832 | tf_op jit(solution)/shard_map/ppermute | solution.py:165
  31.0 0.5 collective-permute-done.7.refs_7_
  31.5 2.6 %collective-permute-start.8 = (bf16[192,256]{1,0:T(8,128)(2,1)S(1)}, bf16[192,256]{1,0:T(8,128)(2,1)S(1)}, u32[]{:S(2)}, u32[]{:S(2)}) collective-permute-start(bf16[192,256]{1,0:T(8,128)(2,1)S(1)} %collective-permute-done.7.refs_7_), channel_id=1, source_target_pairs={{0,8},{8,0},{1,9},{9,1},{2,10},{10,2},{3,11},{11,3},{4,12},{12,4},... | collective-permute-start | bytes 294920 | tf_op jit(solution)/shard_map/ppermute | solution.py:165
  34.1 0.1 pad_add_fusion.1.pos_ref
  34.2 0.9 collective-permute-done.8.refs_8_
  35.1 0.0 collective-permute-done.4.refs_4_
  35.1 0.0 collective-permute-done.2.refs_2_
  35.1 0.0 collective-permute-done.6.refs_6_
  35.1 0.1 all-to-all-done.t_ref
  35.1 15.5 %affinity.1 = (bf16[16,4096,256]{2,1,0:T(8,128)(2,1)}, bf16[16,16,256]{2,1,0:T(8,128)(2,1)}) custom-call(s32[2]{0:T(128)S(1)} %pad_add_fusion.1.pos_ref, bf16[16,208,256]{2,1,0:T(8,128)(2,1)S(1)} %all-to-all-done.t_ref, bf16[2,192,256]{2,1,0:T(8,128)(2,1)S(1)} %pad_maximum_fusion.refs_0_, bf16[2,192,256]{2,1,0:T(8,128)(2,1)S(1)} %collective-permute-done.1.refs_1_, ...), custom_call_target="tpu_custom_call" | custom-call | flops 8589934592 | bytes 33554432 | tf_op jit(solution)/shard_map/affinity/pallas_call | solution.py:188
  50.6 6.9 %all-to-all-start.1 = ((bf16[16,16,256]{2,1,0:T(8,128)(2,1)}), bf16[16,16,256]{2,1,0:T(8,128)(2,1)S(1)}, u32[]{:S(2)}, u32[]{:S(2)}) async-start(bf16[16,16,256]{2,1,0:T(8,128)(2,1)} %get-tuple-element.15), calls=%async_computation.1 | async-start | bytes 262144 | tf_op jit(solution)/shard_map/all_to_all | solution.py:157
  57.5 0.1 pad_add_fusion.pos_ref
  57.6 6.9 %all-to-all-done.1.deg_ref = bf16[16,16,256]{2,1,0:T(8,128)(2,1)S(1)} async-done(((bf16[16,16,256]{2,1,0:T(8,128)(2,1)}), bf16[16,16,256]{2,1,0:T(8,128)(2,1)S(1)}, u32[]{:S(2)}, u32[]{:S(2)}) %all-to-all-start.1) | async-done | bytes 131104 | tf_op jit(solution)/shard_map/all_to_all | solution.py:157
  64.5 12.1 %apply.1 = (f32[8,16,256]{2,1,0:T(8,128)S(1)}, f32[8,16,256]{2,1,0:T(8,128)S(1)}, f32[1,256]{1,0:T(1,128)S(1)}) custom-call(s32[2]{0:T(128)S(1)} %pad_add_fusion.pos_ref, bf16[16,16,256]{2,1,0:T(8,128)(2,1)S(1)} %all-to-all-done.1.deg_ref, bf16[16,208,256]{2,1,0:T(8,128)(2,1)S(1)} %all-to-all-done.t_ref, bf16[16,4096,256]{2,1,0:T(8,128)(2,1)} %get-tuple-element.16.b_ref), custom_call_target="tpu_custom_call" | custom-call | tf_op jit(solution)/shard_map/apply/pallas_call | solution.py:202
  76.6 1.9 %collective-permute-start.9 = (f32[8,16,256]{2,1,0:T(8,128)S(1)}, f32[8,16,256]{2,1,0:T(8,128)S(1)}, u32[]{:S(2)}, u32[]{:S(2)}) collective-permute-start(f32[8,16,256]{2,1,0:T(8,128)S(1)} %get-tuple-element.18), channel_id=1, source_target_pairs={{0,8},{8,0},{1,9},{9,1},{2,10},{10,2},{3,11},{11,3},{4,12},{12,4},... | collective-permute-start | bytes 393224 | tf_op jit(solution)/shard_map/ppermute | solution.py:165
  78.5 1.0 collective-permute-done.9
  79.5 14.4 %all_to_all.20.p_ref = f32[8,16,256]{2,1,0:T(8,128)S(1)} all-to-all(f32[8,16,256]{2,1,0:T(8,128)S(1)} %add.14), channel_id=1, replica_groups=mesh['xl'=2,'z'=8,'core'=2,'y'=4,'xh'=2] {'z'}, dimensions={0} | all-to-all | bytes 262144 | tf_op jit(solution)/shard_map/all_to_all | solution.py:157
  93.9 0.3 project.1
  94.2 2.1 %collective-permute-start.10 = (f32[2,128]{1,0:T(2,128)S(1)}, f32[2,128]{1,0:T(2,128)S(1)}, u32[]{:S(2)}, u32[]{:S(2)}) collective-permute-start(f32[2,128]{1,0:T(2,128)S(1)} %get-tuple-element.20), channel_id=1, source_target_pairs={{0,8},{8,0},{1,9},{9,1},{2,10},{10,2},{3,11},{11,3},{4,12},{12,4},... | collective-permute-start | bytes 3080 | tf_op jit(solution)/shard_map/ppermute | solution.py:165
  96.3 0.8 collective-permute-done.10
  97.2 16.7 %all_to_all.21.gram_ref = f32[128,2,128]{2,1,0:T(2,128)S(1)} all-to-all(f32[128,2,128]{2,1,0:T(2,128)S(1)} %broadcast_in_dim.3), channel_id=1, replica_groups=mesh['xl'=2,'z'=8,'core'=2,'y'=4,'xh'=2] {'xl','z','y','xh'}, dimensions={0} | all-to-all | bytes 262144 | tf_op jit(solution)/shard_map/all_to_all | solution.py:157
  113.9 2.3 %finish.1 = (f32[16,256]{1,0:T(8,128)}, f32[16,16]{1,0:T(8,128)}) custom-call(f32[128,2,128]{2,1,0:T(2,128)S(1)} %all_to_all.21.gram_ref, f32[16,256]{1,0:T(8,128)S(1)} %get-tuple-element.21.q_ref), custom_call_target="tpu_custom_call" | custom-call | tf_op jit(solution)/shard_map/finish/pallas_call | solution.py:224
  (5 shorter events, 0.1 us)
Async XLA Ops:
  2.9 7.7 %copy-start = (bf16[192,256]{1,0:T(8,128)(2,1)S(1)}, bf16[192,256]{1,0:T(8,128)(2,1)}, u32[]{:S(2)}) copy-start(bf16[192,256]{1,0:T(8,128)(2,1)} %get-tuple-element.14) | copy-start | bytes 294916
  2.9 32.2 %all-to-all-start = ((bf16[16,208,256]{2,1,0:T(8,128)(2,1)}), bf16[16,208,256]{2,1,0:T(8,128)(2,1)S(1)}, u32[]{:S(2)}, u32[]{:S(2)}) async-start(bf16[16,208,256]{2,1,0:T(8,128)(2,1)} %get-tuple-element.13), calls=%async_computation | async-start | bytes 3407872 | tf_op jit(solution)/shard_map/all_to_all | solution.py:157
  10.6 2.0 %collective-permute-start = (bf16[192,256]{1,0:T(8,128)(2,1)S(1)}, bf16[192,256]{1,0:T(8,128)(2,1)S(1)}, u32[]{:S(2)}, u32[]{:S(2)}) collective-permute-start(bf16[192,256]{1,0:T(8,128)(2,1)S(1)} %copy-done), channel_id=1, source_target_pairs={{0,8},{8,0},{1,9},{9,1},{2,10},{10,2},{3,11},{11,3},{4,12},{12,4},... | collective-permute-start | bytes 294920 | tf_op jit(solution)/shard_map/ppermute | solution.py:165
  12.6 10.8 %collective-permute-start.3 = (bf16[2,192,256]{2,1,0:T(8,128)(2,1)S(1)}, bf16[2,192,256]{2,1,0:T(8,128)(2,1)S(1)}, u32[]{:S(2)}, u32[]{:S(2)}) collective-permute-start(bf16[2,192,256]{2,1,0:T(8,128)(2,1)S(1)} %pad_maximum_fusion.refs_0_), channel_id=1, source_target_pairs={{0,32},{8,104},{16,48},{24,120},{32,64},{40,8},{48,80},{56,24},{64... | collective-permute-start | bytes 589832 | tf_op jit(solution)/shard_map/ppermute | solution.py:172
  18.7 8.9 %collective-permute-start.1 = (bf16[2,192,256]{2,1,0:T(8,128)(2,1)S(1)}, bf16[2,192,256]{2,1,0:T(8,128)(2,1)S(1)}, u32[]{:S(2)}, u32[]{:S(2)}) collective-permute-start(bf16[2,192,256]{2,1,0:T(8,128)(2,1)S(1)} %pad_maximum_fusion.refs_0_), channel_id=1, source_target_pairs={{0,16},{8,120},{16,32},{24,8},{32,48},{40,24},{48,64},{56,40},{64,... | collective-permute-start | bytes 589832 | tf_op jit(solution)/shard_map/ppermute | solution.py:172
  23.5 4.9 %collective-permute-start.5 = (bf16[2,192,256]{2,1,0:T(8,128)(2,1)S(1)}, bf16[2,192,256]{2,1,0:T(8,128)(2,1)S(1)}, u32[]{:S(2)}, u32[]{:S(2)}) collective-permute-start(bf16[2,192,256]{2,1,0:T(8,128)(2,1)S(1)} %collective-permute-done.3.refs_3_), channel_id=1, source_target_pairs={{0,16},{8,120},{16,32},{24,8},{32,48},{40,24},{48,64},{56,40},{64,... | collective-permute-start | bytes 589832 | tf_op jit(solution)/shard_map/ppermute | solution.py:172
  25.7 5.8 %collective-permute-start.7 = (bf16[192,256]{1,0:T(8,128)(2,1)S(1)}, bf16[192,256]{1,0:T(8,128)(2,1)S(1)}, u32[]{:S(2)}, u32[]{:S(2)}) collective-permute-start(bf16[192,256]{1,0:T(8,128)(2,1)S(1)} %slice_bitcast_fusion), channel_id=1, source_target_pairs={{0,32},{8,104},{16,48},{24,120},{32,64},{40,8},{48,80},{56,24},{64... | collective-permute-start | bytes 294920 | tf_op jit(solution)/shard_map/ppermute | solution.py:172
  27.7 7.4 %collective-permute-start.4 = (bf16[2,192,256]{2,1,0:T(8,128)(2,1)S(1)}, bf16[2,192,256]{2,1,0:T(8,128)(2,1)S(1)}, u32[]{:S(2)}, u32[]{:S(2)}) collective-permute-start(bf16[2,192,256]{2,1,0:T(8,128)(2,1)S(1)} %collective-permute-done.3.refs_3_), channel_id=1, source_target_pairs={{0,8},{8,0},{1,9},{9,1},{2,10},{10,2},{3,11},{11,3},{4,12},{12,4},... | collective-permute-start | bytes 589832 | tf_op jit(solution)/shard_map/ppermute | solution.py:165
  27.7 7.4 %collective-permute-start.2 = (bf16[2,192,256]{2,1,0:T(8,128)(2,1)S(1)}, bf16[2,192,256]{2,1,0:T(8,128)(2,1)S(1)}, u32[]{:S(2)}, u32[]{:S(2)}) collective-permute-start(bf16[2,192,256]{2,1,0:T(8,128)(2,1)S(1)} %collective-permute-done.1.refs_1_), channel_id=1, source_target_pairs={{0,8},{8,0},{1,9},{9,1},{2,10},{10,2},{3,11},{11,3},{4,12},{12,4},... | collective-permute-start | bytes 589832 | tf_op jit(solution)/shard_map/ppermute | solution.py:165
  28.3 6.7 %collective-permute-start.6 = (bf16[2,192,256]{2,1,0:T(8,128)(2,1)S(1)}, bf16[2,192,256]{2,1,0:T(8,128)(2,1)S(1)}, u32[]{:S(2)}, u32[]{:S(2)}) collective-permute-start(bf16[2,192,256]{2,1,0:T(8,128)(2,1)S(1)} %collective-permute-done.5.refs_5_), channel_id=1, source_target_pairs={{0,8},{8,0},{1,9},{9,1},{2,10},{10,2},{3,11},{11,3},{4,12},{12,4},... | collective-permute-start | bytes 589832 | tf_op jit(solution)/shard_map/ppermute | solution.py:165
  31.5 3.5 %collective-permute-start.8 = (bf16[192,256]{1,0:T(8,128)(2,1)S(1)}, bf16[192,256]{1,0:T(8,128)(2,1)S(1)}, u32[]{:S(2)}, u32[]{:S(2)}) collective-permute-start(bf16[192,256]{1,0:T(8,128)(2,1)S(1)} %collective-permute-done.7.refs_7_), channel_id=1, source_target_pairs={{0,8},{8,0},{1,9},{9,1},{2,10},{10,2},{3,11},{11,3},{4,12},{12,4},... | collective-permute-start | bytes 294920 | tf_op jit(solution)/shard_map/ppermute | solution.py:165
  50.6 13.9 %all-to-all-start.1 = ((bf16[16,16,256]{2,1,0:T(8,128)(2,1)}), bf16[16,16,256]{2,1,0:T(8,128)(2,1)S(1)}, u32[]{:S(2)}, u32[]{:S(2)}) async-start(bf16[16,16,256]{2,1,0:T(8,128)(2,1)} %get-tuple-element.15), calls=%async_computation.1 | async-start | bytes 262144 | tf_op jit(solution)/shard_map/all_to_all | solution.py:157
  76.6 2.9 %collective-permute-start.9 = (f32[8,16,256]{2,1,0:T(8,128)S(1)}, f32[8,16,256]{2,1,0:T(8,128)S(1)}, u32[]{:S(2)}, u32[]{:S(2)}) collective-permute-start(f32[8,16,256]{2,1,0:T(8,128)S(1)} %get-tuple-element.18), channel_id=1, source_target_pairs={{0,8},{8,0},{1,9},{9,1},{2,10},{10,2},{3,11},{11,3},{4,12},{12,4},... | collective-permute-start | bytes 393224 | tf_op jit(solution)/shard_map/ppermute | solution.py:165
  94.2 3.0 %collective-permute-start.10 = (f32[2,128]{1,0:T(2,128)S(1)}, f32[2,128]{1,0:T(2,128)S(1)}, u32[]{:S(2)}, u32[]{:S(2)}) collective-permute-start(f32[2,128]{1,0:T(2,128)S(1)} %get-tuple-element.20), channel_id=1, source_target_pairs={{0,8},{8,0},{1,9},{9,1},{2,10},{10,2},{3,11},{11,3},{4,12},{12,4},... | collective-permute-start | bytes 3080 | tf_op jit(solution)/shard_map/ppermute | solution.py:165

commit v15 on v14

--- a/solution.py
+++ b/solution.py
@@ -56,7 +56,7 @@
 
 def affinity_kernel(pos_ref, t_ref, *refs):
     pairs, lone = refs[0:7], refs[7:9]
-    b_ref, deg_ref, s_ref, sum_ref = refs[9:13]
+    b_ref, deg_ref, s_ref, sum_ref, done_ref, sem_ref = refs[9:15]
     z, core = pos_ref[0], pos_ref[1]
     step = pl.program_id(0)
 
@@ -76,14 +76,21 @@
         place(z + 4, core, lone[0][...])
         place(z + 4, 1 - core, lone[1][...])
 
+    def store(turn, j):
+        slot = lax.rem(turn, 2) * 2 + j
+        return pltpu.make_async_copy(done_ref.at[slot], b_ref.at[turn * 2 + j], sem_ref.at[slot])
+
     for j in range(2):
+        pl.when(step >= 2)(lambda: store(step - 2, j).wait())
+        slot = lax.rem(step, 2) * 2 + j
         piece = t_ref[step * 2 + j, 0:DIM, :]
         total = jnp.zeros((8, SEG), F32)
         for r in range(NR):
             score = jnp.dot(s_ref[r], piece, preferred_element_type=F32)
             tile = jnp.exp2(score * SCALE)
             total = total + jnp.sum(tile.reshape(SEG // 8, 8, SEG), axis=0)
-            b_ref[j, r * SEG : (r + 1) * SEG, :] = tile.astype(BF16)
+            done_ref[slot, r * SEG : (r + 1) * SEG, :] = tile.astype(BF16)
+        store(step, j).start()
         sums = jnp.sum(total, axis=0, keepdims=True) * UNSCALE
         sum_ref[pl.ds(step * 2 + j, 1), :] = sums
 
@@ -91,6 +98,9 @@
     def _():
         for k in range(NC):
             deg_ref[k] = sum_ref[...].astype(BF16)
+        for turn in (NC // 2 - 2, NC // 2 - 1):
+            for j in range(2):
+                store(turn, j).wait()
 
 
 def apply_kernel(pos_ref, deg_ref, t_ref, b_ref, mine_ref, other_ref, own_ref, root_ref, held_ref, sem_ref):
@@ -188,10 +198,15 @@
     block, degree = pl.pallas_call(
         affinity_kernel,
         grid=(NC // 2,),
-        out_shape=(shape(NC, NR * SEG, SEG, dtype=BF16), shape(NC, NC, SEG, dtype=BF16)),
+        out_shape=(pltpu.HBM((NC, NR * SEG, SEG), BF16), shape(NC, NC, SEG, dtype=BF16)),
         in_specs=[smem()] + [vmem()] * 10,
-        out_specs=(pl.BlockSpec((2, NR * SEG, SEG), lambda i: (i, 0, 0)), vmem()),
-        scratch_shapes=[pltpu.VMEM((NR, SEG, DIM), BF16), pltpu.VMEM((NC, SEG), F32)],
+        out_specs=(pl.BlockSpec(memory_space=pl.ANY), vmem()),
+        scratch_shapes=[
+            pltpu.VMEM((NR, SEG, DIM), BF16),
+            pltpu.VMEM((NC, SEG), F32),
+            pltpu.VMEM((4, NR * SEG, SEG), BF16),
+            pltpu.SemaphoreType.DMA((4,)),
+        ],
         compiler_params=params(32),
         cost_estimate=pl.CostEstimate(
             flops=2 * 256 * 4096 * 4096, transcendentals=4096 * 4096, bytes_accessed=1 << 25

time: 117 us -> 116 us (level)
  no operation moved by 1% of the time
where the time goes in v15:
time: 116 us
  starting transfers between devices  36.5 us (31%)
  Pallas kernels  31.8 us (27%)
  blocking collectives  31.1 us (27%)
  waiting for transfers between devices  15.2 us (13%)
    all_to_all x2, blocking collectives, to_all(): return lax.all_to_all(copies, axes, split_axis=0, concat_axis=0, tiled=True)  31.1 us
    pallas_call x1, Pallas kernels, per_device(): pl.pallas_call(affinity_kernel, grid=(NC // 2,), out_shape=(pltpu.HBM((NC...  14.8 us
    all_to_all x2, starting transfers between devices, to_all(): return lax.all_to_all(copies, axes, split_axis=0, concat_axis=0, tiled=True)  14.6 us
    pallas_call x1, Pallas kernels, per_device(): pl.pallas_call(apply_kernel, out_shape=(shape(HALF, VEC, SEG), shape(HALF...  12.1 us
    ppermute x4, starting transfers between devices, along(): return lax.ppermute(a, ROWS, turns)  11 us
    ppermute x7, starting transfers between devices, across(): return lax.ppermute(a, 'core', [(0, 1), (1, 0)])  10.8 us
    all_to_all x2, waiting for transfers between devices, to_all(): return lax.all_to_all(copies, axes, split_axis=0, concat_axis=0, tiled=True)  6.92 us
    ppermute x4, waiting for transfers between devices, along(): return lax.ppermute(a, ROWS, turns)  4.65 us
  transfers between devices with their start and end apart: 13, of which 9 were waited for; matrix products, arithmetic and copies ran while one was open for 0% of the time, Pallas kernels for 0%

profile of v15, /device:TPU:1, one launch (start us, length us, event | category | flops | bytes accessed | tf_op | source)
XLA Modules:
  0.0 115.6 jit_solution(17947982254349877249)
XLA Ops:
  0.6 2.3 %unit.1 = (bf16[192,256]{1,0:T(8,128)(2,1)}, bf16[16,208,256]{2,1,0:T(8,128)(2,1)}) custom-call(bf16[192,256]{1,0:T(8,128)(2,1)} %bitcast.10, f32[16,256]{1,0:T(8,128)} %bitcast.13), custom_call_target="tpu_custom_call" | custom-call | tf_op jit(solution)/shard_map/unit/pallas_call | solution.py:188
  2.9 0.0 copy-start
  2.9 7.7 %all-to-all-start = ((bf16[16,208,256]{2,1,0:T(8,128)(2,1)}), bf16[16,208,256]{2,1,0:T(8,128)(2,1)S(1)}, u32[]{:S(2)}, u32[]{:S(2)}) async-start(bf16[16,208,256]{2,1,0:T(8,128)(2,1)} %get-tuple-element.13), calls=%async_computation | async-start | bytes 3407872 | tf_op jit(solution)/shard_map/all_to_all | solution.py:167
  10.6 0.0 copy-done
  10.6 1.0 collective-permute-start
  11.7 0.9 collective-permute-done
  12.6 6.1 %collective-permute-start.3 = (bf16[2,192,256]{2,1,0:T(8,128)(2,1)S(1)}, bf16[2,192,256]{2,1,0:T(8,128)(2,1)S(1)}, u32[]{:S(2)}, u32[]{:S(2)}) collective-permute-start(bf16[2,192,256]{2,1,0:T(8,128)(2,1)S(1)} %pad_maximum_fusion.refs_0_), channel_id=1, source_target_pairs={{0,32},{8,104},{16,48},{24,120},{32,64},{40,8},{48,80},{56,24},{64... | collective-permute-start | bytes 589832 | tf_op jit(solution)/shard_map/ppermute | solution.py:182
  18.7 0.7 collective-permute-start.1
  19.5 4.0 %collective-permute-done.3.refs_3_ = bf16[2,192,256]{2,1,0:T(8,128)(2,1)S(1)} collective-permute-done((bf16[2,192,256]{2,1,0:T(8,128)(2,1)S(1)}, bf16[2,192,256]{2,1,0:T(8,128)(2,1)S(1)}, u32[]{:S(2)}, u32[]{:S(2)}) %collective-permute-start.3) | collective-permute-done | bytes 196640 | tf_op jit(solution)/shard_map/ppermute | solution.py:182
  23.5 2.3 %collective-permute-start.5 = (bf16[2,192,256]{2,1,0:T(8,128)(2,1)S(1)}, bf16[2,192,256]{2,1,0:T(8,128)(2,1)S(1)}, u32[]{:S(2)}, u32[]{:S(2)}) collective-permute-start(bf16[2,192,256]{2,1,0:T(8,128)(2,1)S(1)} %collective-permute-done.3.refs_3_), channel_id=1, source_target_pairs={{0,16},{8,120},{16,32},{24,8},{32,48},{40,24},{48,64},{56,40},{64,... | collective-permute-start | bytes 589832 | tf_op jit(solution)/shard_map/ppermute | solution.py:182
  25.7 1.9 %collective-permute-start.7 = (bf16[192,256]{1,0:T(8,128)(2,1)S(1)}, bf16[192,256]{1,0:T(8,128)(2,1)S(1)}, u32[]{:S(2)}, u32[]{:S(2)}) collective-permute-start(bf16[192,256]{1,0:T(8,128)(2,1)S(1)} %slice_bitcast_fusion), channel_id=1, source_target_pairs={{0,32},{8,104},{16,48},{24,120},{32,64},{40,8},{48,80},{56,24},{64... | collective-permute-start | bytes 294920 | tf_op jit(solution)/shard_map/ppermute | solution.py:182
  27.7 0.0 collective-permute-start.4
  27.7 0.0 collective-permute-done.1.refs_1_
  27.7 0.5 collective-permute-start.2
  28.2 0.1 collective-permute-done.5.refs_5_
  28.3 2.7 %collective-permute-start.6 = (bf16[2,192,256]{2,1,0:T(8,128)(2,1)S(1)}, bf16[2,192,256]{2,1,0:T(8,128)(2,1)S(1)}, u32[]{:S(2)}, u32[]{:S(2)}) collective-permute-start(bf16[2,192,256]{2,1,0:T(8,128)(2,1)S(1)} %collective-permute-done.5.refs_5_), channel_id=1, source_target_pairs={{0,8},{8,0},{1,9},{9,1},{2,10},{10,2},{3,11},{11,3},{4,12},{12,4},... | collective-permute-start | bytes 589832 | tf_op jit(solution)/shard_map/ppermute | solution.py:175
  31.0 0.5 collective-permute-done.7.refs_7_
  31.5 2.6 %collective-permute-start.8 = (bf16[192,256]{1,0:T(8,128)(2,1)S(1)}, bf16[192,256]{1,0:T(8,128)(2,1)S(1)}, u32[]{:S(2)}, u32[]{:S(2)}) collective-permute-start(bf16[192,256]{1,0:T(8,128)(2,1)S(1)} %collective-permute-done.7.refs_7_), channel_id=1, source_target_pairs={{0,8},{8,0},{1,9},{9,1},{2,10},{10,2},{3,11},{11,3},{4,12},{12,4},... | collective-permute-start | bytes 294920 | tf_op jit(solution)/shard_map/ppermute | solution.py:175
  34.1 0.1 pad_add_fusion.1.pos_ref
  34.2 0.9 collective-permute-done.8.refs_8_
  35.1 0.0 collective-permute-done.4.refs_4_
  35.1 0.0 collective-permute-done.2.refs_2_
  35.1 0.0 collective-permute-done.6.refs_6_
  35.1 0.1 all-to-all-done.t_ref
  35.1 14.8 %affinity.1 = (bf16[16,4096,256]{2,1,0:T(8,128)(2,1)}, bf16[16,16,256]{2,1,0:T(8,128)(2,1)}) custom-call(s32[2]{0:T(128)S(1)} %pad_add_fusion.1.pos_ref, bf16[16,208,256]{2,1,0:T(8,128)(2,1)S(1)} %all-to-all-done.t_ref, bf16[2,192,256]{2,1,0:T(8,128)(2,1)S(1)} %pad_maximum_fusion.refs_0_, bf16[2,192,256]{2,1,0:T(8,128)(2,1)S(1)} %collective-permute-done.1.refs_1_, ...), custom_call_target="tpu_custom_call" | custom-call | flops 8589934592 | bytes 33554432 | tf_op jit(solution)/shard_map/affinity/pallas_call | solution.py:198
  50.0 6.9 %all-to-all-start.1 = ((bf16[16,16,256]{2,1,0:T(8,128)(2,1)}), bf16[16,16,256]{2,1,0:T(8,128)(2,1)S(1)}, u32[]{:S(2)}, u32[]{:S(2)}) async-start(bf16[16,16,256]{2,1,0:T(8,128)(2,1)} %get-tuple-element.15), calls=%async_computation.1 | async-start | bytes 262144 | tf_op jit(solution)/shard_map/all_to_all | solution.py:167
  56.9 0.1 pad_add_fusion.pos_ref
  57.0 6.9 %all-to-all-done.1.deg_ref = bf16[16,16,256]{2,1,0:T(8,128)(2,1)S(1)} async-done(((bf16[16,16,256]{2,1,0:T(8,128)(2,1)}), bf16[16,16,256]{2,1,0:T(8,128)(2,1)S(1)}, u32[]{:S(2)}, u32[]{:S(2)}) %all-to-all-start.1) | async-done | bytes 131104 | tf_op jit(solution)/shard_map/all_to_all | solution.py:167
  63.8 12.1 %apply.1 = (f32[8,16,256]{2,1,0:T(8,128)S(1)}, f32[8,16,256]{2,1,0:T(8,128)S(1)}, f32[1,256]{1,0:T(1,128)S(1)}) custom-call(s32[2]{0:T(128)S(1)} %pad_add_fusion.pos_ref, bf16[16,16,256]{2,1,0:T(8,128)(2,1)S(1)} %all-to-all-done.1.deg_ref, bf16[16,208,256]{2,1,0:T(8,128)(2,1)S(1)} %all-to-all-done.t_ref, bf16[16,4096,256]{2,1,0:T(8,128)(2,1)} %get-tuple-element.16.b_ref), custom_call_target="tpu_custom_call" | custom-call | tf_op jit(solution)/shard_map/apply/pallas_call | solution.py:217
  75.9 1.9 %collective-permute-start.9 = (f32[8,16,256]{2,1,0:T(8,128)S(1)}, f32[8,16,256]{2,1,0:T(8,128)S(1)}, u32[]{:S(2)}, u32[]{:S(2)}) collective-permute-start(f32[8,16,256]{2,1,0:T(8,128)S(1)} %get-tuple-element.18), channel_id=1, source_target_pairs={{0,8},{8,0},{1,9},{9,1},{2,10},{10,2},{3,11},{11,3},{4,12},{12,4},... | collective-permute-start | bytes 393224 | tf_op jit(solution)/shard_map/ppermute | solution.py:175
  77.8 1.0 collective-permute-done.9
  78.8 14.4 %all_to_all.20.p_ref = f32[8,16,256]{2,1,0:T(8,128)S(1)} all-to-all(f32[8,16,256]{2,1,0:T(8,128)S(1)} %add.14), channel_id=1, replica_groups=mesh['xl'=2,'z'=8,'core'=2,'y'=4,'xh'=2] {'z'}, dimensions={0} | all-to-all | bytes 262144 | tf_op jit(solution)/shard_map/all_to_all | solution.py:167
  93.3 0.3 project.1
  93.6 2.1 %collective-permute-start.10 = (f32[2,128]{1,0:T(2,128)S(1)}, f32[2,128]{1,0:T(2,128)S(1)}, u32[]{:S(2)}, u32[]{:S(2)}) collective-permute-start(f32[2,128]{1,0:T(2,128)S(1)} %get-tuple-element.20), channel_id=1, source_target_pairs={{0,8},{8,0},{1,9},{9,1},{2,10},{10,2},{3,11},{11,3},{4,12},{12,4},... | collective-permute-start | bytes 3080 | tf_op jit(solution)/shard_map/ppermute | solution.py:175
  95.7 0.8 collective-permute-done.10
  96.6 16.7 %all_to_all.21.gram_ref = f32[128,2,128]{2,1,0:T(2,128)S(1)} all-to-all(f32[128,2,128]{2,1,0:T(2,128)S(1)} %broadcast_in_dim.3), channel_id=1, replica_groups=mesh['xl'=2,'z'=8,'core'=2,'y'=4,'xh'=2] {'xl','z','y','xh'}, dimensions={0} | all-to-all | bytes 262144 | tf_op jit(solution)/shard_map/all_to_all | solution.py:167
  113.3 2.3 %finish.1 = (f32[16,256]{1,0:T(8,128)}, f32[16,16]{1,0:T(8,128)}) custom-call(f32[128,2,128]{2,1,0:T(2,128)S(1)} %all_to_all.21.gram_ref, f32[16,256]{1,0:T(8,128)S(1)} %get-tuple-element.21.q_ref), custom_call_target="tpu_custom_call" | custom-call | tf_op jit(solution)/shard_map/finish/pallas_call | solution.py:239
  (5 shorter events, 0.1 us)
Async XLA Ops:
  2.9 7.7 %copy-start = (bf16[192,256]{1,0:T(8,128)(2,1)S(1)}, bf16[192,256]{1,0:T(8,128)(2,1)}, u32[]{:S(2)}) copy-start(bf16[192,256]{1,0:T(8,128)(2,1)} %get-tuple-element.14) | copy-start | bytes 294916
  2.9 32.2 %all-to-all-start = ((bf16[16,208,256]{2,1,0:T(8,128)(2,1)}), bf16[16,208,256]{2,1,0:T(8,128)(2,1)S(1)}, u32[]{:S(2)}, u32[]{:S(2)}) async-start(bf16[16,208,256]{2,1,0:T(8,128)(2,1)} %get-tuple-element.13), calls=%async_computation | async-start | bytes 3407872 | tf_op jit(solution)/shard_map/all_to_all | solution.py:167
  10.6 2.0 %collective-permute-start = (bf16[192,256]{1,0:T(8,128)(2,1)S(1)}, bf16[192,256]{1,0:T(8,128)(2,1)S(1)}, u32[]{:S(2)}, u32[]{:S(2)}) collective-permute-start(bf16[192,256]{1,0:T(8,128)(2,1)S(1)} %copy-done), channel_id=1, source_target_pairs={{0,8},{8,0},{1,9},{9,1},{2,10},{10,2},{3,11},{11,3},{4,12},{12,4},... | collective-permute-start | bytes 294920 | tf_op jit(solution)/shard_map/ppermute | solution.py:175
  12.6 10.8 %collective-permute-start.3 = (bf16[2,192,256]{2,1,0:T(8,128)(2,1)S(1)}, bf16[2,192,256]{2,1,0:T(8,128)(2,1)S(1)}, u32[]{:S(2)}, u32[]{:S(2)}) collective-permute-start(bf16[2,192,256]{2,1,0:T(8,128)(2,1)S(1)} %pad_maximum_fusion.refs_0_), channel_id=1, source_target_pairs={{0,32},{8,104},{16,48},{24,120},{32,64},{40,8},{48,80},{56,24},{64... | collective-permute-start | bytes 589832 | tf_op jit(solution)/shard_map/ppermute | solution.py:182
  18.7 8.9 %collective-permute-start.1 = (bf16[2,192,256]{2,1,0:T(8,128)(2,1)S(1)}, bf16[2,192,256]{2,1,0:T(8,128)(2,1)S(1)}, u32[]{:S(2)}, u32[]{:S(2)}) collective-permute-start(bf16[2,192,256]{2,1,0:T(8,128)(2,1)S(1)} %pad_maximum_fusion.refs_0_), channel_id=1, source_target_pairs={{0,16},{8,120},{16,32},{24,8},{32,48},{40,24},{48,64},{56,40},{64,... | collective-permute-start | bytes 589832 | tf_op jit(solution)/shard_map/ppermute | solution.py:182
  23.5 4.9 %collective-permute-start.5 = (bf16[2,192,256]{2,1,0:T(8,128)(2,1)S(1)}, bf16[2,192,256]{2,1,0:T(8,128)(2,1)S(1)}, u32[]{:S(2)}, u32[]{:S(2)}) collective-permute-start(bf16[2,192,256]{2,1,0:T(8,128)(2,1)S(1)} %collective-permute-done.3.refs_3_), channel_id=1, source_target_pairs={{0,16},{8,120},{16,32},{24,8},{32,48},{40,24},{48,64},{56,40},{64,... | collective-permute-start | bytes 589832 | tf_op jit(solution)/shard_map/ppermute | solution.py:182
  25.7 5.8 %collective-permute-start.7 = (bf16[192,256]{1,0:T(8,128)(2,1)S(1)}, bf16[192,256]{1,0:T(8,128)(2,1)S(1)}, u32[]{:S(2)}, u32[]{:S(2)}) collective-permute-start(bf16[192,256]{1,0:T(8,128)(2,1)S(1)} %slice_bitcast_fusion), channel_id=1, source_target_pairs={{0,32},{8,104},{16,48},{24,120},{32,64},{40,8},{48,80},{56,24},{64... | collective-permute-start | bytes 294920 | tf_op jit(solution)/shard_map/ppermute | solution.py:182
  27.7 7.4 %collective-permute-start.4 = (bf16[2,192,256]{2,1,0:T(8,128)(2,1)S(1)}, bf16[2,192,256]{2,1,0:T(8,128)(2,1)S(1)}, u32[]{:S(2)}, u32[]{:S(2)}) collective-permute-start(bf16[2,192,256]{2,1,0:T(8,128)(2,1)S(1)} %collective-permute-done.3.refs_3_), channel_id=1, source_target_pairs={{0,8},{8,0},{1,9},{9,1},{2,10},{10,2},{3,11},{11,3},{4,12},{12,4},... | collective-permute-start | bytes 589832 | tf_op jit(solution)/shard_map/ppermute | solution.py:175
  27.7 7.4 %collective-permute-start.2 = (bf16[2,192,256]{2,1,0:T(8,128)(2,1)S(1)}, bf16[2,192,256]{2,1,0:T(8,128)(2,1)S(1)}, u32[]{:S(2)}, u32[]{:S(2)}) collective-permute-start(bf16[2,192,256]{2,1,0:T(8,128)(2,1)S(1)} %collective-permute-done.1.refs_1_), channel_id=1, source_target_pairs={{0,8},{8,0},{1,9},{9,1},{2,10},{10,2},{3,11},{11,3},{4,12},{12,4},... | collective-permute-start | bytes 589832 | tf_op jit(solution)/shard_map/ppermute | solution.py:175
  28.3 6.7 %collective-permute-start.6 = (bf16[2,192,256]{2,1,0:T(8,128)(2,1)S(1)}, bf16[2,192,256]{2,1,0:T(8,128)(2,1)S(1)}, u32[]{:S(2)}, u32[]{:S(2)}) collective-permute-start(bf16[2,192,256]{2,1,0:T(8,128)(2,1)S(1)} %collective-permute-done.5.refs_5_), channel_id=1, source_target_pairs={{0,8},{8,0},{1,9},{9,1},{2,10},{10,2},{3,11},{11,3},{4,12},{12,4},... | collective-permute-start | bytes 589832 | tf_op jit(solution)/shard_map/ppermute | solution.py:175
  31.5 3.5 %collective-permute-start.8 = (bf16[192,256]{1,0:T(8,128)(2,1)S(1)}, bf16[192,256]{1,0:T(8,128)(2,1)S(1)}, u32[]{:S(2)}, u32[]{:S(2)}) collective-permute-start(bf16[192,256]{1,0:T(8,128)(2,1)S(1)} %collective-permute-done.7.refs_7_), channel_id=1, source_target_pairs={{0,8},{8,0},{1,9},{9,1},{2,10},{10,2},{3,11},{11,3},{4,12},{12,4},... | collective-permute-start | bytes 294920 | tf_op jit(solution)/shard_map/ppermute | solution.py:175
  50.0 13.9 %all-to-all-start.1 = ((bf16[16,16,256]{2,1,0:T(8,128)(2,1)}), bf16[16,16,256]{2,1,0:T(8,128)(2,1)S(1)}, u32[]{:S(2)}, u32[]{:S(2)}) async-start(bf16[16,16,256]{2,1,0:T(8,128)(2,1)} %get-tuple-element.15), calls=%async_computation.1 | async-start | bytes 262144 | tf_op jit(solution)/shard_map/all_to_all | solution.py:167
  75.9 2.9 %collective-permute-start.9 = (f32[8,16,256]{2,1,0:T(8,128)S(1)}, f32[8,16,256]{2,1,0:T(8,128)S(1)}, u32[]{:S(2)}, u32[]{:S(2)}) collective-permute-start(f32[8,16,256]{2,1,0:T(8,128)S(1)} %get-tuple-element.18), channel_id=1, source_target_pairs={{0,8},{8,0},{1,9},{9,1},{2,10},{10,2},{3,11},{11,3},{4,12},{12,4},... | collective-permute-start | bytes 393224 | tf_op jit(solution)/shard_map/ppermute | solution.py:175
  93.6 3.0 %collective-permute-start.10 = (f32[2,128]{1,0:T(2,128)S(1)}, f32[2,128]{1,0:T(2,128)S(1)}, u32[]{:S(2)}, u32[]{:S(2)}) collective-permute-start(f32[2,128]{1,0:T(2,128)S(1)} %get-tuple-element.20), channel_id=1, source_target_pairs={{0,8},{8,0},{1,9},{9,1},{2,10},{10,2},{3,11},{11,3},{4,12},{12,4},... | collective-permute-start | bytes 3080 | tf_op jit(solution)/shard_map/ppermute | solution.py:175

commit v16 on v15

--- a/solution.py
+++ b/solution.py
@@ -18,7 +18,7 @@
 DIM = 192
 VEC = 16
 WIDE = DIM + VEC
-DEPTH = 6
+DEPTH = 4
 SCALE = 14.426950408889634
 UNSCALE = 4.5399929762484854e-05
 EPS = 1e-6

time: 116 us -> 116 us (level)
  no operation moved by 1% of the time
where the time goes in v16:
time: 116 us
  starting transfers between devices  36.5 us (31%)
  Pallas kernels  31.8 us (27%)
  blocking collectives  31.1 us (27%)
  waiting for transfers between devices  15.2 us (13%)
    all_to_all x2, blocking collectives, to_all(): return lax.all_to_all(copies, axes, split_axis=0, concat_axis=0, tiled=True)  31.1 us
    pallas_call x1, Pallas kernels, per_device(): pl.pallas_call(affinity_kernel, grid=(NC // 2,), out_shape=(pltpu.HBM((NC...  14.8 us
    all_to_all x2, starting transfers between devices, to_all(): return lax.all_to_all(copies, axes, split_axis=0, concat_axis=0, tiled=True)  14.6 us
    pallas_call x1, Pallas kernels, per_device(): pl.pallas_call(apply_kernel, out_shape=(shape(HALF, VEC, SEG), shape(HALF...  12.1 us
    ppermute x4, starting transfers between devices, along(): return lax.ppermute(a, ROWS, turns)  11 us
    ppermute x7, starting transfers between devices, across(): return lax.ppermute(a, 'core', [(0, 1), (1, 0)])  10.8 us
    all_to_all x2, waiting for transfers between devices, to_all(): return lax.all_to_all(copies, axes, split_axis=0, concat_axis=0, tiled=True)  6.92 us
    ppermute x4, waiting for transfers between devices, along(): return lax.ppermute(a, ROWS, turns)  4.65 us
  transfers between devices with their start and end apart: 13, of which 9 were waited for; matrix products, arithmetic and copies ran while one was open for 0% of the time, Pallas kernels for 0%

profile of v16, /device:TPU:1, one launch (start us, length us, event | category | flops | bytes accessed | tf_op | source)
XLA Modules:
  0.0 115.6 jit_solution(6282780978905596320)
XLA Ops:
  0.6 2.3 %unit.1 = (bf16[192,256]{1,0:T(8,128)(2,1)}, bf16[16,208,256]{2,1,0:T(8,128)(2,1)}) custom-call(bf16[192,256]{1,0:T(8,128)(2,1)} %bitcast.10, f32[16,256]{1,0:T(8,128)} %bitcast.13), custom_call_target="tpu_custom_call" | custom-call | tf_op jit(solution)/shard_map/unit/pallas_call | solution.py:188
  2.9 0.0 copy-start
  2.9 7.7 %all-to-all-start = ((bf16[16,208,256]{2,1,0:T(8,128)(2,1)}), bf16[16,208,256]{2,1,0:T(8,128)(2,1)S(1)}, u32[]{:S(2)}, u32[]{:S(2)}) async-start(bf16[16,208,256]{2,1,0:T(8,128)(2,1)} %get-tuple-element.13), calls=%async_computation | async-start | bytes 3407872 | tf_op jit(solution)/shard_map/all_to_all | solution.py:167
  10.6 0.0 copy-done
  10.6 1.0 collective-permute-start
  11.7 0.9 collective-permute-done
  12.6 6.1 %collective-permute-start.3 = (bf16[2,192,256]{2,1,0:T(8,128)(2,1)S(1)}, bf16[2,192,256]{2,1,0:T(8,128)(2,1)S(1)}, u32[]{:S(2)}, u32[]{:S(2)}) collective-permute-start(bf16[2,192,256]{2,1,0:T(8,128)(2,1)S(1)} %pad_maximum_fusion.refs_0_), channel_id=1, source_target_pairs={{0,32},{8,104},{16,48},{24,120},{32,64},{40,8},{48,80},{56,24},{64... | collective-permute-start | bytes 589832 | tf_op jit(solution)/shard_map/ppermute | solution.py:182
  18.7 0.7 collective-permute-start.1
  19.5 4.0 %collective-permute-done.3.refs_3_ = bf16[2,192,256]{2,1,0:T(8,128)(2,1)S(1)} collective-permute-done((bf16[2,192,256]{2,1,0:T(8,128)(2,1)S(1)}, bf16[2,192,256]{2,1,0:T(8,128)(2,1)S(1)}, u32[]{:S(2)}, u32[]{:S(2)}) %collective-permute-start.3) | collective-permute-done | bytes 196640 | tf_op jit(solution)/shard_map/ppermute | solution.py:182
  23.5 2.3 %collective-permute-start.5 = (bf16[2,192,256]{2,1,0:T(8,128)(2,1)S(1)}, bf16[2,192,256]{2,1,0:T(8,128)(2,1)S(1)}, u32[]{:S(2)}, u32[]{:S(2)}) collective-permute-start(bf16[2,192,256]{2,1,0:T(8,128)(2,1)S(1)} %collective-permute-done.3.refs_3_), channel_id=1, source_target_pairs={{0,16},{8,120},{16,32},{24,8},{32,48},{40,24},{48,64},{56,40},{64,... | collective-permute-start | bytes 589832 | tf_op jit(solution)/shard_map/ppermute | solution.py:182
  25.7 1.9 %collective-permute-start.7 = (bf16[192,256]{1,0:T(8,128)(2,1)S(1)}, bf16[192,256]{1,0:T(8,128)(2,1)S(1)}, u32[]{:S(2)}, u32[]{:S(2)}) collective-permute-start(bf16[192,256]{1,0:T(8,128)(2,1)S(1)} %slice_bitcast_fusion), channel_id=1, source_target_pairs={{0,32},{8,104},{16,48},{24,120},{32,64},{40,8},{48,80},{56,24},{64... | collective-permute-start | bytes 294920 | tf_op jit(solution)/shard_map/ppermute | solution.py:182
  27.7 0.0 collective-permute-start.4
  27.7 0.0 collective-permute-done.1.refs_1_
  27.7 0.5 collective-permute-start.2
  28.2 0.1 collective-permute-done.5.refs_5_
  28.3 2.7 %collective-permute-start.6 = (bf16[2,192,256]{2,1,0:T(8,128)(2,1)S(1)}, bf16[2,192,256]{2,1,0:T(8,128)(2,1)S(1)}, u32[]{:S(2)}, u32[]{:S(2)}) collective-permute-start(bf16[2,192,256]{2,1,0:T(8,128)(2,1)S(1)} %collective-permute-done.5.refs_5_), channel_id=1, source_target_pairs={{0,8},{8,0},{1,9},{9,1},{2,10},{10,2},{3,11},{11,3},{4,12},{12,4},... | collective-permute-start | bytes 589832 | tf_op jit(solution)/shard_map/ppermute | solution.py:175
  31.0 0.5 collective-permute-done.7.refs_7_
  31.5 2.6 %collective-permute-start.8 = (bf16[192,256]{1,0:T(8,128)(2,1)S(1)}, bf16[192,256]{1,0:T(8,128)(2,1)S(1)}, u32[]{:S(2)}, u32[]{:S(2)}) collective-permute-start(bf16[192,256]{1,0:T(8,128)(2,1)S(1)} %collective-permute-done.7.refs_7_), channel_id=1, source_target_pairs={{0,8},{8,0},{1,9},{9,1},{2,10},{10,2},{3,11},{11,3},{4,12},{12,4},... | collective-permute-start | bytes 294920 | tf_op jit(solution)/shard_map/ppermute | solution.py:175
  34.1 0.1 pad_add_fusion.1.pos_ref
  34.2 0.9 collective-permute-done.8.refs_8_
  35.1 0.0 collective-permute-done.4.refs_4_
  35.1 0.0 collective-permute-done.2.refs_2_
  35.1 0.0 collective-permute-done.6.refs_6_
  35.1 0.1 all-to-all-done.t_ref
  35.1 14.8 %affinity.1 = (bf16[16,4096,256]{2,1,0:T(8,128)(2,1)}, bf16[16,16,256]{2,1,0:T(8,128)(2,1)}) custom-call(s32[2]{0:T(128)S(1)} %pad_add_fusion.1.pos_ref, bf16[16,208,256]{2,1,0:T(8,128)(2,1)S(1)} %all-to-all-done.t_ref, bf16[2,192,256]{2,1,0:T(8,128)(2,1)S(1)} %pad_maximum_fusion.refs_0_, bf16[2,192,256]{2,1,0:T(8,128)(2,1)S(1)} %collective-permute-done.1.refs_1_, ...), custom_call_target="tpu_custom_call" | custom-call | flops 8589934592 | bytes 33554432 | tf_op jit(solution)/shard_map/affinity/pallas_call | solution.py:198
  50.0 6.9 %all-to-all-start.1 = ((bf16[16,16,256]{2,1,0:T(8,128)(2,1)}), bf16[16,16,256]{2,1,0:T(8,128)(2,1)S(1)}, u32[]{:S(2)}, u32[]{:S(2)}) async-start(bf16[16,16,256]{2,1,0:T(8,128)(2,1)} %get-tuple-element.15), calls=%async_computation.1 | async-start | bytes 262144 | tf_op jit(solution)/shard_map/all_to_all | solution.py:167
  56.9 0.1 pad_add_fusion.pos_ref
  57.0 6.9 %all-to-all-done.1.deg_ref = bf16[16,16,256]{2,1,0:T(8,128)(2,1)S(1)} async-done(((bf16[16,16,256]{2,1,0:T(8,128)(2,1)}), bf16[16,16,256]{2,1,0:T(8,128)(2,1)S(1)}, u32[]{:S(2)}, u32[]{:S(2)}) %all-to-all-start.1) | async-done | bytes 131104 | tf_op jit(solution)/shard_map/all_to_all | solution.py:167
  63.8 12.1 %apply.1 = (f32[8,16,256]{2,1,0:T(8,128)S(1)}, f32[8,16,256]{2,1,0:T(8,128)S(1)}, f32[1,256]{1,0:T(1,128)S(1)}) custom-call(s32[2]{0:T(128)S(1)} %pad_add_fusion.pos_ref, bf16[16,16,256]{2,1,0:T(8,128)(2,1)S(1)} %all-to-all-done.1.deg_ref, bf16[16,208,256]{2,1,0:T(8,128)(2,1)S(1)} %all-to-all-done.t_ref, bf16[16,4096,256]{2,1,0:T(8,128)(2,1)} %get-tuple-element.16.b_ref), custom_call_target="tpu_custom_call" | custom-call | tf_op jit(solution)/shard_map/apply/pallas_call | solution.py:217
  75.9 1.9 %collective-permute-start.9 = (f32[8,16,256]{2,1,0:T(8,128)S(1)}, f32[8,16,256]{2,1,0:T(8,128)S(1)}, u32[]{:S(2)}, u32[]{:S(2)}) collective-permute-start(f32[8,16,256]{2,1,0:T(8,128)S(1)} %get-tuple-element.18), channel_id=1, source_target_pairs={{0,8},{8,0},{1,9},{9,1},{2,10},{10,2},{3,11},{11,3},{4,12},{12,4},... | collective-permute-start | bytes 393224 | tf_op jit(solution)/shard_map/ppermute | solution.py:175
  77.8 1.0 collective-permute-done.9
  78.8 14.4 %all_to_all.20.p_ref = f32[8,16,256]{2,1,0:T(8,128)S(1)} all-to-all(f32[8,16,256]{2,1,0:T(8,128)S(1)} %add.14), channel_id=1, replica_groups=mesh['xl'=2,'z'=8,'core'=2,'y'=4,'xh'=2] {'z'}, dimensions={0} | all-to-all | bytes 262144 | tf_op jit(solution)/shard_map/all_to_all | solution.py:167
  93.3 0.3 project.1
  93.6 2.1 %collective-permute-start.10 = (f32[2,128]{1,0:T(2,128)S(1)}, f32[2,128]{1,0:T(2,128)S(1)}, u32[]{:S(2)}, u32[]{:S(2)}) collective-permute-start(f32[2,128]{1,0:T(2,128)S(1)} %get-tuple-element.20), channel_id=1, source_target_pairs={{0,8},{8,0},{1,9},{9,1},{2,10},{10,2},{3,11},{11,3},{4,12},{12,4},... | collective-permute-start | bytes 3080 | tf_op jit(solution)/shard_map/ppermute | solution.py:175
  95.7 0.8 collective-permute-done.10
  96.6 16.7 %all_to_all.21.gram_ref = f32[128,2,128]{2,1,0:T(2,128)S(1)} all-to-all(f32[128,2,128]{2,1,0:T(2,128)S(1)} %broadcast_in_dim.3), channel_id=1, replica_groups=mesh['xl'=2,'z'=8,'core'=2,'y'=4,'xh'=2] {'xl','z','y','xh'}, dimensions={0} | all-to-all | bytes 262144 | tf_op jit(solution)/shard_map/all_to_all | solution.py:167
  113.3 2.3 %finish.1 = (f32[16,256]{1,0:T(8,128)}, f32[16,16]{1,0:T(8,128)}) custom-call(f32[128,2,128]{2,1,0:T(2,128)S(1)} %all_to_all.21.gram_ref, f32[16,256]{1,0:T(8,128)S(1)} %get-tuple-element.21.q_ref), custom_call_target="tpu_custom_call" | custom-call | tf_op jit(solution)/shard_map/finish/pallas_call | solution.py:239
  (5 shorter events, 0.1 us)
Async XLA Ops:
  2.9 7.7 %copy-start = (bf16[192,256]{1,0:T(8,128)(2,1)S(1)}, bf16[192,256]{1,0:T(8,128)(2,1)}, u32[]{:S(2)}) copy-start(bf16[192,256]{1,0:T(8,128)(2,1)} %get-tuple-element.14) | copy-start | bytes 294916
  2.9 32.2 %all-to-all-start = ((bf16[16,208,256]{2,1,0:T(8,128)(2,1)}), bf16[16,208,256]{2,1,0:T(8,128)(2,1)S(1)}, u32[]{:S(2)}, u32[]{:S(2)}) async-start(bf16[16,208,256]{2,1,0:T(8,128)(2,1)} %get-tuple-element.13), calls=%async_computation | async-start | bytes 3407872 | tf_op jit(solution)/shard_map/all_to_all | solution.py:167
  10.6 2.0 %collective-permute-start = (bf16[192,256]{1,0:T(8,128)(2,1)S(1)}, bf16[192,256]{1,0:T(8,128)(2,1)S(1)}, u32[]{:S(2)}, u32[]{:S(2)}) collective-permute-start(bf16[192,256]{1,0:T(8,128)(2,1)S(1)} %copy-done), channel_id=1, source_target_pairs={{0,8},{8,0},{1,9},{9,1},{2,10},{10,2},{3,11},{11,3},{4,12},{12,4},... | collective-permute-start | bytes 294920 | tf_op jit(solution)/shard_map/ppermute | solution.py:175
  12.6 10.8 %collective-permute-start.3 = (bf16[2,192,256]{2,1,0:T(8,128)(2,1)S(1)}, bf16[2,192,256]{2,1,0:T(8,128)(2,1)S(1)}, u32[]{:S(2)}, u32[]{:S(2)}) collective-permute-start(bf16[2,192,256]{2,1,0:T(8,128)(2,1)S(1)} %pad_maximum_fusion.refs_0_), channel_id=1, source_target_pairs={{0,32},{8,104},{16,48},{24,120},{32,64},{40,8},{48,80},{56,24},{64... | collective-permute-start | bytes 589832 | tf_op jit(solution)/shard_map/ppermute | solution.py:182
  18.7 8.9 %collective-permute-start.1 = (bf16[2,192,256]{2,1,0:T(8,128)(2,1)S(1)}, bf16[2,192,256]{2,1,0:T(8,128)(2,1)S(1)}, u32[]{:S(2)}, u32[]{:S(2)}) collective-permute-start(bf16[2,192,256]{2,1,0:T(8,128)(2,1)S(1)} %pad_maximum_fusion.refs_0_), channel_id=1, source_target_pairs={{0,16},{8,120},{16,32},{24,8},{32,48},{40,24},{48,64},{56,40},{64,... | collective-permute-start | bytes 589832 | tf_op jit(solution)/shard_map/ppermute | solution.py:182
  23.5 4.9 %collective-permute-start.5 = (bf16[2,192,256]{2,1,0:T(8,128)(2,1)S(1)}, bf16[2,192,256]{2,1,0:T(8,128)(2,1)S(1)}, u32[]{:S(2)}, u32[]{:S(2)}) collective-permute-start(bf16[2,192,256]{2,1,0:T(8,128)(2,1)S(1)} %collective-permute-done.3.refs_3_), channel_id=1, source_target_pairs={{0,16},{8,120},{16,32},{24,8},{32,48},{40,24},{48,64},{56,40},{64,... | collective-permute-start | bytes 589832 | tf_op jit(solution)/shard_map/ppermute | solution.py:182
  25.7 5.8 %collective-permute-start.7 = (bf16[192,256]{1,0:T(8,128)(2,1)S(1)}, bf16[192,256]{1,0:T(8,128)(2,1)S(1)}, u32[]{:S(2)}, u32[]{:S(2)}) collective-permute-start(bf16[192,256]{1,0:T(8,128)(2,1)S(1)} %slice_bitcast_fusion), channel_id=1, source_target_pairs={{0,32},{8,104},{16,48},{24,120},{32,64},{40,8},{48,80},{56,24},{64... | collective-permute-start | bytes 294920 | tf_op jit(solution)/shard_map/ppermute | solution.py:182
  27.7 7.4 %collective-permute-start.4 = (bf16[2,192,256]{2,1,0:T(8,128)(2,1)S(1)}, bf16[2,192,256]{2,1,0:T(8,128)(2,1)S(1)}, u32[]{:S(2)}, u32[]{:S(2)}) collective-permute-start(bf16[2,192,256]{2,1,0:T(8,128)(2,1)S(1)} %collective-permute-done.3.refs_3_), channel_id=1, source_target_pairs={{0,8},{8,0},{1,9},{9,1},{2,10},{10,2},{3,11},{11,3},{4,12},{12,4},... | collective-permute-start | bytes 589832 | tf_op jit(solution)/shard_map/ppermute | solution.py:175
  27.7 7.4 %collective-permute-start.2 = (bf16[2,192,256]{2,1,0:T(8,128)(2,1)S(1)}, bf16[2,192,256]{2,1,0:T(8,128)(2,1)S(1)}, u32[]{:S(2)}, u32[]{:S(2)}) collective-permute-start(bf16[2,192,256]{2,1,0:T(8,128)(2,1)S(1)} %collective-permute-done.1.refs_1_), channel_id=1, source_target_pairs={{0,8},{8,0},{1,9},{9,1},{2,10},{10,2},{3,11},{11,3},{4,12},{12,4},... | collective-permute-start | bytes 589832 | tf_op jit(solution)/shard_map/ppermute | solution.py:175
  28.3 6.7 %collective-permute-start.6 = (bf16[2,192,256]{2,1,0:T(8,128)(2,1)S(1)}, bf16[2,192,256]{2,1,0:T(8,128)(2,1)S(1)}, u32[]{:S(2)}, u32[]{:S(2)}) collective-permute-start(bf16[2,192,256]{2,1,0:T(8,128)(2,1)S(1)} %collective-permute-done.5.refs_5_), channel_id=1, source_target_pairs={{0,8},{8,0},{1,9},{9,1},{2,10},{10,2},{3,11},{11,3},{4,12},{12,4},... | collective-permute-start | bytes 589832 | tf_op jit(solution)/shard_map/ppermute | solution.py:175
  31.5 3.5 %collective-permute-start.8 = (bf16[192,256]{1,0:T(8,128)(2,1)S(1)}, bf16[192,256]{1,0:T(8,128)(2,1)S(1)}, u32[]{:S(2)}, u32[]{:S(2)}) collective-permute-start(bf16[192,256]{1,0:T(8,128)(2,1)S(1)} %collective-permute-done.7.refs_7_), channel_id=1, source_target_pairs={{0,8},{8,0},{1,9},{9,1},{2,10},{10,2},{3,11},{11,3},{4,12},{12,4},... | collective-permute-start | bytes 294920 | tf_op jit(solution)/shard_map/ppermute | solution.py:175
  50.0 13.9 %all-to-all-start.1 = ((bf16[16,16,256]{2,1,0:T(8,128)(2,1)}), bf16[16,16,256]{2,1,0:T(8,128)(2,1)S(1)}, u32[]{:S(2)}, u32[]{:S(2)}) async-start(bf16[16,16,256]{2,1,0:T(8,128)(2,1)} %get-tuple-element.15), calls=%async_computation.1 | async-start | bytes 262144 | tf_op jit(solution)/shard_map/all_to_all | solution.py:167
  75.9 2.9 %collective-permute-start.9 = (f32[8,16,256]{2,1,0:T(8,128)S(1)}, f32[8,16,256]{2,1,0:T(8,128)S(1)}, u32[]{:S(2)}, u32[]{:S(2)}) collective-permute-start(f32[8,16,256]{2,1,0:T(8,128)S(1)} %get-tuple-element.18), channel_id=1, source_target_pairs={{0,8},{8,0},{1,9},{9,1},{2,10},{10,2},{3,11},{11,3},{4,12},{12,4},... | collective-permute-start | bytes 393224 | tf_op jit(solution)/shard_map/ppermute | solution.py:175
  93.6 3.0 %collective-permute-start.10 = (f32[2,128]{1,0:T(2,128)S(1)}, f32[2,128]{1,0:T(2,128)S(1)}, u32[]{:S(2)}, u32[]{:S(2)}) collective-permute-start(f32[2,128]{1,0:T(2,128)S(1)} %get-tuple-element.20), channel_id=1, source_target_pairs={{0,8},{8,0},{1,9},{9,1},{2,10},{10,2},{3,11},{11,3},{4,12},{12,4},... | collective-permute-start | bytes 3080 | tf_op jit(solution)/shard_map/ppermute | solution.py:175
